TPU v7x, 256 devices: a whole 4x4x8 slice. The times are simulated.
256 devices in a mesh: alpha: 8 (over x, z_lo), beta: 32 (over y, z_hi, core).
Axes of the slice: x: 4, y: 4, z: 8 (z_hi: 4, z_lo: 2; z = z_hi * 2 + z_lo), core: 2. Of those that a mesh axis runs over, the one named last changes fastest.
Arguments:
- coef: bfloat16 [8192, 4096], P('alpha', 'beta'), may hold values from -6 to 6
- beta_ops: bfloat16 [4096, 512], P('beta'), may hold values from -0.25 to 0.25
- beta_cols: int32 [32, 4], P('beta'), may hold values from 0 to 31, as said below
- alpha_ops: bfloat16 [8192, 4096], P('alpha'), may hold values from -0.09375 to 0.09375
- alpha_cols: int32 [8, 4], P('alpha'), may hold values from 0 to 7, as said below
- pair_alpha: bfloat16 [8192, 576], P('alpha'), may hold values from -12 to 12
- pair_beta: bfloat16 [4096, 576], P('beta'), may hold values from -0.09375 to 0.09375
- pair_coupling: bfloat16 [576, 576], replicated, may hold values from -0.25 to 0.25
- denominators: float32 [8192, 4096], P('alpha', 'beta'), may hold values from 0.5 to 4
Outputs:
- sigma_scaled: float32 [8192, 4096], P('alpha', 'beta')
Inputs may be any that keep to these rules, and one draw needn't show every extreme that they name: `beta_cols`: the 4 entries of row j are different and each lies within two blocks of j, counted around the beta blocks cyclically. `alpha_cols`: each entry of row i is i or one of its two neighbours, counted around the alpha blocks cyclically; entries may repeat.
All inputs are finite; a program needn't handle non-finite values.
Results may differ from a plain program's by a relative error of at most 0.013.
Values may be sent and summed in bfloat16 or wider, within the bound.
No kernel may reach another device: no remote copies, remote signals or barrier semaphores. Data moves between devices by JAX's collectives and lax.ppermute only.
A program may use at most 128 MiB of HBM per device.

v0:
```python
import jax
import jax.numpy as jnp
from jax import lax
from jax.sharding import Mesh
from jax.sharding import PartitionSpec as P

BETA = ("beta_0", "beta_1", "beta_2")


def padded(block, sides, width, periodic):
    for axis, dim in sides:
        count = lax.axis_size(axis)
        forward = [(i, i + 1) for i in range(count - 1)]
        if periodic:
            forward.append((count - 1, 0))
        backward = [(target, source) for source, target in forward]
        low = lax.ppermute(
            lax.slice_in_dim(block, block.shape[dim] - width, None, axis=dim), axis, forward
        )
        high = lax.ppermute(lax.slice_in_dim(block, 0, width, axis=dim), axis, backward)
        block = jnp.concatenate([low, block, high], axis=dim)
    return block


def shifted(block, axis, distance):
    devices = range(lax.axis_size(axis))
    route = [((i - distance) % len(devices), i) for i in devices]
    return lax.ppermute(block, axis, route)


def rows_for(lines, peers):
    spare = -len(lines) % peers
    return jnp.pad(lines, [(0, spare)] + [(0, 0)] * (lines.ndim - 1))


def from_everyone(array, axis):
    peers = lax.axis_size(axis)
    return lax.all_to_all(
        jnp.broadcast_to(array[None], (peers, *array.shape)), axis, 0, 0, tiled=True
    )


def joined_along(pieces, dim):
    pieces = jnp.moveaxis(pieces, 0, dim)
    shape = pieces.shape
    return pieces.reshape(*shape[:dim], shape[dim] * shape[dim + 1], *shape[dim + 2 :])


def gathered_by_axis(array, axes, dim):
    far, near = axes
    pieces = from_everyone(from_everyone(array, far), near)
    return joined_along(pieces.swapaxes(0, 1).reshape(-1, *array.shape), dim)


def in_blocks(array, dim, peers):
    before, after = (array.shape[:dim], array.shape[dim + 1 :])
    return jnp.moveaxis(array.reshape(*before, peers, -1, *after), dim, 0)


def sum_at_owner(array, axis, dim):
    peers = lax.axis_size(axis)
    pieces = lax.all_to_all(in_blocks(array, dim, peers), axis, 0, 0, tiled=True)
    return jnp.sum(pieces.astype(jnp.float32), axis=0)


def sum_by_axis(array, axes, dim):
    far, near = axes
    pieces = in_blocks(array, dim, lax.axis_size(far))
    nearer = sum_at_owner(pieces, near, dim + 1)
    arrived = lax.all_to_all(
        nearer.astype(jnp.bfloat16), far, split_axis=0, concat_axis=0, tiled=True
    )
    return arrived.astype(jnp.float32).sum(axis=0)


def nested_sum(array, axes):
    lines = array.reshape(-1, array.shape[-1])
    padded = rows_for(lines, lax.axis_size(axes[0]) * lax.axis_size(axes[1]))
    whole = gathered_by_axis(sum_by_axis(padded, axes, 0).astype(jnp.bfloat16), axes, 0)
    return lax.slice_in_dim(whole, 0, len(lines)).reshape(array.shape).astype(jnp.float32)


def spread_blocks(operator_blocks, listed_cols, block_width, block_count):
    row_count = operator_blocks.shape[0]
    listed = listed_cols.shape[0]
    onehot = (listed_cols[:, None] == jnp.arange(block_count, dtype=jnp.int32)[None, :]).astype(
        jnp.bfloat16
    )
    tile_set = operator_blocks.reshape(row_count, listed, block_width)
    placed = jnp.einsum("rkc,kn->rnc", tile_set, onehot, preferred_element_type=jnp.float32)
    return placed.astype(jnp.bfloat16).reshape(row_count, block_count * block_width)


def local(
    coef,
    beta_ops,
    beta_cols,
    alpha_ops,
    alpha_cols,
    pair_alpha,
    pair_beta,
    pair_coupling,
    denominators,
):
    alpha_width = coef.shape[0]
    beta_width = coef.shape[1]
    beta_count = lax.axis_size(BETA)
    alpha_count = lax.axis_size("alpha")
    beta_slots = (beta_cols[0] - lax.axis_index(BETA) + 2 + beta_count) % beta_count
    beta_near_ops = spread_blocks(beta_ops, beta_slots, beta_width, 5)
    middle = padded(coef, ((BETA, 1),), beta_width, True)
    lowest = shifted(coef, BETA, 2)
    highest = shifted(coef, BETA, -2)
    beta_span = jnp.concatenate([lowest, middle, highest], axis=1)
    same_beta = lax.dot_general(
        beta_span, beta_near_ops, (((1,), (1,)), ((), ())), preferred_element_type=jnp.float32
    )
    alpha_slots = (alpha_cols[0] - lax.axis_index("alpha") + 1 + alpha_count) % alpha_count
    alpha_near = spread_blocks(alpha_ops, alpha_slots, alpha_width, 3)
    alpha_span = padded(coef, (("alpha", 0),), alpha_width, True)
    same_alpha = jnp.dot(alpha_near, alpha_span, preferred_element_type=jnp.float32)
    partial_density = jnp.dot(coef, pair_beta, preferred_element_type=jnp.float32)
    density = nested_sum(
        partial_density.astype(jnp.bfloat16), (("beta_0", "beta_1"), "beta_2")
    ).astype(jnp.bfloat16)
    excited = (
        jnp.dot(density, pair_coupling, preferred_element_type=jnp.float32)
        * pair_alpha.astype(jnp.float32)
    ).astype(jnp.bfloat16)
    mixed = lax.dot_general(
        excited, pair_beta, (((1,), (1,)), ((), ())), preferred_element_type=jnp.float32
    )
    return (same_beta + same_alpha + mixed) / denominators


def solution(mesh):
    finer = Mesh(
        mesh.devices.reshape(mesh.shape["alpha"], 4, 4, 2), ("alpha", "beta_0", "beta_1", "beta_2")
    )
    placed = (
        P("alpha", BETA),
        P(BETA, None),
        P(BETA, None),
        P("alpha", None),
        P("alpha", None),
        P("alpha", None),
        P(BETA, None),
        P(),
        P("alpha", BETA),
    )
    return jax.shard_map(
        local, mesh=finer, in_specs=placed, out_specs=P("alpha", BETA), check_vma=False
    )
```

profile of v0, /device:TPU:1, one launch (start us, length us, event | category | flops | bytes accessed | tf_op | source)
XLA Modules:
  0.0 111.7 jit_solution(6854049084133665321)
XLA Ops:
  0.0 2.5 %collective-permute-start.4 = (bf16[1024,128]{1,0:T(8,128)(2,1)}, bf16[1024,128]{1,0:T(8,128)(2,1)}, u32[]{:S(2)}, u32[]{:S(2)}) collective-permute-start(bf16[1024,128]{1,0:T(8,128)(2,1)} %param.9), channel_id=1, source_target_pairs={{0,32},{32,64},{64,96},{96,128},{128,160},{160,192},{192,224},{224... | collective-permute-start | bytes 786440 | tf_op jit(solution)/shard_map/ppermute | solution.py:17
  2.5 2.3 %collective-permute-start.5 = (bf16[1024,128]{1,0:T(8,128)(2,1)}, bf16[1024,128]{1,0:T(8,128)(2,1)}, u32[]{:S(2)}, u32[]{:S(2)}) collective-permute-start(bf16[1024,128]{1,0:T(8,128)(2,1)} %param.9), channel_id=1, source_target_pairs={{32,0},{64,32},{96,64},{128,96},{160,128},{192,160},{224,192},{0,2... | collective-permute-start | bytes 786440 | tf_op jit(solution)/shard_map/ppermute | solution.py:20
  4.7 3.0 %collective-permute-start = (bf16[1024,128]{1,0:T(8,128)(2,1)}, bf16[1024,128]{1,0:T(8,128)(2,1)}, u32[]{:S(2)}, u32[]{:S(2)}) collective-permute-start(bf16[1024,128]{1,0:T(8,128)(2,1)} %param.9), channel_id=1, source_target_pairs={{30,0},{31,1},{0,2},{1,3},{2,4},{3,5},{4,6},{5,7},{6,8},{7,9},{8,1... | collective-permute-start | bytes 786440 | tf_op jit(solution)/shard_map/ppermute | solution.py:28
  7.7 5.3 %collective-permute-start.1 = (bf16[1024,128]{1,0:T(8,128)(2,1)}, bf16[1024,128]{1,0:T(8,128)(2,1)}, u32[]{:S(2)}, u32[]{:S(2)}) collective-permute-start(bf16[1024,128]{1,0:T(8,128)(2,1)} %param.9), channel_id=1, source_target_pairs={{0,1},{1,2},{2,3},{3,4},{4,5},{5,6},{6,7},{7,8},{8,9},{9,10},{10,1... | collective-permute-start | bytes 786440 | tf_op jit(solution)/shard_map/ppermute | solution.py:17
  13.0 1.5 %convolution_convert_fusion = bf16[1024,576]{0,1:T(8,128)(2,1)S(1)} fusion(bf16[1024,128]{1,0:T(8,128)(2,1)} %param.9, bf16[128,576]{0,1:T(8,128)(2,1)} %param.15), kind=kOutput, calls=%fused_computation.2 | convolution fusion | flops 151584768 | bytes 1589248 | tf_op jit(solution)/shard_map/dot_general | solution.py:122
  14.5 0.7 copy.20
  15.3 6.3 %all_to_all.20 = bf16[2,16,32,576]{3,2,1,0:T(8,128)(2,1)S(1)} all-to-all(bf16[2,16,32,576]{3,2,1,0:T(8,128)(2,1)S(1)} %copy.21), channel_id=1, replica_groups=mesh['alpha'=8,'beta_0'=4,'beta_1'=4,'beta_2'=2] {'beta_2'}, dimensions={0} | all-to-all | bytes 2359296 | tf_op jit(solution)/shard_map/all_to_all | solution.py:62
  21.7 1.3 %reduce_sum.24 = bf16[16,32,576]{2,1,0:T(8,128)(2,1)} reduce(bf16[2,16,32,576]{3,2,1,0:T(8,128)(2,1)S(1)} %all_to_all.20, bf16[]{:T(256)} %constant.56.clone.1), dimensions={0}, to_apply=%region_0.1 | reduce | flops 294912 | bytes 1769474 | tf_op jit(solution)/shard_map/reduce_sum | solution.py:63
  23.0 7.0 %all-to-all-start.1 = ((bf16[16,32,576]{2,1,0:T(8,128)(2,1)}), bf16[16,32,576]{2,1,0:T(8,128)(2,1)S(1)}, u32[]{:S(2)}, u32[]{:S(2)}) async-start(bf16[16,32,576]{2,1,0:T(8,128)(2,1)} %reduce_sum.24), calls=%async_computation.1 | async-start | bytes 1310720 | tf_op jit(solution)/shard_map/all_to_all | solution.py:70
  30.0 14.5 %reshape.58 = bf16[1024,4,1024]{2,1,0:T(4,128)(2,1)} reshape(bf16[1024,4096]{1,0:T(8,128)(2,1)} %param.12) | data formatting | bytes 16777216 | tf_op jit(solution)/shard_map/reshape | solution.py:89
  44.5 9.5 %convert_bitcast_fusion = bf16[1024,3,1024]{2,1,0:T(4,128)(2,1)} fusion(bf16[1024,4,1024]{2,1,0:T(4,128)(2,1)} %reshape.58, s32[4]{0:T(128)S(1)} %and_select_fusion), kind=kOutput, calls=%fused_computation | convolution fusion | flops 28311564 | bytes 14680080 | tf_op jit(solution)/shard_map/rkc,kn->rnc/dot_general | solution.py:90
  54.3 0.9 broadcast_in_dim.4
  55.2 8.9 %all-to-all-start.2 = ((bf16[16,32,576]{2,1,0:T(8,128)(2,1)}), bf16[16,32,576]{2,1,0:T(8,128)(2,1)S(1)}, u32[]{:S(2)}, u32[]{:S(2)}) async-start(bf16[16,32,576]{2,1,0:T(8,128)(2,1)} %broadcast_in_dim.4), calls=%async_computation.2 | async-start | bytes 1310720 | tf_op jit(solution)/shard_map/all_to_all | solution.py:38
  64.1 0.3 fusion.3
  64.7 13.1 %copy.19 = bf16[1024,3,1024]{0,2,1:T(8,128)(2,1)} copy(bf16[1024,3,1024]{2,1,0:T(4,128)(2,1)} %convert_bitcast_fusion) | data formatting | bytes 12582912 | tf_op jit(solution)/shard_map/convert_element_type | solution.py:91
  77.8 5.6 %collective-permute-start.3 = (bf16[1024,128]{1,0:T(8,128)(2,1)S(1)}, bf16[1024,128]{1,0:T(8,128)(2,1)S(1)}, u32[]{:S(2)}, u32[]{:S(2)}) collective-permute-start(bf16[1024,128]{1,0:T(8,128)(2,1)S(1)} %copy-done.1), channel_id=1, source_target_pairs={{2,0},{3,1},{4,2},{5,3},{6,4},{7,5},{8,6},{9,7},{10,8},{11,9},{12,... | collective-permute-start | bytes 786440 | tf_op jit(solution)/shard_map/ppermute | solution.py:28
  83.4 1.0 constant_dynamic-update-slice_fusion.4
  84.4 1.0 constant_dynamic-update-slice_fusion.3
  85.6 7.8 %collective-permute-done.3 = bf16[1024,128]{1,0:T(8,128)(2,1)S(1)} collective-permute-done((bf16[1024,128]{1,0:T(8,128)(2,1)S(1)}, bf16[1024,128]{1,0:T(8,128)(2,1)S(1)}, u32[]{:S(2)}, u32[]{:S(2)}) %collective-permute-start.3) | collective-permute-done | bytes 262176 | tf_op jit(solution)/shard_map/ppermute | solution.py:28
  93.5 5.5 %fusion.4 = f32[1024,128]{1,0:T(8,128)} fusion(bf16[1024,3072]{0,1:T(8,128)(2,1)} %bitcast.31, bf16[1024,128]{1,0:T(8,128)(2,1)} %collective-permute-done.5, bf16[1024,128]{1,0:T(8,128)(2,1)S(1)} %copy-done.1, bf16[1024,128]{1,0:T(8,128)(2,1)} %collective-permute-done.4), kind=kOutput, calls=%fused_computation.9 | convolution fusion | flops 807665664 | bytes 7602176 | tf_op jit(solution)/shard_map/dot_general | solution.py:121
  99.0 4.9 %all_to_all.21 = bf16[2,16,32,576]{3,2,1,0:T(8,128)(2,1)S(1)} all-to-all(bf16[2,16,32,576]{3,2,1,0:T(8,128)(2,1)S(1)} %broadcast_in_dim.5), channel_id=1, replica_groups=mesh['alpha'=8,'beta_0'=4,'beta_1'=4,'beta_2'=2] {'beta_2'}, dimensions={0} | all-to-all | bytes 2359296 | tf_op jit(solution)/shard_map/all_to_all | solution.py:38
  104.0 1.3 %copy.22 = bf16[16,2,32,576]{3,2,1,0:T(8,128)(2,1)} copy(bf16[16,2,32,576]{3,2,0,1:T(8,128)(2,1)S(1)} %bitcast.33) | data formatting | bytes 2359296 | tf_op jit(solution)/shard_map/transpose | solution.py:52
  105.2 4.0 %fusion = f32[1024,128]{1,0:T(8,128)} fusion(bf16[128,576]{0,1:T(8,128)(2,1)S(1)} %copy-done.3, bf16[1024,576]{0,1:T(8,128)(2,1)} %param.14, bf16[1024,576]{1,0:T(8,128)(2,1)} %bitcast.34, bf16[576,576]{1,0:T(8,128)(2,1)S(1)} %copy-done), kind=kOutput, calls=%fused_computation.3 | convolution fusion | flops 832241664 | bytes 3694592 | tf_op jit(solution)/shard_map/dot_general | solution.py:130
  109.2 2.5 %fusion.2 = f32[1024,128]{1,0:T(8,128)} fusion(f32[1024,128]{1,0:T(8,128)S(1)} %copy-done.2, f32[1024,128]{1,0:T(8,128)} %fusion, f32[1024,128]{1,0:T(8,128)} %fusion.4, bf16[1024,640]{1,0:T(8,128)(2,1)S(1)} %constant_dynamic-update-slice_fusion, bf16[128,640]{0,1:T(8,128)(2,1)S(1)} %bitcast.35), kind=kOutput, calls=%fused_computation.6 | convolution fusion | flops 168165376 | bytes 3571712 | tf_op jit(solution)/shard_map/dot_general | solution.py:115
  (32 shorter events, 1.0 us)
Async XLA Ops:
  0.0 105.2 %copy-start = (bf16[576,576]{1,0:T(8,128)(2,1)S(1)}, bf16[576,576]{1,0:T(8,128)(2,1)}, u32[]{:S(2)}) copy-start(bf16[576,576]{1,0:T(8,128)(2,1)} %param.16) | copy-start | bytes 1990660
  0.0 93.4 %collective-permute-start.4 = (bf16[1024,128]{1,0:T(8,128)(2,1)}, bf16[1024,128]{1,0:T(8,128)(2,1)}, u32[]{:S(2)}, u32[]{:S(2)}) collective-permute-start(bf16[1024,128]{1,0:T(8,128)(2,1)} %param.9), channel_id=1, source_target_pairs={{0,32},{32,64},{64,96},{96,128},{128,160},{160,192},{192,224},{224... | collective-permute-start | bytes 786440 | tf_op jit(solution)/shard_map/ppermute | solution.py:17
  2.5 91.0 %collective-permute-start.5 = (bf16[1024,128]{1,0:T(8,128)(2,1)}, bf16[1024,128]{1,0:T(8,128)(2,1)}, u32[]{:S(2)}, u32[]{:S(2)}) collective-permute-start(bf16[1024,128]{1,0:T(8,128)(2,1)} %param.9), channel_id=1, source_target_pairs={{32,0},{64,32},{96,64},{128,96},{160,128},{192,160},{224,192},{0,2... | collective-permute-start | bytes 786440 | tf_op jit(solution)/shard_map/ppermute | solution.py:20
  4.7 73.0 %collective-permute-start = (bf16[1024,128]{1,0:T(8,128)(2,1)}, bf16[1024,128]{1,0:T(8,128)(2,1)}, u32[]{:S(2)}, u32[]{:S(2)}) collective-permute-start(bf16[1024,128]{1,0:T(8,128)(2,1)} %param.9), channel_id=1, source_target_pairs={{30,0},{31,1},{0,2},{1,3},{2,4},{3,5},{4,6},{5,7},{6,8},{7,9},{8,1... | collective-permute-start | bytes 786440 | tf_op jit(solution)/shard_map/ppermute | solution.py:28
  7.7 76.6 %collective-permute-start.1 = (bf16[1024,128]{1,0:T(8,128)(2,1)}, bf16[1024,128]{1,0:T(8,128)(2,1)}, u32[]{:S(2)}, u32[]{:S(2)}) collective-permute-start(bf16[1024,128]{1,0:T(8,128)(2,1)} %param.9), channel_id=1, source_target_pairs={{0,1},{1,2},{2,3},{3,4},{4,5},{5,6},{6,7},{7,8},{8,9},{9,10},{10,1... | collective-permute-start | bytes 786440 | tf_op jit(solution)/shard_map/ppermute | solution.py:17
  13.0 72.5 %collective-permute-start.2 = (bf16[1024,128]{1,0:T(8,128)(2,1)}, bf16[1024,128]{1,0:T(8,128)(2,1)S(1)}, u32[]{:S(2)}, u32[]{:S(2)}) collective-permute-start(bf16[1024,128]{1,0:T(8,128)(2,1)} %param.9), channel_id=1, source_target_pairs={{1,0},{2,1},{3,2},{4,3},{5,4},{6,5},{7,6},{8,7},{9,8},{10,9},{11,1... | collective-permute-start | bytes 786440 | tf_op jit(solution)/shard_map/ppermute | solution.py:20
  23.0 31.3 %all-to-all-start.1 = ((bf16[16,32,576]{2,1,0:T(8,128)(2,1)}), bf16[16,32,576]{2,1,0:T(8,128)(2,1)S(1)}, u32[]{:S(2)}, u32[]{:S(2)}) async-start(bf16[16,32,576]{2,1,0:T(8,128)(2,1)} %reduce_sum.24), calls=%async_computation.1 | async-start | bytes 1310720 | tf_op jit(solution)/shard_map/all_to_all | solution.py:70
  29.9 14.6 %copy-start.5 = (s32[1,4]{1,0:T(1,128)S(1)}, s32[1,4]{1,0:T(1,128)}, u32[]{:S(2)}) copy-start(s32[1,4]{1,0:T(1,128)} %param.13) | copy-start | bytes 52
  44.5 9.5 %copy-start.6 = (s32[1,4]{1,0:T(1,128)S(1)}, s32[1,4]{1,0:T(1,128)}, u32[]{:S(2)}) copy-start(s32[1,4]{1,0:T(1,128)} %param.11) | copy-start | bytes 52
  44.5 9.5 %copy-start.4 = (bf16[128,512]{1,0:T(8,128)(2,1)S(1)}, bf16[128,512]{1,0:T(8,128)(2,1)}, u32[]{:S(2)}) copy-start(bf16[128,512]{1,0:T(8,128)(2,1)} %param.10) | copy-start | bytes 393220
  55.2 43.7 %all-to-all-start.2 = ((bf16[16,32,576]{2,1,0:T(8,128)(2,1)}), bf16[16,32,576]{2,1,0:T(8,128)(2,1)S(1)}, u32[]{:S(2)}, u32[]{:S(2)}) async-start(bf16[16,32,576]{2,1,0:T(8,128)(2,1)} %broadcast_in_dim.4), calls=%async_computation.2 | async-start | bytes 1310720 | tf_op jit(solution)/shard_map/all_to_all | solution.py:38
  64.7 13.1 %copy-start.1 = (bf16[1024,128]{1,0:T(8,128)(2,1)S(1)}, bf16[1024,128]{1,0:T(8,128)(2,1)}, u32[]{:S(2)}) copy-start(bf16[1024,128]{1,0:T(8,128)(2,1)} %param.9) | copy-start | bytes 786436
  77.8 15.6 %collective-permute-start.3 = (bf16[1024,128]{1,0:T(8,128)(2,1)S(1)}, bf16[1024,128]{1,0:T(8,128)(2,1)S(1)}, u32[]{:S(2)}, u32[]{:S(2)}) collective-permute-start(bf16[1024,128]{1,0:T(8,128)(2,1)S(1)} %copy-done.1), channel_id=1, source_target_pairs={{2,0},{3,1},{4,2},{5,3},{6,4},{7,5},{8,6},{9,7},{10,8},{11,9},{12,... | collective-permute-start | bytes 786440 | tf_op jit(solution)/shard_map/ppermute | solution.py:28
  103.9 1.3 %copy-start.3 = (bf16[128,576]{0,1:T(8,128)(2,1)S(1)}, bf16[128,576]{0,1:T(8,128)(2,1)}, u32[]{:S(2)}) copy-start(bf16[128,576]{0,1:T(8,128)(2,1)} %param.15) | copy-start | bytes 442372
  105.2 4.0 %copy-start.2 = (f32[1024,128]{1,0:T(8,128)S(1)}, f32[1024,128]{1,0:T(8,128)}, u32[]{:S(2)}) copy-start(f32[1024,128]{1,0:T(8,128)} %param.17) | copy-start | bytes 1572868
where the time goes:
time: 113 us; the launch traced here: 112 us
  starting transfers between devices  34.4 us (30%)
  local copies, waits for them, and re-layouts  33.2 us (29%)
  matrix products  23.2 us (21%)
  blocking collectives  11.3 us (10%)
  waiting for transfers between devices  8 us (7%)
  other arithmetic  1.44 us (1%)
    reshape x2, local copies, waits for them, and re-layouts, spread_blocks(): tile_set = operator_blocks.reshape(row_count, listed, block_width)  14.6 us
    convert_element_type x2, local copies, waits for them, and re-layouts, spread_blocks(): placed.astype(jnp.bfloat16).reshape(row_count, block_count * block_width)  13.3 us
    dot_general x2, matrix products, spread_blocks(): jnp.einsum('rkc,kn->rnc', tile_set, onehot, preferred_element_type=jnp.fl...  9.78 us
    all_to_all x1, starting transfers between devices, from_everyone(): lax.all_to_all(jnp.broadcast_to(array[None], (peers, *array.shape)), axis...  8.89 us
    ppermute x2, starting transfers between devices, shifted(): return lax.ppermute(block, axis, route)  8.58 us
    ppermute x2, waiting for transfers between devices, shifted(): return lax.ppermute(block, axis, route)  7.81 us
    ppermute x2, starting transfers between devices, padded(): lax.ppermute(lax.slice_in_dim(block, block.shape[dim] - width, None, axis...  7.73 us
    all_to_all x1, starting transfers between devices, sum_by_axis(): lax.all_to_all(nearer.astype(jnp.bfloat16), far, split_axis=0, concat_axi...  6.95 us
  transfers between devices with their start and end apart: 8, of which 2 were waited for; matrix products, arithmetic and copies ran while one was open for 45% of the time, Pallas kernels for 0%

commit v1 on v0

v1 whole, which is shorter than its diff:
```python
import jax
import jax.numpy as jnp
from jax import lax
from jax.experimental import pallas as pl
from jax.experimental.pallas import tpu as pltpu
from jax.sharding import Mesh
from jax.sharding import PartitionSpec as P

ALPHA = ("x", "zl")
BETA = ("y", "zh", "c")
F32 = jnp.float32
BF16 = jnp.bfloat16
SMEM = pl.BlockSpec(memory_space=pltpu.SMEM)
VMEM = pl.BlockSpec(memory_space=pltpu.VMEM)
MIB = 1 << 20


def dot(a, b, dims=((1,), (0,))):
    return lax.dot_general(a, b, (dims, ((), ())), preferred_element_type=F32)


def estimate(flops, moved):
    return pl.CostEstimate(flops=flops, bytes_accessed=moved, transcendentals=0)


def swapped(block, axis, mask):
    count = lax.axis_size(axis)
    return lax.ppermute(block, axis, [(i, i ^ mask) for i in range(count)])


def rotated(block, axis, distance):
    count = lax.axis_size(axis)
    return lax.ppermute(block, axis, [(i, (i + distance) % count) for i in range(count)])


def density_parts(where, own, mate, pair_own, pair_mate):
    pairs = pair_own.shape[0]
    width = own.shape[1]

    def kernel(where_ref, own_ref, mate_ref, po_ref, pm_ref, *outs):
        left = jnp.concatenate([po_ref[...], pm_ref[...]], axis=1)
        for k, out in enumerate(outs):
            rows = pl.ds(pl.multiple_of(where_ref[k] * width, width), width)
            right = jnp.concatenate([own_ref[rows, :], mate_ref[rows, :]], axis=1)
            out[...] = dot(left, right, ((1,), (1,))).astype(BF16)

    return pl.pallas_call(
        kernel,
        out_shape=[jax.ShapeDtypeStruct((pairs, width), BF16)] * 4,
        in_specs=[SMEM] + [VMEM] * 4,
        out_specs=[VMEM] * 4,
        compiler_params=pltpu.CompilerParams(vmem_limit_bytes=16 * MIB),
        cost_estimate=estimate(8 * pairs * width * width * 2, 1 * MIB),
        name="density_parts",
    )(where, own, mate, pair_own, pair_mate)


def excited_block(where, near, far, coupling, pair_alpha):
    pairs, width = near.shape

    def kernel(where_ref, near_ref, far_ref, coupling_ref, pa_ref, out_ref):
        total = near_ref[...].astype(F32) + far_ref[...].astype(F32)
        density = total.T.astype(BF16)
        rows = pl.ds(pl.multiple_of(where_ref[0] * width, width), width)
        scale = pa_ref[:, rows].astype(F32).T
        out_ref[...] = (dot(density, coupling_ref[...]) * scale).astype(BF16)

    return pl.pallas_call(
        kernel,
        out_shape=jax.ShapeDtypeStruct((width, pairs), BF16),
        in_specs=[SMEM] + [VMEM] * 4,
        out_specs=VMEM,
        compiler_params=pltpu.CompilerParams(vmem_limit_bytes=16 * MIB),
        cost_estimate=estimate(2 * pairs * pairs * width, 2 * MIB),
        name="excited_block",
    )(where, near, far, coupling, pair_alpha)


def mixed_parts(blocks, pair_own, pair_mate):
    width, pairs = blocks[0].shape

    def kernel(*refs):
        ins, (po_ref, pm_ref, mine, theirs) = refs[:4], refs[4:]
        right = jnp.concatenate([po_ref[...], pm_ref[...]], axis=1)
        for k, block in enumerate(ins):
            both = dot(block[...], right)
            mine[k] = both[:, :width]
            theirs[k] = both[:, width:].astype(BF16)

    return pl.pallas_call(
        kernel,
        out_shape=[
            jax.ShapeDtypeStruct((4, width, width), F32),
            jax.ShapeDtypeStruct((4, width, width), BF16),
        ],
        in_specs=[VMEM] * 6,
        out_specs=[VMEM] * 2,
        compiler_params=pltpu.CompilerParams(vmem_limit_bytes=16 * MIB),
        cost_estimate=estimate(16 * pairs * width * width, 1 * MIB),
        name="mixed_parts",
    )(*blocks, pair_own, pair_mate)


def finished(where, same, mine, theirs, denominators):
    rows, width = same.shape

    def kernel(where_ref, same_ref, mine_ref, theirs_ref, den_ref, out_ref):
        for k in range(4):
            at = pl.ds(pl.multiple_of(where_ref[k] * width, width), width)
            out_ref[at, :] = (same_ref[at, :] + mine_ref[k]) / den_ref[at, :]
            at = pl.ds(pl.multiple_of(where_ref[4 + k] * width, width), width)
            out_ref[at, :] = (same_ref[at, :] + theirs_ref[k].astype(F32)) / den_ref[at, :]

    return pl.pallas_call(
        kernel,
        out_shape=jax.ShapeDtypeStruct((rows, width), F32),
        in_specs=[SMEM] + [VMEM] * 4,
        out_specs=VMEM,
        compiler_params=pltpu.CompilerParams(vmem_limit_bytes=16 * MIB),
        cost_estimate=estimate(rows * width * 2, 2 * MIB),
        name="finished",
    )(where, same, mine, theirs, denominators)


def same_spin_beta(codes, blocks, beta_ops):
    rows, width = blocks[0].shape
    listed = beta_ops.shape[1] // width

    def kernel(codes_ref, *refs):
        ins, (ops_ref, out_ref) = refs[:5], refs[5:]
        placed = []
        for n in range(5):
            tile = jnp.zeros((width, width), F32)
            for k in range(listed):
                part = ops_ref[:, k * width : (k + 1) * width].astype(F32)
                tile = jnp.where(codes_ref[k] == n, part, tile)
            placed.append(tile.astype(BF16))
        left = jnp.concatenate([block[...] for block in ins], axis=1)
        right = jnp.concatenate(placed, axis=1)
        out_ref[...] = dot(left, right, ((1,), (1,)))

    return pl.pallas_call(
        kernel,
        out_shape=jax.ShapeDtypeStruct((rows, width), F32),
        in_specs=[SMEM] + [VMEM] * 6,
        out_specs=VMEM,
        compiler_params=pltpu.CompilerParams(vmem_limit_bytes=24 * MIB),
        cost_estimate=estimate(2 * rows * width * width * 5, 2 * MIB),
        name="same_spin_beta",
    )(codes, *blocks, beta_ops)


def same_spin_alpha(codes, blocks, alpha_ops, start):
    rows, width = start.shape
    depth = blocks[0].shape[0]
    listed = alpha_ops.shape[1] // depth
    half = depth // 2

    def kernel(codes_ref, own_ref, near_ref, far_ref, ops_ref, start_ref, out_ref):
        step = pl.program_id(0)
        code = codes_ref[step // 2]
        at = pl.ds(pl.multiple_of((step % 2) * half, half), half)
        picked = jnp.where(
            code == 0, own_ref[at, :], jnp.where(code == 1, near_ref[at, :], far_ref[at, :])
        )
        term = dot(ops_ref[...], picked)

        @pl.when(step == 0)
        def _():
            out_ref[...] = start_ref[...] + term

        @pl.when(step > 0)
        def _():
            out_ref[...] += term

    whole = lambda shape: pl.BlockSpec(shape, lambda s: (0, 0))
    return pl.pallas_call(
        kernel,
        out_shape=jax.ShapeDtypeStruct((rows, width), F32),
        grid=(listed * 2,),
        in_specs=[
            SMEM,
            whole((depth, width)),
            whole((depth, width)),
            whole((depth, width)),
            pl.BlockSpec((rows, half), lambda s: (0, s)),
            whole((rows, width)),
        ],
        out_specs=whole((rows, width)),
        compiler_params=pltpu.CompilerParams(vmem_limit_bytes=24 * MIB),
        cost_estimate=estimate(2 * rows * width * depth * listed, 10 * MIB),
        name="same_spin_alpha",
    )(codes, *blocks, alpha_ops, start)


def local(
    coef,
    beta_ops,
    beta_cols,
    alpha_ops,
    alpha_cols,
    pair_alpha,
    pair_beta,
    pair_coupling,
    denominators,
):
    beta_count = lax.axis_size(BETA)
    alpha_count = lax.axis_size(ALPHA)
    y, core = lax.axis_index("y"), lax.axis_index("c")
    row_blocks = [(y ^ k) * 2 for k in range(4)]
    where = jnp.stack([r + core for r in row_blocks] + [r + 1 - core for r in row_blocks])
    where = where.astype(jnp.int32)

    pair_t = pair_beta.T
    mate = swapped(coef, "c", 1)
    pair_mate = swapped(pair_t, "c", 1)

    below = rotated(coef, BETA, 2)
    above = rotated(coef, BETA, -2)
    near = swapped(coef, "zl", 1)
    xs, route = lax.axis_size("x"), []
    for i in range(xs):
        route += [(2 * i, 2 * ((i + 1) % xs)), (2 * i + 1, 2 * ((i - 1) % xs) + 1)]
    far = lax.ppermute(near, ALPHA, route)
    crossed = swapped(jnp.where(core == 0, above, below), "c", 1)

    parts = density_parts(where, coef, mate, pair_t, pair_mate)
    got = [swapped(parts[k], "y", k) for k in (1, 3, 2)]
    total = parts[0].astype(F32)
    for part in got:
        total = total + part.astype(F32)
    total = total.astype(BF16)
    total = (total.astype(F32) + swapped(total, "zh", 1).astype(F32)).astype(BF16)
    excited = excited_block(where, total, swapped(total, "zh", 3), pair_coupling, pair_alpha.T)
    blocks = [excited] + [swapped(excited, "y", k) for k in (1, 2, 3)]

    offset = (beta_cols[0] - lax.axis_index(BETA) + 2 + beta_count) % beta_count
    left = jnp.where(core == 0, 1, 3)
    beta_codes = jnp.where(offset == left, 1, jnp.where(offset == 4 - left, 3, offset))
    beta_codes = beta_codes.astype(jnp.int32)
    same = same_spin_beta(beta_codes, [below, crossed, coef, mate, above], beta_ops)

    offset = (alpha_cols[0] - lax.axis_index(ALPHA) + 1 + alpha_count) % alpha_count
    partner = jnp.where(lax.axis_index("zl") == 0, 2, 0)
    alpha_codes = jnp.where(offset == 1, 0, jnp.where(offset == partner, 1, 2)).astype(jnp.int32)
    same = same_spin_alpha(alpha_codes, [coef, near, far], alpha_ops, same)

    mine, theirs = mixed_parts(blocks, pair_t, pair_mate)
    return finished(where, same, mine, swapped(theirs, "c", 1), denominators)


def solution(mesh):
    finer = Mesh(mesh.devices.reshape(4, 2, 4, 4, 2), (*ALPHA, *BETA))
    placed = (
        P(ALPHA, BETA),
        P(BETA, None),
        P(BETA, None),
        P(ALPHA, None),
        P(ALPHA, None),
        P(ALPHA, None),
        P(BETA, None),
        P(),
        P(ALPHA, BETA),
    )
    return jax.shard_map(
        local, mesh=finer, in_specs=placed, out_specs=P(ALPHA, BETA), check_vma=False
    )
```

time: 113 us -> 79 us (0.70)
  local copies, waits for them, and re-layouts: 33.2 us -> 8.57 us
  matrix products: 23.2 us -> 0 us
  waiting for transfers between devices: 8 us -> 23.8 us
  Pallas kernels: 0 us -> 11.3 us
  blocking collectives: 11.3 us -> 0 us
    dot_general x6 -> x0, matrix products: 23.2 us -> none  [the longest x2 9.78 us: spread_blocks(): jnp.einsum('rkc,kn->rnc', tile_set, onehot, preferred_element_type=jnp.fl...]
    ppermute x6 -> x16, waiting for transfers between devices: 7.82 us -> 23.8 us  [the longest x13 19.2 us: swapped(): return lax.ppermute(block, axis, [(i, i ^ mask) for i in range(count)])]
    all_to_all x2 -> x0, starting transfers between devices: 15.8 us -> none  [the longest x1 8.89 us: from_everyone(): lax.all_to_all(jnp.broadcast_to(array[None], (peers, *array.shape)), axis...]
    ppermute x6 -> x16, starting transfers between devices: 18.6 us -> 33.4 us  [the longest x13 26.5 us: swapped(): return lax.ppermute(block, axis, [(i, i ^ mask) for i in range(count)])]
    reshape x2 -> x0, local copies, waits for them, and re-layouts: 14.6 us -> none  [spread_blocks(): tile_set = operator_blocks.reshape(row_count, listed, block_width)]
    convert_element_type x3 -> x0, local copies, waits for them, and re-layouts: 14 us -> none  [the longest x2 13.3 us: spread_blocks(): placed.astype(jnp.bfloat16).reshape(row_count, block_count * block_width)]
    all_to_all x2 -> x0, blocking collectives: 11.3 us -> none  [the longest x1 6.35 us: sum_at_owner(): lax.all_to_all(in_blocks(array, dim, peers), axis, 0, 0, tiled=True)]
    pallas_call x0 -> x6, Pallas kernels: none -> 11.3 us  [the longest x1 5.62 us: same_spin_alpha(): pl.pallas_call(kernel, out_shape=jax.ShapeDtypeStruct((rows, width), F32)...]
  transfers between devices with their start and end apart: 8 -> 16, of which waited for: 2 -> 9; matrix products, arithmetic and copies ran while one was open for 45% -> 2% of each run, Pallas kernels for 0% -> 11%
where the time goes in v1:
time: 79 us; the launch traced here: 78.6 us
  starting transfers between devices  33.4 us (42%)
  waiting for transfers between devices  23.8 us (30%)
  Pallas kernels  11.3 us (14%)
  local copies, waits for them, and re-layouts  8.57 us (11%)
  other arithmetic  1.49 us (2%)
    ppermute x13, starting transfers between devices, swapped(): return lax.ppermute(block, axis, [(i, i ^ mask) for i in range(count)])  26.5 us
    ppermute x13, waiting for transfers between devices, swapped(): return lax.ppermute(block, axis, [(i, i ^ mask) for i in range(count)])  19.2 us
    unnamed x14, local copies, waits for them, and re-layouts  8.49 us
    ppermute x2, starting transfers between devices, rotated(): lax.ppermute(block, axis, [(i, (i + distance) % count) for i in range(cou...  5.68 us
    pallas_call x1, Pallas kernels, same_spin_alpha(): pl.pallas_call(kernel, out_shape=jax.ShapeDtypeStruct((rows, width), F32)...  5.62 us
    ppermute x2, waiting for transfers between devices, rotated(): lax.ppermute(block, axis, [(i, (i + distance) % count) for i in range(cou...  4.52 us
  transfers between devices with their start and end apart: 16, of which 9 were waited for; matrix products, arithmetic and copies ran while one was open for 2% of the time, Pallas kernels for 11%

profile of v1, /device:TPU:1, one launch (start us, length us, event | category | flops | bytes accessed | tf_op | source)
XLA Modules:
  0.0 78.6 jit_solution(2210538314542452852)
XLA Ops:
  0.0 3.2 %collective-permute-start.5 = (bf16[1024,128]{1,0:T(8,128)(2,1)}, bf16[1024,128]{1,0:T(8,128)(2,1)S(1)}, u32[]{:S(2)}, u32[]{:S(2)}) collective-permute-start(bf16[1024,128]{1,0:T(8,128)(2,1)} %own_ref.3), channel_id=1, source_target_pairs={{0,1},{1,0},{2,3},{3,2},{4,5},{5,4},{6,7},{7,6},{8,9},{9,8},{10,11... | collective-permute-start | bytes 786440 | tf_op jit(solution)/shard_map/ppermute | solution.py:28
  3.3 1.5 %collective-permute-done.6.pm_ref.refs_5_ = bf16[576,128]{1,0:T(8,128)(2,1)S(1)} collective-permute-done((bf16[576,128]{1,0:T(8,128)(2,1)}, bf16[576,128]{1,0:T(8,128)(2,1)S(1)}, u32[]{:S(2)}, u32[]{:S(2)}) %collective-permute-start.6) | collective-permute-done | bytes 147488 | tf_op jit(solution)/shard_map/ppermute | solution.py:28
  5.7 1.4 %density_parts.1 = (bf16[576,128]{1,0:T(8,128)(2,1)S(1)}, bf16[576,128]{1,0:T(8,128)(2,1)S(1)}, bf16[576,128]{1,0:T(8,128)(2,1)S(1)}, bf16[576,128]{1,0:T(8,128)(2,1)S(1)}) custom-call(s32[8]{0:T(128)S(1)} %stack.35.where_ref, bf16[1024,128]{1,0:T(8,128)(2,1)} %own_ref.3, bf16[1024,128]{1,0:T(8,128)(2,1)S(1)} %collective-permute-done.5.refs_3_.mate_ref, ...), custom_call_target="tpu_custom_call" | custom-call | flops 150994944 | bytes 1048576 | tf_op jit(solution)/shard_map/density_parts/pallas_call | solution.py:47
  7.3 1.4 %collective-permute-start.8 = (bf16[576,128]{1,0:T(8,128)(2,1)S(1)}, bf16[576,128]{1,0:T(8,128)(2,1)S(1)}, u32[]{:S(2)}, u32[]{:S(2)}) collective-permute-start(bf16[576,128]{1,0:T(8,128)(2,1)S(1)} %get-tuple-element.13), channel_id=1, source_target_pairs={{0,24},{8,16},{16,8},{24,0},{1,25},{9,17},{17,9},{25,1},{2,26},{10... | collective-permute-start | bytes 442376 | tf_op jit(solution)/shard_map/ppermute | solution.py:28
  8.7 1.8 %collective-permute-start.9 = (bf16[576,128]{1,0:T(8,128)(2,1)S(1)}, bf16[576,128]{1,0:T(8,128)(2,1)S(1)}, u32[]{:S(2)}, u32[]{:S(2)}) collective-permute-start(bf16[576,128]{1,0:T(8,128)(2,1)S(1)} %get-tuple-element.14), channel_id=1, source_target_pairs={{0,16},{8,24},{16,0},{24,8},{1,17},{9,25},{17,1},{25,9},{2,18},{10... | collective-permute-start | bytes 442376 | tf_op jit(solution)/shard_map/ppermute | solution.py:28
  10.5 1.8 %collective-permute-done.7 = bf16[576,128]{1,0:T(8,128)(2,1)S(1)} collective-permute-done((bf16[576,128]{1,0:T(8,128)(2,1)S(1)}, bf16[576,128]{1,0:T(8,128)(2,1)S(1)}, u32[]{:S(2)}, u32[]{:S(2)}) %collective-permute-start.7) | collective-permute-done | bytes 147488 | tf_op jit(solution)/shard_map/ppermute | solution.py:28
  12.3 1.9 %collective-permute-done.8 = bf16[576,128]{1,0:T(8,128)(2,1)S(1)} collective-permute-done((bf16[576,128]{1,0:T(8,128)(2,1)S(1)}, bf16[576,128]{1,0:T(8,128)(2,1)S(1)}, u32[]{:S(2)}, u32[]{:S(2)}) %collective-permute-start.8) | collective-permute-done | bytes 147488 | tf_op jit(solution)/shard_map/ppermute | solution.py:28
  14.2 2.0 %collective-permute-done.9 = bf16[576,128]{1,0:T(8,128)(2,1)S(1)} collective-permute-done((bf16[576,128]{1,0:T(8,128)(2,1)S(1)}, bf16[576,128]{1,0:T(8,128)(2,1)S(1)}, u32[]{:S(2)}, u32[]{:S(2)}) %collective-permute-start.9) | collective-permute-done | bytes 147488 | tf_op jit(solution)/shard_map/ppermute | solution.py:28
  16.3 3.0 %collective-permute-start.10 = (bf16[576,128]{1,0:T(8,128)(2,1)S(1)}, bf16[576,128]{1,0:T(8,128)(2,1)S(1)}, u32[]{:S(2)}, u32[]{:S(2)}) collective-permute-start(bf16[576,128]{1,0:T(8,128)(2,1)S(1)} %add_convert_fusion.1), channel_id=1, source_target_pairs={{0,2},{2,0},{4,6},{6,4},{1,3},{3,1},{5,7},{7,5},{8,10},{10,8},{12,... | collective-permute-start | bytes 442376 | tf_op jit(solution)/shard_map/ppermute | solution.py:28
  19.5 5.6 %collective-permute-start.3 = (bf16[1024,128]{1,0:T(8,128)(2,1)}, bf16[1024,128]{1,0:T(8,128)(2,1)S(1)}, u32[]{:S(2)}, u32[]{:S(2)}) collective-permute-start(bf16[1024,128]{1,0:T(8,128)(2,1)} %own_ref.3), channel_id=1, source_target_pairs={{0,30},{1,31},{2,0},{3,1},{4,2},{5,3},{6,4},{7,5},{8,6},{9,7},{10,... | collective-permute-start | bytes 786440 | tf_op jit(solution)/shard_map/ppermute | solution.py:33
  25.1 1.6 %collective-permute-start = (bf16[1024,128]{1,0:T(8,128)(2,1)}, bf16[1024,128]{1,0:T(8,128)(2,1)S(1)}, u32[]{:S(2)}, u32[]{:S(2)}) collective-permute-start(bf16[1024,128]{1,0:T(8,128)(2,1)} %own_ref.3), channel_id=1, source_target_pairs={{0,32},{32,0},{1,33},{33,1},{2,34},{34,2},{3,35},{35,3},{4,36},{36... | collective-permute-start | bytes 786440 | tf_op jit(solution)/shard_map/ppermute | solution.py:28
  26.7 5.9 %collective-permute-start.11 = (bf16[576,128]{1,0:T(8,128)(2,1)S(1)}, bf16[576,128]{1,0:T(8,128)(2,1)S(1)}, u32[]{:S(2)}, u32[]{:S(2)}) collective-permute-start(bf16[576,128]{1,0:T(8,128)(2,1)S(1)} %add_convert_fusion.near_ref), channel_id=1, source_target_pairs={{0,6},{2,4},{4,2},{6,0},{1,7},{3,5},{5,3},{7,1},{8,14},{10,12},{12... | collective-permute-start | bytes 442376 | tf_op jit(solution)/shard_map/ppermute | solution.py:28
  32.6 4.5 %collective-permute-done.3.refs_4_ = bf16[1024,128]{1,0:T(8,128)(2,1)S(1)} collective-permute-done((bf16[1024,128]{1,0:T(8,128)(2,1)}, bf16[1024,128]{1,0:T(8,128)(2,1)S(1)}, u32[]{:S(2)}, u32[]{:S(2)}) %collective-permute-start.3) | collective-permute-done | bytes 262176 | tf_op jit(solution)/shard_map/ppermute | solution.py:33
  37.2 3.1 %collective-permute-start.4 = (bf16[1024,128]{1,0:T(8,128)(2,1)S(1)}, bf16[1024,128]{1,0:T(8,128)(2,1)S(1)}, u32[]{:S(2)}, u32[]{:S(2)}) collective-permute-start(bf16[1024,128]{1,0:T(8,128)(2,1)S(1)} %broadcast_select_fusion), channel_id=1, source_target_pairs={{0,1},{1,0},{2,3},{3,2},{4,5},{5,4},{6,7},{7,6},{8,9},{9,8},{10,11... | collective-permute-start | bytes 786440 | tf_op jit(solution)/shard_map/ppermute | solution.py:28
  40.3 3.2 %collective-permute-done.near_ref = bf16[1024,128]{1,0:T(8,128)(2,1)S(1)} collective-permute-done((bf16[1024,128]{1,0:T(8,128)(2,1)}, bf16[1024,128]{1,0:T(8,128)(2,1)S(1)}, u32[]{:S(2)}, u32[]{:S(2)}) %collective-permute-start) | collective-permute-done | bytes 262176 | tf_op jit(solution)/shard_map/ppermute | solution.py:28
  44.7 2.3 %collective-permute-done.11.far_ref = bf16[576,128]{1,0:T(8,128)(2,1)S(1)} collective-permute-done((bf16[576,128]{1,0:T(8,128)(2,1)S(1)}, bf16[576,128]{1,0:T(8,128)(2,1)S(1)}, u32[]{:S(2)}, u32[]{:S(2)}) %collective-permute-start.11) | collective-permute-done | bytes 147488 | tf_op jit(solution)/shard_map/ppermute | solution.py:28
  50.4 2.8 %collective-permute-start.13 = (bf16[128,576]{1,0:T(8,128)(2,1)S(1)}, bf16[128,576]{1,0:T(8,128)(2,1)S(1)}, u32[]{:S(2)}, u32[]{:S(2)}) collective-permute-start(bf16[128,576]{1,0:T(8,128)(2,1)S(1)} %excited_block.1.refs_0_), channel_id=1, source_target_pairs={{0,16},{8,24},{16,0},{24,8},{1,17},{9,25},{17,1},{25,9},{2,18},{10... | collective-permute-start | bytes 442376 | tf_op jit(solution)/shard_map/ppermute | solution.py:28
  54.9 3.8 %collective-permute-done.13.refs_2_ = bf16[128,576]{1,0:T(8,128)(2,1)S(1)} collective-permute-done((bf16[128,576]{1,0:T(8,128)(2,1)S(1)}, bf16[128,576]{1,0:T(8,128)(2,1)S(1)}, u32[]{:S(2)}, u32[]{:S(2)}) %collective-permute-start.13) | collective-permute-done | bytes 147488 | tf_op jit(solution)/shard_map/ppermute | solution.py:28
  58.7 2.7 %collective-permute-done.14.refs_3_ = bf16[128,576]{1,0:T(8,128)(2,1)S(1)} collective-permute-done((bf16[128,576]{1,0:T(8,128)(2,1)S(1)}, bf16[128,576]{1,0:T(8,128)(2,1)S(1)}, u32[]{:S(2)}, u32[]{:S(2)}) %collective-permute-start.14) | collective-permute-done | bytes 147488 | tf_op jit(solution)/shard_map/ppermute | solution.py:28
  62.7 2.3 %collective-permute-start.15 = (bf16[4,128,128]{2,1,0:T(8,128)(2,1)S(1)}, bf16[4,128,128]{2,1,0:T(8,128)(2,1)S(1)}, u32[]{:S(2)}, u32[]{:S(2)}) collective-permute-start(bf16[4,128,128]{2,1,0:T(8,128)(2,1)S(1)} %get-tuple-element.16), channel_id=1, source_target_pairs={{0,1},{1,0},{2,3},{3,2},{4,5},{5,4},{6,7},{7,6},{8,9},{9,8},{10,11... | collective-permute-start | bytes 393224 | tf_op jit(solution)/shard_map/ppermute | solution.py:28
  66.6 1.5 %same_spin_beta.1.start_ref = f32[1024,128]{1,0:T(8,128)S(1)} custom-call(s32[4]{0:T(128)S(1)} %compare_select_fusion.5.codes_ref, bf16[1024,128]{1,0:T(8,128)(2,1)S(1)} %collective-permute-done.2.refs_0_, bf16[1024,128]{1,0:T(8,128)(2,1)S(1)} %collective-permute-done.4.refs_1_, bf16[1024,128]{1,0:T(8,128)(2,1)} %own_ref.3, ...), custom_call_target="tpu_custom_call" | custom-call | flops 167772160 | bytes 2097152 | tf_op jit(solution)/shard_map/same_spin_beta/pallas_call | solution.py:142
  68.1 3.4 %copy-done = bf16[1024,4096]{1,0:T(8,128)(2,1)S(1)} copy-done((bf16[1024,4096]{1,0:T(8,128)(2,1)S(1)}, bf16[1024,4096]{1,0:T(8,128)(2,1)}, u32[]{:S(2)}) %copy-start) | copy-done | bytes 8388632
  71.5 5.6 %same_spin_alpha.1.same_ref = f32[1024,128]{1,0:T(8,128)S(1)} custom-call(s32[4]{0:T(128)S(1)} %compare_select_fusion.7.codes_ref, bf16[1024,128]{1,0:T(8,128)(2,1)} %own_ref.3, bf16[1024,128]{1,0:T(8,128)(2,1)S(1)} %collective-permute-done.near_ref, bf16[1024,128]{1,0:T(8,128)(2,1)S(1)} %collective-permute-done.1.far_ref, bf16[1024,4096]{1,0:T(8,128)(2,1)S(1)} %copy-done, ...), custom_call_target="tpu_custom_call" | custom-call | flops 1073741824 | bytes 10485760 | tf_op jit(solution)/shard_map/same_spin_alpha/pallas_call | solution.py:177
  77.2 1.4 %finished.1 = f32[1024,128]{1,0:T(8,128)} custom-call(s32[8]{0:T(128)S(1)} %stack.35.where_ref, f32[1024,128]{1,0:T(8,128)S(1)} %same_spin_alpha.1.same_ref, f32[4,128,128]{2,1,0:T(8,128)S(1)} %get-tuple-element.15.mine_ref, bf16[4,128,128]{2,1,0:T(8,128)(2,1)S(1)} %collective-permute-done.15.theirs_ref, f32[1024,128]{1,0:T(8,128)S(1)} %copy-done.5), custom_call_target="tpu_custom_call" | custom-call | flops 262144 | bytes 2097152 | tf_op jit(solution)/shard_map/finished/pallas_call | solution.py:114
  (34 shorter events, 10.6 us)
Async XLA Ops:
  0.0 4.8 %collective-permute-start.5 = (bf16[1024,128]{1,0:T(8,128)(2,1)}, bf16[1024,128]{1,0:T(8,128)(2,1)S(1)}, u32[]{:S(2)}, u32[]{:S(2)}) collective-permute-start(bf16[1024,128]{1,0:T(8,128)(2,1)} %own_ref.3), channel_id=1, source_target_pairs={{0,1},{1,0},{2,3},{3,2},{4,5},{5,4},{6,7},{7,6},{8,9},{9,8},{10,11... | collective-permute-start | bytes 786440 | tf_op jit(solution)/shard_map/ppermute | solution.py:28
  3.2 1.6 %collective-permute-start.6 = (bf16[576,128]{1,0:T(8,128)(2,1)}, bf16[576,128]{1,0:T(8,128)(2,1)S(1)}, u32[]{:S(2)}, u32[]{:S(2)}) collective-permute-start(bf16[576,128]{1,0:T(8,128)(2,1)} %bitcast.15), channel_id=1, source_target_pairs={{0,1},{1,0},{2,3},{3,2},{4,5},{5,4},{6,7},{7,6},{8,9},{9,8},{10,11... | collective-permute-start | bytes 442376 | tf_op jit(solution)/shard_map/ppermute | solution.py:28
  4.8 0.9 %copy-start.3 = (bf16[128,576]{0,1:T(8,128)(2,1)S(1)}, bf16[128,576]{0,1:T(8,128)(2,1)}, u32[]{:S(2)}) copy-start(bf16[128,576]{0,1:T(8,128)(2,1)} %param.15) | copy-start | bytes 442372
  7.2 5.1 %collective-permute-start.7 = (bf16[576,128]{1,0:T(8,128)(2,1)S(1)}, bf16[576,128]{1,0:T(8,128)(2,1)S(1)}, u32[]{:S(2)}, u32[]{:S(2)}) collective-permute-start(bf16[576,128]{1,0:T(8,128)(2,1)S(1)} %get-tuple-element.12), channel_id=1, source_target_pairs={{0,8},{8,0},{16,24},{24,16},{1,9},{9,1},{17,25},{25,17},{2,10},{10... | collective-permute-start | bytes 442376 | tf_op jit(solution)/shard_map/ppermute | solution.py:28
  7.3 6.9 %collective-permute-start.8 = (bf16[576,128]{1,0:T(8,128)(2,1)S(1)}, bf16[576,128]{1,0:T(8,128)(2,1)S(1)}, u32[]{:S(2)}, u32[]{:S(2)}) collective-permute-start(bf16[576,128]{1,0:T(8,128)(2,1)S(1)} %get-tuple-element.13), channel_id=1, source_target_pairs={{0,24},{8,16},{16,8},{24,0},{1,25},{9,17},{17,9},{25,1},{2,26},{10... | collective-permute-start | bytes 442376 | tf_op jit(solution)/shard_map/ppermute | solution.py:28
  8.7 7.5 %collective-permute-start.9 = (bf16[576,128]{1,0:T(8,128)(2,1)S(1)}, bf16[576,128]{1,0:T(8,128)(2,1)S(1)}, u32[]{:S(2)}, u32[]{:S(2)}) collective-permute-start(bf16[576,128]{1,0:T(8,128)(2,1)S(1)} %get-tuple-element.14), channel_id=1, source_target_pairs={{0,16},{8,24},{16,0},{24,8},{1,17},{9,25},{17,1},{25,9},{2,18},{10... | collective-permute-start | bytes 442376 | tf_op jit(solution)/shard_map/ppermute | solution.py:28
  16.3 10.4 %collective-permute-start.10 = (bf16[576,128]{1,0:T(8,128)(2,1)S(1)}, bf16[576,128]{1,0:T(8,128)(2,1)S(1)}, u32[]{:S(2)}, u32[]{:S(2)}) collective-permute-start(bf16[576,128]{1,0:T(8,128)(2,1)S(1)} %add_convert_fusion.1), channel_id=1, source_target_pairs={{0,2},{2,0},{4,6},{6,4},{1,3},{3,1},{5,7},{7,5},{8,10},{10,8},{12,... | collective-permute-start | bytes 442376 | tf_op jit(solution)/shard_map/ppermute | solution.py:28
  19.4 13.3 %collective-permute-start.2 = (bf16[1024,128]{1,0:T(8,128)(2,1)}, bf16[1024,128]{1,0:T(8,128)(2,1)S(1)}, u32[]{:S(2)}, u32[]{:S(2)}) collective-permute-start(bf16[1024,128]{1,0:T(8,128)(2,1)} %own_ref.3), channel_id=1, source_target_pairs={{0,2},{1,3},{2,4},{3,5},{4,6},{5,7},{6,8},{7,9},{8,10},{9,11},{10,... | collective-permute-start | bytes 786440 | tf_op jit(solution)/shard_map/ppermute | solution.py:33
  19.5 17.7 %collective-permute-start.3 = (bf16[1024,128]{1,0:T(8,128)(2,1)}, bf16[1024,128]{1,0:T(8,128)(2,1)S(1)}, u32[]{:S(2)}, u32[]{:S(2)}) collective-permute-start(bf16[1024,128]{1,0:T(8,128)(2,1)} %own_ref.3), channel_id=1, source_target_pairs={{0,30},{1,31},{2,0},{3,1},{4,2},{5,3},{6,4},{7,5},{8,6},{9,7},{10,... | collective-permute-start | bytes 786440 | tf_op jit(solution)/shard_map/ppermute | solution.py:33
  25.1 18.4 %collective-permute-start = (bf16[1024,128]{1,0:T(8,128)(2,1)}, bf16[1024,128]{1,0:T(8,128)(2,1)S(1)}, u32[]{:S(2)}, u32[]{:S(2)}) collective-permute-start(bf16[1024,128]{1,0:T(8,128)(2,1)} %own_ref.3), channel_id=1, source_target_pairs={{0,32},{32,0},{1,33},{33,1},{2,34},{34,2},{3,35},{35,3},{4,36},{36... | collective-permute-start | bytes 786440 | tf_op jit(solution)/shard_map/ppermute | solution.py:28
  26.7 50.5 %copy-start.5 = (f32[1024,128]{1,0:T(8,128)S(1)}, f32[1024,128]{1,0:T(8,128)}, u32[]{:S(2)}) copy-start(f32[1024,128]{1,0:T(8,128)} %den_ref.1) | copy-start | bytes 1572868
  26.7 20.2 %collective-permute-start.11 = (bf16[576,128]{1,0:T(8,128)(2,1)S(1)}, bf16[576,128]{1,0:T(8,128)(2,1)S(1)}, u32[]{:S(2)}, u32[]{:S(2)}) collective-permute-start(bf16[576,128]{1,0:T(8,128)(2,1)S(1)} %add_convert_fusion.near_ref), channel_id=1, source_target_pairs={{0,6},{2,4},{4,2},{6,0},{1,7},{3,5},{5,3},{7,1},{8,14},{10,12},{12... | collective-permute-start | bytes 442376 | tf_op jit(solution)/shard_map/ppermute | solution.py:28
  37.2 28.5 %collective-permute-start.4 = (bf16[1024,128]{1,0:T(8,128)(2,1)S(1)}, bf16[1024,128]{1,0:T(8,128)(2,1)S(1)}, u32[]{:S(2)}, u32[]{:S(2)}) collective-permute-start(bf16[1024,128]{1,0:T(8,128)(2,1)S(1)} %broadcast_select_fusion), channel_id=1, source_target_pairs={{0,1},{1,0},{2,3},{3,2},{4,5},{5,4},{6,7},{7,6},{8,9},{9,8},{10,11... | collective-permute-start | bytes 786440 | tf_op jit(solution)/shard_map/ppermute | solution.py:28
  43.5 24.6 %collective-permute-start.1 = (bf16[1024,128]{1,0:T(8,128)(2,1)S(1)}, bf16[1024,128]{1,0:T(8,128)(2,1)S(1)}, u32[]{:S(2)}, u32[]{:S(2)}) collective-permute-start(bf16[1024,128]{1,0:T(8,128)(2,1)S(1)} %collective-permute-done.near_ref), channel_id=1, source_target_pairs={{0,64},{32,224},{64,128},{96,32},{128,192},{160,96},{192,0},{224,1... | collective-permute-start | bytes 786440 | tf_op jit(solution)/shard_map/ppermute | solution.py:224
  47.0 1.3 %copy-start.1 = (bf16[1024,576]{0,1:T(8,128)(2,1)S(1)}, bf16[1024,576]{0,1:T(8,128)(2,1)}, u32[]{:S(2)}) copy-start(bf16[1024,576]{0,1:T(8,128)(2,1)} %param.14) | copy-start | bytes 3538948
  48.2 1.1 %copy-start.2 = (bf16[576,576]{1,0:T(8,128)(2,1)S(1)}, bf16[576,576]{1,0:T(8,128)(2,1)}, u32[]{:S(2)}) copy-start(bf16[576,576]{1,0:T(8,128)(2,1)} %coupling_ref.1) | copy-start | bytes 1990660
  50.3 4.6 %collective-permute-start.12 = (bf16[128,576]{1,0:T(8,128)(2,1)S(1)}, bf16[128,576]{1,0:T(8,128)(2,1)S(1)}, u32[]{:S(2)}, u32[]{:S(2)}) collective-permute-start(bf16[128,576]{1,0:T(8,128)(2,1)S(1)} %excited_block.1.refs_0_), channel_id=1, source_target_pairs={{0,8},{8,0},{16,24},{24,16},{1,9},{9,1},{17,25},{25,17},{2,10},{10... | collective-permute-start | bytes 442376 | tf_op jit(solution)/shard_map/ppermute | solution.py:28
  50.4 8.3 %collective-permute-start.13 = (bf16[128,576]{1,0:T(8,128)(2,1)S(1)}, bf16[128,576]{1,0:T(8,128)(2,1)S(1)}, u32[]{:S(2)}, u32[]{:S(2)}) collective-permute-start(bf16[128,576]{1,0:T(8,128)(2,1)S(1)} %excited_block.1.refs_0_), channel_id=1, source_target_pairs={{0,16},{8,24},{16,0},{24,8},{1,17},{9,25},{17,1},{25,9},{2,18},{10... | collective-permute-start | bytes 442376 | tf_op jit(solution)/shard_map/ppermute | solution.py:28
  53.1 8.3 %collective-permute-start.14 = (bf16[128,576]{1,0:T(8,128)(2,1)S(1)}, bf16[128,576]{1,0:T(8,128)(2,1)S(1)}, u32[]{:S(2)}, u32[]{:S(2)}) collective-permute-start(bf16[128,576]{1,0:T(8,128)(2,1)S(1)} %excited_block.1.refs_0_), channel_id=1, source_target_pairs={{0,24},{8,16},{16,8},{24,0},{1,25},{9,17},{17,9},{25,1},{2,26},{10... | collective-permute-start | bytes 442376 | tf_op jit(solution)/shard_map/ppermute | solution.py:28
  61.4 0.9 %copy-start.4 = (bf16[128,576]{0,1:T(8,128)(2,1)S(1)}, bf16[128,576]{0,1:T(8,128)(2,1)}, u32[]{:S(2)}) copy-start(bf16[128,576]{0,1:T(8,128)(2,1)} %param.15) | copy-start | bytes 442372
  62.7 14.4 %collective-permute-start.15 = (bf16[4,128,128]{2,1,0:T(8,128)(2,1)S(1)}, bf16[4,128,128]{2,1,0:T(8,128)(2,1)S(1)}, u32[]{:S(2)}, u32[]{:S(2)}) collective-permute-start(bf16[4,128,128]{2,1,0:T(8,128)(2,1)S(1)} %get-tuple-element.16), channel_id=1, source_target_pairs={{0,1},{1,0},{2,3},{3,2},{4,5},{5,4},{6,7},{7,6},{8,9},{9,8},{10,11... | collective-permute-start | bytes 393224 | tf_op jit(solution)/shard_map/ppermute | solution.py:28
  65.7 0.9 %copy-start.6 = (bf16[128,512]{1,0:T(8,128)(2,1)S(1)}, bf16[128,512]{1,0:T(8,128)(2,1)}, u32[]{:S(2)}) copy-start(bf16[128,512]{1,0:T(8,128)(2,1)} %refs_5_.1) | copy-start | bytes 393220
  68.1 3.4 %copy-start = (bf16[1024,4096]{1,0:T(8,128)(2,1)S(1)}, bf16[1024,4096]{1,0:T(8,128)(2,1)}, u32[]{:S(2)}) copy-start(bf16[1024,4096]{1,0:T(8,128)(2,1)} %ops_ref.1) | copy-start | bytes 25165828

commit v2 on v1

v2 whole, which is shorter than its diff:
```python
import jax
import jax.numpy as jnp
from jax import lax
from jax.experimental import pallas as pl
from jax.experimental.pallas import tpu as pltpu
from jax.sharding import Mesh
from jax.sharding import PartitionSpec as P

ALPHA = ("x", "zl")
BETA = ("y", "zh", "c")
F32 = jnp.float32
BF16 = jnp.bfloat16
SMEM = pl.BlockSpec(memory_space=pltpu.SMEM)
VMEM = pl.BlockSpec(memory_space=pltpu.VMEM)
HBM = pl.BlockSpec(memory_space=pltpu.HBM)
ANY = pl.BlockSpec(memory_space=pl.ANY)
MIB = 1 << 20


def dot(a, b, dims=((1,), (0,))):
    return lax.dot_general(a, b, (dims, ((), ())), preferred_element_type=F32)


def swapped(block, axis, mask):
    count = lax.axis_size(axis)
    return lax.ppermute(block, axis, [(i, i ^ mask) for i in range(count)])


def rotated(block, axis, distance):
    count = lax.axis_size(axis)
    return lax.ppermute(block, axis, [(i, (i + distance) % count) for i in range(count)])


def call(kernel, outs, args, specs, cost, scratch=(), aliases=None, out_specs=None, limit=16):
    return pl.pallas_call(
        kernel,
        out_shape=outs,
        in_specs=specs,
        out_specs=out_specs or [VMEM] * len(outs),
        scratch_shapes=list(scratch),
        input_output_aliases=aliases or {},
        compiler_params=pltpu.CompilerParams(vmem_limit_bytes=limit * MIB),
        cost_estimate=pl.CostEstimate(flops=cost[0], bytes_accessed=cost[1], transcendentals=0),
        name=kernel.__name__,
    )(*args)


def shape(dims, kind=BF16):
    return jax.ShapeDtypeStruct(dims, kind)


def block_rows(where_ref, k, width):
    return pl.ds(pl.multiple_of(where_ref[k] * width, width), width)


def own_density(where, coef, pair_t):
    pairs, width = pair_t.shape

    def own_density_kernel(where_ref, coef_ref, pair_ref, coef_out, pair_out, acc_out, sems):
        copies = [
            pltpu.make_async_copy(coef_ref, coef_out, sems.at[0]),
            pltpu.make_async_copy(pair_ref, pair_out, sems.at[1]),
        ]
        for copy in copies:
            copy.start()
        for copy in copies:
            copy.wait()
        left = pair_out[...]
        for k in range(4):
            right = coef_out[block_rows(where_ref, k, width), :]
            acc_out[k] = dot(left, right, ((1,), (1,)))

    return call(
        own_density_kernel,
        [shape(coef.shape), shape(pair_t.shape), shape((4, pairs, width), F32)],
        (where, coef, pair_t),
        [SMEM, HBM, HBM],
        (8 * pairs * width * width, 1 * MIB),
        [pltpu.SemaphoreType.DMA((2,))],
        limit=16,
    )


def density_parts(where, acc, mate, pair_mate):
    pairs, width = pair_mate.shape

    def density_parts_kernel(where_ref, acc_ref, mate_ref, pair_ref, *outs):
        left = pair_ref[...]
        for k, out in enumerate(outs):
            right = mate_ref[block_rows(where_ref, k, width), :]
            out[...] = (acc_ref[k] + dot(left, right, ((1,), (1,)))).astype(BF16)

    return call(
        density_parts_kernel,
        [shape((pairs, width))] * 4,
        (where, acc, mate, pair_mate),
        [SMEM] + [VMEM] * 3,
        (8 * pairs * width * width, 1 * MIB),
    )


def staged(where, cols, coupling, pair_alpha_t, beta_ops, tie):
    pairs, width = coupling.shape[0], beta_ops.shape[0]
    listed = beta_ops.shape[1] // width
    count = lax.axis_size(BETA)

    def staged_kernel(
        where_ref, cols_ref, c_ref, pa_ref, ops_ref, tie_ref, c_out, pa_out, w_out, pa_v, ops_v, sems
    ):
        rows = block_rows(where_ref, 0, width)
        copies = [
            pltpu.make_async_copy(ops_ref, ops_v, sems.at[0]),
            pltpu.make_async_copy(pa_ref.at[:, rows], pa_v, sems.at[1]),
            pltpu.make_async_copy(c_ref, c_out, sems.at[2]),
        ]
        for copy in copies:
            copy.start()
        copies[0].wait()
        core = where_ref[8]
        for n in range(5):
            offset = n if n in (0, 2, 4) else jnp.where(core == 0, n, 4 - n)
            tile = jnp.zeros((width, width), F32)
            for k in range(listed):
                here = lax.rem(cols_ref[0, k] - where_ref[9] + 2 + count, count)
                part = ops_v[:, k * width : (k + 1) * width].astype(F32)
                tile = jnp.where(here == offset, part, tile)
            w_out[:, n * width : (n + 1) * width] = tile.astype(BF16)
        copies[1].wait()
        pa_out[...] = pa_v[...].astype(F32).T
        copies[2].wait()

    return call(
        staged_kernel,
        [shape(coupling.shape), shape((width, pairs), F32), shape((width, 5 * width))],
        (where, cols, coupling, pair_alpha_t, beta_ops, tie),
        [SMEM, SMEM, HBM, HBM, HBM, ANY],
        (pairs * pairs, 2 * MIB),
        [
            pltpu.VMEM((pairs, width), BF16),
            pltpu.VMEM(beta_ops.shape, BF16),
            pltpu.SemaphoreType.DMA((3,)),
        ],
    )


def excited_block(near, far, coupling, scale):
    pairs, width = near.shape

    def excited_block_kernel(near_ref, far_ref, coupling_ref, scale_ref, out_ref):
        total = near_ref[...].astype(F32) + far_ref[...].astype(F32)
        density = total.T.astype(BF16)
        out_ref[...] = (dot(density, coupling_ref[...]) * scale_ref[...]).astype(BF16)

    return call(
        excited_block_kernel,
        [shape((width, pairs))],
        (near, far, coupling, scale),
        [VMEM] * 4,
        (2 * pairs * pairs * width, 2 * MIB),
    )[0]


def mixed_mate(blocks, pair_mate):
    width = blocks[0].shape[0]
    pairs = blocks[0].shape[1]

    def mixed_mate_kernel(*refs):
        right = refs[4][...]
        for k in range(4):
            refs[5][k] = dot(refs[k][...], right).astype(BF16)

    return call(
        mixed_mate_kernel,
        [shape((4, width, width))],
        (*blocks, pair_mate),
        [VMEM] * 5,
        (8 * pairs * width * width, 1 * MIB),
    )[0]


def finished_own(where, same, blocks, pair_own, denominators):
    rows, width = same.shape

    def finished_own_kernel(where_ref, same_ref, e0, e1, e2, e3, pair_ref, den_ref, out, part, sems):
        right = pair_ref[...]
        copies = []
        for k, block in enumerate((e0, e1, e2, e3)):
            at = block_rows(where_ref, k, width)
            part[k] = (same_ref[at, :] + dot(block[...], right)) / den_ref[at, :]
            copies.append(pltpu.make_async_copy(part.at[k], out.at[at, :], sems.at[k]))
            copies[-1].start()
        for copy in copies:
            copy.wait()

    return call(
        finished_own_kernel,
        [shape((rows, width), F32)],
        (where, same, *blocks, pair_own, denominators),
        [SMEM] + [VMEM] * 7,
        (rows * width * 600, 2 * MIB),
        [pltpu.VMEM((4, width, width), F32), pltpu.SemaphoreType.DMA((4,))],
        out_specs=[HBM],
    )[0]


def finished_mate(where, same, theirs, denominators, begun):
    rows, width = same.shape

    def finished_mate_kernel(where_ref, same_ref, theirs_ref, den_ref, begun_ref, out, part, sems):
        copies = []
        for k in range(4):
            at = block_rows(where_ref, 4 + k, width)
            part[k] = (same_ref[at, :] + theirs_ref[k].astype(F32)) / den_ref[at, :]
            copies.append(pltpu.make_async_copy(part.at[k], out.at[at, :], sems.at[k]))
            copies[-1].start()
        for copy in copies:
            copy.wait()

    return call(
        finished_mate_kernel,
        [shape((rows, width), F32)],
        (where, same, theirs, denominators, begun),
        [SMEM] + [VMEM] * 3 + [HBM],
        (rows * width * 2, 2 * MIB),
        [pltpu.VMEM((4, width, width), F32), pltpu.SemaphoreType.DMA((4,))],
        aliases={4: 0},
        out_specs=[HBM],
    )[0]


def same_spin_beta(blocks, placed):
    rows, width = blocks[0].shape

    def same_spin_beta_kernel(b0, b1, b2, b3, b4, w_ref, out_ref):
        left = jnp.concatenate([b[...] for b in (b0, b1, b2, b3, b4)], axis=1)
        out_ref[...] = dot(left, w_ref[...], ((1,), (1,)))

    return call(
        same_spin_beta_kernel,
        [shape((rows, width), F32)],
        (*blocks, placed),
        [VMEM] * 6,
        (2 * rows * width * width * 5, 2 * MIB),
        limit=24,
    )[0]


def same_spin_alpha(where, cols, blocks, alpha_ops, start):
    rows, width = start.shape
    depth = blocks[0].shape[0]
    step = depth // 2
    steps = alpha_ops.shape[1] // step
    count = lax.axis_size(ALPHA)

    def same_spin_alpha_kernel(
        where_ref, cols_ref, own_ref, near_ref, far_ref, ops_ref, start_ref, out_ref, ops_v, sems
    ):
        copies = [
            pltpu.make_async_copy(ops_ref.at[:, s * step : (s + 1) * step], ops_v.at[s], sems.at[s])
            for s in range(steps)
        ]
        for copy in copies:
            copy.start()
        for s, copy in enumerate(copies):
            offset = lax.rem(cols_ref[0, s // 2] - where_ref[10] + 1 + count, count)
            at = slice((s % 2) * step, (s % 2 + 1) * step)
            picked = jnp.where(
                offset == 1,
                own_ref[at, :],
                jnp.where(offset == where_ref[11], near_ref[at, :], far_ref[at, :]),
            )
            copy.wait()
            before = start_ref[...] if s == 0 else out_ref[...]
            out_ref[...] = before + dot(ops_v[s], picked)

    return call(
        same_spin_alpha_kernel,
        [shape((rows, width), F32)],
        (where, cols, *blocks, alpha_ops, start),
        [SMEM, SMEM] + [VMEM] * 3 + [HBM, VMEM],
        (2 * rows * width * depth * 4, 10 * MIB),
        [pltpu.VMEM((steps, rows, step), BF16), pltpu.SemaphoreType.DMA((steps,))],
        limit=48,
    )[0]


def local(
    coef,
    beta_ops,
    beta_cols,
    alpha_ops,
    alpha_cols,
    pair_alpha,
    pair_beta,
    pair_coupling,
    denominators,
):
    y, core = lax.axis_index("y"), lax.axis_index("c")
    low = lax.axis_index("zl")
    row_blocks = [(y ^ k) * 2 for k in range(4)]
    where = [r + core for r in row_blocks] + [r + 1 - core for r in row_blocks]
    where += [core, lax.axis_index(BETA), lax.axis_index(ALPHA), 2 - 2 * low]
    where = jnp.stack(where).astype(jnp.int32)

    pair_t = pair_beta.T
    mate = swapped(coef, "c", 1)
    pair_mate = swapped(pair_t, "c", 1)
    coef_v, pair_v, acc = own_density(where, coef, pair_t)

    below = rotated(coef, BETA, 2)
    above = rotated(coef, BETA, -2)
    near = swapped(coef, "zl", 1)
    xs, route = lax.axis_size("x"), []
    for i in range(xs):
        route += [(2 * i, 2 * ((i + 1) % xs)), (2 * i + 1, 2 * ((i - 1) % xs) + 1)]
    far = lax.ppermute(near, ALPHA, route)

    parts = density_parts(where, acc, mate, pair_mate)
    coupling, scale, placed = staged(
        where, beta_cols, pair_coupling, pair_alpha.T, beta_ops, parts[0]
    )
    got = [swapped(parts[k], "y", k) for k in (1, 3, 2)]
    total = parts[0].astype(F32)
    for part in got:
        total = total + part.astype(F32)
    total = total.astype(BF16)
    total, coupling, scale, placed = lax.optimization_barrier((total, coupling, scale, placed))

    zs = lax.axis_size("zh")
    steps = [[(2 * i + h, 2 * (i ^ m[h]) + h) for i in range(zs) for h in (0, 1)] for m in ((1, 3), (3, 1))]
    first = lax.ppermute(total, ("zh", "c"), steps[0])
    total = (total.astype(F32) + first.astype(F32)).astype(BF16)
    passed = jnp.where(core == 0, above, below)
    total, passed = lax.optimization_barrier((total, passed))
    crossed = swapped(passed, "c", 1)
    second = lax.ppermute(total, ("zh", "c"), steps[1])
    same = same_spin_beta([below, crossed, coef_v, mate, above], placed)
    second, same = lax.optimization_barrier((second, same))

    excited = excited_block(total, second, coupling, scale)
    blocks = [excited] + [swapped(excited, "y", k) for k in (1, 2, 3)]
    same = same_spin_alpha(where, alpha_cols, [coef_v, near, far], alpha_ops, same)
    *blocks, same = lax.optimization_barrier((*blocks, same))

    theirs = mixed_mate(blocks, pair_mate)
    begun = finished_own(where, same, blocks, pair_v, denominators)
    return finished_mate(where, same, swapped(theirs, "c", 1), denominators, begun)


def solution(mesh):
    finer = Mesh(mesh.devices.reshape(4, 2, 4, 4, 2), (*ALPHA, *BETA))
    placed = (
        P(ALPHA, BETA),
        P(BETA, None),
        P(BETA, None),
        P(ALPHA, None),
        P(ALPHA, None),
        P(ALPHA, None),
        P(BETA, None),
        P(),
        P(ALPHA, BETA),
    )
    return jax.shard_map(
        local, mesh=finer, in_specs=placed, out_specs=P(ALPHA, BETA), check_vma=False
    )
```

time: 79 us -> 66.6 us (0.84)
  local copies, waits for them, and re-layouts: 8.57 us -> 1.02 us
  starting transfers between devices: 33.4 us -> 28.3 us
  Pallas kernels: 11.3 us -> 15.6 us
  waiting for transfers between devices: 23.8 us -> 20 us
    ppermute x13 -> x11, waiting for transfers between devices: 19.2 us -> 0.03 us  [swapped(): return lax.ppermute(block, axis, [(i, i ^ mask) for i in range(count)])]
    ppermute x13 -> x11, starting transfers between devices: 26.5 us -> 15.8 us  [swapped(): return lax.ppermute(block, axis, [(i, i ^ mask) for i in range(count)])]
    ppermute x0 -> x2, waiting for transfers between devices: none -> 9.6 us  [the longest x1 6.18 us: local(): first = lax.ppermute(total, ('zh', 'c'), steps[0])]
    unnamed x14, local copies, waits for them, and re-layouts: 8.49 us -> 0.93 us
    ppermute x2, waiting for transfers between devices: 4.52 us -> 10.3 us  [rotated(): lax.ppermute(block, axis, [(i, (i + distance) % count) for i in range(cou...]
    ppermute x0 -> x2, starting transfers between devices: none -> 4.36 us  [the longest x1 3.11 us: local(): first = lax.ppermute(total, ('zh', 'c'), steps[0])]
    pallas_call x6 -> x9, Pallas kernels: 11.3 us -> 15.6 us  [call(): pl.pallas_call(kernel, out_shape=outs, in_specs=specs, out_specs=out_spec...]
    select_n x3 -> x1, other arithmetic: 1.36 us -> 0.03 us  [local(): passed = jnp.where(core == 0, above, below)]
  transfers between devices with their start and end apart: 16 -> 16, of which waited for: 9 -> 4; matrix products, arithmetic and copies ran while one was open for 2% -> 2% of each run, Pallas kernels for 11% -> 19%
where the time goes in v2:
time: 66.6 us; the launch traced here: 66.4 us
  starting transfers between devices  28.3 us (42%)
  waiting for transfers between devices  20 us (30%)
  Pallas kernels  15.6 us (23%)
  other arithmetic  1.2 us (2%)
  local copies, waits for them, and re-layouts  1.02 us (2%)
    ppermute x11, starting transfers between devices, swapped(): return lax.ppermute(block, axis, [(i, i ^ mask) for i in range(count)])  15.8 us
    pallas_call x9, Pallas kernels, call(): pl.pallas_call(kernel, out_shape=outs, in_specs=specs, out_specs=out_spec...  15.6 us
    ppermute x2, waiting for transfers between devices, rotated(): lax.ppermute(block, axis, [(i, (i + distance) % count) for i in range(cou...  10.3 us
    ppermute x2, starting transfers between devices, rotated(): lax.ppermute(block, axis, [(i, (i + distance) % count) for i in range(cou...  6.84 us
    ppermute x1, waiting for transfers between devices, local(): first = lax.ppermute(total, ('zh', 'c'), steps[0])  6.18 us
    ppermute x1, waiting for transfers between devices, local(): second = lax.ppermute(total, ('zh', 'c'), steps[1])  3.41 us
    ppermute x1, starting transfers between devices, local(): first = lax.ppermute(total, ('zh', 'c'), steps[0])  3.11 us
  transfers between devices with their start and end apart: 16, of which 4 were waited for; matrix products, arithmetic and copies ran while one was open for 2% of the time, Pallas kernels for 19%

profile of v2, /device:TPU:1, one launch (start us, length us, event | category | flops | bytes accessed | tf_op | source)
XLA Modules:
  0.0 66.4 jit_solution(17977147020619773126)
XLA Ops:
  0.0 3.2 %collective-permute-start = (bf16[1024,128]{1,0:T(8,128)(2,1)}, bf16[1024,128]{1,0:T(8,128)(2,1)S(1)}, u32[]{:S(2)}, u32[]{:S(2)}) collective-permute-start(bf16[1024,128]{1,0:T(8,128)(2,1)} %coef_ref.1), channel_id=1, source_target_pairs={{0,1},{1,0},{2,3},{3,2},{4,5},{5,4},{6,7},{7,6},{8,9},{9,8},{10,11... | collective-permute-start | bytes 786440 | tf_op jit(solution)/shard_map/ppermute | solution.py:26
  3.3 0.9 %copy-done.3 = bf16[128,576]{0,1:T(8,128)(2,1)S(1)} copy-done((bf16[128,576]{0,1:T(8,128)(2,1)S(1)}, bf16[128,576]{0,1:T(8,128)(2,1)}, u32[]{:S(2)}) %copy-start.3) | copy-done | bytes 147480
  4.3 1.8 %own_density_kernel.1 = (bf16[1024,128]{1,0:T(8,128)(2,1)S(1)}, bf16[576,128]{1,0:T(8,128)(2,1)S(1)}, f32[4,576,128]{2,1,0:T(8,128)S(1)}) custom-call(s32[12]{0:T(128)S(1)} %stack.51.where_ref, bf16[1024,128]{1,0:T(8,128)(2,1)} %coef_ref.1, bf16[576,128]{1,0:T(8,128)(2,1)S(1)} %bitcast.16), custom_call_target="tpu_custom_call" | custom-call | flops 75497472 | bytes 1048576 | tf_op jit(solution)/shard_map/own_density_kernel/pallas_call | solution.py:35
  6.1 1.6 %density_parts_kernel.1 = (bf16[576,128]{1,0:T(8,128)(2,1)S(1)}, bf16[576,128]{1,0:T(8,128)(2,1)}, bf16[576,128]{1,0:T(8,128)(2,1)}, bf16[576,128]{1,0:T(8,128)(2,1)}) custom-call(s32[12]{0:T(128)S(1)} %stack.51.where_ref, f32[4,576,128]{2,1,0:T(8,128)S(1)} %get-tuple-element.28.acc_ref, bf16[1024,128]{1,0:T(8,128)(2,1)S(1)} %collective-permute-done.mate_ref.b3, ...), custom_call_target="tpu_custom_call" | custom-call | flops 75497472 | bytes 1048576 | tf_op jit(solution)/shard_map/density_parts_kernel/pallas_call | solution.py:35
  7.7 1.6 %collective-permute-start.3 = (bf16[576,128]{1,0:T(8,128)(2,1)}, bf16[576,128]{1,0:T(8,128)(2,1)}, u32[]{:S(2)}, u32[]{:S(2)}) collective-permute-start(bf16[576,128]{1,0:T(8,128)(2,1)} %get-tuple-element.31), channel_id=1, source_target_pairs={{0,24},{8,16},{16,8},{24,0},{1,25},{9,17},{17,9},{25,1},{2,26},{10... | collective-permute-start | bytes 442376 | tf_op jit(solution)/shard_map/ppermute | solution.py:26
  9.2 1.7 %collective-permute-start.4 = (bf16[576,128]{1,0:T(8,128)(2,1)}, bf16[576,128]{1,0:T(8,128)(2,1)}, u32[]{:S(2)}, u32[]{:S(2)}) collective-permute-start(bf16[576,128]{1,0:T(8,128)(2,1)} %get-tuple-element.32), channel_id=1, source_target_pairs={{0,16},{8,24},{16,0},{24,8},{1,17},{9,25},{17,1},{25,9},{2,18},{10... | collective-permute-start | bytes 442376 | tf_op jit(solution)/shard_map/ppermute | solution.py:26
  10.9 6.8 %collective-permute-start.6 = (bf16[1024,128]{1,0:T(8,128)(2,1)}, bf16[1024,128]{1,0:T(8,128)(2,1)S(1)}, u32[]{:S(2)}, u32[]{:S(2)}) collective-permute-start(bf16[1024,128]{1,0:T(8,128)(2,1)} %coef_ref.1), channel_id=1, source_target_pairs={{0,30},{1,31},{2,0},{3,1},{4,2},{5,3},{6,4},{7,5},{8,6},{9,7},{10,... | collective-permute-start | bytes 786440 | tf_op jit(solution)/shard_map/ppermute | solution.py:31
  17.8 1.3 %staged_kernel.1 = (bf16[576,576]{1,0:T(8,128)(2,1)S(1)}, f32[128,576]{1,0:T(8,128)S(1)}, bf16[128,640]{1,0:T(8,128)(2,1)S(1)}) custom-call(s32[12]{0:T(128)S(1)} %stack.51.where_ref, s32[1,4]{1,0:T(1,128)S(1)} %copy-done.5, bf16[576,576]{1,0:T(8,128)(2,1)S(1)} %copy-done.2, bf16[576,1024]{1,0:T(8,128)(2,1)S(1)} %bitcast.14, bf16[128,512]{1,0:T(8,128)(2,1)S(1)} %copy-done.4, ...), custom_call_target="tpu_custom_call" | custom-call | flops 331776 | bytes 2097152 | tf_op jit(solution)/shard_map/staged_kernel/pallas_call | solution.py:35
  19.1 0.8 %collective-permute-start.13 = (bf16[1024,128]{1,0:T(8,128)(2,1)}, bf16[1024,128]{1,0:T(8,128)(2,1)S(1)}, u32[]{:S(2)}, u32[]{:S(2)}) collective-permute-start(bf16[1024,128]{1,0:T(8,128)(2,1)} %coef_ref.1), channel_id=1, source_target_pairs={{0,32},{32,0},{1,33},{33,1},{2,34},{34,2},{3,35},{35,3},{4,36},{36... | collective-permute-start | bytes 786440 | tf_op jit(solution)/shard_map/ppermute | solution.py:26
  20.0 1.1 %add_convert_fusion.1 = bf16[576,128]{1,0:T(8,128)(2,1)S(1)} fusion(bf16[576,128]{1,0:T(8,128)(2,1)} %collective-permute-done.4, bf16[576,128]{1,0:T(8,128)(2,1)} %collective-permute-done.3, bf16[576,128]{1,0:T(8,128)(2,1)} %collective-permute-done.2, bf16[576,128]{1,0:T(8,128)(2,1)S(1)} %get-tuple-element.29.tie_ref), kind=kLoop, calls=%fused_computation.1 | loop fusion | flops 589824 | bytes 737280 | tf_op jit(solution)/shard_map/convert_element_type | solution.py:326
  21.1 3.1 %collective-permute-start.5 = (bf16[576,128]{1,0:T(8,128)(2,1)S(1)}, bf16[576,128]{1,0:T(8,128)(2,1)S(1)}, u32[]{:S(2)}, u32[]{:S(2)}) collective-permute-start(bf16[576,128]{1,0:T(8,128)(2,1)S(1)} %add_convert_fusion.1), channel_id=1, source_target_pairs={{0,2},{1,7},{2,0},{3,5},{4,6},{5,3},{6,4},{7,1},{8,10},{9,15},{10,... | collective-permute-start | bytes 442376 | tf_op jit(solution)/shard_map/ppermute | solution.py:331
  24.2 2.5 %collective-permute-done.6.b4 = bf16[1024,128]{1,0:T(8,128)(2,1)S(1)} collective-permute-done((bf16[1024,128]{1,0:T(8,128)(2,1)}, bf16[1024,128]{1,0:T(8,128)(2,1)S(1)}, u32[]{:S(2)}, u32[]{:S(2)}) %collective-permute-start.6) | collective-permute-done | bytes 262176 | tf_op jit(solution)/shard_map/ppermute | solution.py:31
  26.7 7.9 %collective-permute-done.7.b0 = bf16[1024,128]{1,0:T(8,128)(2,1)S(1)} collective-permute-done((bf16[1024,128]{1,0:T(8,128)(2,1)}, bf16[1024,128]{1,0:T(8,128)(2,1)S(1)}, u32[]{:S(2)}, u32[]{:S(2)}) %collective-permute-start.7) | collective-permute-done | bytes 262176 | tf_op jit(solution)/shard_map/ppermute | solution.py:31
  34.6 6.2 %collective-permute-done.5 = bf16[576,128]{1,0:T(8,128)(2,1)S(1)} collective-permute-done((bf16[576,128]{1,0:T(8,128)(2,1)S(1)}, bf16[576,128]{1,0:T(8,128)(2,1)S(1)}, u32[]{:S(2)}, u32[]{:S(2)}) %collective-permute-start.5) | collective-permute-done | bytes 147488 | tf_op jit(solution)/shard_map/ppermute | solution.py:331
  40.9 1.3 %collective-permute-start.14 = (bf16[1024,128]{1,0:T(8,128)(2,1)S(1)}, bf16[1024,128]{1,0:T(8,128)(2,1)S(1)}, u32[]{:S(2)}, u32[]{:S(2)}) collective-permute-start(bf16[1024,128]{1,0:T(8,128)(2,1)S(1)} %collective-permute-done.13.near_ref), channel_id=1, source_target_pairs={{0,64},{32,224},{64,128},{96,32},{128,192},{160,96},{192,0},{224,1... | collective-permute-start | bytes 786440 | tf_op jit(solution)/shard_map/ppermute | solution.py:316
  42.2 1.2 %collective-permute-start.8 = (bf16[576,128]{1,0:T(8,128)(2,1)S(1)}, bf16[576,128]{1,0:T(8,128)(2,1)S(1)}, u32[]{:S(2)}, u32[]{:S(2)}) collective-permute-start(bf16[576,128]{1,0:T(8,128)(2,1)S(1)} %add_convert_fusion.near_ref), channel_id=1, source_target_pairs={{0,6},{1,3},{2,4},{3,1},{4,2},{5,7},{6,0},{7,5},{8,14},{9,11},{10,... | collective-permute-start | bytes 442376 | tf_op jit(solution)/shard_map/ppermute | solution.py:336
  43.5 0.5 same_spin_beta_kernel.1.start_ref
  44.0 3.4 %collective-permute-done.8.far_ref = bf16[576,128]{1,0:T(8,128)(2,1)S(1)} collective-permute-done((bf16[576,128]{1,0:T(8,128)(2,1)S(1)}, bf16[576,128]{1,0:T(8,128)(2,1)S(1)}, u32[]{:S(2)}, u32[]{:S(2)}) %collective-permute-start.8) | collective-permute-done | bytes 147488 | tf_op jit(solution)/shard_map/ppermute | solution.py:336
  47.8 0.9 %collective-permute-start.10 = (bf16[128,576]{1,0:T(8,128)(2,1)S(1)}, bf16[128,576]{1,0:T(8,128)(2,1)S(1)}, u32[]{:S(2)}, u32[]{:S(2)}) collective-permute-start(bf16[128,576]{1,0:T(8,128)(2,1)S(1)} %excited_block_kernel.1.refs_0_.e0), channel_id=1, source_target_pairs={{0,8},{8,0},{16,24},{24,16},{1,9},{9,1},{17,25},{25,17},{2,10},{10... | collective-permute-start | bytes 442376 | tf_op jit(solution)/shard_map/ppermute | solution.py:26
  48.7 3.0 %collective-permute-start.11 = (bf16[128,576]{1,0:T(8,128)(2,1)S(1)}, bf16[128,576]{1,0:T(8,128)(2,1)S(1)}, u32[]{:S(2)}, u32[]{:S(2)}) collective-permute-start(bf16[128,576]{1,0:T(8,128)(2,1)S(1)} %excited_block_kernel.1.refs_0_.e0), channel_id=1, source_target_pairs={{0,16},{8,24},{16,0},{24,8},{1,17},{9,25},{17,1},{25,9},{2,18},{10... | collective-permute-start | bytes 442376 | tf_op jit(solution)/shard_map/ppermute | solution.py:26
  51.8 6.8 %same_spin_alpha_kernel.1.same_ref = f32[1024,128]{1,0:T(8,128)S(1)} custom-call(s32[12]{0:T(128)S(1)} %stack.51.where_ref, s32[1,4]{1,0:T(1,128)S(1)} %copy-done.6, bf16[1024,128]{1,0:T(8,128)(2,1)S(1)} %get-tuple-element.39.b2.own_ref, bf16[1024,128]{1,0:T(8,128)(2,1)S(1)} %collective-permute-done.13.near_ref, ...), custom_call_target="tpu_custom_call" | custom-call | flops 1073741824 | bytes 10485760 | tf_op jit(solution)/shard_map/same_spin_alpha_kernel/pallas_call | solution.py:35
  59.0 4.5 %collective-permute-start.15 = (bf16[4,128,128]{2,1,0:T(8,128)(2,1)S(1)}, bf16[4,128,128]{2,1,0:T(8,128)(2,1)S(1)}, u32[]{:S(2)}, u32[]{:S(2)}) collective-permute-start(bf16[4,128,128]{2,1,0:T(8,128)(2,1)S(1)} %mixed_mate_kernel.1), channel_id=1, source_target_pairs={{0,1},{1,0},{2,3},{3,2},{4,5},{5,4},{6,7},{7,6},{8,9},{9,8},{10,11... | collective-permute-start | bytes 393224 | tf_op jit(solution)/shard_map/ppermute | solution.py:26
  63.4 1.5 %finished_own_kernel.1.begun_ref = f32[1024,128]{1,0:T(8,128)} custom-call(s32[12]{0:T(128)S(1)} %stack.51.where_ref, f32[1024,128]{1,0:T(8,128)S(1)} %same_spin_alpha_kernel.1.same_ref, bf16[128,576]{1,0:T(8,128)(2,1)S(1)} %excited_block_kernel.1.refs_0_.e0, bf16[128,576]{1,0:T(8,128)(2,1)S(1)} %collective-permute-done.10.refs_1_.e1, ...), custom_call_target="tpu_custom_call" | custom-call | flops 78643200 | bytes 2097152 | tf_op jit(solution)/shard_map/finished_own_kernel/pallas_call | solution.py:35
  65.0 1.3 %finished_mate_kernel.1 = f32[1024,128]{1,0:T(8,128)} custom-call(s32[12]{0:T(128)S(1)} %stack.51.where_ref, f32[1024,128]{1,0:T(8,128)S(1)} %same_spin_alpha_kernel.1.same_ref, bf16[4,128,128]{2,1,0:T(8,128)(2,1)S(1)} %collective-permute-done.15.theirs_ref, f32[1024,128]{1,0:T(8,128)S(1)} %copy-done, ...), custom_call_target="tpu_custom_call", output_to_operand_aliasing={{}: (4, {})} | custom-call | flops 262144 | bytes 2097152 | tf_op jit(solution)/shard_map/finished_mate_kernel/pallas_call | solution.py:35
  (35 shorter events, 1.1 us)
Async XLA Ops:
  0.0 17.8 %copy-start.1 = (bf16[1024,576]{0,1:T(8,128)(2,1)S(1)}, bf16[1024,576]{0,1:T(8,128)(2,1)}, u32[]{:S(2)}) copy-start(bf16[1024,576]{0,1:T(8,128)(2,1)} %param.14) | copy-start | bytes 3538948
  0.0 17.8 %copy-start.2 = (bf16[576,576]{1,0:T(8,128)(2,1)S(1)}, bf16[576,576]{1,0:T(8,128)(2,1)}, u32[]{:S(2)}) copy-start(bf16[576,576]{1,0:T(8,128)(2,1)} %c_ref.1) | copy-start | bytes 1990660
  0.0 6.1 %collective-permute-start = (bf16[1024,128]{1,0:T(8,128)(2,1)}, bf16[1024,128]{1,0:T(8,128)(2,1)S(1)}, u32[]{:S(2)}, u32[]{:S(2)}) collective-permute-start(bf16[1024,128]{1,0:T(8,128)(2,1)} %coef_ref.1), channel_id=1, source_target_pairs={{0,1},{1,0},{2,3},{3,2},{4,5},{5,4},{6,7},{7,6},{8,9},{9,8},{10,11... | collective-permute-start | bytes 786440 | tf_op jit(solution)/shard_map/ppermute | solution.py:26
  3.2 2.8 %collective-permute-start.1 = (bf16[576,128]{1,0:T(8,128)(2,1)}, bf16[576,128]{1,0:T(8,128)(2,1)S(1)}, u32[]{:S(2)}, u32[]{:S(2)}) collective-permute-start(bf16[576,128]{1,0:T(8,128)(2,1)} %bitcast.15), channel_id=1, source_target_pairs={{0,1},{1,0},{2,3},{3,2},{4,5},{5,4},{6,7},{7,6},{8,9},{9,8},{10,11... | collective-permute-start | bytes 442376 | tf_op jit(solution)/shard_map/ppermute | solution.py:26
  3.3 0.9 %copy-start.3 = (bf16[128,576]{0,1:T(8,128)(2,1)S(1)}, bf16[128,576]{0,1:T(8,128)(2,1)}, u32[]{:S(2)}) copy-start(bf16[128,576]{0,1:T(8,128)(2,1)} %param.15) | copy-start | bytes 442372
  4.3 13.5 %copy-start.4 = (bf16[128,512]{1,0:T(8,128)(2,1)S(1)}, bf16[128,512]{1,0:T(8,128)(2,1)}, u32[]{:S(2)}) copy-start(bf16[128,512]{1,0:T(8,128)(2,1)} %ops_ref.2) | copy-start | bytes 393220
  4.3 13.5 %copy-start.5 = (s32[1,4]{1,0:T(1,128)S(1)}, s32[1,4]{1,0:T(1,128)}, u32[]{:S(2)}) copy-start(s32[1,4]{1,0:T(1,128)} %cols_ref.2) | copy-start | bytes 52
  7.7 11.5 %collective-permute-start.2 = (bf16[576,128]{1,0:T(8,128)(2,1)}, bf16[576,128]{1,0:T(8,128)(2,1)}, u32[]{:S(2)}, u32[]{:S(2)}) collective-permute-start(bf16[576,128]{1,0:T(8,128)(2,1)} %get-tuple-element.30), channel_id=1, source_target_pairs={{0,8},{8,0},{16,24},{24,16},{1,9},{9,1},{17,25},{25,17},{2,10},{10... | collective-permute-start | bytes 442376 | tf_op jit(solution)/shard_map/ppermute | solution.py:26
  7.7 12.3 %collective-permute-start.3 = (bf16[576,128]{1,0:T(8,128)(2,1)}, bf16[576,128]{1,0:T(8,128)(2,1)}, u32[]{:S(2)}, u32[]{:S(2)}) collective-permute-start(bf16[576,128]{1,0:T(8,128)(2,1)} %get-tuple-element.31), channel_id=1, source_target_pairs={{0,24},{8,16},{16,8},{24,0},{1,25},{9,17},{17,9},{25,1},{2,26},{10... | collective-permute-start | bytes 442376 | tf_op jit(solution)/shard_map/ppermute | solution.py:26
  9.2 10.7 %collective-permute-start.4 = (bf16[576,128]{1,0:T(8,128)(2,1)}, bf16[576,128]{1,0:T(8,128)(2,1)}, u32[]{:S(2)}, u32[]{:S(2)}) collective-permute-start(bf16[576,128]{1,0:T(8,128)(2,1)} %get-tuple-element.32), channel_id=1, source_target_pairs={{0,16},{8,24},{16,0},{24,8},{1,17},{9,25},{17,1},{25,9},{2,18},{10... | collective-permute-start | bytes 442376 | tf_op jit(solution)/shard_map/ppermute | solution.py:26
  10.9 15.8 %collective-permute-start.6 = (bf16[1024,128]{1,0:T(8,128)(2,1)}, bf16[1024,128]{1,0:T(8,128)(2,1)S(1)}, u32[]{:S(2)}, u32[]{:S(2)}) collective-permute-start(bf16[1024,128]{1,0:T(8,128)(2,1)} %coef_ref.1), channel_id=1, source_target_pairs={{0,30},{1,31},{2,0},{3,1},{4,2},{5,3},{6,4},{7,5},{8,6},{9,7},{10,... | collective-permute-start | bytes 786440 | tf_op jit(solution)/shard_map/ppermute | solution.py:31
  17.8 16.8 %collective-permute-start.7 = (bf16[1024,128]{1,0:T(8,128)(2,1)}, bf16[1024,128]{1,0:T(8,128)(2,1)S(1)}, u32[]{:S(2)}, u32[]{:S(2)}) collective-permute-start(bf16[1024,128]{1,0:T(8,128)(2,1)} %coef_ref.1), channel_id=1, source_target_pairs={{0,2},{1,3},{2,4},{3,5},{4,6},{5,7},{6,8},{7,9},{8,10},{9,11},{10,... | collective-permute-start | bytes 786440 | tf_op jit(solution)/shard_map/ppermute | solution.py:31
  19.1 21.8 %collective-permute-start.13 = (bf16[1024,128]{1,0:T(8,128)(2,1)}, bf16[1024,128]{1,0:T(8,128)(2,1)S(1)}, u32[]{:S(2)}, u32[]{:S(2)}) collective-permute-start(bf16[1024,128]{1,0:T(8,128)(2,1)} %coef_ref.1), channel_id=1, source_target_pairs={{0,32},{32,0},{1,33},{33,1},{2,34},{34,2},{3,35},{35,3},{4,36},{36... | collective-permute-start | bytes 786440 | tf_op jit(solution)/shard_map/ppermute | solution.py:26
  21.1 19.7 %collective-permute-start.5 = (bf16[576,128]{1,0:T(8,128)(2,1)S(1)}, bf16[576,128]{1,0:T(8,128)(2,1)S(1)}, u32[]{:S(2)}, u32[]{:S(2)}) collective-permute-start(bf16[576,128]{1,0:T(8,128)(2,1)S(1)} %add_convert_fusion.1), channel_id=1, source_target_pairs={{0,2},{1,7},{2,0},{3,5},{4,6},{5,3},{6,4},{7,1},{8,10},{9,15},{10,... | collective-permute-start | bytes 442376 | tf_op jit(solution)/shard_map/ppermute | solution.py:331
  40.8 2.7 %collective-permute-start.9 = (bf16[1024,128]{1,0:T(8,128)(2,1)S(1)}, bf16[1024,128]{1,0:T(8,128)(2,1)S(1)}, u32[]{:S(2)}, u32[]{:S(2)}) collective-permute-start(bf16[1024,128]{1,0:T(8,128)(2,1)S(1)} %broadcast_select_fusion), channel_id=1, source_target_pairs={{0,1},{1,0},{2,3},{3,2},{4,5},{5,4},{6,7},{7,6},{8,9},{9,8},{10,11... | collective-permute-start | bytes 786440 | tf_op jit(solution)/shard_map/ppermute | solution.py:26
  40.9 10.8 %collective-permute-start.14 = (bf16[1024,128]{1,0:T(8,128)(2,1)S(1)}, bf16[1024,128]{1,0:T(8,128)(2,1)S(1)}, u32[]{:S(2)}, u32[]{:S(2)}) collective-permute-start(bf16[1024,128]{1,0:T(8,128)(2,1)S(1)} %collective-permute-done.13.near_ref), channel_id=1, source_target_pairs={{0,64},{32,224},{64,128},{96,32},{128,192},{160,96},{192,0},{224,1... | collective-permute-start | bytes 786440 | tf_op jit(solution)/shard_map/ppermute | solution.py:316
  42.2 5.2 %collective-permute-start.8 = (bf16[576,128]{1,0:T(8,128)(2,1)S(1)}, bf16[576,128]{1,0:T(8,128)(2,1)S(1)}, u32[]{:S(2)}, u32[]{:S(2)}) collective-permute-start(bf16[576,128]{1,0:T(8,128)(2,1)S(1)} %add_convert_fusion.near_ref), channel_id=1, source_target_pairs={{0,6},{1,3},{2,4},{3,1},{4,2},{5,7},{6,0},{7,5},{8,14},{9,11},{10,... | collective-permute-start | bytes 442376 | tf_op jit(solution)/shard_map/ppermute | solution.py:336
  44.0 7.8 %copy-start.6 = (s32[1,4]{1,0:T(1,128)S(1)}, s32[1,4]{1,0:T(1,128)}, u32[]{:S(2)}) copy-start(s32[1,4]{1,0:T(1,128)} %cols_ref.3) | copy-start | bytes 52
  47.8 10.8 %collective-permute-start.10 = (bf16[128,576]{1,0:T(8,128)(2,1)S(1)}, bf16[128,576]{1,0:T(8,128)(2,1)S(1)}, u32[]{:S(2)}, u32[]{:S(2)}) collective-permute-start(bf16[128,576]{1,0:T(8,128)(2,1)S(1)} %excited_block_kernel.1.refs_0_.e0), channel_id=1, source_target_pairs={{0,8},{8,0},{16,24},{24,16},{1,9},{9,1},{17,25},{25,17},{2,10},{10... | collective-permute-start | bytes 442376 | tf_op jit(solution)/shard_map/ppermute | solution.py:26
  48.7 9.9 %collective-permute-start.11 = (bf16[128,576]{1,0:T(8,128)(2,1)S(1)}, bf16[128,576]{1,0:T(8,128)(2,1)S(1)}, u32[]{:S(2)}, u32[]{:S(2)}) collective-permute-start(bf16[128,576]{1,0:T(8,128)(2,1)S(1)} %excited_block_kernel.1.refs_0_.e0), channel_id=1, source_target_pairs={{0,16},{8,24},{16,0},{24,8},{1,17},{9,25},{17,1},{25,9},{2,18},{10... | collective-permute-start | bytes 442376 | tf_op jit(solution)/shard_map/ppermute | solution.py:26
  51.6 7.0 %collective-permute-start.12 = (bf16[128,576]{1,0:T(8,128)(2,1)S(1)}, bf16[128,576]{1,0:T(8,128)(2,1)S(1)}, u32[]{:S(2)}, u32[]{:S(2)}) collective-permute-start(bf16[128,576]{1,0:T(8,128)(2,1)S(1)} %excited_block_kernel.1.refs_0_.e0), channel_id=1, source_target_pairs={{0,24},{8,16},{16,8},{24,0},{1,25},{9,17},{17,9},{25,1},{2,26},{10... | collective-permute-start | bytes 442376 | tf_op jit(solution)/shard_map/ppermute | solution.py:26
  58.6 4.8 %copy-start = (f32[1024,128]{1,0:T(8,128)S(1)}, f32[1024,128]{1,0:T(8,128)}, u32[]{:S(2)}) copy-start(f32[1024,128]{1,0:T(8,128)} %den_ref.3) | copy-start | bytes 1572868
  59.0 6.0 %collective-permute-start.15 = (bf16[4,128,128]{2,1,0:T(8,128)(2,1)S(1)}, bf16[4,128,128]{2,1,0:T(8,128)(2,1)S(1)}, u32[]{:S(2)}, u32[]{:S(2)}) collective-permute-start(bf16[4,128,128]{2,1,0:T(8,128)(2,1)S(1)} %mixed_mate_kernel.1), channel_id=1, source_target_pairs={{0,1},{1,0},{2,3},{3,2},{4,5},{5,4},{6,7},{7,6},{8,9},{9,8},{10,11... | collective-permute-start | bytes 393224 | tf_op jit(solution)/shard_map/ppermute | solution.py:26

commit v3 on v2

--- a/solution.py
+++ b/solution.py
@@ -32,6 +32,10 @@
 
 
 def call(kernel, outs, args, specs, cost, scratch=(), aliases=None, out_specs=None, limit=16):
+    args = [
+        pltpu.with_memory_space_constraint(arg, pltpu.HBM) if spec is HBM else arg
+        for arg, spec in zip(args, specs)
+    ]
     return pl.pallas_call(
         kernel,
         out_shape=outs,
@@ -53,10 +57,8 @@
     return pl.ds(pl.multiple_of(where_ref[k] * width, width), width)
 
 
-def own_density(where, coef, pair_t):
-    pairs, width = pair_t.shape
-
-    def own_density_kernel(where_ref, coef_ref, pair_ref, coef_out, pair_out, acc_out, sems):
+def loaded(coef, pair_t):
+    def loaded_kernel(coef_ref, pair_ref, coef_out, pair_out, sems):
         copies = [
             pltpu.make_async_copy(coef_ref, coef_out, sems.at[0]),
             pltpu.make_async_copy(pair_ref, pair_out, sems.at[1]),
@@ -65,37 +67,33 @@
             copy.start()
         for copy in copies:
             copy.wait()
-        left = pair_out[...]
-        for k in range(4):
-            right = coef_out[block_rows(where_ref, k, width), :]
-            acc_out[k] = dot(left, right, ((1,), (1,)))
-
-    return call(
-        own_density_kernel,
-        [shape(coef.shape), shape(pair_t.shape), shape((4, pairs, width), F32)],
-        (where, coef, pair_t),
-        [SMEM, HBM, HBM],
-        (8 * pairs * width * width, 1 * MIB),
+
+    return call(
+        loaded_kernel,
+        [shape(coef.shape), shape(pair_t.shape)],
+        (coef, pair_t),
+        [HBM, HBM],
+        (0, 1 * MIB),
         [pltpu.SemaphoreType.DMA((2,))],
-        limit=16,
-    )
-
-
-def density_parts(where, acc, mate, pair_mate):
+    )
+
+
+def density_parts(where, own, mate, pair_own, pair_mate):
     pairs, width = pair_mate.shape
 
-    def density_parts_kernel(where_ref, acc_ref, mate_ref, pair_ref, *outs):
-        left = pair_ref[...]
+    def density_parts_kernel(where_ref, own_ref, mate_ref, po_ref, pm_ref, *outs):
+        left = jnp.concatenate([po_ref[...], pm_ref[...]], axis=1)
         for k, out in enumerate(outs):
-            right = mate_ref[block_rows(where_ref, k, width), :]
-            out[...] = (acc_ref[k] + dot(left, right, ((1,), (1,)))).astype(BF16)
+            rows = block_rows(where_ref, k, width)
+            right = jnp.concatenate([own_ref[rows, :], mate_ref[rows, :]], axis=1)
+            out[...] = dot(left, right, ((1,), (1,))).astype(BF16)
 
     return call(
         density_parts_kernel,
         [shape((pairs, width))] * 4,
-        (where, acc, mate, pair_mate),
-        [SMEM] + [VMEM] * 3,
-        (8 * pairs * width * width, 1 * MIB),
+        (where, own, mate, pair_own, pair_mate),
+        [SMEM] + [VMEM] * 4,
+        (16 * pairs * width * width, 1 * MIB),
     )
 
 
@@ -220,7 +218,7 @@
         finished_mate_kernel,
         [shape((rows, width), F32)],
         (where, same, theirs, denominators, begun),
-        [SMEM] + [VMEM] * 3 + [HBM],
+        [SMEM] + [VMEM] * 3 + [ANY],
         (rows * width * 2, 2 * MIB),
         [pltpu.VMEM((4, width, width), F32), pltpu.SemaphoreType.DMA((4,))],
         aliases={4: 0},
@@ -280,7 +278,7 @@
         [SMEM, SMEM] + [VMEM] * 3 + [HBM, VMEM],
         (2 * rows * width * depth * 4, 10 * MIB),
         [pltpu.VMEM((steps, rows, step), BF16), pltpu.SemaphoreType.DMA((steps,))],
-        limit=48,
+        limit=24,
     )[0]
 
 
@@ -305,7 +303,7 @@
     pair_t = pair_beta.T
     mate = swapped(coef, "c", 1)
     pair_mate = swapped(pair_t, "c", 1)
-    coef_v, pair_v, acc = own_density(where, coef, pair_t)
+    coef_v, pair_v = loaded(coef, pair_t)
 
     below = rotated(coef, BETA, 2)
     above = rotated(coef, BETA, -2)
@@ -315,11 +313,12 @@
         route += [(2 * i, 2 * ((i + 1) % xs)), (2 * i + 1, 2 * ((i - 1) % xs) + 1)]
     far = lax.ppermute(near, ALPHA, route)
 
-    parts = density_parts(where, acc, mate, pair_mate)
+    parts = density_parts(where, coef_v, mate, pair_v, pair_mate)
     coupling, scale, placed = staged(
         where, beta_cols, pair_coupling, pair_alpha.T, beta_ops, parts[0]
     )
     got = [swapped(parts[k], "y", k) for k in (1, 3, 2)]
+    *got, below, above = lax.optimization_barrier((*got, below, above))
     total = parts[0].astype(F32)
     for part in got:
         total = total + part.astype(F32)

time: 66.6 us -> 59.9 us (0.90)
  waiting for transfers between devices: 20 us -> 11 us
  starting transfers between devices: 28.3 us -> 32.2 us
  other arithmetic: 1.2 us -> 0.15 us
  Pallas kernels: 15.6 us -> 14.7 us
    ppermute x2, waiting for transfers between devices: 10.3 us -> 0.07 us  [rotated(): lax.ppermute(block, axis, [(i, (i + distance) % count) for i in range(cou...]
    ppermute x11, starting transfers between devices: 15.8 us -> 19.9 us  [swapped(): return lax.ppermute(block, axis, [(i, i ^ mask) for i in range(count)])]
    ppermute x1, starting transfers between devices: 3.11 us -> 0.77 us  [local(): first = lax.ppermute(total, ('zh', 'c'), steps[0])]
    ppermute x1, starting transfers between devices: 1.25 us -> 3.41 us  [local(): second = lax.ppermute(total, ('zh', 'c'), steps[1])]
    ppermute x1, waiting for transfers between devices: 6.18 us -> 8.04 us  [local(): first = lax.ppermute(total, ('zh', 'c'), steps[0])]
    ppermute x1, waiting for transfers between devices: 3.41 us -> 2.31 us  [local(): second = lax.ppermute(total, ('zh', 'c'), steps[1])]
    convert_element_type x1, other arithmetic: 1.13 us -> 0.08 us  [local(): total = total.astype(BF16)]
    pallas_call x9, Pallas kernels: 15.6 us -> 14.7 us  [call(): pl.pallas_call(kernel, out_shape=outs, in_specs=specs, out_specs=out_spec...]
  transfers between devices with their start and end apart: 16 -> 16, of which waited for: 4 -> 4; matrix products, arithmetic and copies ran while one was open for 2% -> 0% of each run, Pallas kernels for 19% -> 22%
where the time goes in v3:
time: 59.9 us; the launch traced here: 59.1 us
  starting transfers between devices  32.2 us (54%)
  Pallas kernels  14.7 us (25%)
  waiting for transfers between devices  11 us (18%)
  local copies, waits for them, and re-layouts  0.75 us (1%)
    ppermute x11, starting transfers between devices, swapped(): return lax.ppermute(block, axis, [(i, i ^ mask) for i in range(count)])  19.9 us
    pallas_call x9, Pallas kernels, call(): pl.pallas_call(kernel, out_shape=outs, in_specs=specs, out_specs=out_spec...  14.7 us
    ppermute x1, waiting for transfers between devices, local(): first = lax.ppermute(total, ('zh', 'c'), steps[0])  8.04 us
    ppermute x2, starting transfers between devices, rotated(): lax.ppermute(block, axis, [(i, (i + distance) % count) for i in range(cou...  6.82 us
    ppermute x1, starting transfers between devices, local(): second = lax.ppermute(total, ('zh', 'c'), steps[1])  3.41 us
    ppermute x1, waiting for transfers between devices, local(): second = lax.ppermute(total, ('zh', 'c'), steps[1])  2.31 us
    ppermute x1, starting transfers between devices, local(): far = lax.ppermute(near, ALPHA, route)  1.29 us
  transfers between devices with their start and end apart: 16, of which 4 were waited for; matrix products, arithmetic and copies ran while one was open for 0% of the time, Pallas kernels for 22%

profile of v3, /device:TPU:1, one launch (start us, length us, event | category | flops | bytes accessed | tf_op | source)
XLA Modules:
  0.0 59.1 jit_solution(13083748603500040702)
XLA Ops:
  0.0 3.2 %collective-permute-start = (bf16[1024,128]{1,0:T(8,128)(2,1)}, bf16[1024,128]{1,0:T(8,128)(2,1)S(1)}, u32[]{:S(2)}, u32[]{:S(2)}) collective-permute-start(bf16[1024,128]{1,0:T(8,128)(2,1)} %coef_ref.1), channel_id=1, source_target_pairs={{0,1},{1,0},{2,3},{3,2},{4,5},{5,4},{6,7},{7,6},{8,9},{9,8},{10,11... | collective-permute-start | bytes 786440 | tf_op jit(solution)/shard_map/ppermute | solution.py:26
  3.2 1.3 %collective-permute-start.5 = (bf16[1024,128]{1,0:T(8,128)(2,1)}, bf16[1024,128]{1,0:T(8,128)(2,1)S(1)}, u32[]{:S(2)}, u32[]{:S(2)}) collective-permute-start(bf16[1024,128]{1,0:T(8,128)(2,1)} %coef_ref.1), channel_id=1, source_target_pairs={{0,2},{1,3},{2,4},{3,5},{4,6},{5,7},{6,8},{7,9},{8,10},{9,11},{10,... | collective-permute-start | bytes 786440 | tf_op jit(solution)/shard_map/ppermute | solution.py:31
  4.6 5.5 %collective-permute-start.6 = (bf16[1024,128]{1,0:T(8,128)(2,1)}, bf16[1024,128]{1,0:T(8,128)(2,1)S(1)}, u32[]{:S(2)}, u32[]{:S(2)}) collective-permute-start(bf16[1024,128]{1,0:T(8,128)(2,1)} %coef_ref.1), channel_id=1, source_target_pairs={{0,30},{1,31},{2,0},{3,1},{4,2},{5,3},{6,4},{7,5},{8,6},{9,7},{10,... | collective-permute-start | bytes 786440 | tf_op jit(solution)/shard_map/ppermute | solution.py:31
  10.1 1.0 %loaded_kernel.1 = (bf16[1024,128]{1,0:T(8,128)(2,1)S(1)}, bf16[576,128]{1,0:T(8,128)(2,1)S(1)}) custom-call(bf16[1024,128]{1,0:T(8,128)(2,1)} %coef_ref.1, bf16[576,128]{1,0:T(8,128)(2,1)} %bitcast.16), custom_call_target="tpu_custom_call" | custom-call | bytes 1048576 | tf_op jit(solution)/shard_map/loaded_kernel/pallas_call | solution.py:39
  11.2 1.0 %density_parts_kernel.1 = (bf16[576,128]{1,0:T(8,128)(2,1)S(1)}, bf16[576,128]{1,0:T(8,128)(2,1)S(1)}, bf16[576,128]{1,0:T(8,128)(2,1)S(1)}, bf16[576,128]{1,0:T(8,128)(2,1)S(1)}) custom-call(s32[12]{0:T(128)S(1)} %stack.51.where_ref, bf16[1024,128]{1,0:T(8,128)(2,1)S(1)} %get-tuple-element.32.own_ref.b2, ...), custom_call_target="tpu_custom_call" | custom-call | flops 150994944 | bytes 1048576 | tf_op jit(solution)/shard_map/density_parts_kernel/pallas_call | solution.py:39
  12.3 0.6 %collective-permute-start.3 = (bf16[576,128]{1,0:T(8,128)(2,1)S(1)}, bf16[576,128]{1,0:T(8,128)(2,1)S(1)}, u32[]{:S(2)}, u32[]{:S(2)}) collective-permute-start(bf16[576,128]{1,0:T(8,128)(2,1)S(1)} %get-tuple-element.36), channel_id=1, source_target_pairs={{0,24},{8,16},{16,8},{24,0},{1,25},{9,17},{17,9},{25,1},{2,26},{10... | collective-permute-start | bytes 442376 | tf_op jit(solution)/shard_map/ppermute | solution.py:26
  13.0 2.6 %collective-permute-start.4 = (bf16[576,128]{1,0:T(8,128)(2,1)S(1)}, bf16[576,128]{1,0:T(8,128)(2,1)S(1)}, u32[]{:S(2)}, u32[]{:S(2)}) collective-permute-start(bf16[576,128]{1,0:T(8,128)(2,1)S(1)} %get-tuple-element.37), channel_id=1, source_target_pairs={{0,16},{8,24},{16,0},{24,8},{1,17},{9,25},{17,1},{25,9},{2,18},{10... | collective-permute-start | bytes 442376 | tf_op jit(solution)/shard_map/ppermute | solution.py:26
  15.6 0.7 %copy-done.1 = s32[1,4]{1,0:T(1,128)S(1)} copy-done((s32[1,4]{1,0:T(1,128)S(1)}, s32[1,4]{1,0:T(1,128)}, u32[]{:S(2)}) %copy-start.1) | copy-done | bytes 40
  16.2 1.8 %staged_kernel.1 = (bf16[576,576]{1,0:T(8,128)(2,1)S(1)}, f32[128,576]{1,0:T(8,128)S(1)}, bf16[128,640]{1,0:T(8,128)(2,1)S(1)}) custom-call(s32[12]{0:T(128)S(1)} %stack.51.where_ref, s32[1,4]{1,0:T(1,128)S(1)} %copy-done.1, bf16[576,576]{1,0:T(8,128)(2,1)} %c_ref.1, bf16[576,1024]{1,0:T(8,128)(2,1)} %bitcast.14, bf16[128,512]{1,0:T(8,128)(2,1)} %ops_ref.2, ...), custom_call_target="tpu_custom_call" | custom-call | flops 331776 | bytes 2097152 | tf_op jit(solution)/shard_map/staged_kernel/pallas_call | solution.py:39
  18.2 4.8 %collective-permute-start.13 = (bf16[1024,128]{1,0:T(8,128)(2,1)}, bf16[1024,128]{1,0:T(8,128)(2,1)S(1)}, u32[]{:S(2)}, u32[]{:S(2)}) collective-permute-start(bf16[1024,128]{1,0:T(8,128)(2,1)} %coef_ref.1), channel_id=1, source_target_pairs={{0,32},{32,0},{1,33},{33,1},{2,34},{34,2},{3,35},{35,3},{4,36},{36... | collective-permute-start | bytes 786440 | tf_op jit(solution)/shard_map/ppermute | solution.py:26
  23.0 0.6 collective-permute-done.4
  23.7 0.8 %collective-permute-start.7 = (bf16[576,128]{1,0:T(8,128)(2,1)S(1)}, bf16[576,128]{1,0:T(8,128)(2,1)S(1)}, u32[]{:S(2)}, u32[]{:S(2)}) collective-permute-start(bf16[576,128]{1,0:T(8,128)(2,1)S(1)} %add_convert_fusion.1), channel_id=1, source_target_pairs={{0,2},{1,7},{2,0},{3,5},{4,6},{5,3},{6,4},{7,1},{8,10},{9,15},{10,... | collective-permute-start | bytes 442376 | tf_op jit(solution)/shard_map/ppermute | solution.py:330
  24.5 8.0 %collective-permute-done.7 = bf16[576,128]{1,0:T(8,128)(2,1)S(1)} collective-permute-done((bf16[576,128]{1,0:T(8,128)(2,1)S(1)}, bf16[576,128]{1,0:T(8,128)(2,1)S(1)}, u32[]{:S(2)}, u32[]{:S(2)}) %collective-permute-start.7) | collective-permute-done | bytes 147488 | tf_op jit(solution)/shard_map/ppermute | solution.py:330
  32.7 1.3 %collective-permute-start.14 = (bf16[1024,128]{1,0:T(8,128)(2,1)S(1)}, bf16[1024,128]{1,0:T(8,128)(2,1)S(1)}, u32[]{:S(2)}, u32[]{:S(2)}) collective-permute-start(bf16[1024,128]{1,0:T(8,128)(2,1)S(1)} %collective-permute-done.13.near_ref), channel_id=1, source_target_pairs={{0,64},{32,224},{64,128},{96,32},{128,192},{160,96},{192,0},{224,1... | collective-permute-start | bytes 786440 | tf_op jit(solution)/shard_map/ppermute | solution.py:314
  33.9 3.4 %collective-permute-start.8 = (bf16[576,128]{1,0:T(8,128)(2,1)S(1)}, bf16[576,128]{1,0:T(8,128)(2,1)S(1)}, u32[]{:S(2)}, u32[]{:S(2)}) collective-permute-start(bf16[576,128]{1,0:T(8,128)(2,1)S(1)} %add_convert_fusion.near_ref), channel_id=1, source_target_pairs={{0,6},{1,3},{2,4},{3,1},{4,2},{5,7},{6,0},{7,5},{8,14},{9,11},{10,... | collective-permute-start | bytes 442376 | tf_op jit(solution)/shard_map/ppermute | solution.py:335
  37.4 0.5 same_spin_beta_kernel.1.start_ref
  37.9 2.3 %collective-permute-done.8.far_ref = bf16[576,128]{1,0:T(8,128)(2,1)S(1)} collective-permute-done((bf16[576,128]{1,0:T(8,128)(2,1)S(1)}, bf16[576,128]{1,0:T(8,128)(2,1)S(1)}, u32[]{:S(2)}, u32[]{:S(2)}) %collective-permute-start.8) | collective-permute-done | bytes 147488 | tf_op jit(solution)/shard_map/ppermute | solution.py:335
  40.2 0.4 excited_block_kernel.1.refs_0_.e0
  40.8 2.6 %collective-permute-start.11 = (bf16[128,576]{1,0:T(8,128)(2,1)S(1)}, bf16[128,576]{1,0:T(8,128)(2,1)S(1)}, u32[]{:S(2)}, u32[]{:S(2)}) collective-permute-start(bf16[128,576]{1,0:T(8,128)(2,1)S(1)} %excited_block_kernel.1.refs_0_.e0), channel_id=1, source_target_pairs={{0,16},{8,24},{16,0},{24,8},{1,17},{9,25},{17,1},{25,9},{2,18},{10... | collective-permute-start | bytes 442376 | tf_op jit(solution)/shard_map/ppermute | solution.py:26
  43.4 1.1 %collective-permute-start.12 = (bf16[128,576]{1,0:T(8,128)(2,1)S(1)}, bf16[128,576]{1,0:T(8,128)(2,1)S(1)}, u32[]{:S(2)}, u32[]{:S(2)}) collective-permute-start(bf16[128,576]{1,0:T(8,128)(2,1)S(1)} %excited_block_kernel.1.refs_0_.e0), channel_id=1, source_target_pairs={{0,24},{8,16},{16,8},{24,0},{1,25},{9,17},{17,9},{25,1},{2,26},{10... | collective-permute-start | bytes 442376 | tf_op jit(solution)/shard_map/ppermute | solution.py:26
  44.5 6.8 %same_spin_alpha_kernel.1.same_ref = f32[1024,128]{1,0:T(8,128)S(1)} custom-call(s32[12]{0:T(128)S(1)} %stack.51.where_ref, s32[1,4]{1,0:T(1,128)S(1)} %copy-done.2, bf16[1024,128]{1,0:T(8,128)(2,1)S(1)} %get-tuple-element.32.own_ref.b2, bf16[1024,128]{1,0:T(8,128)(2,1)S(1)} %collective-permute-done.13.near_ref, ...), custom_call_target="tpu_custom_call" | custom-call | flops 1073741824 | bytes 10485760 | tf_op jit(solution)/shard_map/same_spin_alpha_kernel/pallas_call | solution.py:39
  51.7 4.4 %collective-permute-start.15 = (bf16[4,128,128]{2,1,0:T(8,128)(2,1)S(1)}, bf16[4,128,128]{2,1,0:T(8,128)(2,1)S(1)}, u32[]{:S(2)}, u32[]{:S(2)}) collective-permute-start(bf16[4,128,128]{2,1,0:T(8,128)(2,1)S(1)} %mixed_mate_kernel.1), channel_id=1, source_target_pairs={{0,1},{1,0},{2,3},{3,2},{4,5},{5,4},{6,7},{7,6},{8,9},{9,8},{10,11... | collective-permute-start | bytes 393224 | tf_op jit(solution)/shard_map/ppermute | solution.py:26
  56.1 1.5 %finished_own_kernel.1.begun_ref = f32[1024,128]{1,0:T(8,128)} custom-call(s32[12]{0:T(128)S(1)} %stack.51.where_ref, f32[1024,128]{1,0:T(8,128)S(1)} %same_spin_alpha_kernel.1.same_ref, bf16[128,576]{1,0:T(8,128)(2,1)S(1)} %excited_block_kernel.1.refs_0_.e0, bf16[128,576]{1,0:T(8,128)(2,1)S(1)} %collective-permute-done.10.refs_1_.e1, ...), custom_call_target="tpu_custom_call" | custom-call | flops 78643200 | bytes 2097152 | tf_op jit(solution)/shard_map/finished_own_kernel/pallas_call | solution.py:39
  57.7 1.3 %finished_mate_kernel.1 = f32[1024,128]{1,0:T(8,128)} custom-call(s32[12]{0:T(128)S(1)} %stack.51.where_ref, f32[1024,128]{1,0:T(8,128)S(1)} %same_spin_alpha_kernel.1.same_ref, bf16[4,128,128]{2,1,0:T(8,128)(2,1)S(1)} %collective-permute-done.15.theirs_ref, f32[1024,128]{1,0:T(8,128)S(1)} %copy-done, ...), custom_call_target="tpu_custom_call", output_to_operand_aliasing={{}: (4, {})} | custom-call | flops 262144 | bytes 2097152 | tf_op jit(solution)/shard_map/finished_mate_kernel/pallas_call | solution.py:39
  (27 shorter events, 1.1 us)
Async XLA Ops:
  0.0 44.5 %copy-start.2 = (s32[1,4]{1,0:T(1,128)S(1)}, s32[1,4]{1,0:T(1,128)}, u32[]{:S(2)}) copy-start(s32[1,4]{1,0:T(1,128)} %cols_ref.3) | copy-start | bytes 52
  0.0 11.2 %collective-permute-start = (bf16[1024,128]{1,0:T(8,128)(2,1)}, bf16[1024,128]{1,0:T(8,128)(2,1)S(1)}, u32[]{:S(2)}, u32[]{:S(2)}) collective-permute-start(bf16[1024,128]{1,0:T(8,128)(2,1)} %coef_ref.1), channel_id=1, source_target_pairs={{0,1},{1,0},{2,3},{3,2},{4,5},{5,4},{6,7},{7,6},{8,9},{9,8},{10,11... | collective-permute-start | bytes 786440 | tf_op jit(solution)/shard_map/ppermute | solution.py:26
  3.2 8.0 %collective-permute-start.1 = (bf16[576,128]{1,0:T(8,128)(2,1)}, bf16[576,128]{1,0:T(8,128)(2,1)S(1)}, u32[]{:S(2)}, u32[]{:S(2)}) collective-permute-start(bf16[576,128]{1,0:T(8,128)(2,1)} %bitcast.15), channel_id=1, source_target_pairs={{0,1},{1,0},{2,3},{3,2},{4,5},{5,4},{6,7},{7,6},{8,9},{9,8},{10,11... | collective-permute-start | bytes 442376 | tf_op jit(solution)/shard_map/ppermute | solution.py:26
  3.2 14.9 %collective-permute-start.5 = (bf16[1024,128]{1,0:T(8,128)(2,1)}, bf16[1024,128]{1,0:T(8,128)(2,1)S(1)}, u32[]{:S(2)}, u32[]{:S(2)}) collective-permute-start(bf16[1024,128]{1,0:T(8,128)(2,1)} %coef_ref.1), channel_id=1, source_target_pairs={{0,2},{1,3},{2,4},{3,5},{4,6},{5,7},{6,8},{7,9},{8,10},{9,11},{10,... | collective-permute-start | bytes 786440 | tf_op jit(solution)/shard_map/ppermute | solution.py:31
  4.6 18.4 %collective-permute-start.6 = (bf16[1024,128]{1,0:T(8,128)(2,1)}, bf16[1024,128]{1,0:T(8,128)(2,1)S(1)}, u32[]{:S(2)}, u32[]{:S(2)}) collective-permute-start(bf16[1024,128]{1,0:T(8,128)(2,1)} %coef_ref.1), channel_id=1, source_target_pairs={{0,30},{1,31},{2,0},{3,1},{4,2},{5,3},{6,4},{7,5},{8,6},{9,7},{10,... | collective-permute-start | bytes 786440 | tf_op jit(solution)/shard_map/ppermute | solution.py:31
  12.2 10.8 %collective-permute-start.2 = (bf16[576,128]{1,0:T(8,128)(2,1)S(1)}, bf16[576,128]{1,0:T(8,128)(2,1)S(1)}, u32[]{:S(2)}, u32[]{:S(2)}) collective-permute-start(bf16[576,128]{1,0:T(8,128)(2,1)S(1)} %get-tuple-element.35), channel_id=1, source_target_pairs={{0,8},{8,0},{16,24},{24,16},{1,9},{9,1},{17,25},{25,17},{2,10},{10... | collective-permute-start | bytes 442376 | tf_op jit(solution)/shard_map/ppermute | solution.py:26
  12.3 10.7 %collective-permute-start.3 = (bf16[576,128]{1,0:T(8,128)(2,1)S(1)}, bf16[576,128]{1,0:T(8,128)(2,1)S(1)}, u32[]{:S(2)}, u32[]{:S(2)}) collective-permute-start(bf16[576,128]{1,0:T(8,128)(2,1)S(1)} %get-tuple-element.36), channel_id=1, source_target_pairs={{0,24},{8,16},{16,8},{24,0},{1,25},{9,17},{17,9},{25,1},{2,26},{10... | collective-permute-start | bytes 442376 | tf_op jit(solution)/shard_map/ppermute | solution.py:26
  13.0 10.6 %collective-permute-start.4 = (bf16[576,128]{1,0:T(8,128)(2,1)S(1)}, bf16[576,128]{1,0:T(8,128)(2,1)S(1)}, u32[]{:S(2)}, u32[]{:S(2)}) collective-permute-start(bf16[576,128]{1,0:T(8,128)(2,1)S(1)} %get-tuple-element.37), channel_id=1, source_target_pairs={{0,16},{8,24},{16,0},{24,8},{1,17},{9,25},{17,1},{25,9},{2,18},{10... | collective-permute-start | bytes 442376 | tf_op jit(solution)/shard_map/ppermute | solution.py:26
  15.6 0.7 %copy-start.1 = (s32[1,4]{1,0:T(1,128)S(1)}, s32[1,4]{1,0:T(1,128)}, u32[]{:S(2)}) copy-start(s32[1,4]{1,0:T(1,128)} %cols_ref.2) | copy-start | bytes 52
  18.1 38.0 %copy-start = (f32[1024,128]{1,0:T(8,128)S(1)}, f32[1024,128]{1,0:T(8,128)}, u32[]{:S(2)}) copy-start(f32[1024,128]{1,0:T(8,128)} %den_ref.3) | copy-start | bytes 1572868
  18.2 14.5 %collective-permute-start.13 = (bf16[1024,128]{1,0:T(8,128)(2,1)}, bf16[1024,128]{1,0:T(8,128)(2,1)S(1)}, u32[]{:S(2)}, u32[]{:S(2)}) collective-permute-start(bf16[1024,128]{1,0:T(8,128)(2,1)} %coef_ref.1), channel_id=1, source_target_pairs={{0,32},{32,0},{1,33},{33,1},{2,34},{34,2},{3,35},{35,3},{4,36},{36... | collective-permute-start | bytes 786440 | tf_op jit(solution)/shard_map/ppermute | solution.py:26
  23.7 8.8 %collective-permute-start.7 = (bf16[576,128]{1,0:T(8,128)(2,1)S(1)}, bf16[576,128]{1,0:T(8,128)(2,1)S(1)}, u32[]{:S(2)}, u32[]{:S(2)}) collective-permute-start(bf16[576,128]{1,0:T(8,128)(2,1)S(1)} %add_convert_fusion.1), channel_id=1, source_target_pairs={{0,2},{1,7},{2,0},{3,5},{4,6},{5,3},{6,4},{7,1},{8,10},{9,15},{10,... | collective-permute-start | bytes 442376 | tf_op jit(solution)/shard_map/ppermute | solution.py:330
  32.5 4.8 %collective-permute-start.9 = (bf16[1024,128]{1,0:T(8,128)(2,1)S(1)}, bf16[1024,128]{1,0:T(8,128)(2,1)S(1)}, u32[]{:S(2)}, u32[]{:S(2)}) collective-permute-start(bf16[1024,128]{1,0:T(8,128)(2,1)S(1)} %broadcast_select_fusion), channel_id=1, source_target_pairs={{0,1},{1,0},{2,3},{3,2},{4,5},{5,4},{6,7},{7,6},{8,9},{9,8},{10,11... | collective-permute-start | bytes 786440 | tf_op jit(solution)/shard_map/ppermute | solution.py:26
  32.7 11.8 %collective-permute-start.14 = (bf16[1024,128]{1,0:T(8,128)(2,1)S(1)}, bf16[1024,128]{1,0:T(8,128)(2,1)S(1)}, u32[]{:S(2)}, u32[]{:S(2)}) collective-permute-start(bf16[1024,128]{1,0:T(8,128)(2,1)S(1)} %collective-permute-done.13.near_ref), channel_id=1, source_target_pairs={{0,64},{32,224},{64,128},{96,32},{128,192},{160,96},{192,0},{224,1... | collective-permute-start | bytes 786440 | tf_op jit(solution)/shard_map/ppermute | solution.py:314
  33.9 6.2 %collective-permute-start.8 = (bf16[576,128]{1,0:T(8,128)(2,1)S(1)}, bf16[576,128]{1,0:T(8,128)(2,1)S(1)}, u32[]{:S(2)}, u32[]{:S(2)}) collective-permute-start(bf16[576,128]{1,0:T(8,128)(2,1)S(1)} %add_convert_fusion.near_ref), channel_id=1, source_target_pairs={{0,6},{1,3},{2,4},{3,1},{4,2},{5,7},{6,0},{7,5},{8,14},{9,11},{10,... | collective-permute-start | bytes 442376 | tf_op jit(solution)/shard_map/ppermute | solution.py:335
  40.6 10.8 %collective-permute-start.10 = (bf16[128,576]{1,0:T(8,128)(2,1)S(1)}, bf16[128,576]{1,0:T(8,128)(2,1)S(1)}, u32[]{:S(2)}, u32[]{:S(2)}) collective-permute-start(bf16[128,576]{1,0:T(8,128)(2,1)S(1)} %excited_block_kernel.1.refs_0_.e0), channel_id=1, source_target_pairs={{0,8},{8,0},{16,24},{24,16},{1,9},{9,1},{17,25},{25,17},{2,10},{10... | collective-permute-start | bytes 442376 | tf_op jit(solution)/shard_map/ppermute | solution.py:26
  40.8 10.5 %collective-permute-start.11 = (bf16[128,576]{1,0:T(8,128)(2,1)S(1)}, bf16[128,576]{1,0:T(8,128)(2,1)S(1)}, u32[]{:S(2)}, u32[]{:S(2)}) collective-permute-start(bf16[128,576]{1,0:T(8,128)(2,1)S(1)} %excited_block_kernel.1.refs_0_.e0), channel_id=1, source_target_pairs={{0,16},{8,24},{16,0},{24,8},{1,17},{9,25},{17,1},{25,9},{2,18},{10... | collective-permute-start | bytes 442376 | tf_op jit(solution)/shard_map/ppermute | solution.py:26
  43.4 7.9 %collective-permute-start.12 = (bf16[128,576]{1,0:T(8,128)(2,1)S(1)}, bf16[128,576]{1,0:T(8,128)(2,1)S(1)}, u32[]{:S(2)}, u32[]{:S(2)}) collective-permute-start(bf16[128,576]{1,0:T(8,128)(2,1)S(1)} %excited_block_kernel.1.refs_0_.e0), channel_id=1, source_target_pairs={{0,24},{8,16},{16,8},{24,0},{1,25},{9,17},{17,9},{25,1},{2,26},{10... | collective-permute-start | bytes 442376 | tf_op jit(solution)/shard_map/ppermute | solution.py:26
  51.7 6.0 %collective-permute-start.15 = (bf16[4,128,128]{2,1,0:T(8,128)(2,1)S(1)}, bf16[4,128,128]{2,1,0:T(8,128)(2,1)S(1)}, u32[]{:S(2)}, u32[]{:S(2)}) collective-permute-start(bf16[4,128,128]{2,1,0:T(8,128)(2,1)S(1)} %mixed_mate_kernel.1), channel_id=1, source_target_pairs={{0,1},{1,0},{2,3},{3,2},{4,5},{5,4},{6,7},{7,6},{8,9},{9,8},{10,11... | collective-permute-start | bytes 393224 | tf_op jit(solution)/shard_map/ppermute | solution.py:26

commit v4 on v3

--- a/solution.py
+++ b/solution.py
@@ -246,30 +246,30 @@
 def same_spin_alpha(where, cols, blocks, alpha_ops, start):
     rows, width = start.shape
     depth = blocks[0].shape[0]
-    step = depth // 2
-    steps = alpha_ops.shape[1] // step
+    span = alpha_ops.shape[1]
+    step = 256
     count = lax.axis_size(ALPHA)
 
     def same_spin_alpha_kernel(
-        where_ref, cols_ref, own_ref, near_ref, far_ref, ops_ref, start_ref, out_ref, ops_v, sems
+        where_ref, cols_ref, own_ref, near_ref, far_ref, ops_ref, start_ref, out_ref, ops_v, picked, sems
     ):
         copies = [
-            pltpu.make_async_copy(ops_ref.at[:, s * step : (s + 1) * step], ops_v.at[s], sems.at[s])
-            for s in range(steps)
+            pltpu.make_async_copy(ops_ref.at[r : r + step, :], ops_v.at[r : r + step, :], sems.at[n])
+            for n, r in enumerate(range(0, rows, step))
         ]
         for copy in copies:
             copy.start()
-        for s, copy in enumerate(copies):
-            offset = lax.rem(cols_ref[0, s // 2] - where_ref[10] + 1 + count, count)
-            at = slice((s % 2) * step, (s % 2 + 1) * step)
-            picked = jnp.where(
+        for k in range(span // depth):
+            offset = lax.rem(cols_ref[0, k] - where_ref[10] + 1 + count, count)
+            picked[k * depth : (k + 1) * depth, :] = jnp.where(
                 offset == 1,
-                own_ref[at, :],
-                jnp.where(offset == where_ref[11], near_ref[at, :], far_ref[at, :]),
+                own_ref[...],
+                jnp.where(offset == where_ref[11], near_ref[...], far_ref[...]),
             )
+        for copy, r in zip(copies, range(0, rows, step)):
             copy.wait()
-            before = start_ref[...] if s == 0 else out_ref[...]
-            out_ref[...] = before + dot(ops_v[s], picked)
+            at = slice(r, r + step)
+            out_ref[at, :] = start_ref[at, :] + dot(ops_v[at, :], picked[...])
 
     return call(
         same_spin_alpha_kernel,
@@ -277,7 +277,11 @@
         (where, cols, *blocks, alpha_ops, start),
         [SMEM, SMEM] + [VMEM] * 3 + [HBM, VMEM],
         (2 * rows * width * depth * 4, 10 * MIB),
-        [pltpu.VMEM((steps, rows, step), BF16), pltpu.SemaphoreType.DMA((steps,))],
+        [
+            pltpu.VMEM((rows, span), BF16),
+            pltpu.VMEM((span, width), BF16),
+            pltpu.SemaphoreType.DMA((rows // step,)),
+        ],
         limit=24,
     )[0]
 
@@ -305,26 +309,28 @@
     pair_mate = swapped(pair_t, "c", 1)
     coef_v, pair_v = loaded(coef, pair_t)
 
-    below = rotated(coef, BETA, 2)
-    above = rotated(coef, BETA, -2)
-    near = swapped(coef, "zl", 1)
+    below = rotated(coef_v, BETA, 2)
+    above = rotated(coef_v, BETA, -2)
     xs, route = lax.axis_size("x"), []
     for i in range(xs):
         route += [(2 * i, 2 * ((i + 1) % xs)), (2 * i + 1, 2 * ((i - 1) % xs) + 1)]
-    far = lax.ppermute(near, ALPHA, route)
 
     parts = density_parts(where, coef_v, mate, pair_v, pair_mate)
     coupling, scale, placed = staged(
         where, beta_cols, pair_coupling, pair_alpha.T, beta_ops, parts[0]
     )
     got = [swapped(parts[k], "y", k) for k in (1, 3, 2)]
+    got_first = got[0]
     *got, below, above = lax.optimization_barrier((*got, below, above))
+    start, _ = lax.optimization_barrier((coef_v, got_first))
+    near = swapped(start, "zl", 1)
     total = parts[0].astype(F32)
     for part in got:
         total = total + part.astype(F32)
     total = total.astype(BF16)
     total, coupling, scale, placed = lax.optimization_barrier((total, coupling, scale, placed))
 
+    far = lax.ppermute(near, ALPHA, route)
     zs = lax.axis_size("zh")
     steps = [[(2 * i + h, 2 * (i ^ m[h]) + h) for i in range(zs) for h in (0, 1)] for m in ((1, 3), (3, 1))]
     first = lax.ppermute(total, ("zh", "c"), steps[0])

time: 59.9 us -> 62.7 us (1.047); the launches traced: 59.1 us -> 62.6 us
  waiting for transfers between devices: 11 us -> 23.1 us
  starting transfers between devices: 32.2 us -> 25.5 us
  Pallas kernels: 14.7 us -> 12.9 us
    ppermute x11, waiting for transfers between devices: 0.59 us -> 8.93 us  [swapped(): return lax.ppermute(block, axis, [(i, i ^ mask) for i in range(count)])]
    ppermute x2, waiting for transfers between devices: 0.07 us -> 3.64 us  [rotated(): lax.ppermute(block, axis, [(i, (i + distance) % count) for i in range(cou...]
    ppermute x1, starting transfers between devices: 3.41 us -> 0.01 us  [local(): second = lax.ppermute(total, ('zh', 'c'), steps[1])]
    ppermute x1, waiting for transfers between devices: 2.31 us -> 5.54 us  [local(): second = lax.ppermute(total, ('zh', 'c'), steps[1])]
    ppermute x1, waiting for transfers between devices: 8.04 us -> 4.95 us  [local(): first = lax.ppermute(total, ('zh', 'c'), steps[0])]
    ppermute x11, starting transfers between devices: 19.9 us -> 17 us  [swapped(): return lax.ppermute(block, axis, [(i, i ^ mask) for i in range(count)])]
    pallas_call x9, Pallas kernels: 14.7 us -> 12.9 us  [call(): pl.pallas_call(kernel, out_shape=outs, in_specs=specs, out_specs=out_spec...]
  transfers between devices with their start and end apart: 16 -> 16, of which waited for: 4 -> 8; matrix products, arithmetic and copies ran while one was open for 0% -> 0% of each run, Pallas kernels for 22% -> 18%
where the time goes in v4:
time: 62.7 us; the launch traced here: 62.6 us
  starting transfers between devices  25.5 us (41%)
  waiting for transfers between devices  23.1 us (37%)
  Pallas kernels  12.9 us (21%)
  local copies, waits for them, and re-layouts  0.75 us (1%)
    ppermute x11, starting transfers between devices, swapped(): return lax.ppermute(block, axis, [(i, i ^ mask) for i in range(count)])  17 us
    pallas_call x9, Pallas kernels, call(): pl.pallas_call(kernel, out_shape=outs, in_specs=specs, out_specs=out_spec...  12.9 us
    ppermute x11, waiting for transfers between devices, swapped(): return lax.ppermute(block, axis, [(i, i ^ mask) for i in range(count)])  8.93 us
    ppermute x2, starting transfers between devices, rotated(): lax.ppermute(block, axis, [(i, (i + distance) % count) for i in range(cou...  6.98 us
    ppermute x1, waiting for transfers between devices, local(): second = lax.ppermute(total, ('zh', 'c'), steps[1])  5.54 us
    ppermute x1, waiting for transfers between devices, local(): first = lax.ppermute(total, ('zh', 'c'), steps[0])  4.95 us
    ppermute x2, waiting for transfers between devices, rotated(): lax.ppermute(block, axis, [(i, (i + distance) % count) for i in range(cou...  3.64 us
  transfers between devices with their start and end apart: 16, of which 8 were waited for; matrix products, arithmetic and copies ran while one was open for 0% of the time, Pallas kernels for 18%

profile of v4, /device:TPU:1, one launch (start us, length us, event | category | flops | bytes accessed | tf_op | source)
XLA Modules:
  0.0 62.6 jit_solution(16580895874623967485)
XLA Ops:
  0.0 3.2 %collective-permute-start = (bf16[1024,128]{1,0:T(8,128)(2,1)}, bf16[1024,128]{1,0:T(8,128)(2,1)S(1)}, u32[]{:S(2)}, u32[]{:S(2)}) collective-permute-start(bf16[1024,128]{1,0:T(8,128)(2,1)} %coef_ref.1), channel_id=1, source_target_pairs={{0,1},{1,0},{2,3},{3,2},{4,5},{5,4},{6,7},{7,6},{8,9},{9,8},{10,11... | collective-permute-start | bytes 786440 | tf_op jit(solution)/shard_map/ppermute | solution.py:26
  3.2 1.0 %loaded_kernel.1 = (bf16[1024,128]{1,0:T(8,128)(2,1)S(1)}, bf16[576,128]{1,0:T(8,128)(2,1)S(1)}) custom-call(bf16[1024,128]{1,0:T(8,128)(2,1)} %coef_ref.1, bf16[576,128]{1,0:T(8,128)(2,1)} %bitcast.16), custom_call_target="tpu_custom_call" | custom-call | bytes 1048576 | tf_op jit(solution)/shard_map/loaded_kernel/pallas_call | solution.py:39
  4.3 1.4 %collective-permute-start.5 = (bf16[1024,128]{1,0:T(8,128)(2,1)S(1)}, bf16[1024,128]{1,0:T(8,128)(2,1)S(1)}, u32[]{:S(2)}, u32[]{:S(2)}) collective-permute-start(bf16[1024,128]{1,0:T(8,128)(2,1)S(1)} %get-tuple-element.54.own_ref.b2), channel_id=1, source_target_pairs={{0,2},{1,3},{2,4},{3,5},{4,6},{5,7},{6,8},{7,9},{8,10},{9,11},{10,... | collective-permute-start | bytes 786440 | tf_op jit(solution)/shard_map/ppermute | solution.py:31
  5.7 5.6 %collective-permute-start.6 = (bf16[1024,128]{1,0:T(8,128)(2,1)S(1)}, bf16[1024,128]{1,0:T(8,128)(2,1)S(1)}, u32[]{:S(2)}, u32[]{:S(2)}) collective-permute-start(bf16[1024,128]{1,0:T(8,128)(2,1)S(1)} %get-tuple-element.54.own_ref.b2), channel_id=1, source_target_pairs={{0,30},{1,31},{2,0},{3,1},{4,2},{5,3},{6,4},{7,5},{8,6},{9,7},{10,... | collective-permute-start | bytes 786440 | tf_op jit(solution)/shard_map/ppermute | solution.py:31
  11.4 1.0 %density_parts_kernel.1 = (bf16[576,128]{1,0:T(8,128)(2,1)S(1)}, bf16[576,128]{1,0:T(8,128)(2,1)S(1)}, bf16[576,128]{1,0:T(8,128)(2,1)S(1)}, bf16[576,128]{1,0:T(8,128)(2,1)S(1)}) custom-call(s32[12]{0:T(128)S(1)} %stack.51.where_ref, bf16[1024,128]{1,0:T(8,128)(2,1)S(1)} %get-tuple-element.54.own_ref.b2, ...), custom_call_target="tpu_custom_call" | custom-call | flops 150994944 | bytes 1048576 | tf_op jit(solution)/shard_map/density_parts_kernel/pallas_call | solution.py:39
  12.5 0.6 collective-permute-start.3
  13.1 2.6 %collective-permute-start.4 = (bf16[576,128]{1,0:T(8,128)(2,1)S(1)}, bf16[576,128]{1,0:T(8,128)(2,1)S(1)}, u32[]{:S(2)}, u32[]{:S(2)}) collective-permute-start(bf16[576,128]{1,0:T(8,128)(2,1)S(1)} %get-tuple-element.38), channel_id=1, source_target_pairs={{0,16},{8,24},{16,0},{24,8},{1,17},{9,25},{17,1},{25,9},{2,18},{10... | collective-permute-start | bytes 442376 | tf_op jit(solution)/shard_map/ppermute | solution.py:26
  15.7 0.7 %copy-done.1 = s32[1,4]{1,0:T(1,128)S(1)} copy-done((s32[1,4]{1,0:T(1,128)S(1)}, s32[1,4]{1,0:T(1,128)}, u32[]{:S(2)}) %copy-start.1) | copy-done | bytes 40
  16.4 1.8 %staged_kernel.1 = (bf16[576,576]{1,0:T(8,128)(2,1)S(1)}, f32[128,576]{1,0:T(8,128)S(1)}, bf16[128,640]{1,0:T(8,128)(2,1)S(1)}) custom-call(s32[12]{0:T(128)S(1)} %stack.51.where_ref, s32[1,4]{1,0:T(1,128)S(1)} %copy-done.1, bf16[576,576]{1,0:T(8,128)(2,1)} %c_ref.1, bf16[576,1024]{1,0:T(8,128)(2,1)} %bitcast.14, bf16[128,512]{1,0:T(8,128)(2,1)} %ops_ref.2, ...), custom_call_target="tpu_custom_call" | custom-call | flops 331776 | bytes 2097152 | tf_op jit(solution)/shard_map/staged_kernel/pallas_call | solution.py:39
  18.2 0.8 %collective-permute-done.5.b0 = bf16[1024,128]{1,0:T(8,128)(2,1)S(1)} collective-permute-done((bf16[1024,128]{1,0:T(8,128)(2,1)S(1)}, bf16[1024,128]{1,0:T(8,128)(2,1)S(1)}, u32[]{:S(2)}, u32[]{:S(2)}) %collective-permute-start.5) | collective-permute-done | bytes 262176 | tf_op jit(solution)/shard_map/ppermute | solution.py:31
  19.0 2.8 %collective-permute-done.6.b4 = bf16[1024,128]{1,0:T(8,128)(2,1)S(1)} collective-permute-done((bf16[1024,128]{1,0:T(8,128)(2,1)S(1)}, bf16[1024,128]{1,0:T(8,128)(2,1)S(1)}, u32[]{:S(2)}, u32[]{:S(2)}) %collective-permute-start.6) | collective-permute-done | bytes 262176 | tf_op jit(solution)/shard_map/ppermute | solution.py:31
  21.9 3.1 %collective-permute-done.4 = bf16[576,128]{1,0:T(8,128)(2,1)S(1)} collective-permute-done((bf16[576,128]{1,0:T(8,128)(2,1)S(1)}, bf16[576,128]{1,0:T(8,128)(2,1)S(1)}, u32[]{:S(2)}, u32[]{:S(2)}) %collective-permute-start.4) | collective-permute-done | bytes 147488 | tf_op jit(solution)/shard_map/ppermute | solution.py:26
  25.4 2.4 %collective-permute-start.13 = (bf16[1024,128]{1,0:T(8,128)(2,1)S(1)}, bf16[1024,128]{1,0:T(8,128)(2,1)S(1)}, u32[]{:S(2)}, u32[]{:S(2)}) collective-permute-start(bf16[1024,128]{1,0:T(8,128)(2,1)S(1)} %get-tuple-element.54.own_ref.b2), channel_id=1, source_target_pairs={{0,32},{32,0},{1,33},{33,1},{2,34},{34,2},{3,35},{35,3},{4,36},{36... | collective-permute-start | bytes 786440 | tf_op jit(solution)/shard_map/ppermute | solution.py:26
  27.8 5.0 %collective-permute-done.7 = bf16[576,128]{1,0:T(8,128)(2,1)S(1)} collective-permute-done((bf16[576,128]{1,0:T(8,128)(2,1)S(1)}, bf16[576,128]{1,0:T(8,128)(2,1)S(1)}, u32[]{:S(2)}, u32[]{:S(2)}) %collective-permute-start.7) | collective-permute-done | bytes 147488 | tf_op jit(solution)/shard_map/ppermute | solution.py:336
  32.9 4.5 %collective-permute-done.13.near_ref = bf16[1024,128]{1,0:T(8,128)(2,1)S(1)} collective-permute-done((bf16[1024,128]{1,0:T(8,128)(2,1)S(1)}, bf16[1024,128]{1,0:T(8,128)(2,1)S(1)}, u32[]{:S(2)}, u32[]{:S(2)}) %collective-permute-start.13) | collective-permute-done | bytes 262176 | tf_op jit(solution)/shard_map/ppermute | solution.py:26
  37.4 1.2 %collective-permute-start.14 = (bf16[1024,128]{1,0:T(8,128)(2,1)S(1)}, bf16[1024,128]{1,0:T(8,128)(2,1)S(1)}, u32[]{:S(2)}, u32[]{:S(2)}) collective-permute-start(bf16[1024,128]{1,0:T(8,128)(2,1)S(1)} %collective-permute-done.13.near_ref), channel_id=1, source_target_pairs={{0,64},{32,224},{64,128},{96,32},{128,192},{160,96},{192,0},{224,1... | collective-permute-start | bytes 786440 | tf_op jit(solution)/shard_map/ppermute | solution.py:333
  38.6 0.5 same_spin_beta_kernel.1.start_ref
  39.2 5.5 %collective-permute-done.8.far_ref = bf16[576,128]{1,0:T(8,128)(2,1)S(1)} collective-permute-done((bf16[576,128]{1,0:T(8,128)(2,1)S(1)}, bf16[576,128]{1,0:T(8,128)(2,1)S(1)}, u32[]{:S(2)}, u32[]{:S(2)}) %collective-permute-start.8) | collective-permute-done | bytes 147488 | tf_op jit(solution)/shard_map/ppermute | solution.py:341
  45.2 3.5 %collective-permute-start.11 = (bf16[128,576]{1,0:T(8,128)(2,1)S(1)}, bf16[128,576]{1,0:T(8,128)(2,1)S(1)}, u32[]{:S(2)}, u32[]{:S(2)}) collective-permute-start(bf16[128,576]{1,0:T(8,128)(2,1)S(1)} %excited_block_kernel.1.refs_0_.e0), channel_id=1, source_target_pairs={{0,16},{8,24},{16,0},{24,8},{1,17},{9,25},{17,1},{25,9},{2,18},{10... | collective-permute-start | bytes 442376 | tf_op jit(solution)/shard_map/ppermute | solution.py:26
  49.0 5.0 %same_spin_alpha_kernel.1.same_ref = f32[1024,128]{1,0:T(8,128)S(1)} custom-call(s32[12]{0:T(128)S(1)} %stack.51.where_ref, s32[1,4]{1,0:T(1,128)S(1)} %copy-done.2, bf16[1024,128]{1,0:T(8,128)(2,1)S(1)} %get-tuple-element.54.own_ref.b2, bf16[1024,128]{1,0:T(8,128)(2,1)S(1)} %collective-permute-done.13.near_ref, ...), custom_call_target="tpu_custom_call" | custom-call | flops 1073741824 | bytes 10485760 | tf_op jit(solution)/shard_map/same_spin_alpha_kernel/pallas_call | solution.py:39
  54.1 1.2 %collective-permute-done.12.refs_3_.e3 = bf16[128,576]{1,0:T(8,128)(2,1)S(1)} collective-permute-done((bf16[128,576]{1,0:T(8,128)(2,1)S(1)}, bf16[128,576]{1,0:T(8,128)(2,1)S(1)}, u32[]{:S(2)}, u32[]{:S(2)}) %collective-permute-start.12) | collective-permute-done | bytes 147488 | tf_op jit(solution)/shard_map/ppermute | solution.py:26
  55.6 4.0 %collective-permute-start.15 = (bf16[4,128,128]{2,1,0:T(8,128)(2,1)S(1)}, bf16[4,128,128]{2,1,0:T(8,128)(2,1)S(1)}, u32[]{:S(2)}, u32[]{:S(2)}) collective-permute-start(bf16[4,128,128]{2,1,0:T(8,128)(2,1)S(1)} %mixed_mate_kernel.1), channel_id=1, source_target_pairs={{0,1},{1,0},{2,3},{3,2},{4,5},{5,4},{6,7},{7,6},{8,9},{9,8},{10,11... | collective-permute-start | bytes 393224 | tf_op jit(solution)/shard_map/ppermute | solution.py:26
  59.6 1.5 %finished_own_kernel.1.begun_ref = f32[1024,128]{1,0:T(8,128)} custom-call(s32[12]{0:T(128)S(1)} %stack.51.where_ref, f32[1024,128]{1,0:T(8,128)S(1)} %same_spin_alpha_kernel.1.same_ref, bf16[128,576]{1,0:T(8,128)(2,1)S(1)} %excited_block_kernel.1.refs_0_.e0, bf16[128,576]{1,0:T(8,128)(2,1)S(1)} %collective-permute-done.10.refs_1_.e1, ...), custom_call_target="tpu_custom_call" | custom-call | flops 78643200 | bytes 2097152 | tf_op jit(solution)/shard_map/finished_own_kernel/pallas_call | solution.py:39
  61.1 1.3 %finished_mate_kernel.1 = f32[1024,128]{1,0:T(8,128)} custom-call(s32[12]{0:T(128)S(1)} %stack.51.where_ref, f32[1024,128]{1,0:T(8,128)S(1)} %same_spin_alpha_kernel.1.same_ref, bf16[4,128,128]{2,1,0:T(8,128)(2,1)S(1)} %collective-permute-done.15.theirs_ref, f32[1024,128]{1,0:T(8,128)S(1)} %copy-done, ...), custom_call_target="tpu_custom_call", output_to_operand_aliasing={{}: (4, {})} | custom-call | flops 262144 | bytes 2097152 | tf_op jit(solution)/shard_map/finished_mate_kernel/pallas_call | solution.py:39
  (27 shorter events, 2.0 us)
Async XLA Ops:
  0.0 49.0 %copy-start.2 = (s32[1,4]{1,0:T(1,128)S(1)}, s32[1,4]{1,0:T(1,128)}, u32[]{:S(2)}) copy-start(s32[1,4]{1,0:T(1,128)} %cols_ref.3) | copy-start | bytes 52
  0.0 11.3 %collective-permute-start = (bf16[1024,128]{1,0:T(8,128)(2,1)}, bf16[1024,128]{1,0:T(8,128)(2,1)S(1)}, u32[]{:S(2)}, u32[]{:S(2)}) collective-permute-start(bf16[1024,128]{1,0:T(8,128)(2,1)} %coef_ref.1), channel_id=1, source_target_pairs={{0,1},{1,0},{2,3},{3,2},{4,5},{5,4},{6,7},{7,6},{8,9},{9,8},{10,11... | collective-permute-start | bytes 786440 | tf_op jit(solution)/shard_map/ppermute | solution.py:26
  3.2 8.1 %collective-permute-start.1 = (bf16[576,128]{1,0:T(8,128)(2,1)}, bf16[576,128]{1,0:T(8,128)(2,1)S(1)}, u32[]{:S(2)}, u32[]{:S(2)}) collective-permute-start(bf16[576,128]{1,0:T(8,128)(2,1)} %bitcast.15), channel_id=1, source_target_pairs={{0,1},{1,0},{2,3},{3,2},{4,5},{5,4},{6,7},{7,6},{8,9},{9,8},{10,11... | collective-permute-start | bytes 442376 | tf_op jit(solution)/shard_map/ppermute | solution.py:26
  4.3 14.8 %collective-permute-start.5 = (bf16[1024,128]{1,0:T(8,128)(2,1)S(1)}, bf16[1024,128]{1,0:T(8,128)(2,1)S(1)}, u32[]{:S(2)}, u32[]{:S(2)}) collective-permute-start(bf16[1024,128]{1,0:T(8,128)(2,1)S(1)} %get-tuple-element.54.own_ref.b2), channel_id=1, source_target_pairs={{0,2},{1,3},{2,4},{3,5},{4,6},{5,7},{6,8},{7,9},{8,10},{9,11},{10,... | collective-permute-start | bytes 786440 | tf_op jit(solution)/shard_map/ppermute | solution.py:31
  5.7 16.2 %collective-permute-start.6 = (bf16[1024,128]{1,0:T(8,128)(2,1)S(1)}, bf16[1024,128]{1,0:T(8,128)(2,1)S(1)}, u32[]{:S(2)}, u32[]{:S(2)}) collective-permute-start(bf16[1024,128]{1,0:T(8,128)(2,1)S(1)} %get-tuple-element.54.own_ref.b2), channel_id=1, source_target_pairs={{0,30},{1,31},{2,0},{3,1},{4,2},{5,3},{6,4},{7,5},{8,6},{9,7},{10,... | collective-permute-start | bytes 786440 | tf_op jit(solution)/shard_map/ppermute | solution.py:31
  12.4 9.5 %collective-permute-start.2 = (bf16[576,128]{1,0:T(8,128)(2,1)S(1)}, bf16[576,128]{1,0:T(8,128)(2,1)S(1)}, u32[]{:S(2)}, u32[]{:S(2)}) collective-permute-start(bf16[576,128]{1,0:T(8,128)(2,1)S(1)} %get-tuple-element.36), channel_id=1, source_target_pairs={{0,8},{8,0},{16,24},{24,16},{1,9},{9,1},{17,25},{25,17},{2,10},{10... | collective-permute-start | bytes 442376 | tf_op jit(solution)/shard_map/ppermute | solution.py:26
  12.5 9.4 %collective-permute-start.3 = (bf16[576,128]{1,0:T(8,128)(2,1)S(1)}, bf16[576,128]{1,0:T(8,128)(2,1)S(1)}, u32[]{:S(2)}, u32[]{:S(2)}) collective-permute-start(bf16[576,128]{1,0:T(8,128)(2,1)S(1)} %get-tuple-element.37), channel_id=1, source_target_pairs={{0,24},{8,16},{16,8},{24,0},{1,25},{9,17},{17,9},{25,1},{2,26},{10... | collective-permute-start | bytes 442376 | tf_op jit(solution)/shard_map/ppermute | solution.py:26
  13.1 11.9 %collective-permute-start.4 = (bf16[576,128]{1,0:T(8,128)(2,1)S(1)}, bf16[576,128]{1,0:T(8,128)(2,1)S(1)}, u32[]{:S(2)}, u32[]{:S(2)}) collective-permute-start(bf16[576,128]{1,0:T(8,128)(2,1)S(1)} %get-tuple-element.38), channel_id=1, source_target_pairs={{0,16},{8,24},{16,0},{24,8},{1,17},{9,25},{17,1},{25,9},{2,18},{10... | collective-permute-start | bytes 442376 | tf_op jit(solution)/shard_map/ppermute | solution.py:26
  15.7 0.7 %copy-start.1 = (s32[1,4]{1,0:T(1,128)S(1)}, s32[1,4]{1,0:T(1,128)}, u32[]{:S(2)}) copy-start(s32[1,4]{1,0:T(1,128)} %cols_ref.2) | copy-start | bytes 52
  18.2 41.4 %copy-start = (f32[1024,128]{1,0:T(8,128)S(1)}, f32[1024,128]{1,0:T(8,128)}, u32[]{:S(2)}) copy-start(f32[1024,128]{1,0:T(8,128)} %den_ref.3) | copy-start | bytes 1572868
  25.1 7.7 %collective-permute-start.7 = (bf16[576,128]{1,0:T(8,128)(2,1)S(1)}, bf16[576,128]{1,0:T(8,128)(2,1)S(1)}, u32[]{:S(2)}, u32[]{:S(2)}) collective-permute-start(bf16[576,128]{1,0:T(8,128)(2,1)S(1)} %add_convert_fusion.1), channel_id=1, source_target_pairs={{0,2},{1,7},{2,0},{3,5},{4,6},{5,3},{6,4},{7,1},{8,10},{9,15},{10,... | collective-permute-start | bytes 442376 | tf_op jit(solution)/shard_map/ppermute | solution.py:336
  25.4 12.0 %collective-permute-start.13 = (bf16[1024,128]{1,0:T(8,128)(2,1)S(1)}, bf16[1024,128]{1,0:T(8,128)(2,1)S(1)}, u32[]{:S(2)}, u32[]{:S(2)}) collective-permute-start(bf16[1024,128]{1,0:T(8,128)(2,1)S(1)} %get-tuple-element.54.own_ref.b2), channel_id=1, source_target_pairs={{0,32},{32,0},{1,33},{33,1},{2,34},{34,2},{3,35},{35,3},{4,36},{36... | collective-permute-start | bytes 786440 | tf_op jit(solution)/shard_map/ppermute | solution.py:26
  32.8 5.8 %collective-permute-start.9 = (bf16[1024,128]{1,0:T(8,128)(2,1)S(1)}, bf16[1024,128]{1,0:T(8,128)(2,1)S(1)}, u32[]{:S(2)}, u32[]{:S(2)}) collective-permute-start(bf16[1024,128]{1,0:T(8,128)(2,1)S(1)} %broadcast_select_fusion), channel_id=1, source_target_pairs={{0,1},{1,0},{2,3},{3,2},{4,5},{5,4},{6,7},{7,6},{8,9},{9,8},{10,11... | collective-permute-start | bytes 786440 | tf_op jit(solution)/shard_map/ppermute | solution.py:26
  37.4 11.6 %collective-permute-start.14 = (bf16[1024,128]{1,0:T(8,128)(2,1)S(1)}, bf16[1024,128]{1,0:T(8,128)(2,1)S(1)}, u32[]{:S(2)}, u32[]{:S(2)}) collective-permute-start(bf16[1024,128]{1,0:T(8,128)(2,1)S(1)} %collective-permute-done.13.near_ref), channel_id=1, source_target_pairs={{0,64},{32,224},{64,128},{96,32},{128,192},{160,96},{192,0},{224,1... | collective-permute-start | bytes 786440 | tf_op jit(solution)/shard_map/ppermute | solution.py:333
  38.6 6.1 %collective-permute-start.8 = (bf16[576,128]{1,0:T(8,128)(2,1)S(1)}, bf16[576,128]{1,0:T(8,128)(2,1)S(1)}, u32[]{:S(2)}, u32[]{:S(2)}) collective-permute-start(bf16[576,128]{1,0:T(8,128)(2,1)S(1)} %add_convert_fusion.near_ref), channel_id=1, source_target_pairs={{0,6},{1,3},{2,4},{3,1},{4,2},{5,7},{6,0},{7,5},{8,14},{9,11},{10,... | collective-permute-start | bytes 442376 | tf_op jit(solution)/shard_map/ppermute | solution.py:341
  45.1 8.9 %collective-permute-start.10 = (bf16[128,576]{1,0:T(8,128)(2,1)S(1)}, bf16[128,576]{1,0:T(8,128)(2,1)S(1)}, u32[]{:S(2)}, u32[]{:S(2)}) collective-permute-start(bf16[128,576]{1,0:T(8,128)(2,1)S(1)} %excited_block_kernel.1.refs_0_.e0), channel_id=1, source_target_pairs={{0,8},{8,0},{16,24},{24,16},{1,9},{9,1},{17,25},{25,17},{2,10},{10... | collective-permute-start | bytes 442376 | tf_op jit(solution)/shard_map/ppermute | solution.py:26
  45.2 8.9 %collective-permute-start.11 = (bf16[128,576]{1,0:T(8,128)(2,1)S(1)}, bf16[128,576]{1,0:T(8,128)(2,1)S(1)}, u32[]{:S(2)}, u32[]{:S(2)}) collective-permute-start(bf16[128,576]{1,0:T(8,128)(2,1)S(1)} %excited_block_kernel.1.refs_0_.e0), channel_id=1, source_target_pairs={{0,16},{8,24},{16,0},{24,8},{1,17},{9,25},{17,1},{25,9},{2,18},{10... | collective-permute-start | bytes 442376 | tf_op jit(solution)/shard_map/ppermute | solution.py:26
  48.7 6.6 %collective-permute-start.12 = (bf16[128,576]{1,0:T(8,128)(2,1)S(1)}, bf16[128,576]{1,0:T(8,128)(2,1)S(1)}, u32[]{:S(2)}, u32[]{:S(2)}) collective-permute-start(bf16[128,576]{1,0:T(8,128)(2,1)S(1)} %excited_block_kernel.1.refs_0_.e0), channel_id=1, source_target_pairs={{0,24},{8,16},{16,8},{24,0},{1,25},{9,17},{17,9},{25,1},{2,26},{10... | collective-permute-start | bytes 442376 | tf_op jit(solution)/shard_map/ppermute | solution.py:26
  55.6 5.5 %collective-permute-start.15 = (bf16[4,128,128]{2,1,0:T(8,128)(2,1)S(1)}, bf16[4,128,128]{2,1,0:T(8,128)(2,1)S(1)}, u32[]{:S(2)}, u32[]{:S(2)}) collective-permute-start(bf16[4,128,128]{2,1,0:T(8,128)(2,1)S(1)} %mixed_mate_kernel.1), channel_id=1, source_target_pairs={{0,1},{1,0},{2,3},{3,2},{4,5},{5,4},{6,7},{7,6},{8,9},{9,8},{10,11... | collective-permute-start | bytes 393224 | tf_op jit(solution)/shard_map/ppermute | solution.py:26

commit v5 on v4

--- a/solution.py
+++ b/solution.py
@@ -24,11 +24,6 @@
 def swapped(block, axis, mask):
     count = lax.axis_size(axis)
     return lax.ppermute(block, axis, [(i, i ^ mask) for i in range(count)])
-
-
-def rotated(block, axis, distance):
-    count = lax.axis_size(axis)
-    return lax.ppermute(block, axis, [(i, (i + distance) % count) for i in range(count)])
 
 
 def call(kernel, outs, args, specs, cost, scratch=(), aliases=None, out_specs=None, limit=16):
@@ -116,7 +111,8 @@
         copies[0].wait()
         core = where_ref[8]
         for n in range(5):
-            offset = n if n in (0, 2, 4) else jnp.where(core == 0, n, 4 - n)
+            side = 2 - where_ref[11] if n in (0, 4) else 2 * core
+            offset = jnp.where(side == 0, n, 4 - n)
             tile = jnp.zeros((width, width), F32)
             for k in range(listed):
                 here = lax.rem(cols_ref[0, k] - where_ref[9] + 2 + count, count)
@@ -309,8 +305,15 @@
     pair_mate = swapped(pair_t, "c", 1)
     coef_v, pair_v = loaded(coef, pair_t)
 
-    below = rotated(coef_v, BETA, 2)
-    above = rotated(coef_v, BETA, -2)
+    near = swapped(coef_v, "zl", 1)
+    chips = lax.axis_size("y") * lax.axis_size("zh")
+    border = []
+    for q in range(chips):
+        for h in (0, 1):
+            low_at, high_at = (2 * q + h, 2 * chips + 2 * ((q - 1) % chips) + h)
+            border += [(low_at, high_at), (high_at, low_at)]
+    over = ("zl", *BETA)
+    across = lax.ppermute(coef_v, over, border)
     xs, route = lax.axis_size("x"), []
     for i in range(xs):
         route += [(2 * i, 2 * ((i + 1) % xs)), (2 * i + 1, 2 * ((i - 1) % xs) + 1)]
@@ -320,10 +323,9 @@
         where, beta_cols, pair_coupling, pair_alpha.T, beta_ops, parts[0]
     )
     got = [swapped(parts[k], "y", k) for k in (1, 3, 2)]
-    got_first = got[0]
-    *got, below, above = lax.optimization_barrier((*got, below, above))
-    start, _ = lax.optimization_barrier((coef_v, got_first))
-    near = swapped(start, "zl", 1)
+    *got, _, _ = lax.optimization_barrier((*got, near, across))
+    onward = lax.ppermute(near, over, border)
+    returned = swapped(across, "zl", 1)
     total = parts[0].astype(F32)
     for part in got:
         total = total + part.astype(F32)
@@ -335,11 +337,11 @@
     steps = [[(2 * i + h, 2 * (i ^ m[h]) + h) for i in range(zs) for h in (0, 1)] for m in ((1, 3), (3, 1))]
     first = lax.ppermute(total, ("zh", "c"), steps[0])
     total = (total.astype(F32) + first.astype(F32)).astype(BF16)
-    passed = jnp.where(core == 0, above, below)
+    passed = jnp.where(core == low, returned, onward)
     total, passed = lax.optimization_barrier((total, passed))
     crossed = swapped(passed, "c", 1)
     second = lax.ppermute(total, ("zh", "c"), steps[1])
-    same = same_spin_beta([below, crossed, coef_v, mate, above], placed)
+    same = same_spin_beta([onward, crossed, coef_v, mate, returned], placed)
     second, same = lax.optimization_barrier((second, same))
 
     excited = excited_block(total, second, coupling, scale)

time: 62.7 us -> 62.1 us (level)
  starting transfers between devices: 25.5 us -> 24.5 us
    ppermute x2, waiting for transfers between devices: 3.64 us -> 0.01 us  [the longest x1 0.01 us: local(): across = lax.ppermute(coef_v, over, border)]
    ppermute x11 -> x12, starting transfers between devices: 17 us -> 13.7 us  [swapped(): return lax.ppermute(block, axis, [(i, i ^ mask) for i in range(count)])]
    ppermute x1, waiting for transfers between devices: 4.95 us -> 7.61 us  [local(): first = lax.ppermute(total, ('zh', 'c'), steps[0])]
    ppermute x11 -> x12, waiting for transfers between devices: 8.93 us -> 11.3 us  [swapped(): return lax.ppermute(block, axis, [(i, i ^ mask) for i in range(count)])]
    ppermute x2, starting transfers between devices: 6.98 us -> 9.34 us  [the longest x1 7.09 us: local(): across = lax.ppermute(coef_v, over, border)]
    ppermute x1, waiting for transfers between devices: 5.54 us -> 4.44 us  [local(): second = lax.ppermute(total, ('zh', 'c'), steps[1])]
  transfers between devices with their start and end apart: 16 -> 17, of which waited for: 8 -> 6; matrix products, arithmetic and copies ran while one was open for 0% -> 0% of each run, Pallas kernels for 18% -> 18%
where the time goes in v5:
time: 62.1 us; the launch traced here: 61.9 us
  starting transfers between devices  24.5 us (39%)
  waiting for transfers between devices  23.4 us (38%)
  Pallas kernels  12.8 us (21%)
  local copies, waits for them, and re-layouts  0.75 us (1%)
    ppermute x12, starting transfers between devices, swapped(): return lax.ppermute(block, axis, [(i, i ^ mask) for i in range(count)])  13.7 us
    pallas_call x9, Pallas kernels, call(): pl.pallas_call(kernel, out_shape=outs, in_specs=specs, out_specs=out_spec...  12.8 us
    ppermute x12, waiting for transfers between devices, swapped(): return lax.ppermute(block, axis, [(i, i ^ mask) for i in range(count)])  11.3 us
    ppermute x1, waiting for transfers between devices, local(): first = lax.ppermute(total, ('zh', 'c'), steps[0])  7.61 us
    ppermute x1, starting transfers between devices, local(): across = lax.ppermute(coef_v, over, border)  7.09 us
    ppermute x1, waiting for transfers between devices, local(): second = lax.ppermute(total, ('zh', 'c'), steps[1])  4.44 us
    ppermute x1, starting transfers between devices, local(): onward = lax.ppermute(near, over, border)  2.25 us
    ppermute x1, starting transfers between devices, local(): far = lax.ppermute(near, ALPHA, route)  1.29 us
  transfers between devices with their start and end apart: 17, of which 6 were waited for; matrix products, arithmetic and copies ran while one was open for 0% of the time, Pallas kernels for 18%

profile of v5, /device:TPU:1, one launch (start us, length us, event | category | flops | bytes accessed | tf_op | source)
XLA Modules:
  0.0 61.9 jit_solution(12997703642041085423)
XLA Ops:
  0.0 3.2 %collective-permute-start = (bf16[1024,128]{1,0:T(8,128)(2,1)}, bf16[1024,128]{1,0:T(8,128)(2,1)S(1)}, u32[]{:S(2)}, u32[]{:S(2)}) collective-permute-start(bf16[1024,128]{1,0:T(8,128)(2,1)} %coef_ref.1), channel_id=1, source_target_pairs={{0,1},{1,0},{2,3},{3,2},{4,5},{5,4},{6,7},{7,6},{8,9},{9,8},{10,11... | collective-permute-start | bytes 786440 | tf_op jit(solution)/shard_map/ppermute | solution.py:26
  3.2 1.0 %loaded_kernel.1 = (bf16[1024,128]{1,0:T(8,128)(2,1)S(1)}, bf16[576,128]{1,0:T(8,128)(2,1)S(1)}) custom-call(bf16[1024,128]{1,0:T(8,128)(2,1)} %coef_ref.1, bf16[576,128]{1,0:T(8,128)(2,1)} %bitcast.16), custom_call_target="tpu_custom_call" | custom-call | bytes 1048576 | tf_op jit(solution)/shard_map/loaded_kernel/pallas_call | solution.py:34
  4.4 7.1 %collective-permute-start.6 = (bf16[1024,128]{1,0:T(8,128)(2,1)S(1)}, bf16[1024,128]{1,0:T(8,128)(2,1)S(1)}, u32[]{:S(2)}, u32[]{:S(2)}) collective-permute-start(bf16[1024,128]{1,0:T(8,128)(2,1)S(1)} %get-tuple-element.30.own_ref.b2), channel_id=1, source_target_pairs={{0,62},{62,0},{1,63},{63,1},{2,32},{32,2},{3,33},{33,3},{4,34},{34... | collective-permute-start | bytes 786440 | tf_op jit(solution)/shard_map/ppermute | solution.py:316
  11.6 1.0 %density_parts_kernel.1 = (bf16[576,128]{1,0:T(8,128)(2,1)S(1)}, bf16[576,128]{1,0:T(8,128)(2,1)S(1)}, bf16[576,128]{1,0:T(8,128)(2,1)S(1)}, bf16[576,128]{1,0:T(8,128)(2,1)S(1)}) custom-call(s32[12]{0:T(128)S(1)} %stack.51.where_ref, bf16[1024,128]{1,0:T(8,128)(2,1)S(1)} %get-tuple-element.30.own_ref.b2, ...), custom_call_target="tpu_custom_call" | custom-call | flops 150994944 | bytes 1048576 | tf_op jit(solution)/shard_map/density_parts_kernel/pallas_call | solution.py:34
  12.7 0.6 collective-permute-start.3
  13.3 2.6 %collective-permute-start.4 = (bf16[576,128]{1,0:T(8,128)(2,1)S(1)}, bf16[576,128]{1,0:T(8,128)(2,1)S(1)}, u32[]{:S(2)}, u32[]{:S(2)}) collective-permute-start(bf16[576,128]{1,0:T(8,128)(2,1)S(1)} %get-tuple-element.35), channel_id=1, source_target_pairs={{0,16},{8,24},{16,0},{24,8},{1,17},{9,25},{17,1},{25,9},{2,18},{10... | collective-permute-start | bytes 442376 | tf_op jit(solution)/shard_map/ppermute | solution.py:26
  15.9 2.3 %collective-permute-start.9 = (bf16[1024,128]{1,0:T(8,128)(2,1)S(1)}, bf16[1024,128]{1,0:T(8,128)(2,1)S(1)}, u32[]{:S(2)}, u32[]{:S(2)}) collective-permute-start(bf16[1024,128]{1,0:T(8,128)(2,1)S(1)} %collective-permute-done.5.near_ref), channel_id=1, source_target_pairs={{0,62},{62,0},{1,63},{63,1},{2,32},{32,2},{3,33},{33,3},{4,34},{34... | collective-permute-start | bytes 786440 | tf_op jit(solution)/shard_map/ppermute | solution.py:327
  18.2 0.7 %copy-done.1 = s32[1,4]{1,0:T(1,128)S(1)} copy-done((s32[1,4]{1,0:T(1,128)S(1)}, s32[1,4]{1,0:T(1,128)}, u32[]{:S(2)}) %copy-start.1) | copy-done | bytes 40
  18.8 1.8 %staged_kernel.1 = (bf16[576,576]{1,0:T(8,128)(2,1)S(1)}, f32[128,576]{1,0:T(8,128)S(1)}, bf16[128,640]{1,0:T(8,128)(2,1)S(1)}) custom-call(s32[12]{0:T(128)S(1)} %stack.51.where_ref, s32[1,4]{1,0:T(1,128)S(1)} %copy-done.1, bf16[576,576]{1,0:T(8,128)(2,1)} %c_ref.1, bf16[576,1024]{1,0:T(8,128)(2,1)} %bitcast.14, bf16[128,512]{1,0:T(8,128)(2,1)} %ops_ref.2, ...), custom_call_target="tpu_custom_call" | custom-call | flops 331776 | bytes 2097152 | tf_op jit(solution)/shard_map/staged_kernel/pallas_call | solution.py:34
  20.7 0.7 %collective-permute-done.3 = bf16[576,128]{1,0:T(8,128)(2,1)S(1)} collective-permute-done((bf16[576,128]{1,0:T(8,128)(2,1)S(1)}, bf16[576,128]{1,0:T(8,128)(2,1)S(1)}, u32[]{:S(2)}, u32[]{:S(2)}) %collective-permute-start.3) | collective-permute-done | bytes 147488 | tf_op jit(solution)/shard_map/ppermute | solution.py:26
  21.4 9.2 %collective-permute-done.4 = bf16[576,128]{1,0:T(8,128)(2,1)S(1)} collective-permute-done((bf16[576,128]{1,0:T(8,128)(2,1)S(1)}, bf16[576,128]{1,0:T(8,128)(2,1)S(1)}, u32[]{:S(2)}, u32[]{:S(2)}) %collective-permute-start.4) | collective-permute-done | bytes 147488 | tf_op jit(solution)/shard_map/ppermute | solution.py:26
  30.8 7.6 %collective-permute-done.7 = bf16[576,128]{1,0:T(8,128)(2,1)S(1)} collective-permute-done((bf16[576,128]{1,0:T(8,128)(2,1)S(1)}, bf16[576,128]{1,0:T(8,128)(2,1)S(1)}, u32[]{:S(2)}, u32[]{:S(2)}) %collective-permute-start.7) | collective-permute-done | bytes 147488 | tf_op jit(solution)/shard_map/ppermute | solution.py:338
  38.6 1.3 %collective-permute-start.15 = (bf16[1024,128]{1,0:T(8,128)(2,1)S(1)}, bf16[1024,128]{1,0:T(8,128)(2,1)S(1)}, u32[]{:S(2)}, u32[]{:S(2)}) collective-permute-start(bf16[1024,128]{1,0:T(8,128)(2,1)S(1)} %collective-permute-done.5.near_ref), channel_id=1, source_target_pairs={{0,64},{32,224},{64,128},{96,32},{128,192},{160,96},{192,0},{224,1... | collective-permute-start | bytes 786440 | tf_op jit(solution)/shard_map/ppermute | solution.py:335
  39.9 0.2 collective-permute-done.11.b1
  40.1 0.5 same_spin_beta_kernel.1.start_ref
  40.6 4.4 %collective-permute-done.10.far_ref = bf16[576,128]{1,0:T(8,128)(2,1)S(1)} collective-permute-done((bf16[576,128]{1,0:T(8,128)(2,1)S(1)}, bf16[576,128]{1,0:T(8,128)(2,1)S(1)}, u32[]{:S(2)}, u32[]{:S(2)}) %collective-permute-start.10) | collective-permute-done | bytes 147488 | tf_op jit(solution)/shard_map/ppermute | solution.py:343
  45.1 0.4 excited_block_kernel.1.refs_0_.e0
  45.6 3.7 %collective-permute-start.14 = (bf16[128,576]{1,0:T(8,128)(2,1)S(1)}, bf16[128,576]{1,0:T(8,128)(2,1)S(1)}, u32[]{:S(2)}, u32[]{:S(2)}) collective-permute-start(bf16[128,576]{1,0:T(8,128)(2,1)S(1)} %excited_block_kernel.1.refs_0_.e0), channel_id=1, source_target_pairs={{0,24},{8,16},{16,8},{24,0},{1,25},{9,17},{17,9},{25,1},{2,26},{10... | collective-permute-start | bytes 442376 | tf_op jit(solution)/shard_map/ppermute | solution.py:26
  49.4 5.0 %same_spin_alpha_kernel.1.same_ref = f32[1024,128]{1,0:T(8,128)S(1)} custom-call(s32[12]{0:T(128)S(1)} %stack.51.where_ref, s32[1,4]{1,0:T(1,128)S(1)} %copy-done.2, bf16[1024,128]{1,0:T(8,128)(2,1)S(1)} %get-tuple-element.30.own_ref.b2, bf16[1024,128]{1,0:T(8,128)(2,1)S(1)} %collective-permute-done.5.near_ref, ...), custom_call_target="tpu_custom_call" | custom-call | flops 1073741824 | bytes 10485760 | tf_op jit(solution)/shard_map/same_spin_alpha_kernel/pallas_call | solution.py:34
  54.4 1.2 %collective-permute-done.14.refs_3_.e3 = bf16[128,576]{1,0:T(8,128)(2,1)S(1)} collective-permute-done((bf16[128,576]{1,0:T(8,128)(2,1)S(1)}, bf16[128,576]{1,0:T(8,128)(2,1)S(1)}, u32[]{:S(2)}, u32[]{:S(2)}) %collective-permute-start.14) | collective-permute-done | bytes 147488 | tf_op jit(solution)/shard_map/ppermute | solution.py:26
  55.5 0.3 mixed_mate_kernel.1
  55.9 3.0 %collective-permute-start.16 = (bf16[4,128,128]{2,1,0:T(8,128)(2,1)S(1)}, bf16[4,128,128]{2,1,0:T(8,128)(2,1)S(1)}, u32[]{:S(2)}, u32[]{:S(2)}) collective-permute-start(bf16[4,128,128]{2,1,0:T(8,128)(2,1)S(1)} %mixed_mate_kernel.1), channel_id=1, source_target_pairs={{0,1},{1,0},{2,3},{3,2},{4,5},{5,4},{6,7},{7,6},{8,9},{9,8},{10,11... | collective-permute-start | bytes 393224 | tf_op jit(solution)/shard_map/ppermute | solution.py:26
  58.9 1.5 %finished_own_kernel.1.begun_ref = f32[1024,128]{1,0:T(8,128)} custom-call(s32[12]{0:T(128)S(1)} %stack.51.where_ref, f32[1024,128]{1,0:T(8,128)S(1)} %same_spin_alpha_kernel.1.same_ref, bf16[128,576]{1,0:T(8,128)(2,1)S(1)} %excited_block_kernel.1.refs_0_.e0, bf16[128,576]{1,0:T(8,128)(2,1)S(1)} %collective-permute-done.12.refs_1_.e1, ...), custom_call_target="tpu_custom_call" | custom-call | flops 78643200 | bytes 2097152 | tf_op jit(solution)/shard_map/finished_own_kernel/pallas_call | solution.py:34
  60.5 1.3 %finished_mate_kernel.1 = f32[1024,128]{1,0:T(8,128)} custom-call(s32[12]{0:T(128)S(1)} %stack.51.where_ref, f32[1024,128]{1,0:T(8,128)S(1)} %same_spin_alpha_kernel.1.same_ref, bf16[4,128,128]{2,1,0:T(8,128)(2,1)S(1)} %collective-permute-done.16.theirs_ref, f32[1024,128]{1,0:T(8,128)S(1)} %copy-done, ...), custom_call_target="tpu_custom_call", output_to_operand_aliasing={{}: (4, {})} | custom-call | flops 262144 | bytes 2097152 | tf_op jit(solution)/shard_map/finished_mate_kernel/pallas_call | solution.py:34
  (29 shorter events, 0.8 us)
Async XLA Ops:
  0.0 49.4 %copy-start.2 = (s32[1,4]{1,0:T(1,128)S(1)}, s32[1,4]{1,0:T(1,128)}, u32[]{:S(2)}) copy-start(s32[1,4]{1,0:T(1,128)} %cols_ref.3) | copy-start | bytes 52
  0.0 11.5 %collective-permute-start = (bf16[1024,128]{1,0:T(8,128)(2,1)}, bf16[1024,128]{1,0:T(8,128)(2,1)S(1)}, u32[]{:S(2)}, u32[]{:S(2)}) collective-permute-start(bf16[1024,128]{1,0:T(8,128)(2,1)} %coef_ref.1), channel_id=1, source_target_pairs={{0,1},{1,0},{2,3},{3,2},{4,5},{5,4},{6,7},{7,6},{8,9},{9,8},{10,11... | collective-permute-start | bytes 786440 | tf_op jit(solution)/shard_map/ppermute | solution.py:26
  3.2 8.3 %collective-permute-start.1 = (bf16[576,128]{1,0:T(8,128)(2,1)}, bf16[576,128]{1,0:T(8,128)(2,1)S(1)}, u32[]{:S(2)}, u32[]{:S(2)}) collective-permute-start(bf16[576,128]{1,0:T(8,128)(2,1)} %bitcast.15), channel_id=1, source_target_pairs={{0,1},{1,0},{2,3},{3,2},{4,5},{5,4},{6,7},{7,6},{8,9},{9,8},{10,11... | collective-permute-start | bytes 442376 | tf_op jit(solution)/shard_map/ppermute | solution.py:26
  4.3 11.7 %collective-permute-start.5 = (bf16[1024,128]{1,0:T(8,128)(2,1)S(1)}, bf16[1024,128]{1,0:T(8,128)(2,1)S(1)}, u32[]{:S(2)}, u32[]{:S(2)}) collective-permute-start(bf16[1024,128]{1,0:T(8,128)(2,1)S(1)} %get-tuple-element.30.own_ref.b2), channel_id=1, source_target_pairs={{0,32},{32,0},{1,33},{33,1},{2,34},{34,2},{3,35},{35,3},{4,36},{36... | collective-permute-start | bytes 786440 | tf_op jit(solution)/shard_map/ppermute | solution.py:26
  4.4 13.8 %collective-permute-start.6 = (bf16[1024,128]{1,0:T(8,128)(2,1)S(1)}, bf16[1024,128]{1,0:T(8,128)(2,1)S(1)}, u32[]{:S(2)}, u32[]{:S(2)}) collective-permute-start(bf16[1024,128]{1,0:T(8,128)(2,1)S(1)} %get-tuple-element.30.own_ref.b2), channel_id=1, source_target_pairs={{0,62},{62,0},{1,63},{63,1},{2,32},{32,2},{3,33},{33,3},{4,34},{34... | collective-permute-start | bytes 786440 | tf_op jit(solution)/shard_map/ppermute | solution.py:316
  12.6 8.1 %collective-permute-start.2 = (bf16[576,128]{1,0:T(8,128)(2,1)S(1)}, bf16[576,128]{1,0:T(8,128)(2,1)S(1)}, u32[]{:S(2)}, u32[]{:S(2)}) collective-permute-start(bf16[576,128]{1,0:T(8,128)(2,1)S(1)} %get-tuple-element.33), channel_id=1, source_target_pairs={{0,8},{8,0},{16,24},{24,16},{1,9},{9,1},{17,25},{25,17},{2,10},{10... | collective-permute-start | bytes 442376 | tf_op jit(solution)/shard_map/ppermute | solution.py:26
  12.7 8.7 %collective-permute-start.3 = (bf16[576,128]{1,0:T(8,128)(2,1)S(1)}, bf16[576,128]{1,0:T(8,128)(2,1)S(1)}, u32[]{:S(2)}, u32[]{:S(2)}) collective-permute-start(bf16[576,128]{1,0:T(8,128)(2,1)S(1)} %get-tuple-element.34), channel_id=1, source_target_pairs={{0,24},{8,16},{16,8},{24,0},{1,25},{9,17},{17,9},{25,1},{2,26},{10... | collective-permute-start | bytes 442376 | tf_op jit(solution)/shard_map/ppermute | solution.py:26
  13.3 17.3 %collective-permute-start.4 = (bf16[576,128]{1,0:T(8,128)(2,1)S(1)}, bf16[576,128]{1,0:T(8,128)(2,1)S(1)}, u32[]{:S(2)}, u32[]{:S(2)}) collective-permute-start(bf16[576,128]{1,0:T(8,128)(2,1)S(1)} %get-tuple-element.35), channel_id=1, source_target_pairs={{0,16},{8,24},{16,0},{24,8},{1,17},{9,25},{17,1},{25,9},{2,18},{10... | collective-permute-start | bytes 442376 | tf_op jit(solution)/shard_map/ppermute | solution.py:26
  15.9 14.8 %collective-permute-start.9 = (bf16[1024,128]{1,0:T(8,128)(2,1)S(1)}, bf16[1024,128]{1,0:T(8,128)(2,1)S(1)}, u32[]{:S(2)}, u32[]{:S(2)}) collective-permute-start(bf16[1024,128]{1,0:T(8,128)(2,1)S(1)} %collective-permute-done.5.near_ref), channel_id=1, source_target_pairs={{0,62},{62,0},{1,63},{63,1},{2,32},{32,2},{3,33},{33,3},{4,34},{34... | collective-permute-start | bytes 786440 | tf_op jit(solution)/shard_map/ppermute | solution.py:327
  18.2 12.6 %collective-permute-start.8 = (bf16[1024,128]{1,0:T(8,128)(2,1)S(1)}, bf16[1024,128]{1,0:T(8,128)(2,1)S(1)}, u32[]{:S(2)}, u32[]{:S(2)}) collective-permute-start(bf16[1024,128]{1,0:T(8,128)(2,1)S(1)} %collective-permute-done.6), channel_id=1, source_target_pairs={{0,32},{32,0},{1,33},{33,1},{2,34},{34,2},{3,35},{35,3},{4,36},{36... | collective-permute-start | bytes 786440 | tf_op jit(solution)/shard_map/ppermute | solution.py:26
  18.2 0.7 %copy-start.1 = (s32[1,4]{1,0:T(1,128)S(1)}, s32[1,4]{1,0:T(1,128)}, u32[]{:S(2)}) copy-start(s32[1,4]{1,0:T(1,128)} %cols_ref.2) | copy-start | bytes 52
  20.7 38.2 %copy-start = (f32[1024,128]{1,0:T(8,128)S(1)}, f32[1024,128]{1,0:T(8,128)}, u32[]{:S(2)}) copy-start(f32[1024,128]{1,0:T(8,128)} %den_ref.3) | copy-start | bytes 1572868
  30.7 7.8 %collective-permute-start.7 = (bf16[576,128]{1,0:T(8,128)(2,1)S(1)}, bf16[576,128]{1,0:T(8,128)(2,1)S(1)}, u32[]{:S(2)}, u32[]{:S(2)}) collective-permute-start(bf16[576,128]{1,0:T(8,128)(2,1)S(1)} %add_convert_fusion.1), channel_id=1, source_target_pairs={{0,2},{1,7},{2,0},{3,5},{4,6},{5,3},{6,4},{7,1},{8,10},{9,15},{10,... | collective-permute-start | bytes 442376 | tf_op jit(solution)/shard_map/ppermute | solution.py:338
  38.5 1.6 %collective-permute-start.11 = (bf16[1024,128]{1,0:T(8,128)(2,1)S(1)}, bf16[1024,128]{1,0:T(8,128)(2,1)S(1)}, u32[]{:S(2)}, u32[]{:S(2)}) collective-permute-start(bf16[1024,128]{1,0:T(8,128)(2,1)S(1)} %broadcast_select_fusion), channel_id=1, source_target_pairs={{0,1},{1,0},{2,3},{3,2},{4,5},{5,4},{6,7},{7,6},{8,9},{9,8},{10,11... | collective-permute-start | bytes 786440 | tf_op jit(solution)/shard_map/ppermute | solution.py:26
  38.6 10.8 %collective-permute-start.15 = (bf16[1024,128]{1,0:T(8,128)(2,1)S(1)}, bf16[1024,128]{1,0:T(8,128)(2,1)S(1)}, u32[]{:S(2)}, u32[]{:S(2)}) collective-permute-start(bf16[1024,128]{1,0:T(8,128)(2,1)S(1)} %collective-permute-done.5.near_ref), channel_id=1, source_target_pairs={{0,64},{32,224},{64,128},{96,32},{128,192},{160,96},{192,0},{224,1... | collective-permute-start | bytes 786440 | tf_op jit(solution)/shard_map/ppermute | solution.py:335
  39.9 5.2 %collective-permute-start.10 = (bf16[576,128]{1,0:T(8,128)(2,1)S(1)}, bf16[576,128]{1,0:T(8,128)(2,1)S(1)}, u32[]{:S(2)}, u32[]{:S(2)}) collective-permute-start(bf16[576,128]{1,0:T(8,128)(2,1)S(1)} %add_convert_fusion.near_ref), channel_id=1, source_target_pairs={{0,6},{1,3},{2,4},{3,1},{4,2},{5,7},{6,0},{7,5},{8,14},{9,11},{10,... | collective-permute-start | bytes 442376 | tf_op jit(solution)/shard_map/ppermute | solution.py:343
  45.4 8.9 %collective-permute-start.12 = (bf16[128,576]{1,0:T(8,128)(2,1)S(1)}, bf16[128,576]{1,0:T(8,128)(2,1)S(1)}, u32[]{:S(2)}, u32[]{:S(2)}) collective-permute-start(bf16[128,576]{1,0:T(8,128)(2,1)S(1)} %excited_block_kernel.1.refs_0_.e0), channel_id=1, source_target_pairs={{0,8},{8,0},{16,24},{24,16},{1,9},{9,1},{17,25},{25,17},{2,10},{10... | collective-permute-start | bytes 442376 | tf_op jit(solution)/shard_map/ppermute | solution.py:26
  45.5 8.8 %collective-permute-start.13 = (bf16[128,576]{1,0:T(8,128)(2,1)S(1)}, bf16[128,576]{1,0:T(8,128)(2,1)S(1)}, u32[]{:S(2)}, u32[]{:S(2)}) collective-permute-start(bf16[128,576]{1,0:T(8,128)(2,1)S(1)} %excited_block_kernel.1.refs_0_.e0), channel_id=1, source_target_pairs={{0,16},{8,24},{16,0},{24,8},{1,17},{9,25},{17,1},{25,9},{2,18},{10... | collective-permute-start | bytes 442376 | tf_op jit(solution)/shard_map/ppermute | solution.py:26
  45.6 9.9 %collective-permute-start.14 = (bf16[128,576]{1,0:T(8,128)(2,1)S(1)}, bf16[128,576]{1,0:T(8,128)(2,1)S(1)}, u32[]{:S(2)}, u32[]{:S(2)}) collective-permute-start(bf16[128,576]{1,0:T(8,128)(2,1)S(1)} %excited_block_kernel.1.refs_0_.e0), channel_id=1, source_target_pairs={{0,24},{8,16},{16,8},{24,0},{1,25},{9,17},{17,9},{25,1},{2,26},{10... | collective-permute-start | bytes 442376 | tf_op jit(solution)/shard_map/ppermute | solution.py:26
  55.9 4.6 %collective-permute-start.16 = (bf16[4,128,128]{2,1,0:T(8,128)(2,1)S(1)}, bf16[4,128,128]{2,1,0:T(8,128)(2,1)S(1)}, u32[]{:S(2)}, u32[]{:S(2)}) collective-permute-start(bf16[4,128,128]{2,1,0:T(8,128)(2,1)S(1)} %mixed_mate_kernel.1), channel_id=1, source_target_pairs={{0,1},{1,0},{2,3},{3,2},{4,5},{5,4},{6,7},{7,6},{8,9},{9,8},{10,11... | collective-permute-start | bytes 393224 | tf_op jit(solution)/shard_map/ppermute | solution.py:26

commit v6 on v5

--- a/solution.py
+++ b/solution.py
@@ -24,6 +24,10 @@
 def swapped(block, axis, mask):
     count = lax.axis_size(axis)
     return lax.ppermute(block, axis, [(i, i ^ mask) for i in range(count)])
+
+
+def crossing(count, masks):
+    return [(2 * i + h, 2 * (i ^ masks[h]) + h) for i in range(count) for h in (0, 1)]
 
 
 def call(kernel, outs, args, specs, cost, scratch=(), aliases=None, out_specs=None, limit=16):
@@ -76,16 +80,20 @@
 def density_parts(where, own, mate, pair_own, pair_mate):
     pairs, width = pair_mate.shape
 
-    def density_parts_kernel(where_ref, own_ref, mate_ref, po_ref, pm_ref, *outs):
+    def density_parts_kernel(where_ref, own_ref, mate_ref, po_ref, pm_ref, sent, kept, passing):
         left = jnp.concatenate([po_ref[...], pm_ref[...]], axis=1)
-        for k, out in enumerate(outs):
-            rows = block_rows(where_ref, k, width)
+        for k in range(4):
+            rows = block_rows(where_ref, 12 + k, width)
             right = jnp.concatenate([own_ref[rows, :], mate_ref[rows, :]], axis=1)
-            out[...] = dot(left, right, ((1,), (1,))).astype(BF16)
+            part = dot(left, right, ((1,), (1,))).astype(BF16)
+            if k < 2:
+                sent[k] = part
+            else:
+                (kept, passing)[k - 2][...] = part
 
     return call(
         density_parts_kernel,
-        [shape((pairs, width))] * 4,
+        [shape((2, pairs, width)), shape((pairs, width)), shape((pairs, width))],
         (where, own, mate, pair_own, pair_mate),
         [SMEM] + [VMEM] * 4,
         (16 * pairs * width * width, 1 * MIB),
@@ -298,6 +306,8 @@
     row_blocks = [(y ^ k) * 2 for k in range(4)]
     where = [r + core for r in row_blocks] + [r + 1 - core for r in row_blocks]
     where += [core, lax.axis_index(BETA), lax.axis_index(ALPHA), 2 - 2 * low]
+    side = 1 + 2 * core
+    where += [(y ^ m) * 2 + core for m in (side, 2, 0, 4 - side)]
     where = jnp.stack(where).astype(jnp.int32)
 
     pair_t = pair_beta.T
@@ -318,29 +328,27 @@
     for i in range(xs):
         route += [(2 * i, 2 * ((i + 1) % xs)), (2 * i + 1, 2 * ((i - 1) % xs) + 1)]
 
-    parts = density_parts(where, coef_v, mate, pair_v, pair_mate)
+    sent, kept, passing = density_parts(where, coef_v, mate, pair_v, pair_mate)
     coupling, scale, placed = staged(
-        where, beta_cols, pair_coupling, pair_alpha.T, beta_ops, parts[0]
-    )
-    got = [swapped(parts[k], "y", k) for k in (1, 3, 2)]
-    *got, _, _ = lax.optimization_barrier((*got, near, across))
+        where, beta_cols, pair_coupling, pair_alpha.T, beta_ops, kept
+    )
+    arrived = lax.ppermute(sent, ("y", "c"), crossing(4, (1, 3)))
+    arrived, _, _ = lax.optimization_barrier((arrived, near, across))
+    passing = (passing.astype(F32) + arrived[1].astype(F32)).astype(BF16)
+    total = kept.astype(F32) + arrived[0].astype(F32)
+    total = total + lax.ppermute(passing, ("y", "c"), crossing(4, (3, 1))).astype(F32)
+    total = total.astype(BF16)
     onward = lax.ppermute(near, over, border)
     returned = swapped(across, "zl", 1)
-    total = parts[0].astype(F32)
-    for part in got:
-        total = total + part.astype(F32)
-    total = total.astype(BF16)
     total, coupling, scale, placed = lax.optimization_barrier((total, coupling, scale, placed))
 
     far = lax.ppermute(near, ALPHA, route)
-    zs = lax.axis_size("zh")
-    steps = [[(2 * i + h, 2 * (i ^ m[h]) + h) for i in range(zs) for h in (0, 1)] for m in ((1, 3), (3, 1))]
-    first = lax.ppermute(total, ("zh", "c"), steps[0])
+    first = lax.ppermute(total, ("zh", "c"), crossing(4, (1, 3)))
     total = (total.astype(F32) + first.astype(F32)).astype(BF16)
     passed = jnp.where(core == low, returned, onward)
     total, passed = lax.optimization_barrier((total, passed))
     crossed = swapped(passed, "c", 1)
-    second = lax.ppermute(total, ("zh", "c"), steps[1])
+    second = lax.ppermute(total, ("zh", "c"), crossing(4, (3, 1)))
     same = same_spin_beta([onward, crossed, coef_v, mate, returned], placed)
     second, same = lax.optimization_barrier((second, same))
 

time: 62.1 us -> 61.5 us (level)
  waiting for transfers between devices: 23.4 us -> 17.2 us
  starting transfers between devices: 24.5 us -> 30.1 us
    ppermute x12 -> x9, waiting for transfers between devices: 11.3 us -> 2.35 us  [swapped(): return lax.ppermute(block, axis, [(i, i ^ mask) for i in range(count)])]
    ppermute x2 -> x4, waiting for transfers between devices: 12.1 us -> 7.52 us  [the longest x1 4.71 us: local(): second = lax.ppermute(total, ('zh', 'c'), crossing(4, (3, 1)))]
    ppermute x1, waiting for transfers between devices: 0.01 us -> 4.06 us  [local(): across = lax.ppermute(coef_v, over, border)]
    ppermute x12 -> x9, starting transfers between devices: 13.7 us -> 17.2 us  [swapped(): return lax.ppermute(block, axis, [(i, i ^ mask) for i in range(count)])]
    ppermute x1, waiting for transfers between devices: 0.01 us -> 3.23 us  [local(): onward = lax.ppermute(near, over, border)]
    ppermute x2 -> x4, starting transfers between devices: 0.1 us -> 3.04 us  [the longest x1 1.74 us: local(): lax.ppermute(passing, ('y', 'c'), crossing(4, (3, 1))).astype(F32)]
    ppermute x1, starting transfers between devices: 7.09 us -> 4.48 us  [local(): across = lax.ppermute(coef_v, over, border)]
    ppermute x1, starting transfers between devices: 2.25 us -> 4.17 us  [local(): onward = lax.ppermute(near, over, border)]
  transfers between devices with their start and end apart: 17 -> 16, of which waited for: 6 -> 6; matrix products, arithmetic and copies ran while one was open for 0% -> 0% of each run, Pallas kernels for 18% -> 17%
where the time goes in v6:
time: 61.5 us; the launch traced here: 61.4 us
  starting transfers between devices  30.1 us (49%)
  waiting for transfers between devices  17.2 us (28%)
  Pallas kernels  12.9 us (21%)
  local copies, waits for them, and re-layouts  0.76 us (1%)
    ppermute x9, starting transfers between devices, swapped(): return lax.ppermute(block, axis, [(i, i ^ mask) for i in range(count)])  17.2 us
    pallas_call x9, Pallas kernels, call(): pl.pallas_call(kernel, out_shape=outs, in_specs=specs, out_specs=out_spec...  12.9 us
    ppermute x1, waiting for transfers between devices, local(): second = lax.ppermute(total, ('zh', 'c'), crossing(4, (3, 1)))  4.71 us
    ppermute x1, starting transfers between devices, local(): across = lax.ppermute(coef_v, over, border)  4.48 us
    ppermute x1, starting transfers between devices, local(): onward = lax.ppermute(near, over, border)  4.17 us
    ppermute x1, waiting for transfers between devices, local(): across = lax.ppermute(coef_v, over, border)  4.06 us
    ppermute x1, waiting for transfers between devices, local(): onward = lax.ppermute(near, over, border)  3.23 us
    ppermute x1, waiting for transfers between devices, local(): first = lax.ppermute(total, ('zh', 'c'), crossing(4, (1, 3)))  2.81 us
  transfers between devices with their start and end apart: 16, of which 6 were waited for; matrix products, arithmetic and copies ran while one was open for 0% of the time, Pallas kernels for 17%

profile of v6, /device:TPU:1, one launch (start us, length us, event | category | flops | bytes accessed | tf_op | source)
XLA Modules:
  0.0 61.4 jit_solution(17365981077746546476)
XLA Ops:
  0.0 3.2 %collective-permute-start = (bf16[1024,128]{1,0:T(8,128)(2,1)}, bf16[1024,128]{1,0:T(8,128)(2,1)S(1)}, u32[]{:S(2)}, u32[]{:S(2)}) collective-permute-start(bf16[1024,128]{1,0:T(8,128)(2,1)} %coef_ref.1), channel_id=1, source_target_pairs={{0,1},{1,0},{2,3},{3,2},{4,5},{5,4},{6,7},{7,6},{8,9},{9,8},{10,11... | collective-permute-start | bytes 786440 | tf_op jit(solution)/shard_map/ppermute | solution.py:26
  3.2 1.0 %loaded_kernel.1 = (bf16[1024,128]{1,0:T(8,128)(2,1)S(1)}, bf16[576,128]{1,0:T(8,128)(2,1)S(1)}) custom-call(bf16[1024,128]{1,0:T(8,128)(2,1)} %coef_ref.1, bf16[576,128]{1,0:T(8,128)(2,1)} %bitcast.24), custom_call_target="tpu_custom_call" | custom-call | bytes 1048576 | tf_op jit(solution)/shard_map/loaded_kernel/pallas_call | solution.py:38
  4.8 1.0 %density_parts_kernel.1 = (bf16[2,576,128]{2,1,0:T(8,128)(2,1)S(1)}, bf16[576,128]{1,0:T(8,128)(2,1)S(1)}, bf16[576,128]{1,0:T(8,128)(2,1)S(1)}) custom-call(s32[16]{0:T(128)S(1)} %stack.61.where_ref, bf16[1024,128]{1,0:T(8,128)(2,1)S(1)} %get-tuple-element.27.own_ref.b2, bf16[1024,128]{1,0:T(8,128)(2,1)S(1)} %collective-permute-done.mate_ref.b3, ...), custom_call_target="tpu_custom_call" | custom-call | flops 150994944 | bytes 1048576 | tf_op jit(solution)/shard_map/density_parts_kernel/pallas_call | solution.py:38
  5.8 1.1 %collective-permute-start.2 = (bf16[2,576,128]{2,1,0:T(8,128)(2,1)S(1)}, bf16[2,576,128]{2,1,0:T(8,128)(2,1)S(1)}, u32[]{:S(2)}, u32[]{:S(2)}) collective-permute-start(bf16[2,576,128]{2,1,0:T(8,128)(2,1)S(1)} %get-tuple-element.30), channel_id=1, source_target_pairs={{0,8},{1,25},{8,0},{9,17},{16,24},{17,9},{24,16},{25,1},{2,10},{3,... | collective-permute-start | bytes 884744 | tf_op jit(solution)/shard_map/ppermute | solution.py:335
  6.9 1.6 %collective-permute-start.3 = (bf16[1024,128]{1,0:T(8,128)(2,1)S(1)}, bf16[1024,128]{1,0:T(8,128)(2,1)S(1)}, u32[]{:S(2)}, u32[]{:S(2)}) collective-permute-start(bf16[1024,128]{1,0:T(8,128)(2,1)S(1)} %get-tuple-element.27.own_ref.b2), channel_id=1, source_target_pairs={{0,32},{32,0},{1,33},{33,1},{2,34},{34,2},{3,35},{35,3},{4,36},{36... | collective-permute-start | bytes 786440 | tf_op jit(solution)/shard_map/ppermute | solution.py:26
  8.6 4.5 %collective-permute-start.4 = (bf16[1024,128]{1,0:T(8,128)(2,1)S(1)}, bf16[1024,128]{1,0:T(8,128)(2,1)S(1)}, u32[]{:S(2)}, u32[]{:S(2)}) collective-permute-start(bf16[1024,128]{1,0:T(8,128)(2,1)S(1)} %get-tuple-element.27.own_ref.b2), channel_id=1, source_target_pairs={{0,62},{62,0},{1,63},{63,1},{2,32},{32,2},{3,33},{33,3},{4,34},{34... | collective-permute-start | bytes 786440 | tf_op jit(solution)/shard_map/ppermute | solution.py:326
  13.1 1.9 %collective-permute-done.3.near_ref = bf16[1024,128]{1,0:T(8,128)(2,1)S(1)} collective-permute-done((bf16[1024,128]{1,0:T(8,128)(2,1)S(1)}, bf16[1024,128]{1,0:T(8,128)(2,1)S(1)}, u32[]{:S(2)}, u32[]{:S(2)}) %collective-permute-start.3) | collective-permute-done | bytes 262176 | tf_op jit(solution)/shard_map/ppermute | solution.py:26
  15.0 4.1 %collective-permute-done.4 = bf16[1024,128]{1,0:T(8,128)(2,1)S(1)} collective-permute-done((bf16[1024,128]{1,0:T(8,128)(2,1)S(1)}, bf16[1024,128]{1,0:T(8,128)(2,1)S(1)}, u32[]{:S(2)}, u32[]{:S(2)}) %collective-permute-start.4) | collective-permute-done | bytes 262176 | tf_op jit(solution)/shard_map/ppermute | solution.py:326
  19.1 1.7 %collective-permute-start.5 = (bf16[576,128]{1,0:T(8,128)(2,1)S(1)}, bf16[576,128]{1,0:T(8,128)(2,1)S(1)}, u32[]{:S(2)}, u32[]{:S(2)}) collective-permute-start(bf16[576,128]{1,0:T(8,128)(2,1)S(1)} %fusion), channel_id=1, source_target_pairs={{0,24},{1,9},{8,16},{9,1},{16,8},{17,25},{24,0},{25,17},{2,26},{3,... | collective-permute-start | bytes 442376 | tf_op jit(solution)/shard_map/ppermute | solution.py:339
  20.8 4.2 %collective-permute-start.8 = (bf16[1024,128]{1,0:T(8,128)(2,1)S(1)}, bf16[1024,128]{1,0:T(8,128)(2,1)S(1)}, u32[]{:S(2)}, u32[]{:S(2)}) collective-permute-start(bf16[1024,128]{1,0:T(8,128)(2,1)S(1)} %collective-permute-done.3.near_ref), channel_id=1, source_target_pairs={{0,62},{62,0},{1,63},{63,1},{2,32},{32,2},{3,33},{33,3},{4,34},{34... | collective-permute-start | bytes 786440 | tf_op jit(solution)/shard_map/ppermute | solution.py:341
  25.0 0.7 %copy-done.1 = s32[1,4]{1,0:T(1,128)S(1)} copy-done((s32[1,4]{1,0:T(1,128)S(1)}, s32[1,4]{1,0:T(1,128)}, u32[]{:S(2)}) %copy-start.1) | copy-done | bytes 40
  25.6 1.8 %staged_kernel.1 = (bf16[576,576]{1,0:T(8,128)(2,1)S(1)}, f32[128,576]{1,0:T(8,128)S(1)}, bf16[128,640]{1,0:T(8,128)(2,1)S(1)}) custom-call(s32[16]{0:T(128)S(1)} %stack.61.where_ref, s32[1,4]{1,0:T(1,128)S(1)} %copy-done.1, bf16[576,576]{1,0:T(8,128)(2,1)} %c_ref.1, bf16[576,1024]{1,0:T(8,128)(2,1)} %bitcast.22, bf16[128,512]{1,0:T(8,128)(2,1)} %ops_ref.2, ...), custom_call_target="tpu_custom_call" | custom-call | flops 331776 | bytes 2097152 | tf_op jit(solution)/shard_map/staged_kernel/pallas_call | solution.py:38
  27.8 3.2 %collective-permute-done.8.b0 = bf16[1024,128]{1,0:T(8,128)(2,1)S(1)} collective-permute-done((bf16[1024,128]{1,0:T(8,128)(2,1)S(1)}, bf16[1024,128]{1,0:T(8,128)(2,1)S(1)}, u32[]{:S(2)}, u32[]{:S(2)}) %collective-permute-start.8) | collective-permute-done | bytes 262176 | tf_op jit(solution)/shard_map/ppermute | solution.py:341
  31.1 2.8 %collective-permute-done.6 = bf16[576,128]{1,0:T(8,128)(2,1)S(1)} collective-permute-done((bf16[576,128]{1,0:T(8,128)(2,1)S(1)}, bf16[576,128]{1,0:T(8,128)(2,1)S(1)}, u32[]{:S(2)}, u32[]{:S(2)}) %collective-permute-start.6) | collective-permute-done | bytes 147488 | tf_op jit(solution)/shard_map/ppermute | solution.py:346
  33.9 3.6 %collective-permute-start.10 = (bf16[1024,128]{1,0:T(8,128)(2,1)S(1)}, bf16[1024,128]{1,0:T(8,128)(2,1)S(1)}, u32[]{:S(2)}, u32[]{:S(2)}) collective-permute-start(bf16[1024,128]{1,0:T(8,128)(2,1)S(1)} %broadcast_select_fusion), channel_id=1, source_target_pairs={{0,1},{1,0},{2,3},{3,2},{4,5},{5,4},{6,7},{7,6},{8,9},{9,8},{10,11... | collective-permute-start | bytes 786440 | tf_op jit(solution)/shard_map/ppermute | solution.py:26
  37.6 1.2 %collective-permute-start.14 = (bf16[1024,128]{1,0:T(8,128)(2,1)S(1)}, bf16[1024,128]{1,0:T(8,128)(2,1)S(1)}, u32[]{:S(2)}, u32[]{:S(2)}) collective-permute-start(bf16[1024,128]{1,0:T(8,128)(2,1)S(1)} %collective-permute-done.3.near_ref), channel_id=1, source_target_pairs={{0,64},{32,224},{64,128},{96,32},{128,192},{160,96},{192,0},{224,1... | collective-permute-start | bytes 786440 | tf_op jit(solution)/shard_map/ppermute | solution.py:345
  39.3 4.7 %collective-permute-done.9.far_ref = bf16[576,128]{1,0:T(8,128)(2,1)S(1)} collective-permute-done((bf16[576,128]{1,0:T(8,128)(2,1)S(1)}, bf16[576,128]{1,0:T(8,128)(2,1)S(1)}, u32[]{:S(2)}, u32[]{:S(2)}) %collective-permute-start.9) | collective-permute-done | bytes 147488 | tf_op jit(solution)/shard_map/ppermute | solution.py:351
  44.4 0.6 collective-permute-start.11
  45.0 1.8 %collective-permute-start.12 = (bf16[128,576]{1,0:T(8,128)(2,1)S(1)}, bf16[128,576]{1,0:T(8,128)(2,1)S(1)}, u32[]{:S(2)}, u32[]{:S(2)}) collective-permute-start(bf16[128,576]{1,0:T(8,128)(2,1)S(1)} %excited_block_kernel.1.refs_0_.e0), channel_id=1, source_target_pairs={{0,16},{8,24},{16,0},{24,8},{1,17},{9,25},{17,1},{25,9},{2,18},{10... | collective-permute-start | bytes 442376 | tf_op jit(solution)/shard_map/ppermute | solution.py:26
  46.8 1.5 %collective-permute-start.13 = (bf16[128,576]{1,0:T(8,128)(2,1)S(1)}, bf16[128,576]{1,0:T(8,128)(2,1)S(1)}, u32[]{:S(2)}, u32[]{:S(2)}) collective-permute-start(bf16[128,576]{1,0:T(8,128)(2,1)S(1)} %excited_block_kernel.1.refs_0_.e0), channel_id=1, source_target_pairs={{0,24},{8,16},{16,8},{24,0},{1,25},{9,17},{17,9},{25,1},{2,26},{10... | collective-permute-start | bytes 442376 | tf_op jit(solution)/shard_map/ppermute | solution.py:26
  48.3 5.0 %same_spin_alpha_kernel.1.same_ref = f32[1024,128]{1,0:T(8,128)S(1)} custom-call(s32[16]{0:T(128)S(1)} %stack.61.where_ref, s32[1,4]{1,0:T(1,128)S(1)} %copy-done.2, bf16[1024,128]{1,0:T(8,128)(2,1)S(1)} %get-tuple-element.27.own_ref.b2, bf16[1024,128]{1,0:T(8,128)(2,1)S(1)} %collective-permute-done.3.near_ref, ...), custom_call_target="tpu_custom_call" | custom-call | flops 1073741824 | bytes 10485760 | tf_op jit(solution)/shard_map/same_spin_alpha_kernel/pallas_call | solution.py:38
  53.7 4.7 %collective-permute-start.15 = (bf16[4,128,128]{2,1,0:T(8,128)(2,1)S(1)}, bf16[4,128,128]{2,1,0:T(8,128)(2,1)S(1)}, u32[]{:S(2)}, u32[]{:S(2)}) collective-permute-start(bf16[4,128,128]{2,1,0:T(8,128)(2,1)S(1)} %mixed_mate_kernel.1), channel_id=1, source_target_pairs={{0,1},{1,0},{2,3},{3,2},{4,5},{5,4},{6,7},{7,6},{8,9},{9,8},{10,11... | collective-permute-start | bytes 393224 | tf_op jit(solution)/shard_map/ppermute | solution.py:26
  58.4 1.5 %finished_own_kernel.1.begun_ref = f32[1024,128]{1,0:T(8,128)} custom-call(s32[16]{0:T(128)S(1)} %stack.61.where_ref, f32[1024,128]{1,0:T(8,128)S(1)} %same_spin_alpha_kernel.1.same_ref, bf16[128,576]{1,0:T(8,128)(2,1)S(1)} %excited_block_kernel.1.refs_0_.e0, bf16[128,576]{1,0:T(8,128)(2,1)S(1)} %collective-permute-done.11.refs_1_.e1, ...), custom_call_target="tpu_custom_call" | custom-call | flops 78643200 | bytes 2097152 | tf_op jit(solution)/shard_map/finished_own_kernel/pallas_call | solution.py:38
  59.9 1.3 %finished_mate_kernel.1 = f32[1024,128]{1,0:T(8,128)} custom-call(s32[16]{0:T(128)S(1)} %stack.61.where_ref, f32[1024,128]{1,0:T(8,128)S(1)} %same_spin_alpha_kernel.1.same_ref, bf16[4,128,128]{2,1,0:T(8,128)(2,1)S(1)} %collective-permute-done.15.theirs_ref, f32[1024,128]{1,0:T(8,128)S(1)} %copy-done, ...), custom_call_target="tpu_custom_call", output_to_operand_aliasing={{}: (4, {})} | custom-call | flops 262144 | bytes 2097152 | tf_op jit(solution)/shard_map/finished_mate_kernel/pallas_call | solution.py:38
  (28 shorter events, 2.2 us)
Async XLA Ops:
  0.0 48.3 %copy-start.2 = (s32[1,4]{1,0:T(1,128)S(1)}, s32[1,4]{1,0:T(1,128)}, u32[]{:S(2)}) copy-start(s32[1,4]{1,0:T(1,128)} %cols_ref.3) | copy-start | bytes 52
  0.0 4.8 %collective-permute-start = (bf16[1024,128]{1,0:T(8,128)(2,1)}, bf16[1024,128]{1,0:T(8,128)(2,1)S(1)}, u32[]{:S(2)}, u32[]{:S(2)}) collective-permute-start(bf16[1024,128]{1,0:T(8,128)(2,1)} %coef_ref.1), channel_id=1, source_target_pairs={{0,1},{1,0},{2,3},{3,2},{4,5},{5,4},{6,7},{7,6},{8,9},{9,8},{10,11... | collective-permute-start | bytes 786440 | tf_op jit(solution)/shard_map/ppermute | solution.py:26
  3.2 1.6 %collective-permute-start.1 = (bf16[576,128]{1,0:T(8,128)(2,1)}, bf16[576,128]{1,0:T(8,128)(2,1)S(1)}, u32[]{:S(2)}, u32[]{:S(2)}) collective-permute-start(bf16[576,128]{1,0:T(8,128)(2,1)} %bitcast.23), channel_id=1, source_target_pairs={{0,1},{1,0},{2,3},{3,2},{4,5},{5,4},{6,7},{7,6},{8,9},{9,8},{10,11... | collective-permute-start | bytes 442376 | tf_op jit(solution)/shard_map/ppermute | solution.py:26
  5.8 13.2 %collective-permute-start.2 = (bf16[2,576,128]{2,1,0:T(8,128)(2,1)S(1)}, bf16[2,576,128]{2,1,0:T(8,128)(2,1)S(1)}, u32[]{:S(2)}, u32[]{:S(2)}) collective-permute-start(bf16[2,576,128]{2,1,0:T(8,128)(2,1)S(1)} %get-tuple-element.30), channel_id=1, source_target_pairs={{0,8},{1,25},{8,0},{9,17},{16,24},{17,9},{24,16},{25,1},{2,10},{3,... | collective-permute-start | bytes 884744 | tf_op jit(solution)/shard_map/ppermute | solution.py:335
  6.9 8.0 %collective-permute-start.3 = (bf16[1024,128]{1,0:T(8,128)(2,1)S(1)}, bf16[1024,128]{1,0:T(8,128)(2,1)S(1)}, u32[]{:S(2)}, u32[]{:S(2)}) collective-permute-start(bf16[1024,128]{1,0:T(8,128)(2,1)S(1)} %get-tuple-element.27.own_ref.b2), channel_id=1, source_target_pairs={{0,32},{32,0},{1,33},{33,1},{2,34},{34,2},{3,35},{35,3},{4,36},{36... | collective-permute-start | bytes 786440 | tf_op jit(solution)/shard_map/ppermute | solution.py:26
  8.6 10.4 %collective-permute-start.4 = (bf16[1024,128]{1,0:T(8,128)(2,1)S(1)}, bf16[1024,128]{1,0:T(8,128)(2,1)S(1)}, u32[]{:S(2)}, u32[]{:S(2)}) collective-permute-start(bf16[1024,128]{1,0:T(8,128)(2,1)S(1)} %get-tuple-element.27.own_ref.b2), channel_id=1, source_target_pairs={{0,62},{62,0},{1,63},{63,1},{2,32},{32,2},{3,33},{33,3},{4,34},{34... | collective-permute-start | bytes 786440 | tf_op jit(solution)/shard_map/ppermute | solution.py:326
  19.1 8.4 %collective-permute-start.5 = (bf16[576,128]{1,0:T(8,128)(2,1)S(1)}, bf16[576,128]{1,0:T(8,128)(2,1)S(1)}, u32[]{:S(2)}, u32[]{:S(2)}) collective-permute-start(bf16[576,128]{1,0:T(8,128)(2,1)S(1)} %fusion), channel_id=1, source_target_pairs={{0,24},{1,9},{8,16},{9,1},{16,8},{17,25},{24,0},{25,17},{2,26},{3,... | collective-permute-start | bytes 442376 | tf_op jit(solution)/shard_map/ppermute | solution.py:339
  20.8 10.2 %collective-permute-start.8 = (bf16[1024,128]{1,0:T(8,128)(2,1)S(1)}, bf16[1024,128]{1,0:T(8,128)(2,1)S(1)}, u32[]{:S(2)}, u32[]{:S(2)}) collective-permute-start(bf16[1024,128]{1,0:T(8,128)(2,1)S(1)} %collective-permute-done.3.near_ref), channel_id=1, source_target_pairs={{0,62},{62,0},{1,63},{63,1},{2,32},{32,2},{3,33},{33,3},{4,34},{34... | collective-permute-start | bytes 786440 | tf_op jit(solution)/shard_map/ppermute | solution.py:341
  25.0 6.0 %collective-permute-start.7 = (bf16[1024,128]{1,0:T(8,128)(2,1)S(1)}, bf16[1024,128]{1,0:T(8,128)(2,1)S(1)}, u32[]{:S(2)}, u32[]{:S(2)}) collective-permute-start(bf16[1024,128]{1,0:T(8,128)(2,1)S(1)} %collective-permute-done.4), channel_id=1, source_target_pairs={{0,32},{32,0},{1,33},{33,1},{2,34},{34,2},{3,35},{35,3},{4,36},{36... | collective-permute-start | bytes 786440 | tf_op jit(solution)/shard_map/ppermute | solution.py:26
  25.0 0.7 %copy-start.1 = (s32[1,4]{1,0:T(1,128)S(1)}, s32[1,4]{1,0:T(1,128)}, u32[]{:S(2)}) copy-start(s32[1,4]{1,0:T(1,128)} %cols_ref.2) | copy-start | bytes 52
  27.5 30.9 %copy-start = (f32[1024,128]{1,0:T(8,128)S(1)}, f32[1024,128]{1,0:T(8,128)}, u32[]{:S(2)}) copy-start(f32[1024,128]{1,0:T(8,128)} %den_ref.3) | copy-start | bytes 1572868
  27.6 6.3 %collective-permute-start.6 = (bf16[576,128]{1,0:T(8,128)(2,1)S(1)}, bf16[576,128]{1,0:T(8,128)(2,1)S(1)}, u32[]{:S(2)}, u32[]{:S(2)}) collective-permute-start(bf16[576,128]{1,0:T(8,128)(2,1)S(1)} %fusion.2), channel_id=1, source_target_pairs={{0,2},{1,7},{2,0},{3,5},{4,6},{5,3},{6,4},{7,1},{8,10},{9,15},{10,... | collective-permute-start | bytes 442376 | tf_op jit(solution)/shard_map/ppermute | solution.py:346
  33.9 4.9 %collective-permute-start.10 = (bf16[1024,128]{1,0:T(8,128)(2,1)S(1)}, bf16[1024,128]{1,0:T(8,128)(2,1)S(1)}, u32[]{:S(2)}, u32[]{:S(2)}) collective-permute-start(bf16[1024,128]{1,0:T(8,128)(2,1)S(1)} %broadcast_select_fusion), channel_id=1, source_target_pairs={{0,1},{1,0},{2,3},{3,2},{4,5},{5,4},{6,7},{7,6},{8,9},{9,8},{10,11... | collective-permute-start | bytes 786440 | tf_op jit(solution)/shard_map/ppermute | solution.py:26
  37.6 10.8 %collective-permute-start.14 = (bf16[1024,128]{1,0:T(8,128)(2,1)S(1)}, bf16[1024,128]{1,0:T(8,128)(2,1)S(1)}, u32[]{:S(2)}, u32[]{:S(2)}) collective-permute-start(bf16[1024,128]{1,0:T(8,128)(2,1)S(1)} %collective-permute-done.3.near_ref), channel_id=1, source_target_pairs={{0,64},{32,224},{64,128},{96,32},{128,192},{160,96},{192,0},{224,1... | collective-permute-start | bytes 786440 | tf_op jit(solution)/shard_map/ppermute | solution.py:345
  38.8 5.2 %collective-permute-start.9 = (bf16[576,128]{1,0:T(8,128)(2,1)S(1)}, bf16[576,128]{1,0:T(8,128)(2,1)S(1)}, u32[]{:S(2)}, u32[]{:S(2)}) collective-permute-start(bf16[576,128]{1,0:T(8,128)(2,1)S(1)} %add_convert_fusion.near_ref), channel_id=1, source_target_pairs={{0,6},{1,3},{2,4},{3,1},{4,2},{5,7},{6,0},{7,5},{8,14},{9,11},{10,... | collective-permute-start | bytes 442376 | tf_op jit(solution)/shard_map/ppermute | solution.py:351
  44.4 8.9 %collective-permute-start.11 = (bf16[128,576]{1,0:T(8,128)(2,1)S(1)}, bf16[128,576]{1,0:T(8,128)(2,1)S(1)}, u32[]{:S(2)}, u32[]{:S(2)}) collective-permute-start(bf16[128,576]{1,0:T(8,128)(2,1)S(1)} %excited_block_kernel.1.refs_0_.e0), channel_id=1, source_target_pairs={{0,8},{8,0},{16,24},{24,16},{1,9},{9,1},{17,25},{25,17},{2,10},{10... | collective-permute-start | bytes 442376 | tf_op jit(solution)/shard_map/ppermute | solution.py:26
  45.0 8.3 %collective-permute-start.12 = (bf16[128,576]{1,0:T(8,128)(2,1)S(1)}, bf16[128,576]{1,0:T(8,128)(2,1)S(1)}, u32[]{:S(2)}, u32[]{:S(2)}) collective-permute-start(bf16[128,576]{1,0:T(8,128)(2,1)S(1)} %excited_block_kernel.1.refs_0_.e0), channel_id=1, source_target_pairs={{0,16},{8,24},{16,0},{24,8},{1,17},{9,25},{17,1},{25,9},{2,18},{10... | collective-permute-start | bytes 442376 | tf_op jit(solution)/shard_map/ppermute | solution.py:26
  46.8 6.5 %collective-permute-start.13 = (bf16[128,576]{1,0:T(8,128)(2,1)S(1)}, bf16[128,576]{1,0:T(8,128)(2,1)S(1)}, u32[]{:S(2)}, u32[]{:S(2)}) collective-permute-start(bf16[128,576]{1,0:T(8,128)(2,1)S(1)} %excited_block_kernel.1.refs_0_.e0), channel_id=1, source_target_pairs={{0,24},{8,16},{16,8},{24,0},{1,25},{9,17},{17,9},{25,1},{2,26},{10... | collective-permute-start | bytes 442376 | tf_op jit(solution)/shard_map/ppermute | solution.py:26
  53.7 6.3 %collective-permute-start.15 = (bf16[4,128,128]{2,1,0:T(8,128)(2,1)S(1)}, bf16[4,128,128]{2,1,0:T(8,128)(2,1)S(1)}, u32[]{:S(2)}, u32[]{:S(2)}) collective-permute-start(bf16[4,128,128]{2,1,0:T(8,128)(2,1)S(1)} %mixed_mate_kernel.1), channel_id=1, source_target_pairs={{0,1},{1,0},{2,3},{3,2},{4,5},{5,4},{6,7},{7,6},{8,9},{9,8},{10,11... | collective-permute-start | bytes 393224 | tf_op jit(solution)/shard_map/ppermute | solution.py:26

commit v7 on v6

--- a/solution.py
+++ b/solution.py
@@ -333,14 +333,16 @@
         where, beta_cols, pair_coupling, pair_alpha.T, beta_ops, kept
     )
     arrived = lax.ppermute(sent, ("y", "c"), crossing(4, (1, 3)))
-    arrived, _, _ = lax.optimization_barrier((arrived, near, across))
+    arrived, coupling, scale, placed = lax.optimization_barrier(
+        (arrived, coupling, scale, placed)
+    )
     passing = (passing.astype(F32) + arrived[1].astype(F32)).astype(BF16)
     total = kept.astype(F32) + arrived[0].astype(F32)
-    total = total + lax.ppermute(passing, ("y", "c"), crossing(4, (3, 1))).astype(F32)
-    total = total.astype(BF16)
+    passed = lax.ppermute(passing, ("y", "c"), crossing(4, (3, 1)))
+    passed, _, _ = lax.optimization_barrier((passed, near, across))
+    total = (total + passed.astype(F32)).astype(BF16)
     onward = lax.ppermute(near, over, border)
     returned = swapped(across, "zl", 1)
-    total, coupling, scale, placed = lax.optimization_barrier((total, coupling, scale, placed))
 
     far = lax.ppermute(near, ALPHA, route)
     first = lax.ppermute(total, ("zh", "c"), crossing(4, (1, 3)))

time: 61.5 us -> 60.2 us (0.979); the launches traced: 61.4 us -> 59.3 us
  waiting for transfers between devices: 17.2 us -> 11.8 us
  other arithmetic: 0.17 us -> 1.8 us
  starting transfers between devices: 30.1 us -> 31.7 us
    ppermute x1, waiting for transfers between devices: 4.06 us -> 0.01 us  [local(): across = lax.ppermute(coef_v, over, border)]
    ppermute x1, starting transfers between devices: 4.17 us -> 7.9 us  [local(): onward = lax.ppermute(near, over, border)]
    ppermute x9, starting transfers between devices: 17.2 us -> 13.6 us  [swapped(): return lax.ppermute(block, axis, [(i, i ^ mask) for i in range(count)])]
    ppermute x1, waiting for transfers between devices: 2.81 us -> 0.01 us  [local(): first = lax.ppermute(total, ('zh', 'c'), crossing(4, (1, 3)))]
    ppermute x9, waiting for transfers between devices: 2.35 us -> 4.79 us  [swapped(): return lax.ppermute(block, axis, [(i, i ^ mask) for i in range(count)])]
    ppermute x1, waiting for transfers between devices: 4.71 us -> 2.82 us  [local(): second = lax.ppermute(total, ('zh', 'c'), crossing(4, (3, 1)))]
    ppermute x1, starting transfers between devices: 0.01 us -> 1.85 us  [local(): second = lax.ppermute(total, ('zh', 'c'), crossing(4, (3, 1)))]
    ppermute x1, waiting for transfers between devices: 3.23 us -> 4.23 us  [local(): onward = lax.ppermute(near, over, border)]
  transfers between devices with their start and end apart: 16 -> 16, of which waited for: 6 -> 5; matrix products, arithmetic and copies ran while one was open for 0% -> 3% of each run, Pallas kernels for 17% -> 17%
where the time goes in v7:
time: 60.2 us; the launch traced here: 59.3 us
  starting transfers between devices  31.7 us (53%)
  Pallas kernels  12.9 us (21%)
  waiting for transfers between devices  11.8 us (20%)
  other arithmetic  1.8 us (3%)
  local copies, waits for them, and re-layouts  0.77 us (1%)
    ppermute x9, starting transfers between devices, swapped(): return lax.ppermute(block, axis, [(i, i ^ mask) for i in range(count)])  13.6 us
    pallas_call x9, Pallas kernels, call(): pl.pallas_call(kernel, out_shape=outs, in_specs=specs, out_specs=out_spec...  12.9 us
    ppermute x1, starting transfers between devices, local(): onward = lax.ppermute(near, over, border)  7.9 us
    ppermute x9, waiting for transfers between devices, swapped(): return lax.ppermute(block, axis, [(i, i ^ mask) for i in range(count)])  4.79 us
    ppermute x1, starting transfers between devices, local(): across = lax.ppermute(coef_v, over, border)  4.48 us
    ppermute x1, waiting for transfers between devices, local(): onward = lax.ppermute(near, over, border)  4.23 us
    ppermute x1, waiting for transfers between devices, local(): second = lax.ppermute(total, ('zh', 'c'), crossing(4, (3, 1)))  2.82 us
    ppermute x1, starting transfers between devices, local(): second = lax.ppermute(total, ('zh', 'c'), crossing(4, (3, 1)))  1.85 us
  transfers between devices with their start and end apart: 16, of which 5 were waited for; matrix products, arithmetic and copies ran while one was open for 3% of the time, Pallas kernels for 17%

profile of v7, /device:TPU:1, one launch (start us, length us, event | category | flops | bytes accessed | tf_op | source)
XLA Modules:
  0.0 59.3 jit_solution(11389131533333195867)
XLA Ops:
  0.0 3.2 %collective-permute-start = (bf16[1024,128]{1,0:T(8,128)(2,1)}, bf16[1024,128]{1,0:T(8,128)(2,1)S(1)}, u32[]{:S(2)}, u32[]{:S(2)}) collective-permute-start(bf16[1024,128]{1,0:T(8,128)(2,1)} %coef_ref.1), channel_id=1, source_target_pairs={{0,1},{1,0},{2,3},{3,2},{4,5},{5,4},{6,7},{7,6},{8,9},{9,8},{10,11... | collective-permute-start | bytes 786440 | tf_op jit(solution)/shard_map/ppermute | solution.py:26
  3.2 1.0 %loaded_kernel.1 = (bf16[1024,128]{1,0:T(8,128)(2,1)S(1)}, bf16[576,128]{1,0:T(8,128)(2,1)S(1)}) custom-call(bf16[1024,128]{1,0:T(8,128)(2,1)} %coef_ref.1, bf16[576,128]{1,0:T(8,128)(2,1)} %bitcast.24), custom_call_target="tpu_custom_call" | custom-call | bytes 1048576 | tf_op jit(solution)/shard_map/loaded_kernel/pallas_call | solution.py:38
  4.8 1.0 %density_parts_kernel.1 = (bf16[2,576,128]{2,1,0:T(8,128)(2,1)S(1)}, bf16[576,128]{1,0:T(8,128)(2,1)S(1)}, bf16[576,128]{1,0:T(8,128)(2,1)S(1)}) custom-call(s32[16]{0:T(128)S(1)} %stack.61.where_ref, bf16[1024,128]{1,0:T(8,128)(2,1)S(1)} %get-tuple-element.27.own_ref.b2, bf16[1024,128]{1,0:T(8,128)(2,1)S(1)} %collective-permute-done.mate_ref.b3, ...), custom_call_target="tpu_custom_call" | custom-call | flops 150994944 | bytes 1048576 | tf_op jit(solution)/shard_map/density_parts_kernel/pallas_call | solution.py:38
  5.9 1.1 %collective-permute-start.2 = (bf16[2,576,128]{2,1,0:T(8,128)(2,1)S(1)}, bf16[2,576,128]{2,1,0:T(8,128)(2,1)S(1)}, u32[]{:S(2)}, u32[]{:S(2)}) collective-permute-start(bf16[2,576,128]{2,1,0:T(8,128)(2,1)S(1)} %get-tuple-element.30), channel_id=1, source_target_pairs={{0,8},{1,25},{8,0},{9,17},{16,24},{17,9},{24,16},{25,1},{2,10},{3,... | collective-permute-start | bytes 884744 | tf_op jit(solution)/shard_map/ppermute | solution.py:335
  6.9 1.6 %collective-permute-start.4 = (bf16[1024,128]{1,0:T(8,128)(2,1)S(1)}, bf16[1024,128]{1,0:T(8,128)(2,1)S(1)}, u32[]{:S(2)}, u32[]{:S(2)}) collective-permute-start(bf16[1024,128]{1,0:T(8,128)(2,1)S(1)} %get-tuple-element.27.own_ref.b2), channel_id=1, source_target_pairs={{0,32},{32,0},{1,33},{33,1},{2,34},{34,2},{3,35},{35,3},{4,36},{36... | collective-permute-start | bytes 786440 | tf_op jit(solution)/shard_map/ppermute | solution.py:26
  8.6 4.5 %collective-permute-start.5 = (bf16[1024,128]{1,0:T(8,128)(2,1)S(1)}, bf16[1024,128]{1,0:T(8,128)(2,1)}, u32[]{:S(2)}, u32[]{:S(2)}) collective-permute-start(bf16[1024,128]{1,0:T(8,128)(2,1)S(1)} %get-tuple-element.27.own_ref.b2), channel_id=1, source_target_pairs={{0,62},{62,0},{1,63},{63,1},{2,32},{32,2},{3,33},{33,3},{4,34},{34... | collective-permute-start | bytes 786440 | tf_op jit(solution)/shard_map/ppermute | solution.py:326
  13.1 0.7 %copy-done.1 = s32[1,4]{1,0:T(1,128)S(1)} copy-done((s32[1,4]{1,0:T(1,128)S(1)}, s32[1,4]{1,0:T(1,128)}, u32[]{:S(2)}) %copy-start.1) | copy-done | bytes 40
  13.7 1.8 %staged_kernel.1 = (bf16[576,576]{1,0:T(8,128)(2,1)S(1)}, f32[128,576]{1,0:T(8,128)S(1)}, bf16[128,640]{1,0:T(8,128)(2,1)S(1)}) custom-call(s32[16]{0:T(128)S(1)} %stack.61.where_ref, s32[1,4]{1,0:T(1,128)S(1)} %copy-done.1, bf16[576,576]{1,0:T(8,128)(2,1)} %c_ref.1, bf16[576,1024]{1,0:T(8,128)(2,1)} %bitcast.22, bf16[128,512]{1,0:T(8,128)(2,1)} %ops_ref.2, ...), custom_call_target="tpu_custom_call" | custom-call | flops 331776 | bytes 2097152 | tf_op jit(solution)/shard_map/staged_kernel/pallas_call | solution.py:38
  15.6 0.7 %fusion = bf16[576,128]{1,0:T(8,128)(2,1)} fusion(bf16[576,128]{1,0:T(8,128)(2,1)S(1)} %get-tuple-element.35, bf16[2,576,128]{2,1,0:T(8,128)(2,1)S(1)} %collective-permute-done.2), kind=kLoop, calls=%fused_computation.1 | loop fusion | flops 294912 | bytes 442368 | tf_op jit(solution)/shard_map/convert_element_type | solution.py:339
  16.3 1.4 %collective-permute-start.3 = (bf16[576,128]{1,0:T(8,128)(2,1)}, bf16[576,128]{1,0:T(8,128)(2,1)}, u32[]{:S(2)}, u32[]{:S(2)}) collective-permute-start(bf16[576,128]{1,0:T(8,128)(2,1)} %fusion), channel_id=1, source_target_pairs={{0,24},{1,9},{8,16},{9,1},{16,8},{17,25},{24,0},{25,17},{2,26},{3,... | collective-permute-start | bytes 442376 | tf_op jit(solution)/shard_map/ppermute | solution.py:341
  17.7 7.9 %collective-permute-start.8 = (bf16[1024,128]{1,0:T(8,128)(2,1)S(1)}, bf16[1024,128]{1,0:T(8,128)(2,1)S(1)}, u32[]{:S(2)}, u32[]{:S(2)}) collective-permute-start(bf16[1024,128]{1,0:T(8,128)(2,1)S(1)} %collective-permute-done.4.near_ref), channel_id=1, source_target_pairs={{0,62},{62,0},{1,63},{63,1},{2,32},{32,2},{3,33},{33,3},{4,34},{34... | collective-permute-start | bytes 786440 | tf_op jit(solution)/shard_map/ppermute | solution.py:344
  25.6 1.0 %fusion.2 = bf16[576,128]{1,0:T(8,128)(2,1)S(1)} fusion(bf16[576,128]{1,0:T(8,128)(2,1)} %collective-permute-done.3, bf16[576,128]{1,0:T(8,128)(2,1)S(1)} %get-tuple-element.29.tie_ref, bf16[2,576,128]{2,1,0:T(8,128)(2,1)} %copy-done.3), kind=kLoop, calls=%fused_computation.4 | loop fusion | flops 442368 | bytes 589824 | tf_op jit(solution)/shard_map/convert_element_type | solution.py:343
  26.7 4.2 %collective-permute-done.8.b0 = bf16[1024,128]{1,0:T(8,128)(2,1)S(1)} collective-permute-done((bf16[1024,128]{1,0:T(8,128)(2,1)S(1)}, bf16[1024,128]{1,0:T(8,128)(2,1)S(1)}, u32[]{:S(2)}, u32[]{:S(2)}) %collective-permute-start.8) | collective-permute-done | bytes 262176 | tf_op jit(solution)/shard_map/ppermute | solution.py:344
  31.0 3.5 %collective-permute-done.7.b4 = bf16[1024,128]{1,0:T(8,128)(2,1)S(1)} collective-permute-done((bf16[1024,128]{1,0:T(8,128)(2,1)}, bf16[1024,128]{1,0:T(8,128)(2,1)S(1)}, u32[]{:S(2)}, u32[]{:S(2)}) %collective-permute-start.7) | collective-permute-done | bytes 262176 | tf_op jit(solution)/shard_map/ppermute | solution.py:26
  34.7 1.3 %collective-permute-start.14 = (bf16[1024,128]{1,0:T(8,128)(2,1)S(1)}, bf16[1024,128]{1,0:T(8,128)(2,1)S(1)}, u32[]{:S(2)}, u32[]{:S(2)}) collective-permute-start(bf16[1024,128]{1,0:T(8,128)(2,1)S(1)} %collective-permute-done.4.near_ref), channel_id=1, source_target_pairs={{0,64},{32,224},{64,128},{96,32},{128,192},{160,96},{192,0},{224,1... | collective-permute-start | bytes 786440 | tf_op jit(solution)/shard_map/ppermute | solution.py:347
  36.0 1.9 %collective-permute-start.9 = (bf16[576,128]{1,0:T(8,128)(2,1)S(1)}, bf16[576,128]{1,0:T(8,128)(2,1)S(1)}, u32[]{:S(2)}, u32[]{:S(2)}) collective-permute-start(bf16[576,128]{1,0:T(8,128)(2,1)S(1)} %add_convert_fusion.near_ref), channel_id=1, source_target_pairs={{0,6},{1,3},{2,4},{3,1},{4,2},{5,7},{6,0},{7,5},{8,14},{9,11},{10,... | collective-permute-start | bytes 442376 | tf_op jit(solution)/shard_map/ppermute | solution.py:353
  38.3 2.8 %collective-permute-done.9.far_ref = bf16[576,128]{1,0:T(8,128)(2,1)S(1)} collective-permute-done((bf16[576,128]{1,0:T(8,128)(2,1)S(1)}, bf16[576,128]{1,0:T(8,128)(2,1)S(1)}, u32[]{:S(2)}, u32[]{:S(2)}) %collective-permute-start.9) | collective-permute-done | bytes 147488 | tf_op jit(solution)/shard_map/ppermute | solution.py:353
  41.5 1.8 %collective-permute-start.11 = (bf16[128,576]{1,0:T(8,128)(2,1)S(1)}, bf16[128,576]{1,0:T(8,128)(2,1)S(1)}, u32[]{:S(2)}, u32[]{:S(2)}) collective-permute-start(bf16[128,576]{1,0:T(8,128)(2,1)S(1)} %excited_block_kernel.1.refs_0_.e0), channel_id=1, source_target_pairs={{0,8},{8,0},{16,24},{24,16},{1,9},{9,1},{17,25},{25,17},{2,10},{10... | collective-permute-start | bytes 442376 | tf_op jit(solution)/shard_map/ppermute | solution.py:26
  43.4 2.2 %collective-permute-start.12 = (bf16[128,576]{1,0:T(8,128)(2,1)S(1)}, bf16[128,576]{1,0:T(8,128)(2,1)S(1)}, u32[]{:S(2)}, u32[]{:S(2)}) collective-permute-start(bf16[128,576]{1,0:T(8,128)(2,1)S(1)} %excited_block_kernel.1.refs_0_.e0), channel_id=1, source_target_pairs={{0,16},{8,24},{16,0},{24,8},{1,17},{9,25},{17,1},{25,9},{2,18},{10... | collective-permute-start | bytes 442376 | tf_op jit(solution)/shard_map/ppermute | solution.py:26
  45.9 5.0 %same_spin_alpha_kernel.1.same_ref = f32[1024,128]{1,0:T(8,128)S(1)} custom-call(s32[16]{0:T(128)S(1)} %stack.61.where_ref, s32[1,4]{1,0:T(1,128)S(1)} %copy-done.2, bf16[1024,128]{1,0:T(8,128)(2,1)S(1)} %get-tuple-element.27.own_ref.b2, bf16[1024,128]{1,0:T(8,128)(2,1)S(1)} %collective-permute-done.4.near_ref, ...), custom_call_target="tpu_custom_call" | custom-call | flops 1073741824 | bytes 10485760 | tf_op jit(solution)/shard_map/same_spin_alpha_kernel/pallas_call | solution.py:38
  50.8 0.8 %collective-permute-done.13.refs_3_.e3 = bf16[128,576]{1,0:T(8,128)(2,1)S(1)} collective-permute-done((bf16[128,576]{1,0:T(8,128)(2,1)S(1)}, bf16[128,576]{1,0:T(8,128)(2,1)S(1)}, u32[]{:S(2)}, u32[]{:S(2)}) %collective-permute-start.13) | collective-permute-done | bytes 147488 | tf_op jit(solution)/shard_map/ppermute | solution.py:26
  52.0 4.3 %collective-permute-start.15 = (bf16[4,128,128]{2,1,0:T(8,128)(2,1)S(1)}, bf16[4,128,128]{2,1,0:T(8,128)(2,1)S(1)}, u32[]{:S(2)}, u32[]{:S(2)}) collective-permute-start(bf16[4,128,128]{2,1,0:T(8,128)(2,1)S(1)} %mixed_mate_kernel.1), channel_id=1, source_target_pairs={{0,1},{1,0},{2,3},{3,2},{4,5},{5,4},{6,7},{7,6},{8,9},{9,8},{10,11... | collective-permute-start | bytes 393224 | tf_op jit(solution)/shard_map/ppermute | solution.py:26
  56.3 1.5 %finished_own_kernel.1.begun_ref = f32[1024,128]{1,0:T(8,128)} custom-call(s32[16]{0:T(128)S(1)} %stack.61.where_ref, f32[1024,128]{1,0:T(8,128)S(1)} %same_spin_alpha_kernel.1.same_ref, bf16[128,576]{1,0:T(8,128)(2,1)S(1)} %excited_block_kernel.1.refs_0_.e0, bf16[128,576]{1,0:T(8,128)(2,1)S(1)} %collective-permute-done.11.refs_1_.e1, ...), custom_call_target="tpu_custom_call" | custom-call | flops 78643200 | bytes 2097152 | tf_op jit(solution)/shard_map/finished_own_kernel/pallas_call | solution.py:38
  57.8 1.3 %finished_mate_kernel.1 = f32[1024,128]{1,0:T(8,128)} custom-call(s32[16]{0:T(128)S(1)} %stack.61.where_ref, f32[1024,128]{1,0:T(8,128)S(1)} %same_spin_alpha_kernel.1.same_ref, bf16[4,128,128]{2,1,0:T(8,128)(2,1)S(1)} %collective-permute-done.15.theirs_ref, f32[1024,128]{1,0:T(8,128)S(1)} %copy-done, ...), custom_call_target="tpu_custom_call", output_to_operand_aliasing={{}: (4, {})} | custom-call | flops 262144 | bytes 2097152 | tf_op jit(solution)/shard_map/finished_mate_kernel/pallas_call | solution.py:38
  (30 shorter events, 2.3 us)
Async XLA Ops:
  0.0 45.9 %copy-start.2 = (s32[1,4]{1,0:T(1,128)S(1)}, s32[1,4]{1,0:T(1,128)}, u32[]{:S(2)}) copy-start(s32[1,4]{1,0:T(1,128)} %cols_ref.3) | copy-start | bytes 52
  0.0 4.8 %collective-permute-start = (bf16[1024,128]{1,0:T(8,128)(2,1)}, bf16[1024,128]{1,0:T(8,128)(2,1)S(1)}, u32[]{:S(2)}, u32[]{:S(2)}) collective-permute-start(bf16[1024,128]{1,0:T(8,128)(2,1)} %coef_ref.1), channel_id=1, source_target_pairs={{0,1},{1,0},{2,3},{3,2},{4,5},{5,4},{6,7},{7,6},{8,9},{9,8},{10,11... | collective-permute-start | bytes 786440 | tf_op jit(solution)/shard_map/ppermute | solution.py:26
  3.2 1.6 %collective-permute-start.1 = (bf16[576,128]{1,0:T(8,128)(2,1)}, bf16[576,128]{1,0:T(8,128)(2,1)S(1)}, u32[]{:S(2)}, u32[]{:S(2)}) collective-permute-start(bf16[576,128]{1,0:T(8,128)(2,1)} %bitcast.23), channel_id=1, source_target_pairs={{0,1},{1,0},{2,3},{3,2},{4,5},{5,4},{6,7},{7,6},{8,9},{9,8},{10,11... | collective-permute-start | bytes 442376 | tf_op jit(solution)/shard_map/ppermute | solution.py:26
  5.9 9.7 %collective-permute-start.2 = (bf16[2,576,128]{2,1,0:T(8,128)(2,1)S(1)}, bf16[2,576,128]{2,1,0:T(8,128)(2,1)S(1)}, u32[]{:S(2)}, u32[]{:S(2)}) collective-permute-start(bf16[2,576,128]{2,1,0:T(8,128)(2,1)S(1)} %get-tuple-element.30), channel_id=1, source_target_pairs={{0,8},{1,25},{8,0},{9,17},{16,24},{17,9},{24,16},{25,1},{2,10},{3,... | collective-permute-start | bytes 884744 | tf_op jit(solution)/shard_map/ppermute | solution.py:335
  6.9 10.7 %collective-permute-start.4 = (bf16[1024,128]{1,0:T(8,128)(2,1)S(1)}, bf16[1024,128]{1,0:T(8,128)(2,1)S(1)}, u32[]{:S(2)}, u32[]{:S(2)}) collective-permute-start(bf16[1024,128]{1,0:T(8,128)(2,1)S(1)} %get-tuple-element.27.own_ref.b2), channel_id=1, source_target_pairs={{0,32},{32,0},{1,33},{33,1},{2,34},{34,2},{3,35},{35,3},{4,36},{36... | collective-permute-start | bytes 786440 | tf_op jit(solution)/shard_map/ppermute | solution.py:26
  8.6 17.0 %collective-permute-start.5 = (bf16[1024,128]{1,0:T(8,128)(2,1)S(1)}, bf16[1024,128]{1,0:T(8,128)(2,1)}, u32[]{:S(2)}, u32[]{:S(2)}) collective-permute-start(bf16[1024,128]{1,0:T(8,128)(2,1)S(1)} %get-tuple-element.27.own_ref.b2), channel_id=1, source_target_pairs={{0,62},{62,0},{1,63},{63,1},{2,32},{32,2},{3,33},{33,3},{4,34},{34... | collective-permute-start | bytes 786440 | tf_op jit(solution)/shard_map/ppermute | solution.py:326
  13.1 0.7 %copy-start.1 = (s32[1,4]{1,0:T(1,128)S(1)}, s32[1,4]{1,0:T(1,128)}, u32[]{:S(2)}) copy-start(s32[1,4]{1,0:T(1,128)} %cols_ref.2) | copy-start | bytes 52
  15.6 10.0 %copy-start.3 = (bf16[2,576,128]{2,1,0:T(8,128)(2,1)}, bf16[2,576,128]{2,1,0:T(8,128)(2,1)S(1)}, u32[]{:S(2)}) copy-start(bf16[2,576,128]{2,1,0:T(8,128)(2,1)S(1)} %collective-permute-done.2) | copy-start | bytes 884740
  15.6 40.7 %copy-start = (f32[1024,128]{1,0:T(8,128)S(1)}, f32[1024,128]{1,0:T(8,128)}, u32[]{:S(2)}) copy-start(f32[1024,128]{1,0:T(8,128)} %den_ref.3) | copy-start | bytes 1572868
  16.3 9.3 %collective-permute-start.3 = (bf16[576,128]{1,0:T(8,128)(2,1)}, bf16[576,128]{1,0:T(8,128)(2,1)}, u32[]{:S(2)}, u32[]{:S(2)}) collective-permute-start(bf16[576,128]{1,0:T(8,128)(2,1)} %fusion), channel_id=1, source_target_pairs={{0,24},{1,9},{8,16},{9,1},{16,8},{17,25},{24,0},{25,17},{2,26},{3,... | collective-permute-start | bytes 442376 | tf_op jit(solution)/shard_map/ppermute | solution.py:341
  17.7 13.3 %collective-permute-start.8 = (bf16[1024,128]{1,0:T(8,128)(2,1)S(1)}, bf16[1024,128]{1,0:T(8,128)(2,1)S(1)}, u32[]{:S(2)}, u32[]{:S(2)}) collective-permute-start(bf16[1024,128]{1,0:T(8,128)(2,1)S(1)} %collective-permute-done.4.near_ref), channel_id=1, source_target_pairs={{0,62},{62,0},{1,63},{63,1},{2,32},{32,2},{3,33},{33,3},{4,34},{34... | collective-permute-start | bytes 786440 | tf_op jit(solution)/shard_map/ppermute | solution.py:344
  25.6 8.9 %collective-permute-start.7 = (bf16[1024,128]{1,0:T(8,128)(2,1)}, bf16[1024,128]{1,0:T(8,128)(2,1)S(1)}, u32[]{:S(2)}, u32[]{:S(2)}) collective-permute-start(bf16[1024,128]{1,0:T(8,128)(2,1)} %collective-permute-done.5), channel_id=1, source_target_pairs={{0,32},{32,0},{1,33},{33,1},{2,34},{34,2},{3,35},{35,3},{4,36},{36... | collective-permute-start | bytes 786440 | tf_op jit(solution)/shard_map/ppermute | solution.py:26
  26.6 7.9 %collective-permute-start.6 = (bf16[576,128]{1,0:T(8,128)(2,1)S(1)}, bf16[576,128]{1,0:T(8,128)(2,1)S(1)}, u32[]{:S(2)}, u32[]{:S(2)}) collective-permute-start(bf16[576,128]{1,0:T(8,128)(2,1)S(1)} %fusion.2), channel_id=1, source_target_pairs={{0,2},{1,7},{2,0},{3,5},{4,6},{5,3},{6,4},{7,1},{8,10},{9,15},{10,... | collective-permute-start | bytes 442376 | tf_op jit(solution)/shard_map/ppermute | solution.py:348
  34.6 3.2 %collective-permute-start.10 = (bf16[1024,128]{1,0:T(8,128)(2,1)S(1)}, bf16[1024,128]{1,0:T(8,128)(2,1)S(1)}, u32[]{:S(2)}, u32[]{:S(2)}) collective-permute-start(bf16[1024,128]{1,0:T(8,128)(2,1)S(1)} %broadcast_select_fusion), channel_id=1, source_target_pairs={{0,1},{1,0},{2,3},{3,2},{4,5},{5,4},{6,7},{7,6},{8,9},{9,8},{10,11... | collective-permute-start | bytes 786440 | tf_op jit(solution)/shard_map/ppermute | solution.py:26
  34.7 11.2 %collective-permute-start.14 = (bf16[1024,128]{1,0:T(8,128)(2,1)S(1)}, bf16[1024,128]{1,0:T(8,128)(2,1)S(1)}, u32[]{:S(2)}, u32[]{:S(2)}) collective-permute-start(bf16[1024,128]{1,0:T(8,128)(2,1)S(1)} %collective-permute-done.4.near_ref), channel_id=1, source_target_pairs={{0,64},{32,224},{64,128},{96,32},{128,192},{160,96},{192,0},{224,1... | collective-permute-start | bytes 786440 | tf_op jit(solution)/shard_map/ppermute | solution.py:347
  36.0 5.2 %collective-permute-start.9 = (bf16[576,128]{1,0:T(8,128)(2,1)S(1)}, bf16[576,128]{1,0:T(8,128)(2,1)S(1)}, u32[]{:S(2)}, u32[]{:S(2)}) collective-permute-start(bf16[576,128]{1,0:T(8,128)(2,1)S(1)} %add_convert_fusion.near_ref), channel_id=1, source_target_pairs={{0,6},{1,3},{2,4},{3,1},{4,2},{5,7},{6,0},{7,5},{8,14},{9,11},{10,... | collective-permute-start | bytes 442376 | tf_op jit(solution)/shard_map/ppermute | solution.py:353
  41.5 9.3 %collective-permute-start.11 = (bf16[128,576]{1,0:T(8,128)(2,1)S(1)}, bf16[128,576]{1,0:T(8,128)(2,1)S(1)}, u32[]{:S(2)}, u32[]{:S(2)}) collective-permute-start(bf16[128,576]{1,0:T(8,128)(2,1)S(1)} %excited_block_kernel.1.refs_0_.e0), channel_id=1, source_target_pairs={{0,8},{8,0},{16,24},{24,16},{1,9},{9,1},{17,25},{25,17},{2,10},{10... | collective-permute-start | bytes 442376 | tf_op jit(solution)/shard_map/ppermute | solution.py:26
  43.4 7.5 %collective-permute-start.12 = (bf16[128,576]{1,0:T(8,128)(2,1)S(1)}, bf16[128,576]{1,0:T(8,128)(2,1)S(1)}, u32[]{:S(2)}, u32[]{:S(2)}) collective-permute-start(bf16[128,576]{1,0:T(8,128)(2,1)S(1)} %excited_block_kernel.1.refs_0_.e0), channel_id=1, source_target_pairs={{0,16},{8,24},{16,0},{24,8},{1,17},{9,25},{17,1},{25,9},{2,18},{10... | collective-permute-start | bytes 442376 | tf_op jit(solution)/shard_map/ppermute | solution.py:26
  45.6 6.1 %collective-permute-start.13 = (bf16[128,576]{1,0:T(8,128)(2,1)S(1)}, bf16[128,576]{1,0:T(8,128)(2,1)S(1)}, u32[]{:S(2)}, u32[]{:S(2)}) collective-permute-start(bf16[128,576]{1,0:T(8,128)(2,1)S(1)} %excited_block_kernel.1.refs_0_.e0), channel_id=1, source_target_pairs={{0,24},{8,16},{16,8},{24,0},{1,25},{9,17},{17,9},{25,1},{2,26},{10... | collective-permute-start | bytes 442376 | tf_op jit(solution)/shard_map/ppermute | solution.py:26
  52.0 5.8 %collective-permute-start.15 = (bf16[4,128,128]{2,1,0:T(8,128)(2,1)S(1)}, bf16[4,128,128]{2,1,0:T(8,128)(2,1)S(1)}, u32[]{:S(2)}, u32[]{:S(2)}) collective-permute-start(bf16[4,128,128]{2,1,0:T(8,128)(2,1)S(1)} %mixed_mate_kernel.1), channel_id=1, source_target_pairs={{0,1},{1,0},{2,3},{3,2},{4,5},{5,4},{6,7},{7,6},{8,9},{9,8},{10,11... | collective-permute-start | bytes 393224 | tf_op jit(solution)/shard_map/ppermute | solution.py:26

commit v8 on v7

--- a/solution.py
+++ b/solution.py
@@ -24,6 +24,11 @@
 def swapped(block, axis, mask):
     count = lax.axis_size(axis)
     return lax.ppermute(block, axis, [(i, i ^ mask) for i in range(count)])
+
+
+def rotated(block, axis, distance):
+    count = lax.axis_size(axis)
+    return lax.ppermute(block, axis, [(i, (i + distance) % count) for i in range(count)])
 
 
 def crossing(count, masks):
@@ -119,8 +124,7 @@
         copies[0].wait()
         core = where_ref[8]
         for n in range(5):
-            side = 2 - where_ref[11] if n in (0, 4) else 2 * core
-            offset = jnp.where(side == 0, n, 4 - n)
+            offset = n if n in (0, 2, 4) else jnp.where(core == 0, n, 4 - n)
             tile = jnp.zeros((width, width), F32)
             for k in range(listed):
                 here = lax.rem(cols_ref[0, k] - where_ref[9] + 2 + count, count)
@@ -316,14 +320,8 @@
     coef_v, pair_v = loaded(coef, pair_t)
 
     near = swapped(coef_v, "zl", 1)
-    chips = lax.axis_size("y") * lax.axis_size("zh")
-    border = []
-    for q in range(chips):
-        for h in (0, 1):
-            low_at, high_at = (2 * q + h, 2 * chips + 2 * ((q - 1) % chips) + h)
-            border += [(low_at, high_at), (high_at, low_at)]
-    over = ("zl", *BETA)
-    across = lax.ppermute(coef_v, over, border)
+    below = rotated(coef_v, BETA, 2)
+    above = rotated(coef_v, BETA, -2)
     xs, route = lax.axis_size("x"), []
     for i in range(xs):
         route += [(2 * i, 2 * ((i + 1) % xs)), (2 * i + 1, 2 * ((i - 1) % xs) + 1)]
@@ -339,19 +337,15 @@
     passing = (passing.astype(F32) + arrived[1].astype(F32)).astype(BF16)
     total = kept.astype(F32) + arrived[0].astype(F32)
     passed = lax.ppermute(passing, ("y", "c"), crossing(4, (3, 1)))
-    passed, _, _ = lax.optimization_barrier((passed, near, across))
     total = (total + passed.astype(F32)).astype(BF16)
-    onward = lax.ppermute(near, over, border)
-    returned = swapped(across, "zl", 1)
 
     far = lax.ppermute(near, ALPHA, route)
     first = lax.ppermute(total, ("zh", "c"), crossing(4, (1, 3)))
+    crossed = swapped(jnp.where(core == 0, above, below), "c", 1)
+    first, crossed = lax.optimization_barrier((first, crossed))
     total = (total.astype(F32) + first.astype(F32)).astype(BF16)
-    passed = jnp.where(core == low, returned, onward)
-    total, passed = lax.optimization_barrier((total, passed))
-    crossed = swapped(passed, "c", 1)
     second = lax.ppermute(total, ("zh", "c"), crossing(4, (3, 1)))
-    same = same_spin_beta([onward, crossed, coef_v, mate, returned], placed)
+    same = same_spin_beta([below, crossed, coef_v, mate, above], placed)
     second, same = lax.optimization_barrier((second, same))
 
     excited = excited_block(total, second, coupling, scale)

time: 60.2 us -> 60.2 us (level); the launches traced: 59.3 us -> 60.1 us
  waiting for transfers between devices: 11.8 us -> 20.6 us
  starting transfers between devices: 31.7 us -> 25.3 us
  other arithmetic: 1.8 us -> 0.17 us
    ppermute x2, starting transfers between devices: 12.4 us -> 5.83 us  [rotated(): lax.ppermute(block, axis, [(i, (i + distance) % count) for i in range(cou...]
    ppermute x2, waiting for transfers between devices: 4.23 us -> 10.4 us  [rotated(): lax.ppermute(block, axis, [(i, (i + distance) % count) for i in range(cou...]
    ppermute x1, waiting for transfers between devices: 0.01 us -> 4.79 us  [local(): first = lax.ppermute(total, ('zh', 'c'), crossing(4, (1, 3)))]
    ppermute x9 -> x8, waiting for transfers between devices: 4.79 us -> 0.45 us  [swapped(): return lax.ppermute(block, axis, [(i, i ^ mask) for i in range(count)])]
    ppermute x1, waiting for transfers between devices: 2.82 us -> 5 us  [local(): second = lax.ppermute(total, ('zh', 'c'), crossing(4, (3, 1)))]
    ppermute x9 -> x8, starting transfers between devices: 13.6 us -> 15.5 us  [swapped(): return lax.ppermute(block, axis, [(i, i ^ mask) for i in range(count)])]
    ppermute x1, starting transfers between devices: 1.85 us -> 0.09 us  [local(): second = lax.ppermute(total, ('zh', 'c'), crossing(4, (3, 1)))]
    convert_element_type x1, other arithmetic: 1.05 us -> 0.06 us  [local(): total = (total + passed.astype(F32)).astype(BF16)]
  transfers between devices with their start and end apart: 16 -> 15, of which waited for: 5 -> 5; matrix products, arithmetic and copies ran while one was open for 3% -> 0% of each run, Pallas kernels for 17% -> 17%
where the time goes in v8:
time: 60.2 us; the launch traced here: 60.1 us
  starting transfers between devices  25.3 us (42%)
  waiting for transfers between devices  20.6 us (34%)
  Pallas kernels  12.9 us (21%)
  local copies, waits for them, and re-layouts  0.76 us (1%)
    ppermute x8, starting transfers between devices, swapped(): return lax.ppermute(block, axis, [(i, i ^ mask) for i in range(count)])  15.5 us
    pallas_call x9, Pallas kernels, call(): pl.pallas_call(kernel, out_shape=outs, in_specs=specs, out_specs=out_spec...  12.9 us
    ppermute x2, waiting for transfers between devices, rotated(): lax.ppermute(block, axis, [(i, (i + distance) % count) for i in range(cou...  10.4 us
    ppermute x2, starting transfers between devices, rotated(): lax.ppermute(block, axis, [(i, (i + distance) % count) for i in range(cou...  5.83 us
    ppermute x1, waiting for transfers between devices, local(): second = lax.ppermute(total, ('zh', 'c'), crossing(4, (3, 1)))  5 us
    ppermute x1, waiting for transfers between devices, local(): first = lax.ppermute(total, ('zh', 'c'), crossing(4, (1, 3)))  4.79 us
    ppermute x1, starting transfers between devices, local(): passed = lax.ppermute(passing, ('y', 'c'), crossing(4, (3, 1)))  1.46 us
    ppermute x1, starting transfers between devices, local(): far = lax.ppermute(near, ALPHA, route)  1.29 us
  transfers between devices with their start and end apart: 15, of which 5 were waited for; matrix products, arithmetic and copies ran while one was open for 0% of the time, Pallas kernels for 17%

profile of v8, /device:TPU:1, one launch (start us, length us, event | category | flops | bytes accessed | tf_op | source)
XLA Modules:
  0.0 60.1 jit_solution(5224557207352703011)
XLA Ops:
  0.0 3.2 %collective-permute-start = (bf16[1024,128]{1,0:T(8,128)(2,1)}, bf16[1024,128]{1,0:T(8,128)(2,1)S(1)}, u32[]{:S(2)}, u32[]{:S(2)}) collective-permute-start(bf16[1024,128]{1,0:T(8,128)(2,1)} %coef_ref.1), channel_id=1, source_target_pairs={{0,1},{1,0},{2,3},{3,2},{4,5},{5,4},{6,7},{7,6},{8,9},{9,8},{10,11... | collective-permute-start | bytes 786440 | tf_op jit(solution)/shard_map/ppermute | solution.py:26
  3.2 1.0 %loaded_kernel.1 = (bf16[1024,128]{1,0:T(8,128)(2,1)S(1)}, bf16[576,128]{1,0:T(8,128)(2,1)S(1)}) custom-call(bf16[1024,128]{1,0:T(8,128)(2,1)} %coef_ref.1, bf16[576,128]{1,0:T(8,128)(2,1)} %bitcast.24), custom_call_target="tpu_custom_call" | custom-call | bytes 1048576 | tf_op jit(solution)/shard_map/loaded_kernel/pallas_call | solution.py:43
  4.4 0.4 collective-permute-done.1.pm_ref.refs_4_
  4.8 1.0 %density_parts_kernel.1 = (bf16[2,576,128]{2,1,0:T(8,128)(2,1)S(1)}, bf16[576,128]{1,0:T(8,128)(2,1)S(1)}, bf16[576,128]{1,0:T(8,128)(2,1)S(1)}) custom-call(s32[16]{0:T(128)S(1)} %stack.61.where_ref, bf16[1024,128]{1,0:T(8,128)(2,1)S(1)} %get-tuple-element.26.own_ref.b2, bf16[1024,128]{1,0:T(8,128)(2,1)S(1)} %collective-permute-done.mate_ref.b3, ...), custom_call_target="tpu_custom_call" | custom-call | flops 150994944 | bytes 1048576 | tf_op jit(solution)/shard_map/density_parts_kernel/pallas_call | solution.py:43
  5.8 1.1 %collective-permute-start.2 = (bf16[2,576,128]{2,1,0:T(8,128)(2,1)S(1)}, bf16[2,576,128]{2,1,0:T(8,128)(2,1)S(1)}, u32[]{:S(2)}, u32[]{:S(2)}) collective-permute-start(bf16[2,576,128]{2,1,0:T(8,128)(2,1)S(1)} %get-tuple-element.29), channel_id=1, source_target_pairs={{0,8},{1,25},{8,0},{9,17},{16,24},{17,9},{24,16},{25,1},{2,10},{3,... | collective-permute-start | bytes 884744 | tf_op jit(solution)/shard_map/ppermute | solution.py:333
  6.9 5.8 %collective-permute-start.5 = (bf16[1024,128]{1,0:T(8,128)(2,1)S(1)}, bf16[1024,128]{1,0:T(8,128)(2,1)S(1)}, u32[]{:S(2)}, u32[]{:S(2)}) collective-permute-start(bf16[1024,128]{1,0:T(8,128)(2,1)S(1)} %get-tuple-element.26.own_ref.b2), channel_id=1, source_target_pairs={{0,30},{1,31},{2,0},{3,1},{4,2},{5,3},{6,4},{7,5},{8,6},{9,7},{10,... | collective-permute-start | bytes 786440 | tf_op jit(solution)/shard_map/ppermute | solution.py:31
  12.8 0.7 %collective-permute-start.12 = (bf16[1024,128]{1,0:T(8,128)(2,1)S(1)}, bf16[1024,128]{1,0:T(8,128)(2,1)S(1)}, u32[]{:S(2)}, u32[]{:S(2)}) collective-permute-start(bf16[1024,128]{1,0:T(8,128)(2,1)S(1)} %get-tuple-element.26.own_ref.b2), channel_id=1, source_target_pairs={{0,32},{32,0},{1,33},{33,1},{2,34},{34,2},{3,35},{35,3},{4,36},{36... | collective-permute-start | bytes 786440 | tf_op jit(solution)/shard_map/ppermute | solution.py:26
  13.5 0.7 %copy-done.1 = s32[1,4]{1,0:T(1,128)S(1)} copy-done((s32[1,4]{1,0:T(1,128)S(1)}, s32[1,4]{1,0:T(1,128)}, u32[]{:S(2)}) %copy-start.1) | copy-done | bytes 40
  14.2 1.8 %staged_kernel.1 = (bf16[576,576]{1,0:T(8,128)(2,1)S(1)}, f32[128,576]{1,0:T(8,128)S(1)}, bf16[128,640]{1,0:T(8,128)(2,1)S(1)}) custom-call(s32[16]{0:T(128)S(1)} %stack.61.where_ref, s32[1,4]{1,0:T(1,128)S(1)} %copy-done.1, bf16[576,576]{1,0:T(8,128)(2,1)} %c_ref.1, bf16[576,1024]{1,0:T(8,128)(2,1)} %bitcast.22, bf16[128,512]{1,0:T(8,128)(2,1)} %ops_ref.2, ...), custom_call_target="tpu_custom_call" | custom-call | flops 331776 | bytes 2097152 | tf_op jit(solution)/shard_map/staged_kernel/pallas_call | solution.py:43
  16.1 1.5 %collective-permute-start.3 = (bf16[576,128]{1,0:T(8,128)(2,1)S(1)}, bf16[576,128]{1,0:T(8,128)(2,1)S(1)}, u32[]{:S(2)}, u32[]{:S(2)}) collective-permute-start(bf16[576,128]{1,0:T(8,128)(2,1)S(1)} %fusion), channel_id=1, source_target_pairs={{0,24},{1,9},{8,16},{9,1},{16,8},{17,25},{24,0},{25,17},{2,26},{3,... | collective-permute-start | bytes 442376 | tf_op jit(solution)/shard_map/ppermute | solution.py:339
  17.5 4.3 %collective-permute-done.5.b4 = bf16[1024,128]{1,0:T(8,128)(2,1)S(1)} collective-permute-done((bf16[1024,128]{1,0:T(8,128)(2,1)S(1)}, bf16[1024,128]{1,0:T(8,128)(2,1)S(1)}, u32[]{:S(2)}, u32[]{:S(2)}) %collective-permute-start.5) | collective-permute-done | bytes 262176 | tf_op jit(solution)/shard_map/ppermute | solution.py:31
  21.8 6.1 %collective-permute-done.6.b0 = bf16[1024,128]{1,0:T(8,128)(2,1)S(1)} collective-permute-done((bf16[1024,128]{1,0:T(8,128)(2,1)S(1)}, bf16[1024,128]{1,0:T(8,128)(2,1)S(1)}, u32[]{:S(2)}, u32[]{:S(2)}) %collective-permute-start.6) | collective-permute-done | bytes 262176 | tf_op jit(solution)/shard_map/ppermute | solution.py:31
  28.0 4.1 %collective-permute-start.7 = (bf16[1024,128]{1,0:T(8,128)(2,1)S(1)}, bf16[1024,128]{1,0:T(8,128)(2,1)S(1)}, u32[]{:S(2)}, u32[]{:S(2)}) collective-permute-start(bf16[1024,128]{1,0:T(8,128)(2,1)S(1)} %broadcast_select_fusion), channel_id=1, source_target_pairs={{0,1},{1,0},{2,3},{3,2},{4,5},{5,4},{6,7},{7,6},{8,9},{9,8},{10,11... | collective-permute-start | bytes 786440 | tf_op jit(solution)/shard_map/ppermute | solution.py:26
  32.2 1.3 %collective-permute-start.13 = (bf16[1024,128]{1,0:T(8,128)(2,1)S(1)}, bf16[1024,128]{1,0:T(8,128)(2,1)S(1)}, u32[]{:S(2)}, u32[]{:S(2)}) collective-permute-start(bf16[1024,128]{1,0:T(8,128)(2,1)S(1)} %collective-permute-done.12.near_ref), channel_id=1, source_target_pairs={{0,64},{32,224},{64,128},{96,32},{128,192},{160,96},{192,0},{224,1... | collective-permute-start | bytes 786440 | tf_op jit(solution)/shard_map/ppermute | solution.py:342
  33.5 4.8 %collective-permute-done.4 = bf16[576,128]{1,0:T(8,128)(2,1)S(1)} collective-permute-done((bf16[576,128]{1,0:T(8,128)(2,1)S(1)}, bf16[576,128]{1,0:T(8,128)(2,1)S(1)}, u32[]{:S(2)}, u32[]{:S(2)}) %collective-permute-start.4) | collective-permute-done | bytes 147488 | tf_op jit(solution)/shard_map/ppermute | solution.py:343
  38.4 0.5 same_spin_beta_kernel.1.start_ref
  38.9 5.0 %collective-permute-done.8.far_ref = bf16[576,128]{1,0:T(8,128)(2,1)S(1)} collective-permute-done((bf16[576,128]{1,0:T(8,128)(2,1)S(1)}, bf16[576,128]{1,0:T(8,128)(2,1)S(1)}, u32[]{:S(2)}, u32[]{:S(2)}) %collective-permute-start.8) | collective-permute-done | bytes 147488 | tf_op jit(solution)/shard_map/ppermute | solution.py:347
  43.9 0.4 excited_block_kernel.1.refs_0_.e0
  44.4 1.0 %collective-permute-start.10 = (bf16[128,576]{1,0:T(8,128)(2,1)S(1)}, bf16[128,576]{1,0:T(8,128)(2,1)S(1)}, u32[]{:S(2)}, u32[]{:S(2)}) collective-permute-start(bf16[128,576]{1,0:T(8,128)(2,1)S(1)} %excited_block_kernel.1.refs_0_.e0), channel_id=1, source_target_pairs={{0,16},{8,24},{16,0},{24,8},{1,17},{9,25},{17,1},{25,9},{2,18},{10... | collective-permute-start | bytes 442376 | tf_op jit(solution)/shard_map/ppermute | solution.py:26
  45.4 2.8 %collective-permute-start.11 = (bf16[128,576]{1,0:T(8,128)(2,1)S(1)}, bf16[128,576]{1,0:T(8,128)(2,1)S(1)}, u32[]{:S(2)}, u32[]{:S(2)}) collective-permute-start(bf16[128,576]{1,0:T(8,128)(2,1)S(1)} %excited_block_kernel.1.refs_0_.e0), channel_id=1, source_target_pairs={{0,24},{8,16},{16,8},{24,0},{1,25},{9,17},{17,9},{25,1},{2,26},{10... | collective-permute-start | bytes 442376 | tf_op jit(solution)/shard_map/ppermute | solution.py:26
  48.3 5.0 %same_spin_alpha_kernel.1.same_ref = f32[1024,128]{1,0:T(8,128)S(1)} custom-call(s32[16]{0:T(128)S(1)} %stack.61.where_ref, s32[1,4]{1,0:T(1,128)S(1)} %copy-done.2, bf16[1024,128]{1,0:T(8,128)(2,1)S(1)} %get-tuple-element.26.own_ref.b2, bf16[1024,128]{1,0:T(8,128)(2,1)S(1)} %collective-permute-done.12.near_ref, ...), custom_call_target="tpu_custom_call" | custom-call | flops 1073741824 | bytes 10485760 | tf_op jit(solution)/shard_map/same_spin_alpha_kernel/pallas_call | solution.py:43
  53.6 3.5 %collective-permute-start.14 = (bf16[4,128,128]{2,1,0:T(8,128)(2,1)S(1)}, bf16[4,128,128]{2,1,0:T(8,128)(2,1)S(1)}, u32[]{:S(2)}, u32[]{:S(2)}) collective-permute-start(bf16[4,128,128]{2,1,0:T(8,128)(2,1)S(1)} %mixed_mate_kernel.1), channel_id=1, source_target_pairs={{0,1},{1,0},{2,3},{3,2},{4,5},{5,4},{6,7},{7,6},{8,9},{9,8},{10,11... | collective-permute-start | bytes 393224 | tf_op jit(solution)/shard_map/ppermute | solution.py:26
  57.1 1.5 %finished_own_kernel.1.begun_ref = f32[1024,128]{1,0:T(8,128)} custom-call(s32[16]{0:T(128)S(1)} %stack.61.where_ref, f32[1024,128]{1,0:T(8,128)S(1)} %same_spin_alpha_kernel.1.same_ref, bf16[128,576]{1,0:T(8,128)(2,1)S(1)} %excited_block_kernel.1.refs_0_.e0, bf16[128,576]{1,0:T(8,128)(2,1)S(1)} %collective-permute-done.9.refs_1_.e1, ...), custom_call_target="tpu_custom_call" | custom-call | flops 78643200 | bytes 2097152 | tf_op jit(solution)/shard_map/finished_own_kernel/pallas_call | solution.py:43
  58.6 1.3 %finished_mate_kernel.1 = f32[1024,128]{1,0:T(8,128)} custom-call(s32[16]{0:T(128)S(1)} %stack.61.where_ref, f32[1024,128]{1,0:T(8,128)S(1)} %same_spin_alpha_kernel.1.same_ref, bf16[4,128,128]{2,1,0:T(8,128)(2,1)S(1)} %collective-permute-done.14.theirs_ref, f32[1024,128]{1,0:T(8,128)S(1)} %copy-done, ...), custom_call_target="tpu_custom_call", output_to_operand_aliasing={{}: (4, {})} | custom-call | flops 262144 | bytes 2097152 | tf_op jit(solution)/shard_map/finished_mate_kernel/pallas_call | solution.py:43
  (26 shorter events, 0.9 us)
Async XLA Ops:
  0.0 48.3 %copy-start.2 = (s32[1,4]{1,0:T(1,128)S(1)}, s32[1,4]{1,0:T(1,128)}, u32[]{:S(2)}) copy-start(s32[1,4]{1,0:T(1,128)} %cols_ref.3) | copy-start | bytes 52
  0.0 4.8 %collective-permute-start = (bf16[1024,128]{1,0:T(8,128)(2,1)}, bf16[1024,128]{1,0:T(8,128)(2,1)S(1)}, u32[]{:S(2)}, u32[]{:S(2)}) collective-permute-start(bf16[1024,128]{1,0:T(8,128)(2,1)} %coef_ref.1), channel_id=1, source_target_pairs={{0,1},{1,0},{2,3},{3,2},{4,5},{5,4},{6,7},{7,6},{8,9},{9,8},{10,11... | collective-permute-start | bytes 786440 | tf_op jit(solution)/shard_map/ppermute | solution.py:26
  3.2 1.6 %collective-permute-start.1 = (bf16[576,128]{1,0:T(8,128)(2,1)}, bf16[576,128]{1,0:T(8,128)(2,1)S(1)}, u32[]{:S(2)}, u32[]{:S(2)}) collective-permute-start(bf16[576,128]{1,0:T(8,128)(2,1)} %bitcast.23), channel_id=1, source_target_pairs={{0,1},{1,0},{2,3},{3,2},{4,5},{5,4},{6,7},{7,6},{8,9},{9,8},{10,11... | collective-permute-start | bytes 442376 | tf_op jit(solution)/shard_map/ppermute | solution.py:26
  5.8 10.2 %collective-permute-start.2 = (bf16[2,576,128]{2,1,0:T(8,128)(2,1)S(1)}, bf16[2,576,128]{2,1,0:T(8,128)(2,1)S(1)}, u32[]{:S(2)}, u32[]{:S(2)}) collective-permute-start(bf16[2,576,128]{2,1,0:T(8,128)(2,1)S(1)} %get-tuple-element.29), channel_id=1, source_target_pairs={{0,8},{1,25},{8,0},{9,17},{16,24},{17,9},{24,16},{25,1},{2,10},{3,... | collective-permute-start | bytes 884744 | tf_op jit(solution)/shard_map/ppermute | solution.py:333
  6.9 14.9 %collective-permute-start.5 = (bf16[1024,128]{1,0:T(8,128)(2,1)S(1)}, bf16[1024,128]{1,0:T(8,128)(2,1)S(1)}, u32[]{:S(2)}, u32[]{:S(2)}) collective-permute-start(bf16[1024,128]{1,0:T(8,128)(2,1)S(1)} %get-tuple-element.26.own_ref.b2), channel_id=1, source_target_pairs={{0,30},{1,31},{2,0},{3,1},{4,2},{5,3},{6,4},{7,5},{8,6},{9,7},{10,... | collective-permute-start | bytes 786440 | tf_op jit(solution)/shard_map/ppermute | solution.py:31
  12.8 15.2 %collective-permute-start.6 = (bf16[1024,128]{1,0:T(8,128)(2,1)S(1)}, bf16[1024,128]{1,0:T(8,128)(2,1)S(1)}, u32[]{:S(2)}, u32[]{:S(2)}) collective-permute-start(bf16[1024,128]{1,0:T(8,128)(2,1)S(1)} %get-tuple-element.26.own_ref.b2), channel_id=1, source_target_pairs={{0,2},{1,3},{2,4},{3,5},{4,6},{5,7},{6,8},{7,9},{8,10},{9,11},{10,... | collective-permute-start | bytes 786440 | tf_op jit(solution)/shard_map/ppermute | solution.py:31
  12.8 19.4 %collective-permute-start.12 = (bf16[1024,128]{1,0:T(8,128)(2,1)S(1)}, bf16[1024,128]{1,0:T(8,128)(2,1)S(1)}, u32[]{:S(2)}, u32[]{:S(2)}) collective-permute-start(bf16[1024,128]{1,0:T(8,128)(2,1)S(1)} %get-tuple-element.26.own_ref.b2), channel_id=1, source_target_pairs={{0,32},{32,0},{1,33},{33,1},{2,34},{34,2},{3,35},{35,3},{4,36},{36... | collective-permute-start | bytes 786440 | tf_op jit(solution)/shard_map/ppermute | solution.py:26
  13.5 0.7 %copy-start.1 = (s32[1,4]{1,0:T(1,128)S(1)}, s32[1,4]{1,0:T(1,128)}, u32[]{:S(2)}) copy-start(s32[1,4]{1,0:T(1,128)} %cols_ref.2) | copy-start | bytes 52
  16.0 41.1 %copy-start = (f32[1024,128]{1,0:T(8,128)S(1)}, f32[1024,128]{1,0:T(8,128)}, u32[]{:S(2)}) copy-start(f32[1024,128]{1,0:T(8,128)} %den_ref.3) | copy-start | bytes 1572868
  16.1 15.9 %collective-permute-start.3 = (bf16[576,128]{1,0:T(8,128)(2,1)S(1)}, bf16[576,128]{1,0:T(8,128)(2,1)S(1)}, u32[]{:S(2)}, u32[]{:S(2)}) collective-permute-start(bf16[576,128]{1,0:T(8,128)(2,1)S(1)} %fusion), channel_id=1, source_target_pairs={{0,24},{1,9},{8,16},{9,1},{16,8},{17,25},{24,0},{25,17},{2,26},{3,... | collective-permute-start | bytes 442376 | tf_op jit(solution)/shard_map/ppermute | solution.py:339
  28.0 5.5 %collective-permute-start.7 = (bf16[1024,128]{1,0:T(8,128)(2,1)S(1)}, bf16[1024,128]{1,0:T(8,128)(2,1)S(1)}, u32[]{:S(2)}, u32[]{:S(2)}) collective-permute-start(bf16[1024,128]{1,0:T(8,128)(2,1)S(1)} %broadcast_select_fusion), channel_id=1, source_target_pairs={{0,1},{1,0},{2,3},{3,2},{4,5},{5,4},{6,7},{7,6},{8,9},{9,8},{10,11... | collective-permute-start | bytes 786440 | tf_op jit(solution)/shard_map/ppermute | solution.py:26
  32.1 6.2 %collective-permute-start.4 = (bf16[576,128]{1,0:T(8,128)(2,1)S(1)}, bf16[576,128]{1,0:T(8,128)(2,1)S(1)}, u32[]{:S(2)}, u32[]{:S(2)}) collective-permute-start(bf16[576,128]{1,0:T(8,128)(2,1)S(1)} %fusion.2), channel_id=1, source_target_pairs={{0,2},{1,7},{2,0},{3,5},{4,6},{5,3},{6,4},{7,1},{8,10},{9,15},{10,... | collective-permute-start | bytes 442376 | tf_op jit(solution)/shard_map/ppermute | solution.py:343
  32.2 16.1 %collective-permute-start.13 = (bf16[1024,128]{1,0:T(8,128)(2,1)S(1)}, bf16[1024,128]{1,0:T(8,128)(2,1)S(1)}, u32[]{:S(2)}, u32[]{:S(2)}) collective-permute-start(bf16[1024,128]{1,0:T(8,128)(2,1)S(1)} %collective-permute-done.12.near_ref), channel_id=1, source_target_pairs={{0,64},{32,224},{64,128},{96,32},{128,192},{160,96},{192,0},{224,1... | collective-permute-start | bytes 786440 | tf_op jit(solution)/shard_map/ppermute | solution.py:342
  38.3 5.6 %collective-permute-start.8 = (bf16[576,128]{1,0:T(8,128)(2,1)S(1)}, bf16[576,128]{1,0:T(8,128)(2,1)S(1)}, u32[]{:S(2)}, u32[]{:S(2)}) collective-permute-start(bf16[576,128]{1,0:T(8,128)(2,1)S(1)} %add_convert_fusion.near_ref), channel_id=1, source_target_pairs={{0,6},{1,3},{2,4},{3,1},{4,2},{5,7},{6,0},{7,5},{8,14},{9,11},{10,... | collective-permute-start | bytes 442376 | tf_op jit(solution)/shard_map/ppermute | solution.py:347
  44.3 8.9 %collective-permute-start.9 = (bf16[128,576]{1,0:T(8,128)(2,1)S(1)}, bf16[128,576]{1,0:T(8,128)(2,1)S(1)}, u32[]{:S(2)}, u32[]{:S(2)}) collective-permute-start(bf16[128,576]{1,0:T(8,128)(2,1)S(1)} %excited_block_kernel.1.refs_0_.e0), channel_id=1, source_target_pairs={{0,8},{8,0},{16,24},{24,16},{1,9},{9,1},{17,25},{25,17},{2,10},{10... | collective-permute-start | bytes 442376 | tf_op jit(solution)/shard_map/ppermute | solution.py:26
  44.4 8.8 %collective-permute-start.10 = (bf16[128,576]{1,0:T(8,128)(2,1)S(1)}, bf16[128,576]{1,0:T(8,128)(2,1)S(1)}, u32[]{:S(2)}, u32[]{:S(2)}) collective-permute-start(bf16[128,576]{1,0:T(8,128)(2,1)S(1)} %excited_block_kernel.1.refs_0_.e0), channel_id=1, source_target_pairs={{0,16},{8,24},{16,0},{24,8},{1,17},{9,25},{17,1},{25,9},{2,18},{10... | collective-permute-start | bytes 442376 | tf_op jit(solution)/shard_map/ppermute | solution.py:26
  45.4 7.8 %collective-permute-start.11 = (bf16[128,576]{1,0:T(8,128)(2,1)S(1)}, bf16[128,576]{1,0:T(8,128)(2,1)S(1)}, u32[]{:S(2)}, u32[]{:S(2)}) collective-permute-start(bf16[128,576]{1,0:T(8,128)(2,1)S(1)} %excited_block_kernel.1.refs_0_.e0), channel_id=1, source_target_pairs={{0,24},{8,16},{16,8},{24,0},{1,25},{9,17},{17,9},{25,1},{2,26},{10... | collective-permute-start | bytes 442376 | tf_op jit(solution)/shard_map/ppermute | solution.py:26
  53.6 5.0 %collective-permute-start.14 = (bf16[4,128,128]{2,1,0:T(8,128)(2,1)S(1)}, bf16[4,128,128]{2,1,0:T(8,128)(2,1)S(1)}, u32[]{:S(2)}, u32[]{:S(2)}) collective-permute-start(bf16[4,128,128]{2,1,0:T(8,128)(2,1)S(1)} %mixed_mate_kernel.1), channel_id=1, source_target_pairs={{0,1},{1,0},{2,3},{3,2},{4,5},{5,4},{6,7},{7,6},{8,9},{9,8},{10,11... | collective-permute-start | bytes 393224 | tf_op jit(solution)/shard_map/ppermute | solution.py:26

commit v9 on v4

--- a/solution.py
+++ b/solution.py
@@ -158,70 +158,45 @@
     )[0]
 
 
-def mixed_mate(blocks, pair_mate):
-    width = blocks[0].shape[0]
-    pairs = blocks[0].shape[1]
-
-    def mixed_mate_kernel(*refs):
-        right = refs[4][...]
-        for k in range(4):
-            refs[5][k] = dot(refs[k][...], right).astype(BF16)
-
-    return call(
-        mixed_mate_kernel,
-        [shape((4, width, width))],
-        (*blocks, pair_mate),
-        [VMEM] * 5,
-        (8 * pairs * width * width, 1 * MIB),
-    )[0]
-
-
-def finished_own(where, same, blocks, pair_own, denominators):
+def mixed_blocks(own, mate, pairs_of):
+    width = own.shape[0]
+
+    def mixed_blocks_kernel(own_ref, mate_ref, p0, p1, p2, p3, *outs):
+        for half, rows in enumerate((own_ref, mate_ref)):
+            for out, right in zip(outs, (p0, p1, p2, p3)):
+                out[half] = dot(rows[...], right[...]).astype(out.dtype)
+
+    return call(
+        mixed_blocks_kernel,
+        [shape((2, width, width), F32)] + [shape((2, width, width))] * 3,
+        (own, mate, *pairs_of),
+        [VMEM] * 6,
+        (16 * own.size * width, 1 * MIB),
+    )
+
+
+def finished(where, same, parts, denominators):
     rows, width = same.shape
 
-    def finished_own_kernel(where_ref, same_ref, e0, e1, e2, e3, pair_ref, den_ref, out, part, sems):
-        right = pair_ref[...]
+    def finished_kernel(where_ref, same_ref, m0, m1, m2, m3, den_ref, out, held, sems):
         copies = []
-        for k, block in enumerate((e0, e1, e2, e3)):
-            at = block_rows(where_ref, k, width)
-            part[k] = (same_ref[at, :] + dot(block[...], right)) / den_ref[at, :]
-            copies.append(pltpu.make_async_copy(part.at[k], out.at[at, :], sems.at[k]))
-            copies[-1].start()
+        for k, part in enumerate((m0, m1, m2, m3)):
+            for half in (0, 1):
+                n = 2 * k + half
+                at = block_rows(where_ref, k + 4 * half, width)
+                held[n] = (same_ref[at, :] + part[half].astype(F32)) / den_ref[at, :]
+                copies.append(pltpu.make_async_copy(held.at[n], out.at[at, :], sems.at[n]))
+                copies[-1].start()
         for copy in copies:
             copy.wait()
 
     return call(
-        finished_own_kernel,
+        finished_kernel,
         [shape((rows, width), F32)],
-        (where, same, *blocks, pair_own, denominators),
-        [SMEM] + [VMEM] * 7,
-        (rows * width * 600, 2 * MIB),
-        [pltpu.VMEM((4, width, width), F32), pltpu.SemaphoreType.DMA((4,))],
-        out_specs=[HBM],
-    )[0]
-
-
-def finished_mate(where, same, theirs, denominators, begun):
-    rows, width = same.shape
-
-    def finished_mate_kernel(where_ref, same_ref, theirs_ref, den_ref, begun_ref, out, part, sems):
-        copies = []
-        for k in range(4):
-            at = block_rows(where_ref, 4 + k, width)
-            part[k] = (same_ref[at, :] + theirs_ref[k].astype(F32)) / den_ref[at, :]
-            copies.append(pltpu.make_async_copy(part.at[k], out.at[at, :], sems.at[k]))
-            copies[-1].start()
-        for copy in copies:
-            copy.wait()
-
-    return call(
-        finished_mate_kernel,
-        [shape((rows, width), F32)],
-        (where, same, theirs, denominators, begun),
-        [SMEM] + [VMEM] * 3 + [ANY],
+        (where, same, *parts, denominators),
+        [SMEM] + [VMEM] * 6,
         (rows * width * 2, 2 * MIB),
-        [pltpu.VMEM((4, width, width), F32), pltpu.SemaphoreType.DMA((4,))],
-        aliases={4: 0},
+        [pltpu.VMEM((8, width, width), F32), pltpu.SemaphoreType.DMA((8,))],
         out_specs=[HBM],
     )[0]
 
@@ -320,10 +295,8 @@
         where, beta_cols, pair_coupling, pair_alpha.T, beta_ops, parts[0]
     )
     got = [swapped(parts[k], "y", k) for k in (1, 3, 2)]
-    got_first = got[0]
     *got, below, above = lax.optimization_barrier((*got, below, above))
-    start, _ = lax.optimization_barrier((coef_v, got_first))
-    near = swapped(start, "zl", 1)
+    near = swapped(coef_v, "zl", 1)
     total = parts[0].astype(F32)
     for part in got:
         total = total + part.astype(F32)
@@ -334,22 +307,23 @@
     zs = lax.axis_size("zh")
     steps = [[(2 * i + h, 2 * (i ^ m[h]) + h) for i in range(zs) for h in (0, 1)] for m in ((1, 3), (3, 1))]
     first = lax.ppermute(total, ("zh", "c"), steps[0])
+    sent, _ = lax.optimization_barrier((pair_v, total))
+    pairs = [pair_v] + [swapped(sent, "y", k) for k in (1, 2, 3)]
+    crossed = swapped(jnp.where(core == 0, above, below), "c", 1)
     total = (total.astype(F32) + first.astype(F32)).astype(BF16)
-    passed = jnp.where(core == 0, above, below)
-    total, passed = lax.optimization_barrier((total, passed))
-    crossed = swapped(passed, "c", 1)
+    total, crossed, pairs[1], pairs[3] = lax.optimization_barrier(
+        (total, crossed, pairs[1], pairs[3])
+    )
     second = lax.ppermute(total, ("zh", "c"), steps[1])
     same = same_spin_beta([below, crossed, coef_v, mate, above], placed)
-    second, same = lax.optimization_barrier((second, same))
+    second, same, pairs[2] = lax.optimization_barrier((second, same, pairs[2]))
 
     excited = excited_block(total, second, coupling, scale)
-    blocks = [excited] + [swapped(excited, "y", k) for k in (1, 2, 3)]
+    mine, *out = mixed_blocks(excited, swapped(excited, "c", 1), pairs)
+    back = [swapped(block, "y", k) for k, block in zip((1, 2, 3), out)]
     same = same_spin_alpha(where, alpha_cols, [coef_v, near, far], alpha_ops, same)
-    *blocks, same = lax.optimization_barrier((*blocks, same))
-
-    theirs = mixed_mate(blocks, pair_mate)
-    begun = finished_own(where, same, blocks, pair_v, denominators)
-    return finished_mate(where, same, swapped(theirs, "c", 1), denominators, begun)
+    *back, same = lax.optimization_barrier((*back, same))
+    return finished(where, same, [mine, *back], denominators)
 
 
 def solution(mesh):

time: 62.7 us -> 58.6 us (0.935)
  waiting for transfers between devices: 23.1 us -> 13.7 us
  starting transfers between devices: 25.5 us -> 31.4 us
  Pallas kernels: 12.9 us -> 11.6 us
    ppermute x1, waiting for transfers between devices: 4.95 us -> 1.03 us  [local(): first = lax.ppermute(total, ('zh', 'c'), steps[0])]
    ppermute x11 -> x14, starting transfers between devices: 17 us -> 20.3 us  [swapped(): return lax.ppermute(block, axis, [(i, i ^ mask) for i in range(count)])]
    ppermute x1, waiting for transfers between devices: 5.54 us -> 2.48 us  [local(): second = lax.ppermute(total, ('zh', 'c'), steps[1])]
    ppermute x1, starting transfers between devices: 0.01 us -> 2.63 us  [local(): second = lax.ppermute(total, ('zh', 'c'), steps[1])]
    ppermute x11 -> x14, waiting for transfers between devices: 8.93 us -> 6.57 us  [swapped(): return lax.ppermute(block, axis, [(i, i ^ mask) for i in range(count)])]
    pallas_call x9 -> x8, Pallas kernels: 12.9 us -> 11.6 us  [call(): pl.pallas_call(kernel, out_shape=outs, in_specs=specs, out_specs=out_spec...]
  transfers between devices with their start and end apart: 16 -> 19, of which waited for: 8 -> 7; matrix products, arithmetic and copies ran while one was open for 0% -> 0% of each run, Pallas kernels for 18% -> 18%
where the time goes in v9:
time: 58.6 us; the launch traced here: 57.9 us
  starting transfers between devices  31.4 us (54%)
  waiting for transfers between devices  13.7 us (23%)
  Pallas kernels  11.6 us (20%)
  local copies, waits for them, and re-layouts  0.75 us (1%)
    ppermute x14, starting transfers between devices, swapped(): return lax.ppermute(block, axis, [(i, i ^ mask) for i in range(count)])  20.3 us
    pallas_call x8, Pallas kernels, call(): pl.pallas_call(kernel, out_shape=outs, in_specs=specs, out_specs=out_spec...  11.6 us
    ppermute x2, starting transfers between devices, rotated(): lax.ppermute(block, axis, [(i, (i + distance) % count) for i in range(cou...  6.98 us
    ppermute x14, waiting for transfers between devices, swapped(): return lax.ppermute(block, axis, [(i, i ^ mask) for i in range(count)])  6.57 us
    ppermute x2, waiting for transfers between devices, rotated(): lax.ppermute(block, axis, [(i, (i + distance) % count) for i in range(cou...  3.64 us
    ppermute x1, starting transfers between devices, local(): second = lax.ppermute(total, ('zh', 'c'), steps[1])  2.63 us
    ppermute x1, waiting for transfers between devices, local(): second = lax.ppermute(total, ('zh', 'c'), steps[1])  2.48 us
    ppermute x1, starting transfers between devices, local(): far = lax.ppermute(near, ALPHA, route)  1.21 us
  transfers between devices with their start and end apart: 19, of which 7 were waited for; matrix products, arithmetic and copies ran while one was open for 0% of the time, Pallas kernels for 18%

profile of v9, /device:TPU:1, one launch (start us, length us, event | category | flops | bytes accessed | tf_op | source)
XLA Modules:
  0.0 57.9 jit_solution(435606482600209770)
XLA Ops:
  0.0 3.2 %collective-permute-start = (bf16[1024,128]{1,0:T(8,128)(2,1)}, bf16[1024,128]{1,0:T(8,128)(2,1)S(1)}, u32[]{:S(2)}, u32[]{:S(2)}) collective-permute-start(bf16[1024,128]{1,0:T(8,128)(2,1)} %coef_ref.1), channel_id=1, source_target_pairs={{0,1},{1,0},{2,3},{3,2},{4,5},{5,4},{6,7},{7,6},{8,9},{9,8},{10,11... | collective-permute-start | bytes 786440 | tf_op jit(solution)/shard_map/ppermute | solution.py:26
  3.2 1.0 %loaded_kernel.1 = (bf16[1024,128]{1,0:T(8,128)(2,1)S(1)}, bf16[576,128]{1,0:T(8,128)(2,1)S(1)}) custom-call(bf16[1024,128]{1,0:T(8,128)(2,1)} %coef_ref.1, bf16[576,128]{1,0:T(8,128)(2,1)} %bitcast.16), custom_call_target="tpu_custom_call" | custom-call | bytes 1048576 | tf_op jit(solution)/shard_map/loaded_kernel/pallas_call | solution.py:39
  4.3 1.4 %collective-permute-start.5 = (bf16[1024,128]{1,0:T(8,128)(2,1)S(1)}, bf16[1024,128]{1,0:T(8,128)(2,1)S(1)}, u32[]{:S(2)}, u32[]{:S(2)}) collective-permute-start(bf16[1024,128]{1,0:T(8,128)(2,1)S(1)} %get-tuple-element.39.own_ref.b2), channel_id=1, source_target_pairs={{0,2},{1,3},{2,4},{3,5},{4,6},{5,7},{6,8},{7,9},{8,10},{9,11},{10,... | collective-permute-start | bytes 786440 | tf_op jit(solution)/shard_map/ppermute | solution.py:31
  5.7 5.6 %collective-permute-start.6 = (bf16[1024,128]{1,0:T(8,128)(2,1)S(1)}, bf16[1024,128]{1,0:T(8,128)(2,1)S(1)}, u32[]{:S(2)}, u32[]{:S(2)}) collective-permute-start(bf16[1024,128]{1,0:T(8,128)(2,1)S(1)} %get-tuple-element.39.own_ref.b2), channel_id=1, source_target_pairs={{0,30},{1,31},{2,0},{3,1},{4,2},{5,3},{6,4},{7,5},{8,6},{9,7},{10,... | collective-permute-start | bytes 786440 | tf_op jit(solution)/shard_map/ppermute | solution.py:31
  11.4 1.0 %density_parts_kernel.1 = (bf16[576,128]{1,0:T(8,128)(2,1)S(1)}, bf16[576,128]{1,0:T(8,128)(2,1)S(1)}, bf16[576,128]{1,0:T(8,128)(2,1)S(1)}, bf16[576,128]{1,0:T(8,128)(2,1)S(1)}) custom-call(s32[12]{0:T(128)S(1)} %stack.51.where_ref, bf16[1024,128]{1,0:T(8,128)(2,1)S(1)} %get-tuple-element.39.own_ref.b2, ...), custom_call_target="tpu_custom_call" | custom-call | flops 150994944 | bytes 1048576 | tf_op jit(solution)/shard_map/density_parts_kernel/pallas_call | solution.py:39
  13.1 2.6 %collective-permute-start.4 = (bf16[576,128]{1,0:T(8,128)(2,1)S(1)}, bf16[576,128]{1,0:T(8,128)(2,1)S(1)}, u32[]{:S(2)}, u32[]{:S(2)}) collective-permute-start(bf16[576,128]{1,0:T(8,128)(2,1)S(1)} %get-tuple-element.44), channel_id=1, source_target_pairs={{0,16},{8,24},{16,0},{24,8},{1,17},{9,25},{17,1},{25,9},{2,18},{10... | collective-permute-start | bytes 442376 | tf_op jit(solution)/shard_map/ppermute | solution.py:26
  16.4 1.8 %staged_kernel.1 = (bf16[576,576]{1,0:T(8,128)(2,1)S(1)}, f32[128,576]{1,0:T(8,128)S(1)}, bf16[128,640]{1,0:T(8,128)(2,1)S(1)}) custom-call(s32[12]{0:T(128)S(1)} %stack.51.where_ref, s32[1,4]{1,0:T(1,128)S(1)} %copy-done.1, bf16[576,576]{1,0:T(8,128)(2,1)} %c_ref.1, bf16[576,1024]{1,0:T(8,128)(2,1)} %bitcast.14, bf16[128,512]{1,0:T(8,128)(2,1)} %ops_ref.2, ...), custom_call_target="tpu_custom_call" | custom-call | flops 331776 | bytes 2097152 | tf_op jit(solution)/shard_map/staged_kernel/pallas_call | solution.py:39
  19.0 2.8 %collective-permute-done.6.b4 = bf16[1024,128]{1,0:T(8,128)(2,1)S(1)} collective-permute-done((bf16[1024,128]{1,0:T(8,128)(2,1)S(1)}, bf16[1024,128]{1,0:T(8,128)(2,1)S(1)}, u32[]{:S(2)}, u32[]{:S(2)}) %collective-permute-start.6) | collective-permute-done | bytes 262176 | tf_op jit(solution)/shard_map/ppermute | solution.py:31
  21.9 3.1 %collective-permute-done.4 = bf16[576,128]{1,0:T(8,128)(2,1)S(1)} collective-permute-done((bf16[576,128]{1,0:T(8,128)(2,1)S(1)}, bf16[576,128]{1,0:T(8,128)(2,1)S(1)}, u32[]{:S(2)}, u32[]{:S(2)}) %collective-permute-start.4) | collective-permute-done | bytes 147488 | tf_op jit(solution)/shard_map/ppermute | solution.py:26
  25.4 1.4 %collective-permute-start.8 = (bf16[1024,128]{1,0:T(8,128)(2,1)S(1)}, bf16[1024,128]{1,0:T(8,128)(2,1)S(1)}, u32[]{:S(2)}, u32[]{:S(2)}) collective-permute-start(bf16[1024,128]{1,0:T(8,128)(2,1)S(1)} %broadcast_select_fusion), channel_id=1, source_target_pairs={{0,1},{1,0},{2,3},{3,2},{4,5},{5,4},{6,7},{7,6},{8,9},{9,8},{10,11... | collective-permute-start | bytes 786440 | tf_op jit(solution)/shard_map/ppermute | solution.py:26
  26.8 2.1 %collective-permute-start.17 = (bf16[1024,128]{1,0:T(8,128)(2,1)S(1)}, bf16[1024,128]{1,0:T(8,128)(2,1)S(1)}, u32[]{:S(2)}, u32[]{:S(2)}) collective-permute-start(bf16[1024,128]{1,0:T(8,128)(2,1)S(1)} %get-tuple-element.39.own_ref.b2), channel_id=1, source_target_pairs={{0,32},{32,0},{1,33},{33,1},{2,34},{34,2},{3,35},{35,3},{4,36},{36... | collective-permute-start | bytes 786440 | tf_op jit(solution)/shard_map/ppermute | solution.py:26
  28.8 1.4 %collective-permute-start.10 = (bf16[576,128]{1,0:T(8,128)(2,1)S(1)}, bf16[576,128]{1,0:T(8,128)(2,1)S(1)}, u32[]{:S(2)}, u32[]{:S(2)}) collective-permute-start(bf16[576,128]{1,0:T(8,128)(2,1)S(1)} %get-tuple-element.54.po_ref.p0), channel_id=1, source_target_pairs={{0,24},{8,16},{16,8},{24,0},{1,25},{9,17},{17,9},{25,1},{2,26},{10... | collective-permute-start | bytes 442376 | tf_op jit(solution)/shard_map/ppermute | solution.py:26
  30.3 1.0 %collective-permute-done.7 = bf16[576,128]{1,0:T(8,128)(2,1)S(1)} collective-permute-done((bf16[576,128]{1,0:T(8,128)(2,1)S(1)}, bf16[576,128]{1,0:T(8,128)(2,1)S(1)}, u32[]{:S(2)}, u32[]{:S(2)}) %collective-permute-start.7) | collective-permute-done | bytes 147488 | tf_op jit(solution)/shard_map/ppermute | solution.py:309
  31.3 1.4 %collective-permute-start.12 = (bf16[576,128]{1,0:T(8,128)(2,1)S(1)}, bf16[576,128]{1,0:T(8,128)(2,1)S(1)}, u32[]{:S(2)}, u32[]{:S(2)}) collective-permute-start(bf16[576,128]{1,0:T(8,128)(2,1)S(1)} %get-tuple-element.54.po_ref.p0), channel_id=1, source_target_pairs={{0,16},{8,24},{16,0},{24,8},{1,17},{9,25},{17,1},{25,9},{2,18},{10... | collective-permute-start | bytes 442376 | tf_op jit(solution)/shard_map/ppermute | solution.py:26
  32.8 2.4 %collective-permute-done.10.p3 = bf16[576,128]{1,0:T(8,128)(2,1)S(1)} collective-permute-done((bf16[576,128]{1,0:T(8,128)(2,1)S(1)}, bf16[576,128]{1,0:T(8,128)(2,1)S(1)}, u32[]{:S(2)}, u32[]{:S(2)}) %collective-permute-start.10) | collective-permute-done | bytes 147488 | tf_op jit(solution)/shard_map/ppermute | solution.py:26
  35.1 2.6 %collective-permute-start.11 = (bf16[576,128]{1,0:T(8,128)(2,1)S(1)}, bf16[576,128]{1,0:T(8,128)(2,1)S(1)}, u32[]{:S(2)}, u32[]{:S(2)}) collective-permute-start(bf16[576,128]{1,0:T(8,128)(2,1)S(1)} %add_convert_fusion.near_ref), channel_id=1, source_target_pairs={{0,6},{1,3},{2,4},{3,1},{4,2},{5,7},{6,0},{7,5},{8,14},{9,11},{10,... | collective-permute-start | bytes 442376 | tf_op jit(solution)/shard_map/ppermute | solution.py:317
  37.8 1.2 %collective-permute-start.18 = (bf16[1024,128]{1,0:T(8,128)(2,1)S(1)}, bf16[1024,128]{1,0:T(8,128)(2,1)S(1)}, u32[]{:S(2)}, u32[]{:S(2)}) collective-permute-start(bf16[1024,128]{1,0:T(8,128)(2,1)S(1)} %collective-permute-done.17.near_ref), channel_id=1, source_target_pairs={{0,64},{32,224},{64,128},{96,32},{128,192},{160,96},{192,0},{224,1... | collective-permute-start | bytes 786440 | tf_op jit(solution)/shard_map/ppermute | solution.py:306
  39.5 2.5 %collective-permute-done.11.far_ref = bf16[576,128]{1,0:T(8,128)(2,1)S(1)} collective-permute-done((bf16[576,128]{1,0:T(8,128)(2,1)S(1)}, bf16[576,128]{1,0:T(8,128)(2,1)S(1)}, u32[]{:S(2)}, u32[]{:S(2)}) %collective-permute-start.11) | collective-permute-done | bytes 147488 | tf_op jit(solution)/shard_map/ppermute | solution.py:317
  42.3 3.5 %collective-permute-start.13 = (bf16[128,576]{1,0:T(8,128)(2,1)S(1)}, bf16[128,576]{1,0:T(8,128)(2,1)S(1)}, u32[]{:S(2)}, u32[]{:S(2)}) collective-permute-start(bf16[128,576]{1,0:T(8,128)(2,1)S(1)} %excited_block_kernel.1.own_ref), channel_id=1, source_target_pairs={{0,1},{1,0},{2,3},{3,2},{4,5},{5,4},{6,7},{7,6},{8,9},{9,8},{10,11... | collective-permute-start | bytes 442376 | tf_op jit(solution)/shard_map/ppermute | solution.py:26
  45.8 1.0 %collective-permute-done.13.mate_ref = bf16[128,576]{1,0:T(8,128)(2,1)S(1)} collective-permute-done((bf16[128,576]{1,0:T(8,128)(2,1)S(1)}, bf16[128,576]{1,0:T(8,128)(2,1)S(1)}, u32[]{:S(2)}, u32[]{:S(2)}) %collective-permute-start.13) | collective-permute-done | bytes 147488 | tf_op jit(solution)/shard_map/ppermute | solution.py:26
  47.5 2.6 %collective-permute-start.15 = (bf16[2,128,128]{2,1,0:T(8,128)(2,1)S(1)}, bf16[2,128,128]{2,1,0:T(8,128)(2,1)S(1)}, u32[]{:S(2)}, u32[]{:S(2)}) collective-permute-start(bf16[2,128,128]{2,1,0:T(8,128)(2,1)S(1)} %get-tuple-element.65), channel_id=1, source_target_pairs={{0,16},{8,24},{16,0},{24,8},{1,17},{9,25},{17,1},{25,9},{2,18},{10... | collective-permute-start | bytes 196616 | tf_op jit(solution)/shard_map/ppermute | solution.py:26
  50.1 1.2 %collective-permute-start.16 = (bf16[2,128,128]{2,1,0:T(8,128)(2,1)S(1)}, bf16[2,128,128]{2,1,0:T(8,128)(2,1)S(1)}, u32[]{:S(2)}, u32[]{:S(2)}) collective-permute-start(bf16[2,128,128]{2,1,0:T(8,128)(2,1)S(1)} %get-tuple-element.66), channel_id=1, source_target_pairs={{0,24},{8,16},{16,8},{24,0},{1,25},{9,17},{17,9},{25,1},{2,26},{10... | collective-permute-start | bytes 196616 | tf_op jit(solution)/shard_map/ppermute | solution.py:26
  51.3 5.0 %same_spin_alpha_kernel.1.same_ref = f32[1024,128]{1,0:T(8,128)S(1)} custom-call(s32[12]{0:T(128)S(1)} %stack.51.where_ref, s32[1,4]{1,0:T(1,128)S(1)} %copy-done.2, bf16[1024,128]{1,0:T(8,128)(2,1)S(1)} %get-tuple-element.39.own_ref.b2, bf16[1024,128]{1,0:T(8,128)(2,1)S(1)} %collective-permute-done.17.near_ref, ...), custom_call_target="tpu_custom_call" | custom-call | flops 1073741824 | bytes 10485760 | tf_op jit(solution)/shard_map/same_spin_alpha_kernel/pallas_call | solution.py:39
  56.3 1.4 %finished_kernel.1 = f32[1024,128]{1,0:T(8,128)} custom-call(s32[12]{0:T(128)S(1)} %stack.51.where_ref, f32[1024,128]{1,0:T(8,128)S(1)} %same_spin_alpha_kernel.1.same_ref, f32[2,128,128]{2,1,0:T(8,128)S(1)} %get-tuple-element.69.m0, bf16[2,128,128]{2,1,0:T(8,128)(2,1)S(1)} %collective-permute-done.14.m1, ...), custom_call_target="tpu_custom_call" | custom-call | flops 262144 | bytes 2097152 | tf_op jit(solution)/shard_map/finished_kernel/pallas_call | solution.py:39
  (32 shorter events, 4.2 us)
Async XLA Ops:
  0.0 51.3 %copy-start.2 = (s32[1,4]{1,0:T(1,128)S(1)}, s32[1,4]{1,0:T(1,128)}, u32[]{:S(2)}) copy-start(s32[1,4]{1,0:T(1,128)} %cols_ref.3) | copy-start | bytes 52
  0.0 11.3 %collective-permute-start = (bf16[1024,128]{1,0:T(8,128)(2,1)}, bf16[1024,128]{1,0:T(8,128)(2,1)S(1)}, u32[]{:S(2)}, u32[]{:S(2)}) collective-permute-start(bf16[1024,128]{1,0:T(8,128)(2,1)} %coef_ref.1), channel_id=1, source_target_pairs={{0,1},{1,0},{2,3},{3,2},{4,5},{5,4},{6,7},{7,6},{8,9},{9,8},{10,11... | collective-permute-start | bytes 786440 | tf_op jit(solution)/shard_map/ppermute | solution.py:26
  3.2 8.1 %collective-permute-start.1 = (bf16[576,128]{1,0:T(8,128)(2,1)}, bf16[576,128]{1,0:T(8,128)(2,1)S(1)}, u32[]{:S(2)}, u32[]{:S(2)}) collective-permute-start(bf16[576,128]{1,0:T(8,128)(2,1)} %bitcast.15), channel_id=1, source_target_pairs={{0,1},{1,0},{2,3},{3,2},{4,5},{5,4},{6,7},{7,6},{8,9},{9,8},{10,11... | collective-permute-start | bytes 442376 | tf_op jit(solution)/shard_map/ppermute | solution.py:26
  4.3 14.8 %collective-permute-start.5 = (bf16[1024,128]{1,0:T(8,128)(2,1)S(1)}, bf16[1024,128]{1,0:T(8,128)(2,1)S(1)}, u32[]{:S(2)}, u32[]{:S(2)}) collective-permute-start(bf16[1024,128]{1,0:T(8,128)(2,1)S(1)} %get-tuple-element.39.own_ref.b2), channel_id=1, source_target_pairs={{0,2},{1,3},{2,4},{3,5},{4,6},{5,7},{6,8},{7,9},{8,10},{9,11},{10,... | collective-permute-start | bytes 786440 | tf_op jit(solution)/shard_map/ppermute | solution.py:31
  5.7 16.2 %collective-permute-start.6 = (bf16[1024,128]{1,0:T(8,128)(2,1)S(1)}, bf16[1024,128]{1,0:T(8,128)(2,1)S(1)}, u32[]{:S(2)}, u32[]{:S(2)}) collective-permute-start(bf16[1024,128]{1,0:T(8,128)(2,1)S(1)} %get-tuple-element.39.own_ref.b2), channel_id=1, source_target_pairs={{0,30},{1,31},{2,0},{3,1},{4,2},{5,3},{6,4},{7,5},{8,6},{9,7},{10,... | collective-permute-start | bytes 786440 | tf_op jit(solution)/shard_map/ppermute | solution.py:31
  12.4 9.5 %collective-permute-start.2 = (bf16[576,128]{1,0:T(8,128)(2,1)S(1)}, bf16[576,128]{1,0:T(8,128)(2,1)S(1)}, u32[]{:S(2)}, u32[]{:S(2)}) collective-permute-start(bf16[576,128]{1,0:T(8,128)(2,1)S(1)} %get-tuple-element.42), channel_id=1, source_target_pairs={{0,8},{8,0},{16,24},{24,16},{1,9},{9,1},{17,25},{25,17},{2,10},{10... | collective-permute-start | bytes 442376 | tf_op jit(solution)/shard_map/ppermute | solution.py:26
  12.5 9.4 %collective-permute-start.3 = (bf16[576,128]{1,0:T(8,128)(2,1)S(1)}, bf16[576,128]{1,0:T(8,128)(2,1)S(1)}, u32[]{:S(2)}, u32[]{:S(2)}) collective-permute-start(bf16[576,128]{1,0:T(8,128)(2,1)S(1)} %get-tuple-element.43), channel_id=1, source_target_pairs={{0,24},{8,16},{16,8},{24,0},{1,25},{9,17},{17,9},{25,1},{2,26},{10... | collective-permute-start | bytes 442376 | tf_op jit(solution)/shard_map/ppermute | solution.py:26
  13.1 11.9 %collective-permute-start.4 = (bf16[576,128]{1,0:T(8,128)(2,1)S(1)}, bf16[576,128]{1,0:T(8,128)(2,1)S(1)}, u32[]{:S(2)}, u32[]{:S(2)}) collective-permute-start(bf16[576,128]{1,0:T(8,128)(2,1)S(1)} %get-tuple-element.44), channel_id=1, source_target_pairs={{0,16},{8,24},{16,0},{24,8},{1,17},{9,25},{17,1},{25,9},{2,18},{10... | collective-permute-start | bytes 442376 | tf_op jit(solution)/shard_map/ppermute | solution.py:26
  15.7 0.7 %copy-start.1 = (s32[1,4]{1,0:T(1,128)S(1)}, s32[1,4]{1,0:T(1,128)}, u32[]{:S(2)}) copy-start(s32[1,4]{1,0:T(1,128)} %cols_ref.2) | copy-start | bytes 52
  18.2 38.1 %copy-start = (f32[1024,128]{1,0:T(8,128)S(1)}, f32[1024,128]{1,0:T(8,128)}, u32[]{:S(2)}) copy-start(f32[1024,128]{1,0:T(8,128)} %den_ref.1) | copy-start | bytes 1572868
  25.1 6.2 %collective-permute-start.7 = (bf16[576,128]{1,0:T(8,128)(2,1)S(1)}, bf16[576,128]{1,0:T(8,128)(2,1)S(1)}, u32[]{:S(2)}, u32[]{:S(2)}) collective-permute-start(bf16[576,128]{1,0:T(8,128)(2,1)S(1)} %add_convert_fusion.1), channel_id=1, source_target_pairs={{0,2},{1,7},{2,0},{3,5},{4,6},{5,3},{6,4},{7,1},{8,10},{9,15},{10,... | collective-permute-start | bytes 442376 | tf_op jit(solution)/shard_map/ppermute | solution.py:309
  25.4 9.7 %collective-permute-start.8 = (bf16[1024,128]{1,0:T(8,128)(2,1)S(1)}, bf16[1024,128]{1,0:T(8,128)(2,1)S(1)}, u32[]{:S(2)}, u32[]{:S(2)}) collective-permute-start(bf16[1024,128]{1,0:T(8,128)(2,1)S(1)} %broadcast_select_fusion), channel_id=1, source_target_pairs={{0,1},{1,0},{2,3},{3,2},{4,5},{5,4},{6,7},{7,6},{8,9},{9,8},{10,11... | collective-permute-start | bytes 786440 | tf_op jit(solution)/shard_map/ppermute | solution.py:26
  26.8 11.0 %collective-permute-start.17 = (bf16[1024,128]{1,0:T(8,128)(2,1)S(1)}, bf16[1024,128]{1,0:T(8,128)(2,1)S(1)}, u32[]{:S(2)}, u32[]{:S(2)}) collective-permute-start(bf16[1024,128]{1,0:T(8,128)(2,1)S(1)} %get-tuple-element.39.own_ref.b2), channel_id=1, source_target_pairs={{0,32},{32,0},{1,33},{33,1},{2,34},{34,2},{3,35},{35,3},{4,36},{36... | collective-permute-start | bytes 786440 | tf_op jit(solution)/shard_map/ppermute | solution.py:26
  28.8 6.3 %collective-permute-start.10 = (bf16[576,128]{1,0:T(8,128)(2,1)S(1)}, bf16[576,128]{1,0:T(8,128)(2,1)S(1)}, u32[]{:S(2)}, u32[]{:S(2)}) collective-permute-start(bf16[576,128]{1,0:T(8,128)(2,1)S(1)} %get-tuple-element.54.po_ref.p0), channel_id=1, source_target_pairs={{0,24},{8,16},{16,8},{24,0},{1,25},{9,17},{17,9},{25,1},{2,26},{10... | collective-permute-start | bytes 442376 | tf_op jit(solution)/shard_map/ppermute | solution.py:26
  30.3 4.8 %collective-permute-start.9 = (bf16[576,128]{1,0:T(8,128)(2,1)S(1)}, bf16[576,128]{1,0:T(8,128)(2,1)S(1)}, u32[]{:S(2)}, u32[]{:S(2)}) collective-permute-start(bf16[576,128]{1,0:T(8,128)(2,1)S(1)} %get-tuple-element.54.po_ref.p0), channel_id=1, source_target_pairs={{0,8},{8,0},{16,24},{24,16},{1,9},{9,1},{17,25},{25,17},{2,10},{10... | collective-permute-start | bytes 442376 | tf_op jit(solution)/shard_map/ppermute | solution.py:26
  31.3 8.2 %collective-permute-start.12 = (bf16[576,128]{1,0:T(8,128)(2,1)S(1)}, bf16[576,128]{1,0:T(8,128)(2,1)S(1)}, u32[]{:S(2)}, u32[]{:S(2)}) collective-permute-start(bf16[576,128]{1,0:T(8,128)(2,1)S(1)} %get-tuple-element.54.po_ref.p0), channel_id=1, source_target_pairs={{0,16},{8,24},{16,0},{24,8},{1,17},{9,25},{17,1},{25,9},{2,18},{10... | collective-permute-start | bytes 442376 | tf_op jit(solution)/shard_map/ppermute | solution.py:26
  35.1 6.8 %collective-permute-start.11 = (bf16[576,128]{1,0:T(8,128)(2,1)S(1)}, bf16[576,128]{1,0:T(8,128)(2,1)S(1)}, u32[]{:S(2)}, u32[]{:S(2)}) collective-permute-start(bf16[576,128]{1,0:T(8,128)(2,1)S(1)} %add_convert_fusion.near_ref), channel_id=1, source_target_pairs={{0,6},{1,3},{2,4},{3,1},{4,2},{5,7},{6,0},{7,5},{8,14},{9,11},{10,... | collective-permute-start | bytes 442376 | tf_op jit(solution)/shard_map/ppermute | solution.py:317
  37.8 13.6 %collective-permute-start.18 = (bf16[1024,128]{1,0:T(8,128)(2,1)S(1)}, bf16[1024,128]{1,0:T(8,128)(2,1)S(1)}, u32[]{:S(2)}, u32[]{:S(2)}) collective-permute-start(bf16[1024,128]{1,0:T(8,128)(2,1)S(1)} %collective-permute-done.17.near_ref), channel_id=1, source_target_pairs={{0,64},{32,224},{64,128},{96,32},{128,192},{160,96},{192,0},{224,1... | collective-permute-start | bytes 786440 | tf_op jit(solution)/shard_map/ppermute | solution.py:306
  42.3 4.5 %collective-permute-start.13 = (bf16[128,576]{1,0:T(8,128)(2,1)S(1)}, bf16[128,576]{1,0:T(8,128)(2,1)S(1)}, u32[]{:S(2)}, u32[]{:S(2)}) collective-permute-start(bf16[128,576]{1,0:T(8,128)(2,1)S(1)} %excited_block_kernel.1.own_ref), channel_id=1, source_target_pairs={{0,1},{1,0},{2,3},{3,2},{4,5},{5,4},{6,7},{7,6},{8,9},{9,8},{10,11... | collective-permute-start | bytes 442376 | tf_op jit(solution)/shard_map/ppermute | solution.py:26
  47.4 8.9 %collective-permute-start.14 = (bf16[2,128,128]{2,1,0:T(8,128)(2,1)S(1)}, bf16[2,128,128]{2,1,0:T(8,128)(2,1)S(1)}, u32[]{:S(2)}, u32[]{:S(2)}) collective-permute-start(bf16[2,128,128]{2,1,0:T(8,128)(2,1)S(1)} %get-tuple-element.64), channel_id=1, source_target_pairs={{0,8},{8,0},{16,24},{24,16},{1,9},{9,1},{17,25},{25,17},{2,10},{10... | collective-permute-start | bytes 196616 | tf_op jit(solution)/shard_map/ppermute | solution.py:26
  47.5 8.8 %collective-permute-start.15 = (bf16[2,128,128]{2,1,0:T(8,128)(2,1)S(1)}, bf16[2,128,128]{2,1,0:T(8,128)(2,1)S(1)}, u32[]{:S(2)}, u32[]{:S(2)}) collective-permute-start(bf16[2,128,128]{2,1,0:T(8,128)(2,1)S(1)} %get-tuple-element.65), channel_id=1, source_target_pairs={{0,16},{8,24},{16,0},{24,8},{1,17},{9,25},{17,1},{25,9},{2,18},{10... | collective-permute-start | bytes 196616 | tf_op jit(solution)/shard_map/ppermute | solution.py:26
  50.1 6.2 %collective-permute-start.16 = (bf16[2,128,128]{2,1,0:T(8,128)(2,1)S(1)}, bf16[2,128,128]{2,1,0:T(8,128)(2,1)S(1)}, u32[]{:S(2)}, u32[]{:S(2)}) collective-permute-start(bf16[2,128,128]{2,1,0:T(8,128)(2,1)S(1)} %get-tuple-element.66), channel_id=1, source_target_pairs={{0,24},{8,16},{16,8},{24,0},{1,25},{9,17},{17,9},{25,1},{2,26},{10... | collective-permute-start | bytes 196616 | tf_op jit(solution)/shard_map/ppermute | solution.py:26

commit v10 on v9

--- a/solution.py
+++ b/solution.py
@@ -29,6 +29,10 @@
 def rotated(block, axis, distance):
     count = lax.axis_size(axis)
     return lax.ppermute(block, axis, [(i, (i + distance) % count) for i in range(count)])
+
+
+def crossing(masks):
+    return [(2 * i + h, 2 * (i ^ masks[h]) + h) for i in range(4) for h in (0, 1)]
 
 
 def call(kernel, outs, args, specs, cost, scratch=(), aliases=None, out_specs=None, limit=16):
@@ -158,19 +162,20 @@
     )[0]
 
 
-def mixed_blocks(own, mate, pairs_of):
+def mixed_blocks(own, mate, pair_own, beside, beyond):
     width = own.shape[0]
 
-    def mixed_blocks_kernel(own_ref, mate_ref, p0, p1, p2, p3, *outs):
+    def mixed_blocks_kernel(own_ref, mate_ref, pair_ref, beside_ref, beyond_ref, *outs):
+        rights = (pair_ref[...], beside_ref[...], beyond_ref[1], beyond_ref[0])
         for half, rows in enumerate((own_ref, mate_ref)):
-            for out, right in zip(outs, (p0, p1, p2, p3)):
-                out[half] = dot(rows[...], right[...]).astype(out.dtype)
+            for out, right in zip(outs, rights):
+                out[half] = dot(rows[...], right).astype(out.dtype)
 
     return call(
         mixed_blocks_kernel,
         [shape((2, width, width), F32)] + [shape((2, width, width))] * 3,
-        (own, mate, *pairs_of),
-        [VMEM] * 6,
+        (own, mate, pair_own, beside, beyond),
+        [VMEM] * 5,
         (16 * own.size * width, 1 * MIB),
     )
 
@@ -274,7 +279,8 @@
 ):
     y, core = lax.axis_index("y"), lax.axis_index("c")
     low = lax.axis_index("zl")
-    row_blocks = [(y ^ k) * 2 for k in range(4)]
+    side = 1 + 2 * core
+    row_blocks = [(y ^ m) * 2 for m in (0, side, 2, 4 - side)]
     where = [r + core for r in row_blocks] + [r + 1 - core for r in row_blocks]
     where += [core, lax.axis_index(BETA), lax.axis_index(ALPHA), 2 - 2 * low]
     where = jnp.stack(where).astype(jnp.int32)
@@ -294,7 +300,8 @@
     coupling, scale, placed = staged(
         where, beta_cols, pair_coupling, pair_alpha.T, beta_ops, parts[0]
     )
-    got = [swapped(parts[k], "y", k) for k in (1, 3, 2)]
+    turns = (None, crossing((1, 3)), crossing((2, 2)), crossing((3, 1)))
+    got = [lax.ppermute(parts[k], ("y", "c"), turns[k]) for k in (1, 3, 2)]
     *got, below, above = lax.optimization_barrier((*got, below, above))
     near = swapped(coef_v, "zl", 1)
     total = parts[0].astype(F32)
@@ -304,25 +311,21 @@
     total, coupling, scale, placed = lax.optimization_barrier((total, coupling, scale, placed))
 
     far = lax.ppermute(near, ALPHA, route)
-    zs = lax.axis_size("zh")
-    steps = [[(2 * i + h, 2 * (i ^ m[h]) + h) for i in range(zs) for h in (0, 1)] for m in ((1, 3), (3, 1))]
-    first = lax.ppermute(total, ("zh", "c"), steps[0])
+    first = lax.ppermute(total, ("zh", "c"), turns[1])
     sent, _ = lax.optimization_barrier((pair_v, total))
-    pairs = [pair_v] + [swapped(sent, "y", k) for k in (1, 2, 3)]
+    beside = lax.ppermute(sent, ("y", "c"), turns[1])
     crossed = swapped(jnp.where(core == 0, above, below), "c", 1)
     total = (total.astype(F32) + first.astype(F32)).astype(BF16)
-    total, crossed, pairs[1], pairs[3] = lax.optimization_barrier(
-        (total, crossed, pairs[1], pairs[3])
-    )
-    second = lax.ppermute(total, ("zh", "c"), steps[1])
+    total, crossed, beside = lax.optimization_barrier((total, crossed, beside))
+    beyond = lax.ppermute(jnp.stack([pair_v, beside]), ("y", "c"), turns[3])
+    second = lax.ppermute(total, ("zh", "c"), turns[3])
     same = same_spin_beta([below, crossed, coef_v, mate, above], placed)
-    second, same, pairs[2] = lax.optimization_barrier((second, same, pairs[2]))
+    same = same_spin_alpha(where, alpha_cols, [coef_v, near, far], alpha_ops, same)
+    second, same = lax.optimization_barrier((second, same))
 
     excited = excited_block(total, second, coupling, scale)
-    mine, *out = mixed_blocks(excited, swapped(excited, "c", 1), pairs)
-    back = [swapped(block, "y", k) for k, block in zip((1, 2, 3), out)]
-    same = same_spin_alpha(where, alpha_cols, [coef_v, near, far], alpha_ops, same)
-    *back, same = lax.optimization_barrier((*back, same))
+    mine, *out = mixed_blocks(excited, swapped(excited, "c", 1), pair_v, beside, beyond)
+    back = [lax.ppermute(out[k - 1], ("y", "c"), turns[k]) for k in (1, 2, 3)]
     return finished(where, same, [mine, *back], denominators)
 
 

time: 58.6 us -> 61.2 us (1.044)
  the two profiles are of different devices: /device:TPU:1 before, /device:TPU:66 now
where the time goes in v10:
time: 61.2 us; the launch traced here: 61.1 us
  starting transfers between devices  28 us (46%)
  waiting for transfers between devices  19.6 us (32%)
  Pallas kernels  11.6 us (19%)
  local copies, waits for them, and re-layouts  1.4 us (2%)
    pallas_call x8, Pallas kernels, call(): pl.pallas_call(kernel, out_shape=outs, in_specs=specs, out_specs=out_spec...  11.6 us
    ppermute x2, waiting for transfers between devices, rotated(): lax.ppermute(block, axis, [(i, (i + distance) % count) for i in range(cou...  6.96 us
    ppermute x5, waiting for transfers between devices, swapped(): return lax.ppermute(block, axis, [(i, i ^ mask) for i in range(count)])  6.66 us
    ppermute x3, starting transfers between devices, local(): back = [lax.ppermute(out[k - 1], ('y', 'c'), turns[k]) for k in (1, 2, 3)]  4.79 us
    ppermute x3, starting transfers between devices, local(): got = [lax.ppermute(parts[k], ('y', 'c'), turns[k]) for k in (1, 3, 2)]  4.57 us
    ppermute x2, starting transfers between devices, rotated(): lax.ppermute(block, axis, [(i, (i + distance) % count) for i in range(cou...  4.56 us
    ppermute x1, starting transfers between devices, local(): beyond = lax.ppermute(jnp.stack([pair_v, beside]), ('y', 'c'), turns[3])  4.3 us
    ppermute x1, starting transfers between devices, local(): second = lax.ppermute(total, ('zh', 'c'), turns[3])  3.92 us
  transfers between devices with their start and end apart: 18, of which 7 were waited for; matrix products, arithmetic and copies ran while one was open for 0% of the time, Pallas kernels for 16%

profile of v10, /device:TPU:66, one launch (start us, length us, event | category | flops | bytes accessed | tf_op | source)
XLA Modules:
  0.0 61.1 jit_solution(6400391774490587912)
XLA Ops:
  0.5 1.0 %loaded_kernel.1 = (bf16[1024,128]{1,0:T(8,128)(2,1)S(1)}, bf16[576,128]{1,0:T(8,128)(2,1)S(1)}) custom-call(bf16[1024,128]{1,0:T(8,128)(2,1)} %coef_ref.1, bf16[576,128]{1,0:T(8,128)(2,1)} %bitcast.20), custom_call_target="tpu_custom_call" | custom-call | bytes 1048576 | tf_op jit(solution)/shard_map/loaded_kernel/pallas_call | solution.py:43
  1.5 4.6 %collective-permute-start.5 = (bf16[1024,128]{1,0:T(8,128)(2,1)S(1)}, bf16[1024,128]{1,0:T(8,128)(2,1)S(1)}, u32[]{:S(2)}, u32[]{:S(2)}) collective-permute-start(bf16[1024,128]{1,0:T(8,128)(2,1)S(1)} %get-tuple-element.33.own_ref.b2), channel_id=1, source_target_pairs={{0,2},{1,3},{2,4},{3,5},{4,6},{5,7},{6,8},{7,9},{8,10},{9,11},{10,... | collective-permute-start | bytes 786440 | tf_op jit(solution)/shard_map/ppermute | solution.py:31
  6.2 1.0 %density_parts_kernel.1 = (bf16[576,128]{1,0:T(8,128)(2,1)S(1)}, bf16[576,128]{1,0:T(8,128)(2,1)S(1)}, bf16[576,128]{1,0:T(8,128)(2,1)S(1)}, bf16[576,128]{1,0:T(8,128)(2,1)S(1)}) custom-call(s32[12]{0:T(128)S(1)} %stack.60.where_ref, bf16[1024,128]{1,0:T(8,128)(2,1)S(1)} %get-tuple-element.33.own_ref.b2, ...), custom_call_target="tpu_custom_call" | custom-call | flops 150994944 | bytes 1048576 | tf_op jit(solution)/shard_map/density_parts_kernel/pallas_call | solution.py:43
  7.2 1.7 %collective-permute-start.2 = (bf16[576,128]{1,0:T(8,128)(2,1)S(1)}, bf16[576,128]{1,0:T(8,128)(2,1)S(1)}, u32[]{:S(2)}, u32[]{:S(2)}) collective-permute-start(bf16[576,128]{1,0:T(8,128)(2,1)S(1)} %get-tuple-element.36), channel_id=1, source_target_pairs={{0,8},{1,25},{8,0},{9,17},{16,24},{17,9},{24,16},{25,1},{2,10},{3,... | collective-permute-start | bytes 442376 | tf_op jit(solution)/shard_map/ppermute | solution.py:304
  8.9 2.2 %collective-permute-start.3 = (bf16[576,128]{1,0:T(8,128)(2,1)S(1)}, bf16[576,128]{1,0:T(8,128)(2,1)S(1)}, u32[]{:S(2)}, u32[]{:S(2)}) collective-permute-start(bf16[576,128]{1,0:T(8,128)(2,1)S(1)} %get-tuple-element.37), channel_id=1, source_target_pairs={{0,24},{1,9},{8,16},{9,1},{16,8},{17,25},{24,0},{25,17},{2,26},{3,... | collective-permute-start | bytes 442376 | tf_op jit(solution)/shard_map/ppermute | solution.py:304
  11.1 0.7 %collective-permute-start.4 = (bf16[576,128]{1,0:T(8,128)(2,1)S(1)}, bf16[576,128]{1,0:T(8,128)(2,1)S(1)}, u32[]{:S(2)}, u32[]{:S(2)}) collective-permute-start(bf16[576,128]{1,0:T(8,128)(2,1)S(1)} %get-tuple-element.38), channel_id=1, source_target_pairs={{0,16},{1,17},{8,24},{9,25},{16,0},{17,1},{24,8},{25,9},{2,18},{3,... | collective-permute-start | bytes 442376 | tf_op jit(solution)/shard_map/ppermute | solution.py:304
  11.8 0.7 %copy-done.1 = s32[1,4]{1,0:T(1,128)S(1)} copy-done((s32[1,4]{1,0:T(1,128)S(1)}, s32[1,4]{1,0:T(1,128)}, u32[]{:S(2)}) %copy-start.1) | copy-done | bytes 40
  12.4 1.8 %staged_kernel.1 = (bf16[576,576]{1,0:T(8,128)(2,1)S(1)}, f32[128,576]{1,0:T(8,128)S(1)}, bf16[128,640]{1,0:T(8,128)(2,1)S(1)}) custom-call(s32[12]{0:T(128)S(1)} %stack.60.where_ref, s32[1,4]{1,0:T(1,128)S(1)} %copy-done.1, bf16[576,576]{1,0:T(8,128)(2,1)} %c_ref.1, bf16[576,1024]{1,0:T(8,128)(2,1)} %bitcast.18, bf16[128,512]{1,0:T(8,128)(2,1)} %ops_ref.2, ...), custom_call_target="tpu_custom_call" | custom-call | flops 331776 | bytes 2097152 | tf_op jit(solution)/shard_map/staged_kernel/pallas_call | solution.py:43
  14.3 3.0 %collective-permute-done.5.b0 = bf16[1024,128]{1,0:T(8,128)(2,1)S(1)} collective-permute-done((bf16[1024,128]{1,0:T(8,128)(2,1)S(1)}, bf16[1024,128]{1,0:T(8,128)(2,1)S(1)}, u32[]{:S(2)}, u32[]{:S(2)}) %collective-permute-start.5) | collective-permute-done | bytes 262176 | tf_op jit(solution)/shard_map/ppermute | solution.py:31
  17.8 3.9 %collective-permute-done.6.b4 = bf16[1024,128]{1,0:T(8,128)(2,1)S(1)} collective-permute-done((bf16[1024,128]{1,0:T(8,128)(2,1)S(1)}, bf16[1024,128]{1,0:T(8,128)(2,1)S(1)}, u32[]{:S(2)}, u32[]{:S(2)}) %collective-permute-start.6) | collective-permute-done | bytes 262176 | tf_op jit(solution)/shard_map/ppermute | solution.py:31
  21.8 1.6 %collective-permute-start.7 = (bf16[576,128]{1,0:T(8,128)(2,1)S(1)}, bf16[576,128]{1,0:T(8,128)(2,1)S(1)}, u32[]{:S(2)}, u32[]{:S(2)}) collective-permute-start(bf16[576,128]{1,0:T(8,128)(2,1)S(1)} %add_convert_fusion.1), channel_id=1, source_target_pairs={{0,2},{1,7},{2,0},{3,5},{4,6},{5,3},{6,4},{7,1},{8,10},{9,15},{10,... | collective-permute-start | bytes 442376 | tf_op jit(solution)/shard_map/ppermute | solution.py:314
  23.5 5.3 %collective-permute-done.11.near_ref = bf16[1024,128]{1,0:T(8,128)(2,1)S(1)} collective-permute-done((bf16[1024,128]{1,0:T(8,128)(2,1)S(1)}, bf16[1024,128]{1,0:T(8,128)(2,1)S(1)}, u32[]{:S(2)}, u32[]{:S(2)}) %collective-permute-start.11) | collective-permute-done | bytes 262176 | tf_op jit(solution)/shard_map/ppermute | solution.py:26
  28.8 1.5 %collective-permute-start.12 = (bf16[1024,128]{1,0:T(8,128)(2,1)S(1)}, bf16[1024,128]{1,0:T(8,128)(2,1)S(1)}, u32[]{:S(2)}, u32[]{:S(2)}) collective-permute-start(bf16[1024,128]{1,0:T(8,128)(2,1)S(1)} %collective-permute-done.11.near_ref), channel_id=1, source_target_pairs={{0,64},{32,224},{64,128},{96,32},{128,192},{160,96},{192,0},{224,1... | collective-permute-start | bytes 786440 | tf_op jit(solution)/shard_map/ppermute | solution.py:313
  30.3 1.6 %collective-permute-start.9 = (bf16[576,128]{1,0:T(8,128)(2,1)S(1)}, bf16[576,128]{1,0:T(8,128)(2,1)S(1)}, u32[]{:S(2)}, u32[]{:S(2)}) collective-permute-start(bf16[576,128]{1,0:T(8,128)(2,1)S(1)} %get-tuple-element.48.po_ref.pair_ref), channel_id=1, source_target_pairs={{0,8},{1,25},{8,0},{9,17},{16,24},{17,9},{24,16},{25,1},{2,10},{3,... | collective-permute-start | bytes 442376 | tf_op jit(solution)/shard_map/ppermute | solution.py:316
  32.0 3.5 %collective-permute-done.9.beside_ref = bf16[576,128]{1,0:T(8,128)(2,1)S(1)} collective-permute-done((bf16[576,128]{1,0:T(8,128)(2,1)S(1)}, bf16[576,128]{1,0:T(8,128)(2,1)S(1)}, u32[]{:S(2)}, u32[]{:S(2)}) %collective-permute-start.9) | collective-permute-done | bytes 147488 | tf_op jit(solution)/shard_map/ppermute | solution.py:316
  35.4 3.9 %collective-permute-start.10 = (bf16[576,128]{1,0:T(8,128)(2,1)S(1)}, bf16[576,128]{1,0:T(8,128)(2,1)S(1)}, u32[]{:S(2)}, u32[]{:S(2)}) collective-permute-start(bf16[576,128]{1,0:T(8,128)(2,1)S(1)} %add_convert_fusion.near_ref), channel_id=1, source_target_pairs={{0,6},{1,3},{2,4},{3,1},{4,2},{5,7},{6,0},{7,5},{8,14},{9,11},{10,... | collective-permute-start | bytes 442376 | tf_op jit(solution)/shard_map/ppermute | solution.py:321
  39.4 4.3 %collective-permute-start.14 = (bf16[2,576,128]{2,1,0:T(8,128)(2,1)S(1)}, bf16[2,576,128]{2,1,0:T(8,128)(2,1)S(1)}, u32[]{:S(2)}, u32[]{:S(2)}) collective-permute-start(bf16[2,576,128]{2,1,0:T(8,128)(2,1)S(1)} %pad_maximum_fusion), channel_id=1, source_target_pairs={{0,24},{1,9},{8,16},{9,1},{16,8},{17,25},{24,0},{25,17},{2,26},{3,... | collective-permute-start | bytes 884744 | tf_op jit(solution)/shard_map/ppermute | solution.py:320
  44.2 0.6 %copy-done.2 = s32[1,4]{1,0:T(1,128)S(1)} copy-done((s32[1,4]{1,0:T(1,128)S(1)}, s32[1,4]{1,0:T(1,128)}, u32[]{:S(2)}) %copy-start.2) | copy-done | bytes 40
  44.9 5.0 %same_spin_alpha_kernel.1.same_ref = f32[1024,128]{1,0:T(8,128)S(1)} custom-call(s32[12]{0:T(128)S(1)} %stack.60.where_ref, s32[1,4]{1,0:T(1,128)S(1)} %copy-done.2, bf16[1024,128]{1,0:T(8,128)(2,1)S(1)} %get-tuple-element.33.own_ref.b2, bf16[1024,128]{1,0:T(8,128)(2,1)S(1)} %collective-permute-done.11.near_ref, ...), custom_call_target="tpu_custom_call" | custom-call | flops 1073741824 | bytes 10485760 | tf_op jit(solution)/shard_map/same_spin_alpha_kernel/pallas_call | solution.py:43
  50.3 1.4 %collective-permute-done.13.mate_ref = bf16[128,576]{1,0:T(8,128)(2,1)S(1)} collective-permute-done((bf16[128,576]{1,0:T(8,128)(2,1)S(1)}, bf16[128,576]{1,0:T(8,128)(2,1)S(1)}, u32[]{:S(2)}, u32[]{:S(2)}) %collective-permute-start.13) | collective-permute-done | bytes 147488 | tf_op jit(solution)/shard_map/ppermute | solution.py:26
  52.6 1.2 %collective-permute-start.16 = (bf16[2,128,128]{2,1,0:T(8,128)(2,1)S(1)}, bf16[2,128,128]{2,1,0:T(8,128)(2,1)S(1)}, u32[]{:S(2)}, u32[]{:S(2)}) collective-permute-start(bf16[2,128,128]{2,1,0:T(8,128)(2,1)S(1)} %get-tuple-element.59), channel_id=1, source_target_pairs={{0,16},{1,17},{8,24},{9,25},{16,0},{17,1},{24,8},{25,9},{2,18},{3,... | collective-permute-start | bytes 196616 | tf_op jit(solution)/shard_map/ppermute | solution.py:328
  53.8 3.2 %collective-permute-start.17 = (bf16[2,128,128]{2,1,0:T(8,128)(2,1)S(1)}, bf16[2,128,128]{2,1,0:T(8,128)(2,1)S(1)}, u32[]{:S(2)}, u32[]{:S(2)}) collective-permute-start(bf16[2,128,128]{2,1,0:T(8,128)(2,1)S(1)} %get-tuple-element.60), channel_id=1, source_target_pairs={{0,24},{1,9},{8,16},{9,1},{16,8},{17,25},{24,0},{25,17},{2,26},{3,... | collective-permute-start | bytes 196616 | tf_op jit(solution)/shard_map/ppermute | solution.py:328
  57.0 1.9 %collective-permute-done.16.m2 = bf16[2,128,128]{2,1,0:T(8,128)(2,1)S(1)} collective-permute-done((bf16[2,128,128]{2,1,0:T(8,128)(2,1)S(1)}, bf16[2,128,128]{2,1,0:T(8,128)(2,1)S(1)}, u32[]{:S(2)}, u32[]{:S(2)}) %collective-permute-start.16) | collective-permute-done | bytes 65568 | tf_op jit(solution)/shard_map/ppermute | solution.py:328
  59.5 1.4 %finished_kernel.1 = f32[1024,128]{1,0:T(8,128)} custom-call(s32[12]{0:T(128)S(1)} %stack.60.where_ref, f32[1024,128]{1,0:T(8,128)S(1)} %same_spin_alpha_kernel.1.same_ref, f32[2,128,128]{2,1,0:T(8,128)S(1)} %get-tuple-element.57.m0, bf16[2,128,128]{2,1,0:T(8,128)(2,1)S(1)} %collective-permute-done.15.m1, ...), custom_call_target="tpu_custom_call" | custom-call | flops 262144 | bytes 2097152 | tf_op jit(solution)/shard_map/finished_kernel/pallas_call | solution.py:43
  (31 shorter events, 3.9 us)
Async XLA Ops:
  0.0 6.2 %collective-permute-start = (bf16[1024,128]{1,0:T(8,128)(2,1)}, bf16[1024,128]{1,0:T(8,128)(2,1)S(1)}, u32[]{:S(2)}, u32[]{:S(2)}) collective-permute-start(bf16[1024,128]{1,0:T(8,128)(2,1)} %coef_ref.1), channel_id=1, source_target_pairs={{0,1},{1,0},{2,3},{3,2},{4,5},{5,4},{6,7},{7,6},{8,9},{9,8},{10,11... | collective-permute-start | bytes 786440 | tf_op jit(solution)/shard_map/ppermute | solution.py:26
  0.0 6.2 %collective-permute-start.1 = (bf16[576,128]{1,0:T(8,128)(2,1)}, bf16[576,128]{1,0:T(8,128)(2,1)S(1)}, u32[]{:S(2)}, u32[]{:S(2)}) collective-permute-start(bf16[576,128]{1,0:T(8,128)(2,1)} %bitcast.19), channel_id=1, source_target_pairs={{0,1},{1,0},{2,3},{3,2},{4,5},{5,4},{6,7},{7,6},{8,9},{9,8},{10,11... | collective-permute-start | bytes 442376 | tf_op jit(solution)/shard_map/ppermute | solution.py:26
  1.5 15.8 %collective-permute-start.5 = (bf16[1024,128]{1,0:T(8,128)(2,1)S(1)}, bf16[1024,128]{1,0:T(8,128)(2,1)S(1)}, u32[]{:S(2)}, u32[]{:S(2)}) collective-permute-start(bf16[1024,128]{1,0:T(8,128)(2,1)S(1)} %get-tuple-element.33.own_ref.b2), channel_id=1, source_target_pairs={{0,2},{1,3},{2,4},{3,5},{4,6},{5,7},{6,8},{7,9},{8,10},{9,11},{10,... | collective-permute-start | bytes 786440 | tf_op jit(solution)/shard_map/ppermute | solution.py:31
  6.1 15.6 %collective-permute-start.6 = (bf16[1024,128]{1,0:T(8,128)(2,1)S(1)}, bf16[1024,128]{1,0:T(8,128)(2,1)S(1)}, u32[]{:S(2)}, u32[]{:S(2)}) collective-permute-start(bf16[1024,128]{1,0:T(8,128)(2,1)S(1)} %get-tuple-element.33.own_ref.b2), channel_id=1, source_target_pairs={{0,30},{1,31},{2,0},{3,1},{4,2},{5,3},{6,4},{7,5},{8,6},{9,7},{10,... | collective-permute-start | bytes 786440 | tf_op jit(solution)/shard_map/ppermute | solution.py:31
  7.2 14.5 %collective-permute-start.2 = (bf16[576,128]{1,0:T(8,128)(2,1)S(1)}, bf16[576,128]{1,0:T(8,128)(2,1)S(1)}, u32[]{:S(2)}, u32[]{:S(2)}) collective-permute-start(bf16[576,128]{1,0:T(8,128)(2,1)S(1)} %get-tuple-element.36), channel_id=1, source_target_pairs={{0,8},{1,25},{8,0},{9,17},{16,24},{17,9},{24,16},{25,1},{2,10},{3,... | collective-permute-start | bytes 442376 | tf_op jit(solution)/shard_map/ppermute | solution.py:304
  8.9 12.8 %collective-permute-start.3 = (bf16[576,128]{1,0:T(8,128)(2,1)S(1)}, bf16[576,128]{1,0:T(8,128)(2,1)S(1)}, u32[]{:S(2)}, u32[]{:S(2)}) collective-permute-start(bf16[576,128]{1,0:T(8,128)(2,1)S(1)} %get-tuple-element.37), channel_id=1, source_target_pairs={{0,24},{1,9},{8,16},{9,1},{16,8},{17,25},{24,0},{25,17},{2,26},{3,... | collective-permute-start | bytes 442376 | tf_op jit(solution)/shard_map/ppermute | solution.py:304
  11.1 10.7 %collective-permute-start.4 = (bf16[576,128]{1,0:T(8,128)(2,1)S(1)}, bf16[576,128]{1,0:T(8,128)(2,1)S(1)}, u32[]{:S(2)}, u32[]{:S(2)}) collective-permute-start(bf16[576,128]{1,0:T(8,128)(2,1)S(1)} %get-tuple-element.38), channel_id=1, source_target_pairs={{0,16},{1,17},{8,24},{9,25},{16,0},{17,1},{24,8},{25,9},{2,18},{3,... | collective-permute-start | bytes 442376 | tf_op jit(solution)/shard_map/ppermute | solution.py:304
  11.8 0.7 %copy-start.1 = (s32[1,4]{1,0:T(1,128)S(1)}, s32[1,4]{1,0:T(1,128)}, u32[]{:S(2)}) copy-start(s32[1,4]{1,0:T(1,128)} %cols_ref.2) | copy-start | bytes 52
  17.3 11.5 %collective-permute-start.11 = (bf16[1024,128]{1,0:T(8,128)(2,1)S(1)}, bf16[1024,128]{1,0:T(8,128)(2,1)S(1)}, u32[]{:S(2)}, u32[]{:S(2)}) collective-permute-start(bf16[1024,128]{1,0:T(8,128)(2,1)S(1)} %get-tuple-element.33.own_ref.b2), channel_id=1, source_target_pairs={{0,32},{32,0},{1,33},{33,1},{2,34},{34,2},{3,35},{35,3},{4,36},{36... | collective-permute-start | bytes 786440 | tf_op jit(solution)/shard_map/ppermute | solution.py:26
  21.8 37.7 %copy-start = (f32[1024,128]{1,0:T(8,128)S(1)}, f32[1024,128]{1,0:T(8,128)}, u32[]{:S(2)}) copy-start(f32[1024,128]{1,0:T(8,128)} %den_ref.1) | copy-start | bytes 1572868
  21.8 10.1 %collective-permute-start.7 = (bf16[576,128]{1,0:T(8,128)(2,1)S(1)}, bf16[576,128]{1,0:T(8,128)(2,1)S(1)}, u32[]{:S(2)}, u32[]{:S(2)}) collective-permute-start(bf16[576,128]{1,0:T(8,128)(2,1)S(1)} %add_convert_fusion.1), channel_id=1, source_target_pairs={{0,2},{1,7},{2,0},{3,5},{4,6},{5,3},{6,4},{7,1},{8,10},{9,15},{10,... | collective-permute-start | bytes 442376 | tf_op jit(solution)/shard_map/ppermute | solution.py:314
  23.4 12.0 %collective-permute-start.8 = (bf16[1024,128]{1,0:T(8,128)(2,1)S(1)}, bf16[1024,128]{1,0:T(8,128)(2,1)S(1)}, u32[]{:S(2)}, u32[]{:S(2)}) collective-permute-start(bf16[1024,128]{1,0:T(8,128)(2,1)S(1)} %broadcast_select_fusion), channel_id=1, source_target_pairs={{0,1},{1,0},{2,3},{3,2},{4,5},{5,4},{6,7},{7,6},{8,9},{9,8},{10,11... | collective-permute-start | bytes 786440 | tf_op jit(solution)/shard_map/ppermute | solution.py:26
  28.8 15.4 %collective-permute-start.12 = (bf16[1024,128]{1,0:T(8,128)(2,1)S(1)}, bf16[1024,128]{1,0:T(8,128)(2,1)S(1)}, u32[]{:S(2)}, u32[]{:S(2)}) collective-permute-start(bf16[1024,128]{1,0:T(8,128)(2,1)S(1)} %collective-permute-done.11.near_ref), channel_id=1, source_target_pairs={{0,64},{32,224},{64,128},{96,32},{128,192},{160,96},{192,0},{224,1... | collective-permute-start | bytes 786440 | tf_op jit(solution)/shard_map/ppermute | solution.py:313
  30.3 5.1 %collective-permute-start.9 = (bf16[576,128]{1,0:T(8,128)(2,1)S(1)}, bf16[576,128]{1,0:T(8,128)(2,1)S(1)}, u32[]{:S(2)}, u32[]{:S(2)}) collective-permute-start(bf16[576,128]{1,0:T(8,128)(2,1)S(1)} %get-tuple-element.48.po_ref.pair_ref), channel_id=1, source_target_pairs={{0,8},{1,25},{8,0},{9,17},{16,24},{17,9},{24,16},{25,1},{2,10},{3,... | collective-permute-start | bytes 442376 | tf_op jit(solution)/shard_map/ppermute | solution.py:316
  35.4 14.4 %collective-permute-start.10 = (bf16[576,128]{1,0:T(8,128)(2,1)S(1)}, bf16[576,128]{1,0:T(8,128)(2,1)S(1)}, u32[]{:S(2)}, u32[]{:S(2)}) collective-permute-start(bf16[576,128]{1,0:T(8,128)(2,1)S(1)} %add_convert_fusion.near_ref), channel_id=1, source_target_pairs={{0,6},{1,3},{2,4},{3,1},{4,2},{5,7},{6,0},{7,5},{8,14},{9,11},{10,... | collective-permute-start | bytes 442376 | tf_op jit(solution)/shard_map/ppermute | solution.py:321
  39.4 12.3 %collective-permute-start.14 = (bf16[2,576,128]{2,1,0:T(8,128)(2,1)S(1)}, bf16[2,576,128]{2,1,0:T(8,128)(2,1)S(1)}, u32[]{:S(2)}, u32[]{:S(2)}) collective-permute-start(bf16[2,576,128]{2,1,0:T(8,128)(2,1)S(1)} %pad_maximum_fusion), channel_id=1, source_target_pairs={{0,24},{1,9},{8,16},{9,1},{16,8},{17,25},{24,0},{25,17},{2,26},{3,... | collective-permute-start | bytes 884744 | tf_op jit(solution)/shard_map/ppermute | solution.py:320
  44.2 0.7 %copy-start.2 = (s32[1,4]{1,0:T(1,128)S(1)}, s32[1,4]{1,0:T(1,128)}, u32[]{:S(2)}) copy-start(s32[1,4]{1,0:T(1,128)} %cols_ref.3) | copy-start | bytes 52
  50.2 1.5 %collective-permute-start.13 = (bf16[128,576]{1,0:T(8,128)(2,1)S(1)}, bf16[128,576]{1,0:T(8,128)(2,1)S(1)}, u32[]{:S(2)}, u32[]{:S(2)}) collective-permute-start(bf16[128,576]{1,0:T(8,128)(2,1)S(1)} %excited_block_kernel.1.own_ref), channel_id=1, source_target_pairs={{0,1},{1,0},{2,3},{3,2},{4,5},{5,4},{6,7},{7,6},{8,9},{9,8},{10,11... | collective-permute-start | bytes 442376 | tf_op jit(solution)/shard_map/ppermute | solution.py:26
  52.2 4.8 %collective-permute-start.15 = (bf16[2,128,128]{2,1,0:T(8,128)(2,1)S(1)}, bf16[2,128,128]{2,1,0:T(8,128)(2,1)S(1)}, u32[]{:S(2)}, u32[]{:S(2)}) collective-permute-start(bf16[2,128,128]{2,1,0:T(8,128)(2,1)S(1)} %get-tuple-element.58), channel_id=1, source_target_pairs={{0,8},{1,25},{8,0},{9,17},{16,24},{17,9},{24,16},{25,1},{2,10},{3,... | collective-permute-start | bytes 196616 | tf_op jit(solution)/shard_map/ppermute | solution.py:328
  52.6 6.3 %collective-permute-start.16 = (bf16[2,128,128]{2,1,0:T(8,128)(2,1)S(1)}, bf16[2,128,128]{2,1,0:T(8,128)(2,1)S(1)}, u32[]{:S(2)}, u32[]{:S(2)}) collective-permute-start(bf16[2,128,128]{2,1,0:T(8,128)(2,1)S(1)} %get-tuple-element.59), channel_id=1, source_target_pairs={{0,16},{1,17},{8,24},{9,25},{16,0},{17,1},{24,8},{25,9},{2,18},{3,... | collective-permute-start | bytes 196616 | tf_op jit(solution)/shard_map/ppermute | solution.py:328
  53.8 5.7 %collective-permute-start.17 = (bf16[2,128,128]{2,1,0:T(8,128)(2,1)S(1)}, bf16[2,128,128]{2,1,0:T(8,128)(2,1)S(1)}, u32[]{:S(2)}, u32[]{:S(2)}) collective-permute-start(bf16[2,128,128]{2,1,0:T(8,128)(2,1)S(1)} %get-tuple-element.60), channel_id=1, source_target_pairs={{0,24},{1,9},{8,16},{9,1},{16,8},{17,25},{24,0},{25,17},{2,26},{3,... | collective-permute-start | bytes 196616 | tf_op jit(solution)/shard_map/ppermute | solution.py:328

commit v11 on v10

--- a/solution.py
+++ b/solution.py
@@ -223,19 +223,22 @@
     )[0]
 
 
-def same_spin_alpha(where, cols, blocks, alpha_ops, start):
+def same_spin_alpha(where, cols, blocks, alpha_ops, start, part):
     rows, width = start.shape
     depth = blocks[0].shape[0]
     span = alpha_ops.shape[1]
     step = 256
+    half = rows // 2
+    mine = range(part * half, (part + 1) * half, step)
+    rest = slice((1 - part) * half, (2 - part) * half)
     count = lax.axis_size(ALPHA)
 
     def same_spin_alpha_kernel(
         where_ref, cols_ref, own_ref, near_ref, far_ref, ops_ref, start_ref, out_ref, ops_v, picked, sems
     ):
         copies = [
-            pltpu.make_async_copy(ops_ref.at[r : r + step, :], ops_v.at[r : r + step, :], sems.at[n])
-            for n, r in enumerate(range(0, rows, step))
+            pltpu.make_async_copy(ops_ref.at[r : r + step, :], ops_v.at[n], sems.at[n])
+            for n, r in enumerate(mine)
         ]
         for copy in copies:
             copy.start()
@@ -246,23 +249,24 @@
                 own_ref[...],
                 jnp.where(offset == where_ref[11], near_ref[...], far_ref[...]),
             )
-        for copy, r in zip(copies, range(0, rows, step)):
-            copy.wait()
+        out_ref[rest, :] = start_ref[rest, :]
+        for n, r in enumerate(mine):
+            copies[n].wait()
             at = slice(r, r + step)
-            out_ref[at, :] = start_ref[at, :] + dot(ops_v[at, :], picked[...])
+            out_ref[at, :] = start_ref[at, :] + dot(ops_v[n], picked[...])
 
     return call(
         same_spin_alpha_kernel,
         [shape((rows, width), F32)],
         (where, cols, *blocks, alpha_ops, start),
         [SMEM, SMEM] + [VMEM] * 3 + [HBM, VMEM],
-        (2 * rows * width * depth * 4, 10 * MIB),
+        (rows * width * depth * 4, 5 * MIB),
         [
-            pltpu.VMEM((rows, span), BF16),
+            pltpu.VMEM((half // step, step, span), BF16),
             pltpu.VMEM((span, width), BF16),
-            pltpu.SemaphoreType.DMA((rows // step,)),
+            pltpu.SemaphoreType.DMA((half // step,)),
         ],
-        limit=24,
+        limit=16,
     )[0]
 
 
@@ -315,17 +319,21 @@
     sent, _ = lax.optimization_barrier((pair_v, total))
     beside = lax.ppermute(sent, ("y", "c"), turns[1])
     crossed = swapped(jnp.where(core == 0, above, below), "c", 1)
+    first, beside = lax.optimization_barrier((first, beside))
     total = (total.astype(F32) + first.astype(F32)).astype(BF16)
-    total, crossed, beside = lax.optimization_barrier((total, crossed, beside))
+    total, crossed = lax.optimization_barrier((total, crossed))
     beyond = lax.ppermute(jnp.stack([pair_v, beside]), ("y", "c"), turns[3])
     second = lax.ppermute(total, ("zh", "c"), turns[3])
     same = same_spin_beta([below, crossed, coef_v, mate, above], placed)
-    same = same_spin_alpha(where, alpha_cols, [coef_v, near, far], alpha_ops, same)
+    around = [coef_v, near, far]
+    same = same_spin_alpha(where, alpha_cols, around, alpha_ops, same, 0)
     second, same = lax.optimization_barrier((second, same))
 
     excited = excited_block(total, second, coupling, scale)
     mine, *out = mixed_blocks(excited, swapped(excited, "c", 1), pair_v, beside, beyond)
     back = [lax.ppermute(out[k - 1], ("y", "c"), turns[k]) for k in (1, 2, 3)]
+    same = same_spin_alpha(where, alpha_cols, around, alpha_ops, same, 1)
+    *back, same = lax.optimization_barrier((*back, same))
     return finished(where, same, [mine, *back], denominators)
 
 

time: 61.2 us -> 56.8 us (0.928)
  the two profiles are of different devices: /device:TPU:66 before, /device:TPU:1 now
where the time goes in v11:
time: 56.8 us; the launch traced here: 56.3 us
  starting transfers between devices  35.9 us (63%)
  Pallas kernels  13.7 us (24%)
  waiting for transfers between devices  4.71 us (8%)
  local copies, waits for them, and re-layouts  1.4 us (2%)
    pallas_call x9, Pallas kernels, call(): pl.pallas_call(kernel, out_shape=outs, in_specs=specs, out_specs=out_spec...  13.7 us
    ppermute x5, starting transfers between devices, swapped(): return lax.ppermute(block, axis, [(i, i ^ mask) for i in range(count)])  12.4 us
    ppermute x2, starting transfers between devices, rotated(): lax.ppermute(block, axis, [(i, (i + distance) % count) for i in range(cou...  6.9 us
    ppermute x1, starting transfers between devices, local(): beside = lax.ppermute(sent, ('y', 'c'), turns[1])  5.57 us
    ppermute x3, starting transfers between devices, local(): got = [lax.ppermute(parts[k], ('y', 'c'), turns[k]) for k in (1, 3, 2)]  3.95 us
    ppermute x3, starting transfers between devices, local(): back = [lax.ppermute(out[k - 1], ('y', 'c'), turns[k]) for k in (1, 2, 3)]  3.33 us
    ppermute x1, starting transfers between devices, local(): beyond = lax.ppermute(jnp.stack([pair_v, beside]), ('y', 'c'), turns[3])  1.43 us
    ppermute x1, waiting for transfers between devices, local(): far = lax.ppermute(near, ALPHA, route)  1.39 us
  transfers between devices with their start and end apart: 18, of which 6 were waited for; matrix products, arithmetic and copies ran while one was open for 0% of the time, Pallas kernels for 21%

profile of v11, /device:TPU:1, one launch (start us, length us, event | category | flops | bytes accessed | tf_op | source)
XLA Modules:
  0.0 56.3 jit_solution(12105386566548435403)
XLA Ops:
  0.0 3.2 %collective-permute-start = (bf16[1024,128]{1,0:T(8,128)(2,1)}, bf16[1024,128]{1,0:T(8,128)(2,1)S(1)}, u32[]{:S(2)}, u32[]{:S(2)}) collective-permute-start(bf16[1024,128]{1,0:T(8,128)(2,1)} %coef_ref.1), channel_id=1, source_target_pairs={{0,1},{1,0},{2,3},{3,2},{4,5},{5,4},{6,7},{7,6},{8,9},{9,8},{10,11... | collective-permute-start | bytes 786440 | tf_op jit(solution)/shard_map/ppermute | solution.py:26
  3.2 1.0 %loaded_kernel.1 = (bf16[1024,128]{1,0:T(8,128)(2,1)S(1)}, bf16[576,128]{1,0:T(8,128)(2,1)S(1)}) custom-call(bf16[1024,128]{1,0:T(8,128)(2,1)} %coef_ref.1, bf16[576,128]{1,0:T(8,128)(2,1)} %bitcast.20), custom_call_target="tpu_custom_call" | custom-call | bytes 1048576 | tf_op jit(solution)/shard_map/loaded_kernel/pallas_call | solution.py:43
  4.3 1.3 %collective-permute-start.5 = (bf16[1024,128]{1,0:T(8,128)(2,1)S(1)}, bf16[1024,128]{1,0:T(8,128)(2,1)S(1)}, u32[]{:S(2)}, u32[]{:S(2)}) collective-permute-start(bf16[1024,128]{1,0:T(8,128)(2,1)S(1)} %get-tuple-element.38.own_ref.b2), channel_id=1, source_target_pairs={{0,2},{1,3},{2,4},{3,5},{4,6},{5,7},{6,8},{7,9},{8,10},{9,11},{10,... | collective-permute-start | bytes 786440 | tf_op jit(solution)/shard_map/ppermute | solution.py:31
  5.6 5.6 %collective-permute-start.6 = (bf16[1024,128]{1,0:T(8,128)(2,1)S(1)}, bf16[1024,128]{1,0:T(8,128)(2,1)S(1)}, u32[]{:S(2)}, u32[]{:S(2)}) collective-permute-start(bf16[1024,128]{1,0:T(8,128)(2,1)S(1)} %get-tuple-element.38.own_ref.b2), channel_id=1, source_target_pairs={{0,30},{1,31},{2,0},{3,1},{4,2},{5,3},{6,4},{7,5},{8,6},{9,7},{10,... | collective-permute-start | bytes 786440 | tf_op jit(solution)/shard_map/ppermute | solution.py:31
  11.3 1.0 %density_parts_kernel.1 = (bf16[576,128]{1,0:T(8,128)(2,1)S(1)}, bf16[576,128]{1,0:T(8,128)(2,1)S(1)}, bf16[576,128]{1,0:T(8,128)(2,1)S(1)}, bf16[576,128]{1,0:T(8,128)(2,1)S(1)}) custom-call(s32[12]{0:T(128)S(1)} %stack.60.where_ref, bf16[1024,128]{1,0:T(8,128)(2,1)S(1)} %get-tuple-element.38.own_ref.b2, ...), custom_call_target="tpu_custom_call" | custom-call | flops 150994944 | bytes 1048576 | tf_op jit(solution)/shard_map/density_parts_kernel/pallas_call | solution.py:43
  12.3 0.5 collective-permute-start.2
  12.8 3.4 %collective-permute-start.4 = (bf16[576,128]{1,0:T(8,128)(2,1)S(1)}, bf16[576,128]{1,0:T(8,128)(2,1)S(1)}, u32[]{:S(2)}, u32[]{:S(2)}) collective-permute-start(bf16[576,128]{1,0:T(8,128)(2,1)S(1)} %get-tuple-element.43), channel_id=1, source_target_pairs={{0,16},{1,17},{8,24},{9,25},{16,0},{17,1},{24,8},{25,9},{2,18},{3,... | collective-permute-start | bytes 442376 | tf_op jit(solution)/shard_map/ppermute | solution.py:308
  16.2 0.7 %copy-done.2 = s32[1,4]{1,0:T(1,128)S(1)} copy-done((s32[1,4]{1,0:T(1,128)S(1)}, s32[1,4]{1,0:T(1,128)}, u32[]{:S(2)}) %copy-start.2) | copy-done | bytes 40
  16.9 1.8 %staged_kernel.1 = (bf16[576,576]{1,0:T(8,128)(2,1)S(1)}, f32[128,576]{1,0:T(8,128)S(1)}, bf16[128,640]{1,0:T(8,128)(2,1)S(1)}) custom-call(s32[12]{0:T(128)S(1)} %stack.60.where_ref, s32[1,4]{1,0:T(1,128)S(1)} %copy-done.2, bf16[576,576]{1,0:T(8,128)(2,1)} %c_ref.1, bf16[576,1024]{1,0:T(8,128)(2,1)} %bitcast.18, bf16[128,512]{1,0:T(8,128)(2,1)} %ops_ref.3, ...), custom_call_target="tpu_custom_call" | custom-call | flops 331776 | bytes 2097152 | tf_op jit(solution)/shard_map/staged_kernel/pallas_call | solution.py:43
  18.9 4.9 %collective-permute-start.11 = (bf16[1024,128]{1,0:T(8,128)(2,1)S(1)}, bf16[1024,128]{1,0:T(8,128)(2,1)S(1)}, u32[]{:S(2)}, u32[]{:S(2)}) collective-permute-start(bf16[1024,128]{1,0:T(8,128)(2,1)S(1)} %get-tuple-element.38.own_ref.b2), channel_id=1, source_target_pairs={{0,32},{32,0},{1,33},{33,1},{2,34},{34,2},{3,35},{35,3},{4,36},{36... | collective-permute-start | bytes 786440 | tf_op jit(solution)/shard_map/ppermute | solution.py:26
  23.8 1.0 %collective-permute-done.4 = bf16[576,128]{1,0:T(8,128)(2,1)S(1)} collective-permute-done((bf16[576,128]{1,0:T(8,128)(2,1)S(1)}, bf16[576,128]{1,0:T(8,128)(2,1)S(1)}, u32[]{:S(2)}, u32[]{:S(2)}) %collective-permute-start.4) | collective-permute-done | bytes 147488 | tf_op jit(solution)/shard_map/ppermute | solution.py:308
  25.3 5.6 %collective-permute-start.8 = (bf16[576,128]{1,0:T(8,128)(2,1)S(1)}, bf16[576,128]{1,0:T(8,128)(2,1)S(1)}, u32[]{:S(2)}, u32[]{:S(2)}) collective-permute-start(bf16[576,128]{1,0:T(8,128)(2,1)S(1)} %get-tuple-element.51.po_ref.pair_ref), channel_id=1, source_target_pairs={{0,8},{1,25},{8,0},{9,17},{16,24},{17,9},{24,16},{25,1},{2,10},{3,... | collective-permute-start | bytes 442376 | tf_op jit(solution)/shard_map/ppermute | solution.py:320
  31.1 1.2 %collective-permute-start.12 = (bf16[1024,128]{1,0:T(8,128)(2,1)S(1)}, bf16[1024,128]{1,0:T(8,128)(2,1)S(1)}, u32[]{:S(2)}, u32[]{:S(2)}) collective-permute-start(bf16[1024,128]{1,0:T(8,128)(2,1)S(1)} %collective-permute-done.11.near_ref), channel_id=1, source_target_pairs={{0,64},{32,224},{64,128},{96,32},{128,192},{160,96},{192,0},{224,1... | collective-permute-start | bytes 786440 | tf_op jit(solution)/shard_map/ppermute | solution.py:317
  32.3 1.1 %collective-permute-done.8.beside_ref = bf16[576,128]{1,0:T(8,128)(2,1)S(1)} collective-permute-done((bf16[576,128]{1,0:T(8,128)(2,1)S(1)}, bf16[576,128]{1,0:T(8,128)(2,1)S(1)}, u32[]{:S(2)}, u32[]{:S(2)}) %collective-permute-start.8) | collective-permute-done | bytes 147488 | tf_op jit(solution)/shard_map/ppermute | solution.py:320
  33.5 0.7 %collective-permute-start.10 = (bf16[576,128]{1,0:T(8,128)(2,1)S(1)}, bf16[576,128]{1,0:T(8,128)(2,1)S(1)}, u32[]{:S(2)}, u32[]{:S(2)}) collective-permute-start(bf16[576,128]{1,0:T(8,128)(2,1)S(1)} %add_convert_fusion.near_ref), channel_id=1, source_target_pairs={{0,6},{1,3},{2,4},{3,1},{4,2},{5,7},{6,0},{7,5},{8,14},{9,11},{10,... | collective-permute-start | bytes 442376 | tf_op jit(solution)/shard_map/ppermute | solution.py:326
  34.2 1.4 %collective-permute-start.14 = (bf16[2,576,128]{2,1,0:T(8,128)(2,1)S(1)}, bf16[2,576,128]{2,1,0:T(8,128)(2,1)S(1)}, u32[]{:S(2)}, u32[]{:S(2)}) collective-permute-start(bf16[2,576,128]{2,1,0:T(8,128)(2,1)S(1)} %pad_maximum_fusion), channel_id=1, source_target_pairs={{0,24},{1,9},{8,16},{9,1},{16,8},{17,25},{24,0},{25,17},{2,26},{3,... | collective-permute-start | bytes 884744 | tf_op jit(solution)/shard_map/ppermute | solution.py:325
  36.1 1.4 %collective-permute-done.12.far_ref = bf16[1024,128]{1,0:T(8,128)(2,1)S(1)} collective-permute-done((bf16[1024,128]{1,0:T(8,128)(2,1)S(1)}, bf16[1024,128]{1,0:T(8,128)(2,1)S(1)}, u32[]{:S(2)}, u32[]{:S(2)}) %collective-permute-start.12) | collective-permute-done | bytes 262176 | tf_op jit(solution)/shard_map/ppermute | solution.py:317
  37.5 0.7 %copy-done.1 = s32[1,4]{1,0:T(1,128)S(1)} copy-done((s32[1,4]{1,0:T(1,128)S(1)}, s32[1,4]{1,0:T(1,128)}, u32[]{:S(2)}) %copy-start.1) | copy-done | bytes 40
  38.2 3.5 %same_spin_alpha_kernel.2.start_ref = f32[1024,128]{1,0:T(8,128)S(1)} custom-call(s32[12]{0:T(128)S(1)} %stack.60.where_ref, s32[1,4]{1,0:T(1,128)S(1)} %copy-done.1, bf16[1024,128]{1,0:T(8,128)(2,1)S(1)} %get-tuple-element.38.own_ref.b2, bf16[1024,128]{1,0:T(8,128)(2,1)S(1)} %collective-permute-done.11.near_ref, ...), custom_call_target="tpu_custom_call" | custom-call | flops 536870912 | bytes 5242880 | tf_op jit(solution)/shard_map/same_spin_alpha_kernel/pallas_call | solution.py:43
  42.1 4.1 %collective-permute-start.13 = (bf16[128,576]{1,0:T(8,128)(2,1)S(1)}, bf16[128,576]{1,0:T(8,128)(2,1)S(1)}, u32[]{:S(2)}, u32[]{:S(2)}) collective-permute-start(bf16[128,576]{1,0:T(8,128)(2,1)S(1)} %excited_block_kernel.1.own_ref), channel_id=1, source_target_pairs={{0,1},{1,0},{2,3},{3,2},{4,5},{5,4},{6,7},{7,6},{8,9},{9,8},{10,11... | collective-permute-start | bytes 442376 | tf_op jit(solution)/shard_map/ppermute | solution.py:26
  46.2 1.0 %collective-permute-done.13.mate_ref = bf16[128,576]{1,0:T(8,128)(2,1)S(1)} collective-permute-done((bf16[128,576]{1,0:T(8,128)(2,1)S(1)}, bf16[128,576]{1,0:T(8,128)(2,1)S(1)}, u32[]{:S(2)}, u32[]{:S(2)}) %collective-permute-start.13) | collective-permute-done | bytes 147488 | tf_op jit(solution)/shard_map/ppermute | solution.py:26
  48.1 3.0 %collective-permute-start.17 = (bf16[2,128,128]{2,1,0:T(8,128)(2,1)S(1)}, bf16[2,128,128]{2,1,0:T(8,128)(2,1)S(1)}, u32[]{:S(2)}, u32[]{:S(2)}) collective-permute-start(bf16[2,128,128]{2,1,0:T(8,128)(2,1)S(1)} %get-tuple-element.64), channel_id=1, source_target_pairs={{0,24},{1,9},{8,16},{9,1},{16,8},{17,25},{24,0},{25,17},{2,26},{3,... | collective-permute-start | bytes 196616 | tf_op jit(solution)/shard_map/ppermute | solution.py:334
  51.1 3.5 %same_spin_alpha_kernel.3.same_ref = f32[1024,128]{1,0:T(8,128)S(1)} custom-call(s32[12]{0:T(128)S(1)} %stack.60.where_ref, s32[1,4]{1,0:T(1,128)S(1)} %copy-done.1, bf16[1024,128]{1,0:T(8,128)(2,1)S(1)} %get-tuple-element.38.own_ref.b2, bf16[1024,128]{1,0:T(8,128)(2,1)S(1)} %collective-permute-done.11.near_ref, ...), custom_call_target="tpu_custom_call" | custom-call | flops 536870912 | bytes 5242880 | tf_op jit(solution)/shard_map/same_spin_alpha_kernel/pallas_call | solution.py:43
  54.7 1.4 %finished_kernel.1 = f32[1024,128]{1,0:T(8,128)} custom-call(s32[12]{0:T(128)S(1)} %stack.60.where_ref, f32[1024,128]{1,0:T(8,128)S(1)} %same_spin_alpha_kernel.3.same_ref, f32[2,128,128]{2,1,0:T(8,128)S(1)} %get-tuple-element.67.m0, bf16[2,128,128]{2,1,0:T(8,128)(2,1)S(1)} %collective-permute-done.15.m1, ...), custom_call_target="tpu_custom_call" | custom-call | flops 262144 | bytes 2097152 | tf_op jit(solution)/shard_map/finished_kernel/pallas_call | solution.py:43
  (32 shorter events, 2.7 us)
Async XLA Ops:
  0.0 11.3 %collective-permute-start = (bf16[1024,128]{1,0:T(8,128)(2,1)}, bf16[1024,128]{1,0:T(8,128)(2,1)S(1)}, u32[]{:S(2)}, u32[]{:S(2)}) collective-permute-start(bf16[1024,128]{1,0:T(8,128)(2,1)} %coef_ref.1), channel_id=1, source_target_pairs={{0,1},{1,0},{2,3},{3,2},{4,5},{5,4},{6,7},{7,6},{8,9},{9,8},{10,11... | collective-permute-start | bytes 786440 | tf_op jit(solution)/shard_map/ppermute | solution.py:26
  3.2 8.0 %collective-permute-start.1 = (bf16[576,128]{1,0:T(8,128)(2,1)}, bf16[576,128]{1,0:T(8,128)(2,1)S(1)}, u32[]{:S(2)}, u32[]{:S(2)}) collective-permute-start(bf16[576,128]{1,0:T(8,128)(2,1)} %bitcast.19), channel_id=1, source_target_pairs={{0,1},{1,0},{2,3},{3,2},{4,5},{5,4},{6,7},{7,6},{8,9},{9,8},{10,11... | collective-permute-start | bytes 442376 | tf_op jit(solution)/shard_map/ppermute | solution.py:26
  4.3 14.6 %collective-permute-start.5 = (bf16[1024,128]{1,0:T(8,128)(2,1)S(1)}, bf16[1024,128]{1,0:T(8,128)(2,1)S(1)}, u32[]{:S(2)}, u32[]{:S(2)}) collective-permute-start(bf16[1024,128]{1,0:T(8,128)(2,1)S(1)} %get-tuple-element.38.own_ref.b2), channel_id=1, source_target_pairs={{0,2},{1,3},{2,4},{3,5},{4,6},{5,7},{6,8},{7,9},{8,10},{9,11},{10,... | collective-permute-start | bytes 786440 | tf_op jit(solution)/shard_map/ppermute | solution.py:31
  5.6 18.2 %collective-permute-start.6 = (bf16[1024,128]{1,0:T(8,128)(2,1)S(1)}, bf16[1024,128]{1,0:T(8,128)(2,1)S(1)}, u32[]{:S(2)}, u32[]{:S(2)}) collective-permute-start(bf16[1024,128]{1,0:T(8,128)(2,1)S(1)} %get-tuple-element.38.own_ref.b2), channel_id=1, source_target_pairs={{0,30},{1,31},{2,0},{3,1},{4,2},{5,3},{6,4},{7,5},{8,6},{9,7},{10,... | collective-permute-start | bytes 786440 | tf_op jit(solution)/shard_map/ppermute | solution.py:31
  12.3 11.5 %collective-permute-start.2 = (bf16[576,128]{1,0:T(8,128)(2,1)S(1)}, bf16[576,128]{1,0:T(8,128)(2,1)S(1)}, u32[]{:S(2)}, u32[]{:S(2)}) collective-permute-start(bf16[576,128]{1,0:T(8,128)(2,1)S(1)} %get-tuple-element.41), channel_id=1, source_target_pairs={{0,8},{1,25},{8,0},{9,17},{16,24},{17,9},{24,16},{25,1},{2,10},{3,... | collective-permute-start | bytes 442376 | tf_op jit(solution)/shard_map/ppermute | solution.py:308
  12.8 11.0 %collective-permute-start.3 = (bf16[576,128]{1,0:T(8,128)(2,1)S(1)}, bf16[576,128]{1,0:T(8,128)(2,1)S(1)}, u32[]{:S(2)}, u32[]{:S(2)}) collective-permute-start(bf16[576,128]{1,0:T(8,128)(2,1)S(1)} %get-tuple-element.42), channel_id=1, source_target_pairs={{0,24},{1,9},{8,16},{9,1},{16,8},{17,25},{24,0},{25,17},{2,26},{3,... | collective-permute-start | bytes 442376 | tf_op jit(solution)/shard_map/ppermute | solution.py:308
  12.8 11.9 %collective-permute-start.4 = (bf16[576,128]{1,0:T(8,128)(2,1)S(1)}, bf16[576,128]{1,0:T(8,128)(2,1)S(1)}, u32[]{:S(2)}, u32[]{:S(2)}) collective-permute-start(bf16[576,128]{1,0:T(8,128)(2,1)S(1)} %get-tuple-element.43), channel_id=1, source_target_pairs={{0,16},{1,17},{8,24},{9,25},{16,0},{17,1},{24,8},{25,9},{2,18},{3,... | collective-permute-start | bytes 442376 | tf_op jit(solution)/shard_map/ppermute | solution.py:308
  16.2 0.7 %copy-start.2 = (s32[1,4]{1,0:T(1,128)S(1)}, s32[1,4]{1,0:T(1,128)}, u32[]{:S(2)}) copy-start(s32[1,4]{1,0:T(1,128)} %cols_ref.3) | copy-start | bytes 52
  18.9 12.2 %collective-permute-start.11 = (bf16[1024,128]{1,0:T(8,128)(2,1)S(1)}, bf16[1024,128]{1,0:T(8,128)(2,1)S(1)}, u32[]{:S(2)}, u32[]{:S(2)}) collective-permute-start(bf16[1024,128]{1,0:T(8,128)(2,1)S(1)} %get-tuple-element.38.own_ref.b2), channel_id=1, source_target_pairs={{0,32},{32,0},{1,33},{33,1},{2,34},{34,2},{3,35},{35,3},{4,36},{36... | collective-permute-start | bytes 786440 | tf_op jit(solution)/shard_map/ppermute | solution.py:26
  24.9 8.6 %collective-permute-start.7 = (bf16[576,128]{1,0:T(8,128)(2,1)S(1)}, bf16[576,128]{1,0:T(8,128)(2,1)S(1)}, u32[]{:S(2)}, u32[]{:S(2)}) collective-permute-start(bf16[576,128]{1,0:T(8,128)(2,1)S(1)} %add_convert_fusion.1), channel_id=1, source_target_pairs={{0,2},{1,7},{2,0},{3,5},{4,6},{5,3},{6,4},{7,1},{8,10},{9,15},{10,... | collective-permute-start | bytes 442376 | tf_op jit(solution)/shard_map/ppermute | solution.py:318
  25.3 8.1 %collective-permute-start.8 = (bf16[576,128]{1,0:T(8,128)(2,1)S(1)}, bf16[576,128]{1,0:T(8,128)(2,1)S(1)}, u32[]{:S(2)}, u32[]{:S(2)}) collective-permute-start(bf16[576,128]{1,0:T(8,128)(2,1)S(1)} %get-tuple-element.51.po_ref.pair_ref), channel_id=1, source_target_pairs={{0,8},{1,25},{8,0},{9,17},{16,24},{17,9},{24,16},{25,1},{2,10},{3,... | collective-permute-start | bytes 442376 | tf_op jit(solution)/shard_map/ppermute | solution.py:320
  30.9 2.6 %collective-permute-start.9 = (bf16[1024,128]{1,0:T(8,128)(2,1)S(1)}, bf16[1024,128]{1,0:T(8,128)(2,1)S(1)}, u32[]{:S(2)}, u32[]{:S(2)}) collective-permute-start(bf16[1024,128]{1,0:T(8,128)(2,1)S(1)} %broadcast_select_fusion), channel_id=1, source_target_pairs={{0,1},{1,0},{2,3},{3,2},{4,5},{5,4},{6,7},{7,6},{8,9},{9,8},{10,11... | collective-permute-start | bytes 786440 | tf_op jit(solution)/shard_map/ppermute | solution.py:26
  31.1 6.5 %collective-permute-start.12 = (bf16[1024,128]{1,0:T(8,128)(2,1)S(1)}, bf16[1024,128]{1,0:T(8,128)(2,1)S(1)}, u32[]{:S(2)}, u32[]{:S(2)}) collective-permute-start(bf16[1024,128]{1,0:T(8,128)(2,1)S(1)} %collective-permute-done.11.near_ref), channel_id=1, source_target_pairs={{0,64},{32,224},{64,128},{96,32},{128,192},{160,96},{192,0},{224,1... | collective-permute-start | bytes 786440 | tf_op jit(solution)/shard_map/ppermute | solution.py:317
  33.5 8.3 %collective-permute-start.10 = (bf16[576,128]{1,0:T(8,128)(2,1)S(1)}, bf16[576,128]{1,0:T(8,128)(2,1)S(1)}, u32[]{:S(2)}, u32[]{:S(2)}) collective-permute-start(bf16[576,128]{1,0:T(8,128)(2,1)S(1)} %add_convert_fusion.near_ref), channel_id=1, source_target_pairs={{0,6},{1,3},{2,4},{3,1},{4,2},{5,7},{6,0},{7,5},{8,14},{9,11},{10,... | collective-permute-start | bytes 442376 | tf_op jit(solution)/shard_map/ppermute | solution.py:326
  34.2 12.0 %collective-permute-start.14 = (bf16[2,576,128]{2,1,0:T(8,128)(2,1)S(1)}, bf16[2,576,128]{2,1,0:T(8,128)(2,1)S(1)}, u32[]{:S(2)}, u32[]{:S(2)}) collective-permute-start(bf16[2,576,128]{2,1,0:T(8,128)(2,1)S(1)} %pad_maximum_fusion), channel_id=1, source_target_pairs={{0,24},{1,9},{8,16},{9,1},{16,8},{17,25},{24,0},{25,17},{2,26},{3,... | collective-permute-start | bytes 884744 | tf_op jit(solution)/shard_map/ppermute | solution.py:325
  37.5 0.7 %copy-start.1 = (s32[1,4]{1,0:T(1,128)S(1)}, s32[1,4]{1,0:T(1,128)}, u32[]{:S(2)}) copy-start(s32[1,4]{1,0:T(1,128)} %cols_ref.5) | copy-start | bytes 52
  41.7 13.0 %copy-start = (f32[1024,128]{1,0:T(8,128)S(1)}, f32[1024,128]{1,0:T(8,128)}, u32[]{:S(2)}) copy-start(f32[1024,128]{1,0:T(8,128)} %den_ref.1) | copy-start | bytes 1572868
  42.1 5.1 %collective-permute-start.13 = (bf16[128,576]{1,0:T(8,128)(2,1)S(1)}, bf16[128,576]{1,0:T(8,128)(2,1)S(1)}, u32[]{:S(2)}, u32[]{:S(2)}) collective-permute-start(bf16[128,576]{1,0:T(8,128)(2,1)S(1)} %excited_block_kernel.1.own_ref), channel_id=1, source_target_pairs={{0,1},{1,0},{2,3},{3,2},{4,5},{5,4},{6,7},{7,6},{8,9},{9,8},{10,11... | collective-permute-start | bytes 442376 | tf_op jit(solution)/shard_map/ppermute | solution.py:26
  47.8 6.9 %collective-permute-start.15 = (bf16[2,128,128]{2,1,0:T(8,128)(2,1)S(1)}, bf16[2,128,128]{2,1,0:T(8,128)(2,1)S(1)}, u32[]{:S(2)}, u32[]{:S(2)}) collective-permute-start(bf16[2,128,128]{2,1,0:T(8,128)(2,1)S(1)} %get-tuple-element.62), channel_id=1, source_target_pairs={{0,8},{1,25},{8,0},{9,17},{16,24},{17,9},{24,16},{25,1},{2,10},{3,... | collective-permute-start | bytes 196616 | tf_op jit(solution)/shard_map/ppermute | solution.py:334
  47.9 6.8 %collective-permute-start.16 = (bf16[2,128,128]{2,1,0:T(8,128)(2,1)S(1)}, bf16[2,128,128]{2,1,0:T(8,128)(2,1)S(1)}, u32[]{:S(2)}, u32[]{:S(2)}) collective-permute-start(bf16[2,128,128]{2,1,0:T(8,128)(2,1)S(1)} %get-tuple-element.63), channel_id=1, source_target_pairs={{0,16},{1,17},{8,24},{9,25},{16,0},{17,1},{24,8},{25,9},{2,18},{3,... | collective-permute-start | bytes 196616 | tf_op jit(solution)/shard_map/ppermute | solution.py:334
  48.1 6.6 %collective-permute-start.17 = (bf16[2,128,128]{2,1,0:T(8,128)(2,1)S(1)}, bf16[2,128,128]{2,1,0:T(8,128)(2,1)S(1)}, u32[]{:S(2)}, u32[]{:S(2)}) collective-permute-start(bf16[2,128,128]{2,1,0:T(8,128)(2,1)S(1)} %get-tuple-element.64), channel_id=1, source_target_pairs={{0,24},{1,9},{8,16},{9,1},{16,8},{17,25},{24,0},{25,17},{2,26},{3,... | collective-permute-start | bytes 196616 | tf_op jit(solution)/shard_map/ppermute | solution.py:334

commit v12 on v11

--- a/solution.py
+++ b/solution.py
@@ -123,7 +123,7 @@
             offset = n if n in (0, 2, 4) else jnp.where(core == 0, n, 4 - n)
             tile = jnp.zeros((width, width), F32)
             for k in range(listed):
-                here = lax.rem(cols_ref[0, k] - where_ref[9] + 2 + count, count)
+                here = lax.rem(cols_ref[k] - where_ref[9] + 2 + count, count)
                 part = ops_v[:, k * width : (k + 1) * width].astype(F32)
                 tile = jnp.where(here == offset, part, tile)
             w_out[:, n * width : (n + 1) * width] = tile.astype(BF16)
@@ -223,50 +223,69 @@
     )[0]
 
 
-def same_spin_alpha(where, cols, blocks, alpha_ops, start, part):
+def alpha_rows(ops_ref, picked, start_ref, out_ref, ops_v, sems, part, select):
+    step = ops_v.shape[1]
+    half = start_ref.shape[0] // 2
+    mine = range(part * half, (part + 1) * half, step)
+    rest = slice((1 - part) * half, (2 - part) * half)
+    copies = [
+        pltpu.make_async_copy(ops_ref.at[r : r + step, :], ops_v.at[n], sems.at[n])
+        for n, r in enumerate(mine)
+    ]
+    for copy in copies:
+        copy.start()
+    select()
+    out_ref[rest, :] = start_ref[rest, :]
+    for n, r in enumerate(mine):
+        copies[n].wait()
+        at = slice(r, r + step)
+        out_ref[at, :] = start_ref[at, :] + dot(ops_v[n], picked[...])
+
+
+def same_spin_alpha(where, cols, blocks, alpha_ops, start):
     rows, width = start.shape
     depth = blocks[0].shape[0]
     span = alpha_ops.shape[1]
-    step = 256
-    half = rows // 2
-    mine = range(part * half, (part + 1) * half, step)
-    rest = slice((1 - part) * half, (2 - part) * half)
     count = lax.axis_size(ALPHA)
 
     def same_spin_alpha_kernel(
-        where_ref, cols_ref, own_ref, near_ref, far_ref, ops_ref, start_ref, out_ref, ops_v, picked, sems
+        where_ref, cols_ref, own_ref, near_ref, far_ref, ops_ref, start_ref, out_ref, picked, ops_v, sems
     ):
-        copies = [
-            pltpu.make_async_copy(ops_ref.at[r : r + step, :], ops_v.at[n], sems.at[n])
-            for n, r in enumerate(mine)
-        ]
-        for copy in copies:
-            copy.start()
-        for k in range(span // depth):
-            offset = lax.rem(cols_ref[0, k] - where_ref[10] + 1 + count, count)
-            picked[k * depth : (k + 1) * depth, :] = jnp.where(
-                offset == 1,
-                own_ref[...],
-                jnp.where(offset == where_ref[11], near_ref[...], far_ref[...]),
-            )
-        out_ref[rest, :] = start_ref[rest, :]
-        for n, r in enumerate(mine):
-            copies[n].wait()
-            at = slice(r, r + step)
-            out_ref[at, :] = start_ref[at, :] + dot(ops_v[n], picked[...])
+        def select():
+            for k in range(span // depth):
+                offset = lax.rem(cols_ref[4 + k] - where_ref[10] + 1 + count, count)
+                picked[k * depth : (k + 1) * depth, :] = jnp.where(
+                    offset == 1,
+                    own_ref[...],
+                    jnp.where(offset == where_ref[11], near_ref[...], far_ref[...]),
+                )
+
+        alpha_rows(ops_ref, picked, start_ref, out_ref, ops_v, sems, 0, select)
 
     return call(
         same_spin_alpha_kernel,
-        [shape((rows, width), F32)],
+        [shape((rows, width), F32), shape((span, width))],
         (where, cols, *blocks, alpha_ops, start),
         [SMEM, SMEM] + [VMEM] * 3 + [HBM, VMEM],
         (rows * width * depth * 4, 5 * MIB),
-        [
-            pltpu.VMEM((half // step, step, span), BF16),
-            pltpu.VMEM((span, width), BF16),
-            pltpu.SemaphoreType.DMA((half // step,)),
-        ],
-        limit=16,
+        [pltpu.VMEM((2, rows // 4, span), BF16), pltpu.SemaphoreType.DMA((2,))],
+    )
+
+
+def rest_of_alpha(picked, alpha_ops, start):
+    rows, width = start.shape
+    span = alpha_ops.shape[1]
+
+    def rest_of_alpha_kernel(picked, ops_ref, start_ref, out_ref, ops_v, sems):
+        alpha_rows(ops_ref, picked, start_ref, out_ref, ops_v, sems, 1, lambda: None)
+
+    return call(
+        rest_of_alpha_kernel,
+        [shape((rows, width), F32)],
+        (picked, alpha_ops, start),
+        [VMEM, HBM, VMEM],
+        (rows * width * span, 5 * MIB),
+        [pltpu.VMEM((2, rows // 4, span), BF16), pltpu.SemaphoreType.DMA((2,))],
     )[0]
 
 
@@ -288,6 +307,7 @@
     where = [r + core for r in row_blocks] + [r + 1 - core for r in row_blocks]
     where += [core, lax.axis_index(BETA), lax.axis_index(ALPHA), 2 - 2 * low]
     where = jnp.stack(where).astype(jnp.int32)
+    cols = jnp.concatenate([beta_cols[0], alpha_cols[0]])
 
     pair_t = pair_beta.T
     mate = swapped(coef, "c", 1)
@@ -302,11 +322,11 @@
 
     parts = density_parts(where, coef_v, mate, pair_v, pair_mate)
     coupling, scale, placed = staged(
-        where, beta_cols, pair_coupling, pair_alpha.T, beta_ops, parts[0]
+        where, cols, pair_coupling, pair_alpha.T, beta_ops, parts[0]
     )
     turns = (None, crossing((1, 3)), crossing((2, 2)), crossing((3, 1)))
     got = [lax.ppermute(parts[k], ("y", "c"), turns[k]) for k in (1, 3, 2)]
-    *got, below, above = lax.optimization_barrier((*got, below, above))
+    *got, below = lax.optimization_barrier((*got, below))
     near = swapped(coef_v, "zl", 1)
     total = parts[0].astype(F32)
     for part in got:
@@ -326,13 +346,13 @@
     second = lax.ppermute(total, ("zh", "c"), turns[3])
     same = same_spin_beta([below, crossed, coef_v, mate, above], placed)
     around = [coef_v, near, far]
-    same = same_spin_alpha(where, alpha_cols, around, alpha_ops, same, 0)
+    same, picked = same_spin_alpha(where, cols, around, alpha_ops, same)
     second, same = lax.optimization_barrier((second, same))
 
     excited = excited_block(total, second, coupling, scale)
     mine, *out = mixed_blocks(excited, swapped(excited, "c", 1), pair_v, beside, beyond)
     back = [lax.ppermute(out[k - 1], ("y", "c"), turns[k]) for k in (1, 2, 3)]
-    same = same_spin_alpha(where, alpha_cols, around, alpha_ops, same, 1)
+    same = rest_of_alpha(picked, alpha_ops, same)
     *back, same = lax.optimization_barrier((*back, same))
     return finished(where, same, [mine, *back], denominators)
 

time: 56.8 us -> 59.3 us (1.044)
  waiting for transfers between devices: 4.71 us -> 12.8 us
  starting transfers between devices: 35.9 us -> 31.9 us
  local copies, waits for them, and re-layouts: 1.4 us -> 0.09 us
  other arithmetic: 0.19 us -> 0.93 us
    ppermute x5, waiting for transfers between devices: 1.1 us -> 8.01 us  [swapped(): return lax.ppermute(block, axis, [(i, i ^ mask) for i in range(count)])]
    ppermute x1, starting transfers between devices: 5.57 us -> 2.18 us  [local(): beside = lax.ppermute(sent, ('y', 'c'), turns[1])]
    ppermute x1, waiting for transfers between devices: 1.39 us -> 3.89 us  [local(): far = lax.ppermute(near, ALPHA, route)]
    unnamed x6 -> x2, local copies, waits for them, and re-layouts: 1.32 us -> 0.01 us
    ppermute x1, waiting for transfers between devices: 1.1 us -> 0.01 us  [local(): beside = lax.ppermute(sent, ('y', 'c'), turns[1])]
    ppermute x3, waiting for transfers between devices: 0.97 us -> 0.01 us  [local(): got = [lax.ppermute(parts[k], ('y', 'c'), turns[k]) for k in (1, 3, 2)]]
    ppermute x5, starting transfers between devices: 12.4 us -> 13.2 us  [swapped(): return lax.ppermute(block, axis, [(i, i ^ mask) for i in range(count)])]
    ppermute x1, starting transfers between devices: 1.43 us -> 0.62 us  [local(): beyond = lax.ppermute(jnp.stack([pair_v, beside]), ('y', 'c'), turns[3])]
  transfers between devices with their start and end apart: 18 -> 18, of which waited for: 6 -> 5; matrix products, arithmetic and copies ran while one was open for 0% -> 2% of each run, Pallas kernels for 21% -> 19%
where the time goes in v12:
time: 59.3 us; the launch traced here: 59.2 us
  starting transfers between devices  31.9 us (54%)
  Pallas kernels  13.2 us (22%)
  waiting for transfers between devices  12.8 us (22%)
  other arithmetic  0.93 us (2%)
    ppermute x5, starting transfers between devices, swapped(): return lax.ppermute(block, axis, [(i, i ^ mask) for i in range(count)])  13.2 us
    pallas_call x9, Pallas kernels, call(): pl.pallas_call(kernel, out_shape=outs, in_specs=specs, out_specs=out_spec...  13.2 us
    ppermute x5, waiting for transfers between devices, swapped(): return lax.ppermute(block, axis, [(i, i ^ mask) for i in range(count)])  8.01 us
    ppermute x2, starting transfers between devices, rotated(): lax.ppermute(block, axis, [(i, (i + distance) % count) for i in range(cou...  7.04 us
    ppermute x3, starting transfers between devices, local(): got = [lax.ppermute(parts[k], ('y', 'c'), turns[k]) for k in (1, 3, 2)]  4.1 us
    ppermute x1, waiting for transfers between devices, local(): far = lax.ppermute(near, ALPHA, route)  3.89 us
    ppermute x3, starting transfers between devices, local(): back = [lax.ppermute(out[k - 1], ('y', 'c'), turns[k]) for k in (1, 2, 3)]  3.34 us
    ppermute x1, starting transfers between devices, local(): beside = lax.ppermute(sent, ('y', 'c'), turns[1])  2.18 us
  transfers between devices with their start and end apart: 18, of which 5 were waited for; matrix products, arithmetic and copies ran while one was open for 2% of the time, Pallas kernels for 19%

profile of v12, /device:TPU:1, one launch (start us, length us, event | category | flops | bytes accessed | tf_op | source)
XLA Modules:
  0.0 59.2 jit_solution(5295099349004577930)
XLA Ops:
  0.0 3.2 %collective-permute-start = (bf16[1024,128]{1,0:T(8,128)(2,1)}, bf16[1024,128]{1,0:T(8,128)(2,1)S(1)}, u32[]{:S(2)}, u32[]{:S(2)}) collective-permute-start(bf16[1024,128]{1,0:T(8,128)(2,1)} %coef_ref.1), channel_id=1, source_target_pairs={{0,1},{1,0},{2,3},{3,2},{4,5},{5,4},{6,7},{7,6},{8,9},{9,8},{10,11... | collective-permute-start | bytes 786440 | tf_op jit(solution)/shard_map/ppermute | solution.py:26
  3.2 1.0 %loaded_kernel.1 = (bf16[1024,128]{1,0:T(8,128)(2,1)S(1)}, bf16[576,128]{1,0:T(8,128)(2,1)S(1)}) custom-call(bf16[1024,128]{1,0:T(8,128)(2,1)} %coef_ref.1, bf16[576,128]{1,0:T(8,128)(2,1)} %bitcast.22), custom_call_target="tpu_custom_call" | custom-call | bytes 1048576 | tf_op jit(solution)/shard_map/loaded_kernel/pallas_call | solution.py:43
  4.3 1.3 %collective-permute-start.5 = (bf16[1024,128]{1,0:T(8,128)(2,1)S(1)}, bf16[1024,128]{1,0:T(8,128)(2,1)S(1)}, u32[]{:S(2)}, u32[]{:S(2)}) collective-permute-start(bf16[1024,128]{1,0:T(8,128)(2,1)S(1)} %get-tuple-element.39.own_ref.b2), channel_id=1, source_target_pairs={{0,2},{1,3},{2,4},{3,5},{4,6},{5,7},{6,8},{7,9},{8,10},{9,11},{10,... | collective-permute-start | bytes 786440 | tf_op jit(solution)/shard_map/ppermute | solution.py:31
  5.7 1.0 %density_parts_kernel.1 = (bf16[576,128]{1,0:T(8,128)(2,1)S(1)}, bf16[576,128]{1,0:T(8,128)(2,1)S(1)}, bf16[576,128]{1,0:T(8,128)(2,1)S(1)}, bf16[576,128]{1,0:T(8,128)(2,1)S(1)}) custom-call(s32[12]{0:T(128)S(1)} %stack.60.where_ref, bf16[1024,128]{1,0:T(8,128)(2,1)S(1)} %get-tuple-element.39.own_ref.b2, ...), custom_call_target="tpu_custom_call" | custom-call | flops 150994944 | bytes 1048576 | tf_op jit(solution)/shard_map/density_parts_kernel/pallas_call | solution.py:43
  6.7 2.8 %collective-permute-start.2 = (bf16[576,128]{1,0:T(8,128)(2,1)S(1)}, bf16[576,128]{1,0:T(8,128)(2,1)S(1)}, u32[]{:S(2)}, u32[]{:S(2)}) collective-permute-start(bf16[576,128]{1,0:T(8,128)(2,1)S(1)} %get-tuple-element.42), channel_id=1, source_target_pairs={{0,8},{1,25},{8,0},{9,17},{16,24},{17,9},{24,16},{25,1},{2,10},{3,... | collective-permute-start | bytes 442376 | tf_op jit(solution)/shard_map/ppermute | solution.py:328
  9.5 1.3 %collective-permute-start.4 = (bf16[576,128]{1,0:T(8,128)(2,1)S(1)}, bf16[576,128]{1,0:T(8,128)(2,1)S(1)}, u32[]{:S(2)}, u32[]{:S(2)}) collective-permute-start(bf16[576,128]{1,0:T(8,128)(2,1)S(1)} %get-tuple-element.44), channel_id=1, source_target_pairs={{0,16},{1,17},{8,24},{9,25},{16,0},{17,1},{24,8},{25,9},{2,18},{3,... | collective-permute-start | bytes 442376 | tf_op jit(solution)/shard_map/ppermute | solution.py:328
  10.8 5.7 %collective-permute-start.8 = (bf16[1024,128]{1,0:T(8,128)(2,1)S(1)}, bf16[1024,128]{1,0:T(8,128)(2,1)S(1)}, u32[]{:S(2)}, u32[]{:S(2)}) collective-permute-start(bf16[1024,128]{1,0:T(8,128)(2,1)S(1)} %get-tuple-element.39.own_ref.b2), channel_id=1, source_target_pairs={{0,30},{1,31},{2,0},{3,1},{4,2},{5,3},{6,4},{7,5},{8,6},{9,7},{10,... | collective-permute-start | bytes 786440 | tf_op jit(solution)/shard_map/ppermute | solution.py:31
  16.5 0.7 %pad_add_fusion.cols_ref = s32[8]{0:T(128)S(1)} fusion(s32[4]{0:T(128)} %bitcast.23, s32[4]{0:T(128)} %bitcast.24), kind=kLoop, calls=%fused_computation.4 | loop fusion | flops 8 | bytes 64 | tf_op jit(solution)/shard_map/concatenate | solution.py:310
  17.3 1.8 %staged_kernel.1 = (bf16[576,576]{1,0:T(8,128)(2,1)S(1)}, f32[128,576]{1,0:T(8,128)S(1)}, bf16[128,640]{1,0:T(8,128)(2,1)S(1)}) custom-call(s32[12]{0:T(128)S(1)} %stack.60.where_ref, s32[8]{0:T(128)S(1)} %pad_add_fusion.cols_ref, bf16[576,576]{1,0:T(8,128)(2,1)} %c_ref.1, bf16[576,1024]{1,0:T(8,128)(2,1)} %bitcast.20, bf16[128,512]{1,0:T(8,128)(2,1)} %ops_ref.3, ...), custom_call_target="tpu_custom_call" | custom-call | flops 331776 | bytes 2097152 | tf_op jit(solution)/shard_map/staged_kernel/pallas_call | solution.py:43
  19.1 4.7 %collective-permute-start.11 = (bf16[1024,128]{1,0:T(8,128)(2,1)S(1)}, bf16[1024,128]{1,0:T(8,128)(2,1)S(1)}, u32[]{:S(2)}, u32[]{:S(2)}) collective-permute-start(bf16[1024,128]{1,0:T(8,128)(2,1)S(1)} %get-tuple-element.39.own_ref.b2), channel_id=1, source_target_pairs={{0,32},{32,0},{1,33},{33,1},{2,34},{34,2},{3,35},{35,3},{4,36},{36... | collective-permute-start | bytes 786440 | tf_op jit(solution)/shard_map/ppermute | solution.py:26
  24.0 2.2 %collective-permute-start.7 = (bf16[576,128]{1,0:T(8,128)(2,1)S(1)}, bf16[576,128]{1,0:T(8,128)(2,1)S(1)}, u32[]{:S(2)}, u32[]{:S(2)}) collective-permute-start(bf16[576,128]{1,0:T(8,128)(2,1)S(1)} %get-tuple-element.52.po_ref.pair_ref), channel_id=1, source_target_pairs={{0,8},{1,25},{8,0},{9,17},{16,24},{17,9},{24,16},{25,1},{2,10},{3,... | collective-permute-start | bytes 442376 | tf_op jit(solution)/shard_map/ppermute | solution.py:340
  26.2 0.8 %collective-permute-done.8.b4 = bf16[1024,128]{1,0:T(8,128)(2,1)S(1)} collective-permute-done((bf16[1024,128]{1,0:T(8,128)(2,1)S(1)}, bf16[1024,128]{1,0:T(8,128)(2,1)S(1)}, u32[]{:S(2)}, u32[]{:S(2)}) %collective-permute-start.8) | collective-permute-done | bytes 262176 | tf_op jit(solution)/shard_map/ppermute | solution.py:31
  27.0 1.4 %collective-permute-start.9 = (bf16[1024,128]{1,0:T(8,128)(2,1)S(1)}, bf16[1024,128]{1,0:T(8,128)(2,1)S(1)}, u32[]{:S(2)}, u32[]{:S(2)}) collective-permute-start(bf16[1024,128]{1,0:T(8,128)(2,1)S(1)} %broadcast_select_fusion), channel_id=1, source_target_pairs={{0,1},{1,0},{2,3},{3,2},{4,5},{5,4},{6,7},{7,6},{8,9},{9,8},{10,11... | collective-permute-start | bytes 786440 | tf_op jit(solution)/shard_map/ppermute | solution.py:26
  28.4 7.0 %collective-permute-done.11.near_ref = bf16[1024,128]{1,0:T(8,128)(2,1)S(1)} collective-permute-done((bf16[1024,128]{1,0:T(8,128)(2,1)S(1)}, bf16[1024,128]{1,0:T(8,128)(2,1)S(1)}, u32[]{:S(2)}, u32[]{:S(2)}) %collective-permute-start.11) | collective-permute-done | bytes 262176 | tf_op jit(solution)/shard_map/ppermute | solution.py:26
  35.4 1.2 %collective-permute-start.12 = (bf16[1024,128]{1,0:T(8,128)(2,1)S(1)}, bf16[1024,128]{1,0:T(8,128)(2,1)S(1)}, u32[]{:S(2)}, u32[]{:S(2)}) collective-permute-start(bf16[1024,128]{1,0:T(8,128)(2,1)S(1)} %collective-permute-done.11.near_ref), channel_id=1, source_target_pairs={{0,64},{32,224},{64,128},{96,32},{128,192},{160,96},{192,0},{224,1... | collective-permute-start | bytes 786440 | tf_op jit(solution)/shard_map/ppermute | solution.py:337
  36.8 0.6 %collective-permute-start.14 = (bf16[2,576,128]{2,1,0:T(8,128)(2,1)S(1)}, bf16[2,576,128]{2,1,0:T(8,128)(2,1)S(1)}, u32[]{:S(2)}, u32[]{:S(2)}) collective-permute-start(bf16[2,576,128]{2,1,0:T(8,128)(2,1)S(1)} %pad_maximum_fusion), channel_id=1, source_target_pairs={{0,24},{1,9},{8,16},{9,1},{16,8},{17,25},{24,0},{25,17},{2,26},{3,... | collective-permute-start | bytes 884744 | tf_op jit(solution)/shard_map/ppermute | solution.py:345
  37.9 3.9 %collective-permute-done.12.far_ref = bf16[1024,128]{1,0:T(8,128)(2,1)S(1)} collective-permute-done((bf16[1024,128]{1,0:T(8,128)(2,1)S(1)}, bf16[1024,128]{1,0:T(8,128)(2,1)S(1)}, u32[]{:S(2)}, u32[]{:S(2)}) %collective-permute-start.12) | collective-permute-done | bytes 262176 | tf_op jit(solution)/shard_map/ppermute | solution.py:337
  41.8 3.5 %same_spin_alpha_kernel.1 = (f32[1024,128]{1,0:T(8,128)S(1)}, bf16[4096,128]{1,0:T(8,128)(2,1)S(1)}) custom-call(s32[12]{0:T(128)S(1)} %stack.60.where_ref, s32[8]{0:T(128)S(1)} %pad_add_fusion.cols_ref, bf16[1024,128]{1,0:T(8,128)(2,1)S(1)} %get-tuple-element.39.own_ref.b2, bf16[1024,128]{1,0:T(8,128)(2,1)S(1)} %collective-permute-done.11.near_ref, ...), custom_call_target="tpu_custom_call" | custom-call | flops 536870912 | bytes 5242880 | tf_op jit(solution)/shard_map/same_spin_alpha_kernel/pallas_call | solution.py:43
  45.8 3.9 %collective-permute-start.13 = (bf16[128,576]{1,0:T(8,128)(2,1)S(1)}, bf16[128,576]{1,0:T(8,128)(2,1)S(1)}, u32[]{:S(2)}, u32[]{:S(2)}) collective-permute-start(bf16[128,576]{1,0:T(8,128)(2,1)S(1)} %excited_block_kernel.1.own_ref), channel_id=1, source_target_pairs={{0,1},{1,0},{2,3},{3,2},{4,5},{5,4},{6,7},{7,6},{8,9},{9,8},{10,11... | collective-permute-start | bytes 442376 | tf_op jit(solution)/shard_map/ppermute | solution.py:26
  49.7 1.0 %collective-permute-done.13.mate_ref = bf16[128,576]{1,0:T(8,128)(2,1)S(1)} collective-permute-done((bf16[128,576]{1,0:T(8,128)(2,1)S(1)}, bf16[128,576]{1,0:T(8,128)(2,1)S(1)}, u32[]{:S(2)}, u32[]{:S(2)}) %collective-permute-start.13) | collective-permute-done | bytes 147488 | tf_op jit(solution)/shard_map/ppermute | solution.py:26
  51.6 0.9 %collective-permute-start.16 = (bf16[2,128,128]{2,1,0:T(8,128)(2,1)S(1)}, bf16[2,128,128]{2,1,0:T(8,128)(2,1)S(1)}, u32[]{:S(2)}, u32[]{:S(2)}) collective-permute-start(bf16[2,128,128]{2,1,0:T(8,128)(2,1)S(1)} %get-tuple-element.64), channel_id=1, source_target_pairs={{0,16},{1,17},{8,24},{9,25},{16,0},{17,1},{24,8},{25,9},{2,18},{3,... | collective-permute-start | bytes 196616 | tf_op jit(solution)/shard_map/ppermute | solution.py:354
  52.5 2.1 %collective-permute-start.17 = (bf16[2,128,128]{2,1,0:T(8,128)(2,1)S(1)}, bf16[2,128,128]{2,1,0:T(8,128)(2,1)S(1)}, u32[]{:S(2)}, u32[]{:S(2)}) collective-permute-start(bf16[2,128,128]{2,1,0:T(8,128)(2,1)S(1)} %get-tuple-element.65), channel_id=1, source_target_pairs={{0,24},{1,9},{8,16},{9,1},{16,8},{17,25},{24,0},{25,17},{2,26},{3,... | collective-permute-start | bytes 196616 | tf_op jit(solution)/shard_map/ppermute | solution.py:354
  54.5 3.0 %rest_of_alpha_kernel.1.same_ref = f32[1024,128]{1,0:T(8,128)S(1)} custom-call(bf16[4096,128]{1,0:T(8,128)(2,1)S(1)} %get-tuple-element.66.picked, bf16[1024,4096]{1,0:T(8,128)(2,1)} %ops_ref.5, f32[1024,128]{1,0:T(8,128)S(1)} %get-tuple-element.67.start_ref), custom_call_target="tpu_custom_call" | custom-call | flops 536870912 | bytes 5242880 | tf_op jit(solution)/shard_map/rest_of_alpha_kernel/pallas_call | solution.py:43
  57.6 1.4 %finished_kernel.1 = f32[1024,128]{1,0:T(8,128)} custom-call(s32[12]{0:T(128)S(1)} %stack.60.where_ref, f32[1024,128]{1,0:T(8,128)S(1)} %rest_of_alpha_kernel.1.same_ref, f32[2,128,128]{2,1,0:T(8,128)S(1)} %get-tuple-element.69.m0, bf16[2,128,128]{2,1,0:T(8,128)(2,1)S(1)} %collective-permute-done.15.m1, bf16[2,128,128]{2,1,0:T(8,128)(2,1)S(1)} %collective-permute-done.16.m2, ...), custom_call_target="tpu_custom_call" | custom-call | flops 262144 | bytes 2097152 | tf_op jit(solution)/shard_map/finished_kernel/pallas_call | solution.py:43
  (29 shorter events, 2.3 us)
Async XLA Ops:
  0.0 5.7 %collective-permute-start = (bf16[1024,128]{1,0:T(8,128)(2,1)}, bf16[1024,128]{1,0:T(8,128)(2,1)S(1)}, u32[]{:S(2)}, u32[]{:S(2)}) collective-permute-start(bf16[1024,128]{1,0:T(8,128)(2,1)} %coef_ref.1), channel_id=1, source_target_pairs={{0,1},{1,0},{2,3},{3,2},{4,5},{5,4},{6,7},{7,6},{8,9},{9,8},{10,11... | collective-permute-start | bytes 786440 | tf_op jit(solution)/shard_map/ppermute | solution.py:26
  3.2 2.4 %collective-permute-start.1 = (bf16[576,128]{1,0:T(8,128)(2,1)}, bf16[576,128]{1,0:T(8,128)(2,1)S(1)}, u32[]{:S(2)}, u32[]{:S(2)}) collective-permute-start(bf16[576,128]{1,0:T(8,128)(2,1)} %bitcast.21), channel_id=1, source_target_pairs={{0,1},{1,0},{2,3},{3,2},{4,5},{5,4},{6,7},{7,6},{8,9},{9,8},{10,11... | collective-permute-start | bytes 442376 | tf_op jit(solution)/shard_map/ppermute | solution.py:26
  4.3 14.9 %collective-permute-start.5 = (bf16[1024,128]{1,0:T(8,128)(2,1)S(1)}, bf16[1024,128]{1,0:T(8,128)(2,1)S(1)}, u32[]{:S(2)}, u32[]{:S(2)}) collective-permute-start(bf16[1024,128]{1,0:T(8,128)(2,1)S(1)} %get-tuple-element.39.own_ref.b2), channel_id=1, source_target_pairs={{0,2},{1,3},{2,4},{3,5},{4,6},{5,7},{6,8},{7,9},{8,10},{9,11},{10,... | collective-permute-start | bytes 786440 | tf_op jit(solution)/shard_map/ppermute | solution.py:31
  6.7 17.1 %collective-permute-start.2 = (bf16[576,128]{1,0:T(8,128)(2,1)S(1)}, bf16[576,128]{1,0:T(8,128)(2,1)S(1)}, u32[]{:S(2)}, u32[]{:S(2)}) collective-permute-start(bf16[576,128]{1,0:T(8,128)(2,1)S(1)} %get-tuple-element.42), channel_id=1, source_target_pairs={{0,8},{1,25},{8,0},{9,17},{16,24},{17,9},{24,16},{25,1},{2,10},{3,... | collective-permute-start | bytes 442376 | tf_op jit(solution)/shard_map/ppermute | solution.py:328
  9.5 14.3 %collective-permute-start.3 = (bf16[576,128]{1,0:T(8,128)(2,1)S(1)}, bf16[576,128]{1,0:T(8,128)(2,1)S(1)}, u32[]{:S(2)}, u32[]{:S(2)}) collective-permute-start(bf16[576,128]{1,0:T(8,128)(2,1)S(1)} %get-tuple-element.43), channel_id=1, source_target_pairs={{0,24},{1,9},{8,16},{9,1},{16,8},{17,25},{24,0},{25,17},{2,26},{3,... | collective-permute-start | bytes 442376 | tf_op jit(solution)/shard_map/ppermute | solution.py:328
  9.5 14.3 %collective-permute-start.4 = (bf16[576,128]{1,0:T(8,128)(2,1)S(1)}, bf16[576,128]{1,0:T(8,128)(2,1)S(1)}, u32[]{:S(2)}, u32[]{:S(2)}) collective-permute-start(bf16[576,128]{1,0:T(8,128)(2,1)S(1)} %get-tuple-element.44), channel_id=1, source_target_pairs={{0,16},{1,17},{8,24},{9,25},{16,0},{17,1},{24,8},{25,9},{2,18},{3,... | collective-permute-start | bytes 442376 | tf_op jit(solution)/shard_map/ppermute | solution.py:328
  10.8 16.1 %collective-permute-start.8 = (bf16[1024,128]{1,0:T(8,128)(2,1)S(1)}, bf16[1024,128]{1,0:T(8,128)(2,1)S(1)}, u32[]{:S(2)}, u32[]{:S(2)}) collective-permute-start(bf16[1024,128]{1,0:T(8,128)(2,1)S(1)} %get-tuple-element.39.own_ref.b2), channel_id=1, source_target_pairs={{0,30},{1,31},{2,0},{3,1},{4,2},{5,3},{6,4},{7,5},{8,6},{9,7},{10,... | collective-permute-start | bytes 786440 | tf_op jit(solution)/shard_map/ppermute | solution.py:31
  19.1 16.3 %collective-permute-start.11 = (bf16[1024,128]{1,0:T(8,128)(2,1)S(1)}, bf16[1024,128]{1,0:T(8,128)(2,1)S(1)}, u32[]{:S(2)}, u32[]{:S(2)}) collective-permute-start(bf16[1024,128]{1,0:T(8,128)(2,1)S(1)} %get-tuple-element.39.own_ref.b2), channel_id=1, source_target_pairs={{0,32},{32,0},{1,33},{33,1},{2,34},{34,2},{3,35},{35,3},{4,36},{36... | collective-permute-start | bytes 786440 | tf_op jit(solution)/shard_map/ppermute | solution.py:26
  23.9 12.7 %collective-permute-start.6 = (bf16[576,128]{1,0:T(8,128)(2,1)S(1)}, bf16[576,128]{1,0:T(8,128)(2,1)S(1)}, u32[]{:S(2)}, u32[]{:S(2)}) collective-permute-start(bf16[576,128]{1,0:T(8,128)(2,1)S(1)} %add_convert_fusion.1), channel_id=1, source_target_pairs={{0,2},{1,7},{2,0},{3,5},{4,6},{5,3},{6,4},{7,1},{8,10},{9,15},{10,... | collective-permute-start | bytes 442376 | tf_op jit(solution)/shard_map/ppermute | solution.py:338
  24.0 12.6 %collective-permute-start.7 = (bf16[576,128]{1,0:T(8,128)(2,1)S(1)}, bf16[576,128]{1,0:T(8,128)(2,1)S(1)}, u32[]{:S(2)}, u32[]{:S(2)}) collective-permute-start(bf16[576,128]{1,0:T(8,128)(2,1)S(1)} %get-tuple-element.52.po_ref.pair_ref), channel_id=1, source_target_pairs={{0,8},{1,25},{8,0},{9,17},{16,24},{17,9},{24,16},{25,1},{2,10},{3,... | collective-permute-start | bytes 442376 | tf_op jit(solution)/shard_map/ppermute | solution.py:340
  27.0 9.7 %collective-permute-start.9 = (bf16[1024,128]{1,0:T(8,128)(2,1)S(1)}, bf16[1024,128]{1,0:T(8,128)(2,1)S(1)}, u32[]{:S(2)}, u32[]{:S(2)}) collective-permute-start(bf16[1024,128]{1,0:T(8,128)(2,1)S(1)} %broadcast_select_fusion), channel_id=1, source_target_pairs={{0,1},{1,0},{2,3},{3,2},{4,5},{5,4},{6,7},{7,6},{8,9},{9,8},{10,11... | collective-permute-start | bytes 786440 | tf_op jit(solution)/shard_map/ppermute | solution.py:26
  35.4 6.4 %collective-permute-start.12 = (bf16[1024,128]{1,0:T(8,128)(2,1)S(1)}, bf16[1024,128]{1,0:T(8,128)(2,1)S(1)}, u32[]{:S(2)}, u32[]{:S(2)}) collective-permute-start(bf16[1024,128]{1,0:T(8,128)(2,1)S(1)} %collective-permute-done.11.near_ref), channel_id=1, source_target_pairs={{0,64},{32,224},{64,128},{96,32},{128,192},{160,96},{192,0},{224,1... | collective-permute-start | bytes 786440 | tf_op jit(solution)/shard_map/ppermute | solution.py:337
  36.7 8.7 %collective-permute-start.10 = (bf16[576,128]{1,0:T(8,128)(2,1)S(1)}, bf16[576,128]{1,0:T(8,128)(2,1)S(1)}, u32[]{:S(2)}, u32[]{:S(2)}) collective-permute-start(bf16[576,128]{1,0:T(8,128)(2,1)S(1)} %add_convert_fusion.near_ref), channel_id=1, source_target_pairs={{0,6},{1,3},{2,4},{3,1},{4,2},{5,7},{6,0},{7,5},{8,14},{9,11},{10,... | collective-permute-start | bytes 442376 | tf_op jit(solution)/shard_map/ppermute | solution.py:346
  36.8 12.8 %collective-permute-start.14 = (bf16[2,576,128]{2,1,0:T(8,128)(2,1)S(1)}, bf16[2,576,128]{2,1,0:T(8,128)(2,1)S(1)}, u32[]{:S(2)}, u32[]{:S(2)}) collective-permute-start(bf16[2,576,128]{2,1,0:T(8,128)(2,1)S(1)} %pad_maximum_fusion), channel_id=1, source_target_pairs={{0,24},{1,9},{8,16},{9,1},{16,8},{17,25},{24,0},{25,17},{2,26},{3,... | collective-permute-start | bytes 884744 | tf_op jit(solution)/shard_map/ppermute | solution.py:345
  45.4 12.2 %copy-start = (f32[1024,128]{1,0:T(8,128)S(1)}, f32[1024,128]{1,0:T(8,128)}, u32[]{:S(2)}) copy-start(f32[1024,128]{1,0:T(8,128)} %den_ref.1) | copy-start | bytes 1572868
  45.8 4.9 %collective-permute-start.13 = (bf16[128,576]{1,0:T(8,128)(2,1)S(1)}, bf16[128,576]{1,0:T(8,128)(2,1)S(1)}, u32[]{:S(2)}, u32[]{:S(2)}) collective-permute-start(bf16[128,576]{1,0:T(8,128)(2,1)S(1)} %excited_block_kernel.1.own_ref), channel_id=1, source_target_pairs={{0,1},{1,0},{2,3},{3,2},{4,5},{5,4},{6,7},{7,6},{8,9},{9,8},{10,11... | collective-permute-start | bytes 442376 | tf_op jit(solution)/shard_map/ppermute | solution.py:26
  51.2 6.4 %collective-permute-start.15 = (bf16[2,128,128]{2,1,0:T(8,128)(2,1)S(1)}, bf16[2,128,128]{2,1,0:T(8,128)(2,1)S(1)}, u32[]{:S(2)}, u32[]{:S(2)}) collective-permute-start(bf16[2,128,128]{2,1,0:T(8,128)(2,1)S(1)} %get-tuple-element.63), channel_id=1, source_target_pairs={{0,8},{1,25},{8,0},{9,17},{16,24},{17,9},{24,16},{25,1},{2,10},{3,... | collective-permute-start | bytes 196616 | tf_op jit(solution)/shard_map/ppermute | solution.py:354
  51.6 6.0 %collective-permute-start.16 = (bf16[2,128,128]{2,1,0:T(8,128)(2,1)S(1)}, bf16[2,128,128]{2,1,0:T(8,128)(2,1)S(1)}, u32[]{:S(2)}, u32[]{:S(2)}) collective-permute-start(bf16[2,128,128]{2,1,0:T(8,128)(2,1)S(1)} %get-tuple-element.64), channel_id=1, source_target_pairs={{0,16},{1,17},{8,24},{9,25},{16,0},{17,1},{24,8},{25,9},{2,18},{3,... | collective-permute-start | bytes 196616 | tf_op jit(solution)/shard_map/ppermute | solution.py:354
  52.5 5.2 %collective-permute-start.17 = (bf16[2,128,128]{2,1,0:T(8,128)(2,1)S(1)}, bf16[2,128,128]{2,1,0:T(8,128)(2,1)S(1)}, u32[]{:S(2)}, u32[]{:S(2)}) collective-permute-start(bf16[2,128,128]{2,1,0:T(8,128)(2,1)S(1)} %get-tuple-element.65), channel_id=1, source_target_pairs={{0,24},{1,9},{8,16},{9,1},{16,8},{17,25},{24,0},{25,17},{2,26},{3,... | collective-permute-start | bytes 196616 | tf_op jit(solution)/shard_map/ppermute | solution.py:354

commit v13 on v12

--- a/solution.py
+++ b/solution.py
@@ -326,7 +326,7 @@
     )
     turns = (None, crossing((1, 3)), crossing((2, 2)), crossing((3, 1)))
     got = [lax.ppermute(parts[k], ("y", "c"), turns[k]) for k in (1, 3, 2)]
-    *got, below = lax.optimization_barrier((*got, below))
+    *got, below, above = lax.optimization_barrier((*got, below, above))
     near = swapped(coef_v, "zl", 1)
     total = parts[0].astype(F32)
     for part in got:

time: 59.3 us -> 56.1 us (0.946); the launches traced: 59.2 us -> 55.1 us
  waiting for transfers between devices: 12.8 us -> 4.69 us
  starting transfers between devices: 31.9 us -> 35.9 us
    ppermute x5, waiting for transfers between devices: 8.01 us -> 1.1 us  [swapped(): return lax.ppermute(block, axis, [(i, i ^ mask) for i in range(count)])]
    ppermute x1, starting transfers between devices: 2.18 us -> 5.57 us  [local(): beside = lax.ppermute(sent, ('y', 'c'), turns[1])]
    ppermute x1, waiting for transfers between devices: 3.89 us -> 1.39 us  [local(): far = lax.ppermute(near, ALPHA, route)]
    ppermute x1, waiting for transfers between devices: 0.01 us -> 1.1 us  [local(): beside = lax.ppermute(sent, ('y', 'c'), turns[1])]
    ppermute x3, waiting for transfers between devices: 0.01 us -> 0.97 us  [local(): got = [lax.ppermute(parts[k], ('y', 'c'), turns[k]) for k in (1, 3, 2)]]
    ppermute x5, starting transfers between devices: 13.2 us -> 12.4 us  [swapped(): return lax.ppermute(block, axis, [(i, i ^ mask) for i in range(count)])]
    ppermute x1, starting transfers between devices: 0.62 us -> 1.43 us  [local(): beyond = lax.ppermute(jnp.stack([pair_v, beside]), ('y', 'c'), turns[3])]
    ppermute x2, waiting for transfers between devices: 0.78 us -> 0.04 us  [rotated(): lax.ppermute(block, axis, [(i, (i + distance) % count) for i in range(cou...]
  transfers between devices with their start and end apart: 18 -> 18, of which waited for: 5 -> 6; matrix products, arithmetic and copies ran while one was open for 2% -> 2% of each run, Pallas kernels for 19% -> 20%
where the time goes in v13:
time: 56.1 us; the launch traced here: 55.1 us
  starting transfers between devices  35.9 us (64%)
  Pallas kernels  13.2 us (24%)
  waiting for transfers between devices  4.69 us (8%)
  other arithmetic  0.93 us (2%)
    pallas_call x9, Pallas kernels, call(): pl.pallas_call(kernel, out_shape=outs, in_specs=specs, out_specs=out_spec...  13.2 us
    ppermute x5, starting transfers between devices, swapped(): return lax.ppermute(block, axis, [(i, i ^ mask) for i in range(count)])  12.4 us
    ppermute x2, starting transfers between devices, rotated(): lax.ppermute(block, axis, [(i, (i + distance) % count) for i in range(cou...  6.9 us
    ppermute x1, starting transfers between devices, local(): beside = lax.ppermute(sent, ('y', 'c'), turns[1])  5.57 us
    ppermute x3, starting transfers between devices, local(): got = [lax.ppermute(parts[k], ('y', 'c'), turns[k]) for k in (1, 3, 2)]  3.95 us
    ppermute x3, starting transfers between devices, local(): back = [lax.ppermute(out[k - 1], ('y', 'c'), turns[k]) for k in (1, 2, 3)]  3.33 us
    ppermute x1, starting transfers between devices, local(): beyond = lax.ppermute(jnp.stack([pair_v, beside]), ('y', 'c'), turns[3])  1.43 us
    ppermute x1, waiting for transfers between devices, local(): far = lax.ppermute(near, ALPHA, route)  1.39 us
  transfers between devices with their start and end apart: 18, of which 6 were waited for; matrix products, arithmetic and copies ran while one was open for 2% of the time, Pallas kernels for 20%

profile of v13, /device:TPU:1, one launch (start us, length us, event | category | flops | bytes accessed | tf_op | source)
XLA Modules:
  0.0 55.1 jit_solution(15271109262254168291)
XLA Ops:
  0.0 3.2 %collective-permute-start = (bf16[1024,128]{1,0:T(8,128)(2,1)}, bf16[1024,128]{1,0:T(8,128)(2,1)S(1)}, u32[]{:S(2)}, u32[]{:S(2)}) collective-permute-start(bf16[1024,128]{1,0:T(8,128)(2,1)} %coef_ref.1), channel_id=1, source_target_pairs={{0,1},{1,0},{2,3},{3,2},{4,5},{5,4},{6,7},{7,6},{8,9},{9,8},{10,11... | collective-permute-start | bytes 786440 | tf_op jit(solution)/shard_map/ppermute | solution.py:26
  3.2 1.0 %loaded_kernel.1 = (bf16[1024,128]{1,0:T(8,128)(2,1)S(1)}, bf16[576,128]{1,0:T(8,128)(2,1)S(1)}) custom-call(bf16[1024,128]{1,0:T(8,128)(2,1)} %coef_ref.1, bf16[576,128]{1,0:T(8,128)(2,1)} %bitcast.22), custom_call_target="tpu_custom_call" | custom-call | bytes 1048576 | tf_op jit(solution)/shard_map/loaded_kernel/pallas_call | solution.py:43
  4.3 1.3 %collective-permute-start.5 = (bf16[1024,128]{1,0:T(8,128)(2,1)S(1)}, bf16[1024,128]{1,0:T(8,128)(2,1)S(1)}, u32[]{:S(2)}, u32[]{:S(2)}) collective-permute-start(bf16[1024,128]{1,0:T(8,128)(2,1)S(1)} %get-tuple-element.40.own_ref.b2), channel_id=1, source_target_pairs={{0,2},{1,3},{2,4},{3,5},{4,6},{5,7},{6,8},{7,9},{8,10},{9,11},{10,... | collective-permute-start | bytes 786440 | tf_op jit(solution)/shard_map/ppermute | solution.py:31
  5.6 5.6 %collective-permute-start.6 = (bf16[1024,128]{1,0:T(8,128)(2,1)S(1)}, bf16[1024,128]{1,0:T(8,128)(2,1)S(1)}, u32[]{:S(2)}, u32[]{:S(2)}) collective-permute-start(bf16[1024,128]{1,0:T(8,128)(2,1)S(1)} %get-tuple-element.40.own_ref.b2), channel_id=1, source_target_pairs={{0,30},{1,31},{2,0},{3,1},{4,2},{5,3},{6,4},{7,5},{8,6},{9,7},{10,... | collective-permute-start | bytes 786440 | tf_op jit(solution)/shard_map/ppermute | solution.py:31
  11.3 1.0 %density_parts_kernel.1 = (bf16[576,128]{1,0:T(8,128)(2,1)S(1)}, bf16[576,128]{1,0:T(8,128)(2,1)S(1)}, bf16[576,128]{1,0:T(8,128)(2,1)S(1)}, bf16[576,128]{1,0:T(8,128)(2,1)S(1)}) custom-call(s32[12]{0:T(128)S(1)} %stack.60.where_ref, bf16[1024,128]{1,0:T(8,128)(2,1)S(1)} %get-tuple-element.40.own_ref.b2, ...), custom_call_target="tpu_custom_call" | custom-call | flops 150994944 | bytes 1048576 | tf_op jit(solution)/shard_map/density_parts_kernel/pallas_call | solution.py:43
  12.3 0.5 collective-permute-start.2
  12.8 3.4 %collective-permute-start.4 = (bf16[576,128]{1,0:T(8,128)(2,1)S(1)}, bf16[576,128]{1,0:T(8,128)(2,1)S(1)}, u32[]{:S(2)}, u32[]{:S(2)}) collective-permute-start(bf16[576,128]{1,0:T(8,128)(2,1)S(1)} %get-tuple-element.45), channel_id=1, source_target_pairs={{0,16},{1,17},{8,24},{9,25},{16,0},{17,1},{24,8},{25,9},{2,18},{3,... | collective-permute-start | bytes 442376 | tf_op jit(solution)/shard_map/ppermute | solution.py:328
  16.2 0.7 %pad_add_fusion.cols_ref = s32[8]{0:T(128)S(1)} fusion(s32[4]{0:T(128)} %bitcast.23, s32[4]{0:T(128)} %bitcast.24), kind=kLoop, calls=%fused_computation.4 | loop fusion | flops 8 | bytes 64 | tf_op jit(solution)/shard_map/concatenate | solution.py:310
  17.0 1.8 %staged_kernel.1 = (bf16[576,576]{1,0:T(8,128)(2,1)S(1)}, f32[128,576]{1,0:T(8,128)S(1)}, bf16[128,640]{1,0:T(8,128)(2,1)S(1)}) custom-call(s32[12]{0:T(128)S(1)} %stack.60.where_ref, s32[8]{0:T(128)S(1)} %pad_add_fusion.cols_ref, bf16[576,576]{1,0:T(8,128)(2,1)} %c_ref.1, bf16[576,1024]{1,0:T(8,128)(2,1)} %bitcast.20, bf16[128,512]{1,0:T(8,128)(2,1)} %ops_ref.3, ...), custom_call_target="tpu_custom_call" | custom-call | flops 331776 | bytes 2097152 | tf_op jit(solution)/shard_map/staged_kernel/pallas_call | solution.py:43
  18.9 4.9 %collective-permute-start.11 = (bf16[1024,128]{1,0:T(8,128)(2,1)S(1)}, bf16[1024,128]{1,0:T(8,128)(2,1)S(1)}, u32[]{:S(2)}, u32[]{:S(2)}) collective-permute-start(bf16[1024,128]{1,0:T(8,128)(2,1)S(1)} %get-tuple-element.40.own_ref.b2), channel_id=1, source_target_pairs={{0,32},{32,0},{1,33},{33,1},{2,34},{34,2},{3,35},{35,3},{4,36},{36... | collective-permute-start | bytes 786440 | tf_op jit(solution)/shard_map/ppermute | solution.py:26
  23.8 1.0 %collective-permute-done.4 = bf16[576,128]{1,0:T(8,128)(2,1)S(1)} collective-permute-done((bf16[576,128]{1,0:T(8,128)(2,1)S(1)}, bf16[576,128]{1,0:T(8,128)(2,1)S(1)}, u32[]{:S(2)}, u32[]{:S(2)}) %collective-permute-start.4) | collective-permute-done | bytes 147488 | tf_op jit(solution)/shard_map/ppermute | solution.py:328
  25.3 5.6 %collective-permute-start.8 = (bf16[576,128]{1,0:T(8,128)(2,1)S(1)}, bf16[576,128]{1,0:T(8,128)(2,1)S(1)}, u32[]{:S(2)}, u32[]{:S(2)}) collective-permute-start(bf16[576,128]{1,0:T(8,128)(2,1)S(1)} %get-tuple-element.53.po_ref.pair_ref), channel_id=1, source_target_pairs={{0,8},{1,25},{8,0},{9,17},{16,24},{17,9},{24,16},{25,1},{2,10},{3,... | collective-permute-start | bytes 442376 | tf_op jit(solution)/shard_map/ppermute | solution.py:340
  31.1 1.2 %collective-permute-start.12 = (bf16[1024,128]{1,0:T(8,128)(2,1)S(1)}, bf16[1024,128]{1,0:T(8,128)(2,1)S(1)}, u32[]{:S(2)}, u32[]{:S(2)}) collective-permute-start(bf16[1024,128]{1,0:T(8,128)(2,1)S(1)} %collective-permute-done.11.near_ref), channel_id=1, source_target_pairs={{0,64},{32,224},{64,128},{96,32},{128,192},{160,96},{192,0},{224,1... | collective-permute-start | bytes 786440 | tf_op jit(solution)/shard_map/ppermute | solution.py:337
  32.3 1.1 %collective-permute-done.8.beside_ref = bf16[576,128]{1,0:T(8,128)(2,1)S(1)} collective-permute-done((bf16[576,128]{1,0:T(8,128)(2,1)S(1)}, bf16[576,128]{1,0:T(8,128)(2,1)S(1)}, u32[]{:S(2)}, u32[]{:S(2)}) %collective-permute-start.8) | collective-permute-done | bytes 147488 | tf_op jit(solution)/shard_map/ppermute | solution.py:340
  33.5 0.7 %collective-permute-start.10 = (bf16[576,128]{1,0:T(8,128)(2,1)S(1)}, bf16[576,128]{1,0:T(8,128)(2,1)S(1)}, u32[]{:S(2)}, u32[]{:S(2)}) collective-permute-start(bf16[576,128]{1,0:T(8,128)(2,1)S(1)} %add_convert_fusion.near_ref), channel_id=1, source_target_pairs={{0,6},{1,3},{2,4},{3,1},{4,2},{5,7},{6,0},{7,5},{8,14},{9,11},{10,... | collective-permute-start | bytes 442376 | tf_op jit(solution)/shard_map/ppermute | solution.py:346
  34.2 1.4 %collective-permute-start.14 = (bf16[2,576,128]{2,1,0:T(8,128)(2,1)S(1)}, bf16[2,576,128]{2,1,0:T(8,128)(2,1)S(1)}, u32[]{:S(2)}, u32[]{:S(2)}) collective-permute-start(bf16[2,576,128]{2,1,0:T(8,128)(2,1)S(1)} %pad_maximum_fusion), channel_id=1, source_target_pairs={{0,24},{1,9},{8,16},{9,1},{16,8},{17,25},{24,0},{25,17},{2,26},{3,... | collective-permute-start | bytes 884744 | tf_op jit(solution)/shard_map/ppermute | solution.py:345
  35.6 0.5 same_spin_beta_kernel.1.start_ref
  36.1 1.4 %collective-permute-done.12.far_ref = bf16[1024,128]{1,0:T(8,128)(2,1)S(1)} collective-permute-done((bf16[1024,128]{1,0:T(8,128)(2,1)S(1)}, bf16[1024,128]{1,0:T(8,128)(2,1)S(1)}, u32[]{:S(2)}, u32[]{:S(2)}) %collective-permute-start.12) | collective-permute-done | bytes 262176 | tf_op jit(solution)/shard_map/ppermute | solution.py:337
  37.5 3.5 %same_spin_alpha_kernel.1 = (f32[1024,128]{1,0:T(8,128)S(1)}, bf16[4096,128]{1,0:T(8,128)(2,1)S(1)}) custom-call(s32[12]{0:T(128)S(1)} %stack.60.where_ref, s32[8]{0:T(128)S(1)} %pad_add_fusion.cols_ref, bf16[1024,128]{1,0:T(8,128)(2,1)S(1)} %get-tuple-element.40.own_ref.b2, bf16[1024,128]{1,0:T(8,128)(2,1)S(1)} %collective-permute-done.11.near_ref, ...), custom_call_target="tpu_custom_call" | custom-call | flops 536870912 | bytes 5242880 | tf_op jit(solution)/shard_map/same_spin_alpha_kernel/pallas_call | solution.py:43
  41.5 4.1 %collective-permute-start.13 = (bf16[128,576]{1,0:T(8,128)(2,1)S(1)}, bf16[128,576]{1,0:T(8,128)(2,1)S(1)}, u32[]{:S(2)}, u32[]{:S(2)}) collective-permute-start(bf16[128,576]{1,0:T(8,128)(2,1)S(1)} %excited_block_kernel.1.own_ref), channel_id=1, source_target_pairs={{0,1},{1,0},{2,3},{3,2},{4,5},{5,4},{6,7},{7,6},{8,9},{9,8},{10,11... | collective-permute-start | bytes 442376 | tf_op jit(solution)/shard_map/ppermute | solution.py:26
  45.6 1.0 %collective-permute-done.13.mate_ref = bf16[128,576]{1,0:T(8,128)(2,1)S(1)} collective-permute-done((bf16[128,576]{1,0:T(8,128)(2,1)S(1)}, bf16[128,576]{1,0:T(8,128)(2,1)S(1)}, u32[]{:S(2)}, u32[]{:S(2)}) %collective-permute-start.13) | collective-permute-done | bytes 147488 | tf_op jit(solution)/shard_map/ppermute | solution.py:26
  47.4 3.0 %collective-permute-start.17 = (bf16[2,128,128]{2,1,0:T(8,128)(2,1)S(1)}, bf16[2,128,128]{2,1,0:T(8,128)(2,1)S(1)}, u32[]{:S(2)}, u32[]{:S(2)}) collective-permute-start(bf16[2,128,128]{2,1,0:T(8,128)(2,1)S(1)} %get-tuple-element.67), channel_id=1, source_target_pairs={{0,24},{1,9},{8,16},{9,1},{16,8},{17,25},{24,0},{25,17},{2,26},{3,... | collective-permute-start | bytes 196616 | tf_op jit(solution)/shard_map/ppermute | solution.py:354
  50.5 3.0 %rest_of_alpha_kernel.1.same_ref = f32[1024,128]{1,0:T(8,128)S(1)} custom-call(bf16[4096,128]{1,0:T(8,128)(2,1)S(1)} %get-tuple-element.68.picked, bf16[1024,4096]{1,0:T(8,128)(2,1)} %ops_ref.5, f32[1024,128]{1,0:T(8,128)S(1)} %get-tuple-element.69.start_ref), custom_call_target="tpu_custom_call" | custom-call | flops 536870912 | bytes 5242880 | tf_op jit(solution)/shard_map/rest_of_alpha_kernel/pallas_call | solution.py:43
  53.6 1.4 %finished_kernel.1 = f32[1024,128]{1,0:T(8,128)} custom-call(s32[12]{0:T(128)S(1)} %stack.60.where_ref, f32[1024,128]{1,0:T(8,128)S(1)} %rest_of_alpha_kernel.1.same_ref, f32[2,128,128]{2,1,0:T(8,128)S(1)} %get-tuple-element.71.m0, bf16[2,128,128]{2,1,0:T(8,128)(2,1)S(1)} %collective-permute-done.15.m1, bf16[2,128,128]{2,1,0:T(8,128)(2,1)S(1)} %collective-permute-done.16.m2, ...), custom_call_target="tpu_custom_call" | custom-call | flops 262144 | bytes 2097152 | tf_op jit(solution)/shard_map/finished_kernel/pallas_call | solution.py:43
  (29 shorter events, 2.2 us)
Async XLA Ops:
  0.0 11.3 %collective-permute-start = (bf16[1024,128]{1,0:T(8,128)(2,1)}, bf16[1024,128]{1,0:T(8,128)(2,1)S(1)}, u32[]{:S(2)}, u32[]{:S(2)}) collective-permute-start(bf16[1024,128]{1,0:T(8,128)(2,1)} %coef_ref.1), channel_id=1, source_target_pairs={{0,1},{1,0},{2,3},{3,2},{4,5},{5,4},{6,7},{7,6},{8,9},{9,8},{10,11... | collective-permute-start | bytes 786440 | tf_op jit(solution)/shard_map/ppermute | solution.py:26
  3.2 8.0 %collective-permute-start.1 = (bf16[576,128]{1,0:T(8,128)(2,1)}, bf16[576,128]{1,0:T(8,128)(2,1)S(1)}, u32[]{:S(2)}, u32[]{:S(2)}) collective-permute-start(bf16[576,128]{1,0:T(8,128)(2,1)} %bitcast.21), channel_id=1, source_target_pairs={{0,1},{1,0},{2,3},{3,2},{4,5},{5,4},{6,7},{7,6},{8,9},{9,8},{10,11... | collective-permute-start | bytes 442376 | tf_op jit(solution)/shard_map/ppermute | solution.py:26
  4.3 14.6 %collective-permute-start.5 = (bf16[1024,128]{1,0:T(8,128)(2,1)S(1)}, bf16[1024,128]{1,0:T(8,128)(2,1)S(1)}, u32[]{:S(2)}, u32[]{:S(2)}) collective-permute-start(bf16[1024,128]{1,0:T(8,128)(2,1)S(1)} %get-tuple-element.40.own_ref.b2), channel_id=1, source_target_pairs={{0,2},{1,3},{2,4},{3,5},{4,6},{5,7},{6,8},{7,9},{8,10},{9,11},{10,... | collective-permute-start | bytes 786440 | tf_op jit(solution)/shard_map/ppermute | solution.py:31
  5.6 18.2 %collective-permute-start.6 = (bf16[1024,128]{1,0:T(8,128)(2,1)S(1)}, bf16[1024,128]{1,0:T(8,128)(2,1)S(1)}, u32[]{:S(2)}, u32[]{:S(2)}) collective-permute-start(bf16[1024,128]{1,0:T(8,128)(2,1)S(1)} %get-tuple-element.40.own_ref.b2), channel_id=1, source_target_pairs={{0,30},{1,31},{2,0},{3,1},{4,2},{5,3},{6,4},{7,5},{8,6},{9,7},{10,... | collective-permute-start | bytes 786440 | tf_op jit(solution)/shard_map/ppermute | solution.py:31
  12.3 11.5 %collective-permute-start.2 = (bf16[576,128]{1,0:T(8,128)(2,1)S(1)}, bf16[576,128]{1,0:T(8,128)(2,1)S(1)}, u32[]{:S(2)}, u32[]{:S(2)}) collective-permute-start(bf16[576,128]{1,0:T(8,128)(2,1)S(1)} %get-tuple-element.43), channel_id=1, source_target_pairs={{0,8},{1,25},{8,0},{9,17},{16,24},{17,9},{24,16},{25,1},{2,10},{3,... | collective-permute-start | bytes 442376 | tf_op jit(solution)/shard_map/ppermute | solution.py:328
  12.8 11.0 %collective-permute-start.3 = (bf16[576,128]{1,0:T(8,128)(2,1)S(1)}, bf16[576,128]{1,0:T(8,128)(2,1)S(1)}, u32[]{:S(2)}, u32[]{:S(2)}) collective-permute-start(bf16[576,128]{1,0:T(8,128)(2,1)S(1)} %get-tuple-element.44), channel_id=1, source_target_pairs={{0,24},{1,9},{8,16},{9,1},{16,8},{17,25},{24,0},{25,17},{2,26},{3,... | collective-permute-start | bytes 442376 | tf_op jit(solution)/shard_map/ppermute | solution.py:328
  12.8 11.9 %collective-permute-start.4 = (bf16[576,128]{1,0:T(8,128)(2,1)S(1)}, bf16[576,128]{1,0:T(8,128)(2,1)S(1)}, u32[]{:S(2)}, u32[]{:S(2)}) collective-permute-start(bf16[576,128]{1,0:T(8,128)(2,1)S(1)} %get-tuple-element.45), channel_id=1, source_target_pairs={{0,16},{1,17},{8,24},{9,25},{16,0},{17,1},{24,8},{25,9},{2,18},{3,... | collective-permute-start | bytes 442376 | tf_op jit(solution)/shard_map/ppermute | solution.py:328
  18.9 12.2 %collective-permute-start.11 = (bf16[1024,128]{1,0:T(8,128)(2,1)S(1)}, bf16[1024,128]{1,0:T(8,128)(2,1)S(1)}, u32[]{:S(2)}, u32[]{:S(2)}) collective-permute-start(bf16[1024,128]{1,0:T(8,128)(2,1)S(1)} %get-tuple-element.40.own_ref.b2), channel_id=1, source_target_pairs={{0,32},{32,0},{1,33},{33,1},{2,34},{34,2},{3,35},{35,3},{4,36},{36... | collective-permute-start | bytes 786440 | tf_op jit(solution)/shard_map/ppermute | solution.py:26
  24.9 8.6 %collective-permute-start.7 = (bf16[576,128]{1,0:T(8,128)(2,1)S(1)}, bf16[576,128]{1,0:T(8,128)(2,1)S(1)}, u32[]{:S(2)}, u32[]{:S(2)}) collective-permute-start(bf16[576,128]{1,0:T(8,128)(2,1)S(1)} %add_convert_fusion.1), channel_id=1, source_target_pairs={{0,2},{1,7},{2,0},{3,5},{4,6},{5,3},{6,4},{7,1},{8,10},{9,15},{10,... | collective-permute-start | bytes 442376 | tf_op jit(solution)/shard_map/ppermute | solution.py:338
  25.3 8.1 %collective-permute-start.8 = (bf16[576,128]{1,0:T(8,128)(2,1)S(1)}, bf16[576,128]{1,0:T(8,128)(2,1)S(1)}, u32[]{:S(2)}, u32[]{:S(2)}) collective-permute-start(bf16[576,128]{1,0:T(8,128)(2,1)S(1)} %get-tuple-element.53.po_ref.pair_ref), channel_id=1, source_target_pairs={{0,8},{1,25},{8,0},{9,17},{16,24},{17,9},{24,16},{25,1},{2,10},{3,... | collective-permute-start | bytes 442376 | tf_op jit(solution)/shard_map/ppermute | solution.py:340
  30.9 2.6 %collective-permute-start.9 = (bf16[1024,128]{1,0:T(8,128)(2,1)S(1)}, bf16[1024,128]{1,0:T(8,128)(2,1)S(1)}, u32[]{:S(2)}, u32[]{:S(2)}) collective-permute-start(bf16[1024,128]{1,0:T(8,128)(2,1)S(1)} %broadcast_select_fusion), channel_id=1, source_target_pairs={{0,1},{1,0},{2,3},{3,2},{4,5},{5,4},{6,7},{7,6},{8,9},{9,8},{10,11... | collective-permute-start | bytes 786440 | tf_op jit(solution)/shard_map/ppermute | solution.py:26
  31.1 6.5 %collective-permute-start.12 = (bf16[1024,128]{1,0:T(8,128)(2,1)S(1)}, bf16[1024,128]{1,0:T(8,128)(2,1)S(1)}, u32[]{:S(2)}, u32[]{:S(2)}) collective-permute-start(bf16[1024,128]{1,0:T(8,128)(2,1)S(1)} %collective-permute-done.11.near_ref), channel_id=1, source_target_pairs={{0,64},{32,224},{64,128},{96,32},{128,192},{160,96},{192,0},{224,1... | collective-permute-start | bytes 786440 | tf_op jit(solution)/shard_map/ppermute | solution.py:337
  33.5 7.6 %collective-permute-start.10 = (bf16[576,128]{1,0:T(8,128)(2,1)S(1)}, bf16[576,128]{1,0:T(8,128)(2,1)S(1)}, u32[]{:S(2)}, u32[]{:S(2)}) collective-permute-start(bf16[576,128]{1,0:T(8,128)(2,1)S(1)} %add_convert_fusion.near_ref), channel_id=1, source_target_pairs={{0,6},{1,3},{2,4},{3,1},{4,2},{5,7},{6,0},{7,5},{8,14},{9,11},{10,... | collective-permute-start | bytes 442376 | tf_op jit(solution)/shard_map/ppermute | solution.py:346
  34.2 11.4 %collective-permute-start.14 = (bf16[2,576,128]{2,1,0:T(8,128)(2,1)S(1)}, bf16[2,576,128]{2,1,0:T(8,128)(2,1)S(1)}, u32[]{:S(2)}, u32[]{:S(2)}) collective-permute-start(bf16[2,576,128]{2,1,0:T(8,128)(2,1)S(1)} %pad_maximum_fusion), channel_id=1, source_target_pairs={{0,24},{1,9},{8,16},{9,1},{16,8},{17,25},{24,0},{25,17},{2,26},{3,... | collective-permute-start | bytes 884744 | tf_op jit(solution)/shard_map/ppermute | solution.py:345
  41.1 12.5 %copy-start = (f32[1024,128]{1,0:T(8,128)S(1)}, f32[1024,128]{1,0:T(8,128)}, u32[]{:S(2)}) copy-start(f32[1024,128]{1,0:T(8,128)} %den_ref.1) | copy-start | bytes 1572868
  41.5 5.1 %collective-permute-start.13 = (bf16[128,576]{1,0:T(8,128)(2,1)S(1)}, bf16[128,576]{1,0:T(8,128)(2,1)S(1)}, u32[]{:S(2)}, u32[]{:S(2)}) collective-permute-start(bf16[128,576]{1,0:T(8,128)(2,1)S(1)} %excited_block_kernel.1.own_ref), channel_id=1, source_target_pairs={{0,1},{1,0},{2,3},{3,2},{4,5},{5,4},{6,7},{7,6},{8,9},{9,8},{10,11... | collective-permute-start | bytes 442376 | tf_op jit(solution)/shard_map/ppermute | solution.py:26
  47.1 6.4 %collective-permute-start.15 = (bf16[2,128,128]{2,1,0:T(8,128)(2,1)S(1)}, bf16[2,128,128]{2,1,0:T(8,128)(2,1)S(1)}, u32[]{:S(2)}, u32[]{:S(2)}) collective-permute-start(bf16[2,128,128]{2,1,0:T(8,128)(2,1)S(1)} %get-tuple-element.65), channel_id=1, source_target_pairs={{0,8},{1,25},{8,0},{9,17},{16,24},{17,9},{24,16},{25,1},{2,10},{3,... | collective-permute-start | bytes 196616 | tf_op jit(solution)/shard_map/ppermute | solution.py:354
  47.2 6.3 %collective-permute-start.16 = (bf16[2,128,128]{2,1,0:T(8,128)(2,1)S(1)}, bf16[2,128,128]{2,1,0:T(8,128)(2,1)S(1)}, u32[]{:S(2)}, u32[]{:S(2)}) collective-permute-start(bf16[2,128,128]{2,1,0:T(8,128)(2,1)S(1)} %get-tuple-element.66), channel_id=1, source_target_pairs={{0,16},{1,17},{8,24},{9,25},{16,0},{17,1},{24,8},{25,9},{2,18},{3,... | collective-permute-start | bytes 196616 | tf_op jit(solution)/shard_map/ppermute | solution.py:354
  47.4 6.1 %collective-permute-start.17 = (bf16[2,128,128]{2,1,0:T(8,128)(2,1)S(1)}, bf16[2,128,128]{2,1,0:T(8,128)(2,1)S(1)}, u32[]{:S(2)}, u32[]{:S(2)}) collective-permute-start(bf16[2,128,128]{2,1,0:T(8,128)(2,1)S(1)} %get-tuple-element.67), channel_id=1, source_target_pairs={{0,24},{1,9},{8,16},{9,1},{16,8},{17,25},{24,0},{25,17},{2,26},{3,... | collective-permute-start | bytes 196616 | tf_op jit(solution)/shard_map/ppermute | solution.py:354

commit v14 on v13

--- a/solution.py
+++ b/solution.py
@@ -90,11 +90,17 @@
         for k, out in enumerate(outs):
             rows = block_rows(where_ref, k, width)
             right = jnp.concatenate([own_ref[rows, :], mate_ref[rows, :]], axis=1)
-            out[...] = dot(left, right, ((1,), (1,))).astype(BF16)
-
+            part = dot(left, right, ((1,), (1,))).astype(BF16)
+            if k == 1:
+                out[0] = part
+                out[1] = po_ref[...]
+            else:
+                out[...] = part
+
+    one = shape((pairs, width))
     return call(
         density_parts_kernel,
-        [shape((pairs, width))] * 4,
+        [one, shape((2, pairs, width)), one, one],
         (where, own, mate, pair_own, pair_mate),
         [SMEM] + [VMEM] * 4,
         (16 * pairs * width * width, 1 * MIB),
@@ -325,9 +331,13 @@
         where, cols, pair_coupling, pair_alpha.T, beta_ops, parts[0]
     )
     turns = (None, crossing((1, 3)), crossing((2, 2)), crossing((3, 1)))
-    got = [lax.ppermute(parts[k], ("y", "c"), turns[k]) for k in (1, 3, 2)]
-    *got, below, above = lax.optimization_barrier((*got, below, above))
+    both = lax.ppermute(parts[1], ("y", "c"), turns[1])
+    other = lax.ppermute(parts[3], ("y", "c"), turns[3])
+    across, other = lax.optimization_barrier((parts[2], other))
+    got = [both, other, lax.ppermute(across, ("y", "c"), turns[2])]
     near = swapped(coef_v, "zl", 1)
+    *got, below, above, near = lax.optimization_barrier((*got, below, above, near))
+    got[0], beside = got[0][0], got[0][1]
     total = parts[0].astype(F32)
     for part in got:
         total = total + part.astype(F32)
@@ -336,10 +346,7 @@
 
     far = lax.ppermute(near, ALPHA, route)
     first = lax.ppermute(total, ("zh", "c"), turns[1])
-    sent, _ = lax.optimization_barrier((pair_v, total))
-    beside = lax.ppermute(sent, ("y", "c"), turns[1])
     crossed = swapped(jnp.where(core == 0, above, below), "c", 1)
-    first, beside = lax.optimization_barrier((first, beside))
     total = (total.astype(F32) + first.astype(F32)).astype(BF16)
     total, crossed = lax.optimization_barrier((total, crossed))
     beyond = lax.ppermute(jnp.stack([pair_v, beside]), ("y", "c"), turns[3])

time: 56.1 us -> 60.7 us (1.082)
  waiting for transfers between devices: 4.69 us -> 20.5 us
  starting transfers between devices: 35.9 us -> 24.6 us
    ppermute x2, waiting for transfers between devices: 0.04 us -> 7.93 us  [rotated(): lax.ppermute(block, axis, [(i, (i + distance) % count) for i in range(cou...]
    ppermute x4 -> x3, starting transfers between devices: 9.51 us -> 2.89 us  [the longest x1 1.45 us: local(): both = lax.ppermute(parts[1], ('y', 'c'), turns[1])]
    ppermute x5, starting transfers between devices: 12.4 us -> 6.19 us  [swapped(): return lax.ppermute(block, axis, [(i, i ^ mask) for i in range(count)])]
    ppermute x5, waiting for transfers between devices: 1.1 us -> 6.98 us  [swapped(): return lax.ppermute(block, axis, [(i, i ^ mask) for i in range(count)])]
    ppermute x1, waiting for transfers between devices: 0.01 us -> 3.43 us  [local(): first = lax.ppermute(total, ('zh', 'c'), turns[1])]
    ppermute x4 -> x3, waiting for transfers between devices: 2.07 us -> 0.01 us  [the longest x1 0.01 us: local(): other = lax.ppermute(parts[3], ('y', 'c'), turns[3])]
    ppermute x1, starting transfers between devices: 0.45 us -> 2.02 us  [local(): first = lax.ppermute(total, ('zh', 'c'), turns[1])]
    ppermute x1, starting transfers between devices: 0.7 us -> 1.88 us  [local(): second = lax.ppermute(total, ('zh', 'c'), turns[3])]
  transfers between devices with their start and end apart: 18 -> 17, of which waited for: 6 -> 8; matrix products, arithmetic and copies ran while one was open for 2% -> 2% of each run, Pallas kernels for 20% -> 17%
where the time goes in v14:
time: 60.7 us; the launch traced here: 59.6 us
  starting transfers between devices  24.6 us (41%)
  waiting for transfers between devices  20.5 us (34%)
  Pallas kernels  13.2 us (22%)
  other arithmetic  0.94 us (2%)
    pallas_call x9, Pallas kernels, call(): pl.pallas_call(kernel, out_shape=outs, in_specs=specs, out_specs=out_spec...  13.2 us
    ppermute x2, waiting for transfers between devices, rotated(): lax.ppermute(block, axis, [(i, (i + distance) % count) for i in range(cou...  7.93 us
    ppermute x5, waiting for transfers between devices, swapped(): return lax.ppermute(block, axis, [(i, i ^ mask) for i in range(count)])  6.98 us
    ppermute x2, starting transfers between devices, rotated(): lax.ppermute(block, axis, [(i, (i + distance) % count) for i in range(cou...  6.51 us
    ppermute x5, starting transfers between devices, swapped(): return lax.ppermute(block, axis, [(i, i ^ mask) for i in range(count)])  6.19 us
    ppermute x1, waiting for transfers between devices, local(): first = lax.ppermute(total, ('zh', 'c'), turns[1])  3.43 us
    ppermute x3, starting transfers between devices, local(): back = [lax.ppermute(out[k - 1], ('y', 'c'), turns[k]) for k in (1, 2, 3)]  3.34 us
    ppermute x1, starting transfers between devices, local(): first = lax.ppermute(total, ('zh', 'c'), turns[1])  2.02 us
  transfers between devices with their start and end apart: 17, of which 8 were waited for; matrix products, arithmetic and copies ran while one was open for 2% of the time, Pallas kernels for 17%

profile of v14, /device:TPU:1, one launch (start us, length us, event | category | flops | bytes accessed | tf_op | source)
XLA Modules:
  0.0 59.6 jit_solution(6215659820139985506)
XLA Ops:
  0.0 3.2 %collective-permute-start = (bf16[1024,128]{1,0:T(8,128)(2,1)}, bf16[1024,128]{1,0:T(8,128)(2,1)S(1)}, u32[]{:S(2)}, u32[]{:S(2)}) collective-permute-start(bf16[1024,128]{1,0:T(8,128)(2,1)} %coef_ref.1), channel_id=1, source_target_pairs={{0,1},{1,0},{2,3},{3,2},{4,5},{5,4},{6,7},{7,6},{8,9},{9,8},{10,11... | collective-permute-start | bytes 786440 | tf_op jit(solution)/shard_map/ppermute | solution.py:26
  3.2 1.0 %loaded_kernel.1 = (bf16[1024,128]{1,0:T(8,128)(2,1)S(1)}, bf16[576,128]{1,0:T(8,128)(2,1)S(1)}) custom-call(bf16[1024,128]{1,0:T(8,128)(2,1)} %coef_ref.1, bf16[576,128]{1,0:T(8,128)(2,1)} %bitcast.25), custom_call_target="tpu_custom_call" | custom-call | bytes 1048576 | tf_op jit(solution)/shard_map/loaded_kernel/pallas_call | solution.py:43
  4.8 1.0 %density_parts_kernel.1 = (bf16[576,128]{1,0:T(8,128)(2,1)S(1)}, bf16[2,576,128]{2,1,0:T(8,128)(2,1)S(1)}, bf16[576,128]{1,0:T(8,128)(2,1)S(1)}, bf16[576,128]{1,0:T(8,128)(2,1)S(1)}) custom-call(s32[12]{0:T(128)S(1)} %stack.57.where_ref, bf16[1024,128]{1,0:T(8,128)(2,1)S(1)} %get-tuple-element.40.own_ref.b2, ...), custom_call_target="tpu_custom_call" | custom-call | flops 150994944 | bytes 1048576 | tf_op jit(solution)/shard_map/density_parts_kernel/pallas_call | solution.py:43
  5.9 1.5 %collective-permute-start.2 = (bf16[2,576,128]{2,1,0:T(8,128)(2,1)S(1)}, bf16[2,576,128]{2,1,0:T(8,128)(2,1)S(1)}, u32[]{:S(2)}, u32[]{:S(2)}) collective-permute-start(bf16[2,576,128]{2,1,0:T(8,128)(2,1)S(1)} %get-tuple-element.43), channel_id=1, source_target_pairs={{0,8},{1,25},{8,0},{9,17},{16,24},{17,9},{24,16},{25,1},{2,10},{3,... | collective-permute-start | bytes 884744 | tf_op jit(solution)/shard_map/ppermute | solution.py:334
  7.4 3.0 %collective-permute-start.5 = (bf16[1024,128]{1,0:T(8,128)(2,1)S(1)}, bf16[1024,128]{1,0:T(8,128)(2,1)S(1)}, u32[]{:S(2)}, u32[]{:S(2)}) collective-permute-start(bf16[1024,128]{1,0:T(8,128)(2,1)S(1)} %get-tuple-element.40.own_ref.b2), channel_id=1, source_target_pairs={{0,2},{1,3},{2,4},{3,5},{4,6},{5,7},{6,8},{7,9},{8,10},{9,11},{10,... | collective-permute-start | bytes 786440 | tf_op jit(solution)/shard_map/ppermute | solution.py:31
  10.4 3.5 %collective-permute-start.6 = (bf16[1024,128]{1,0:T(8,128)(2,1)S(1)}, bf16[1024,128]{1,0:T(8,128)(2,1)S(1)}, u32[]{:S(2)}, u32[]{:S(2)}) collective-permute-start(bf16[1024,128]{1,0:T(8,128)(2,1)S(1)} %get-tuple-element.40.own_ref.b2), channel_id=1, source_target_pairs={{0,30},{1,31},{2,0},{3,1},{4,2},{5,3},{6,4},{7,5},{8,6},{9,7},{10,... | collective-permute-start | bytes 786440 | tf_op jit(solution)/shard_map/ppermute | solution.py:31
  14.7 1.3 %collective-permute-start.4 = (bf16[576,128]{1,0:T(8,128)(2,1)S(1)}, bf16[576,128]{1,0:T(8,128)(2,1)S(1)}, u32[]{:S(2)}, u32[]{:S(2)}) collective-permute-start(bf16[576,128]{1,0:T(8,128)(2,1)S(1)} %get-tuple-element.47), channel_id=1, source_target_pairs={{0,16},{1,17},{8,24},{9,25},{16,0},{17,1},{24,8},{25,9},{2,18},{3,... | collective-permute-start | bytes 442376 | tf_op jit(solution)/shard_map/ppermute | solution.py:337
  16.8 1.8 %staged_kernel.1 = (bf16[576,576]{1,0:T(8,128)(2,1)S(1)}, f32[128,576]{1,0:T(8,128)S(1)}, bf16[128,640]{1,0:T(8,128)(2,1)S(1)}) custom-call(s32[12]{0:T(128)S(1)} %stack.57.where_ref, s32[8]{0:T(128)S(1)} %pad_add_fusion.cols_ref, bf16[576,576]{1,0:T(8,128)(2,1)} %c_ref.1, bf16[576,1024]{1,0:T(8,128)(2,1)} %bitcast.23, bf16[128,512]{1,0:T(8,128)(2,1)} %ops_ref.3, ...), custom_call_target="tpu_custom_call" | custom-call | flops 331776 | bytes 2097152 | tf_op jit(solution)/shard_map/staged_kernel/pallas_call | solution.py:43
  18.7 3.2 %collective-permute-done.5.b0 = bf16[1024,128]{1,0:T(8,128)(2,1)S(1)} collective-permute-done((bf16[1024,128]{1,0:T(8,128)(2,1)S(1)}, bf16[1024,128]{1,0:T(8,128)(2,1)S(1)}, u32[]{:S(2)}, u32[]{:S(2)}) %collective-permute-start.5) | collective-permute-done | bytes 262176 | tf_op jit(solution)/shard_map/ppermute | solution.py:31
  21.8 4.7 %collective-permute-done.6.b4 = bf16[1024,128]{1,0:T(8,128)(2,1)S(1)} collective-permute-done((bf16[1024,128]{1,0:T(8,128)(2,1)S(1)}, bf16[1024,128]{1,0:T(8,128)(2,1)S(1)}, u32[]{:S(2)}, u32[]{:S(2)}) %collective-permute-start.6) | collective-permute-done | bytes 262176 | tf_op jit(solution)/shard_map/ppermute | solution.py:31
  26.6 5.5 %collective-permute-done.7.near_ref = bf16[1024,128]{1,0:T(8,128)(2,1)S(1)} collective-permute-done((bf16[1024,128]{1,0:T(8,128)(2,1)S(1)}, bf16[1024,128]{1,0:T(8,128)(2,1)S(1)}, u32[]{:S(2)}, u32[]{:S(2)}) %collective-permute-start.7) | collective-permute-done | bytes 262176 | tf_op jit(solution)/shard_map/ppermute | solution.py:26
  32.1 1.1 %collective-permute-start.9 = (bf16[1024,128]{1,0:T(8,128)(2,1)S(1)}, bf16[1024,128]{1,0:T(8,128)(2,1)S(1)}, u32[]{:S(2)}, u32[]{:S(2)}) collective-permute-start(bf16[1024,128]{1,0:T(8,128)(2,1)S(1)} %broadcast_select_fusion), channel_id=1, source_target_pairs={{0,1},{1,0},{2,3},{3,2},{4,5},{5,4},{6,7},{7,6},{8,9},{9,8},{10,11... | collective-permute-start | bytes 786440 | tf_op jit(solution)/shard_map/ppermute | solution.py:26
  33.4 2.0 %collective-permute-start.8 = (bf16[576,128]{1,0:T(8,128)(2,1)S(1)}, bf16[576,128]{1,0:T(8,128)(2,1)S(1)}, u32[]{:S(2)}, u32[]{:S(2)}) collective-permute-start(bf16[576,128]{1,0:T(8,128)(2,1)S(1)} %fusion.2), channel_id=1, source_target_pairs={{0,2},{1,7},{2,0},{3,5},{4,6},{5,3},{6,4},{7,1},{8,10},{9,15},{10,... | collective-permute-start | bytes 442376 | tf_op jit(solution)/shard_map/ppermute | solution.py:348
  35.4 1.3 %collective-permute-start.11 = (bf16[1024,128]{1,0:T(8,128)(2,1)S(1)}, bf16[1024,128]{1,0:T(8,128)(2,1)S(1)}, u32[]{:S(2)}, u32[]{:S(2)}) collective-permute-start(bf16[1024,128]{1,0:T(8,128)(2,1)S(1)} %collective-permute-done.7.near_ref), channel_id=1, source_target_pairs={{0,64},{32,224},{64,128},{96,32},{128,192},{160,96},{192,0},{224,1... | collective-permute-start | bytes 786440 | tf_op jit(solution)/shard_map/ppermute | solution.py:347
  36.7 3.4 %collective-permute-done.8 = bf16[576,128]{1,0:T(8,128)(2,1)S(1)} collective-permute-done((bf16[576,128]{1,0:T(8,128)(2,1)S(1)}, bf16[576,128]{1,0:T(8,128)(2,1)S(1)}, u32[]{:S(2)}, u32[]{:S(2)}) %collective-permute-start.8) | collective-permute-done | bytes 147488 | tf_op jit(solution)/shard_map/ppermute | solution.py:348
  40.2 1.9 %collective-permute-start.10 = (bf16[576,128]{1,0:T(8,128)(2,1)S(1)}, bf16[576,128]{1,0:T(8,128)(2,1)S(1)}, u32[]{:S(2)}, u32[]{:S(2)}) collective-permute-start(bf16[576,128]{1,0:T(8,128)(2,1)S(1)} %add_convert_fusion.near_ref), channel_id=1, source_target_pairs={{0,6},{1,3},{2,4},{3,1},{4,2},{5,7},{6,0},{7,5},{8,14},{9,11},{10,... | collective-permute-start | bytes 442376 | tf_op jit(solution)/shard_map/ppermute | solution.py:353
  43.0 1.3 %collective-permute-done.11.far_ref = bf16[1024,128]{1,0:T(8,128)(2,1)S(1)} collective-permute-done((bf16[1024,128]{1,0:T(8,128)(2,1)S(1)}, bf16[1024,128]{1,0:T(8,128)(2,1)S(1)}, u32[]{:S(2)}, u32[]{:S(2)}) %collective-permute-start.11) | collective-permute-done | bytes 262176 | tf_op jit(solution)/shard_map/ppermute | solution.py:347
  44.3 3.5 %same_spin_alpha_kernel.1 = (f32[1024,128]{1,0:T(8,128)S(1)}, bf16[4096,128]{1,0:T(8,128)(2,1)S(1)}) custom-call(s32[12]{0:T(128)S(1)} %stack.57.where_ref, s32[8]{0:T(128)S(1)} %pad_add_fusion.cols_ref, bf16[1024,128]{1,0:T(8,128)(2,1)S(1)} %get-tuple-element.40.own_ref.b2, bf16[1024,128]{1,0:T(8,128)(2,1)S(1)} %collective-permute-done.7.near_ref, ...), custom_call_target="tpu_custom_call" | custom-call | flops 536870912 | bytes 5242880 | tf_op jit(solution)/shard_map/same_spin_alpha_kernel/pallas_call | solution.py:43
  48.3 1.0 %collective-permute-start.12 = (bf16[128,576]{1,0:T(8,128)(2,1)S(1)}, bf16[128,576]{1,0:T(8,128)(2,1)S(1)}, u32[]{:S(2)}, u32[]{:S(2)}) collective-permute-start(bf16[128,576]{1,0:T(8,128)(2,1)S(1)} %excited_block_kernel.1.own_ref), channel_id=1, source_target_pairs={{0,1},{1,0},{2,3},{3,2},{4,5},{5,4},{6,7},{7,6},{8,9},{9,8},{10,11... | collective-permute-start | bytes 442376 | tf_op jit(solution)/shard_map/ppermute | solution.py:26
  49.3 1.0 %collective-permute-done.12.mate_ref = bf16[128,576]{1,0:T(8,128)(2,1)S(1)} collective-permute-done((bf16[128,576]{1,0:T(8,128)(2,1)S(1)}, bf16[128,576]{1,0:T(8,128)(2,1)S(1)}, u32[]{:S(2)}, u32[]{:S(2)}) %collective-permute-start.12) | collective-permute-done | bytes 147488 | tf_op jit(solution)/shard_map/ppermute | solution.py:26
  50.8 2.0 %collective-permute-start.14 = (bf16[2,128,128]{2,1,0:T(8,128)(2,1)S(1)}, bf16[2,128,128]{2,1,0:T(8,128)(2,1)S(1)}, u32[]{:S(2)}, u32[]{:S(2)}) collective-permute-start(bf16[2,128,128]{2,1,0:T(8,128)(2,1)S(1)} %get-tuple-element.65), channel_id=1, source_target_pairs={{0,8},{1,25},{8,0},{9,17},{16,24},{17,9},{24,16},{25,1},{2,10},{3,... | collective-permute-start | bytes 196616 | tf_op jit(solution)/shard_map/ppermute | solution.py:361
  52.9 1.3 %collective-permute-start.16 = (bf16[2,128,128]{2,1,0:T(8,128)(2,1)S(1)}, bf16[2,128,128]{2,1,0:T(8,128)(2,1)S(1)}, u32[]{:S(2)}, u32[]{:S(2)}) collective-permute-start(bf16[2,128,128]{2,1,0:T(8,128)(2,1)S(1)} %get-tuple-element.67), channel_id=1, source_target_pairs={{0,24},{1,9},{8,16},{9,1},{16,8},{17,25},{24,0},{25,17},{2,26},{3,... | collective-permute-start | bytes 196616 | tf_op jit(solution)/shard_map/ppermute | solution.py:361
  54.2 3.0 %rest_of_alpha_kernel.1.same_ref = f32[1024,128]{1,0:T(8,128)S(1)} custom-call(bf16[4096,128]{1,0:T(8,128)(2,1)S(1)} %get-tuple-element.68.picked, bf16[1024,4096]{1,0:T(8,128)(2,1)} %ops_ref.5, f32[1024,128]{1,0:T(8,128)S(1)} %get-tuple-element.69.start_ref), custom_call_target="tpu_custom_call" | custom-call | flops 536870912 | bytes 5242880 | tf_op jit(solution)/shard_map/rest_of_alpha_kernel/pallas_call | solution.py:43
  58.0 1.4 %finished_kernel.1 = f32[1024,128]{1,0:T(8,128)} custom-call(s32[12]{0:T(128)S(1)} %stack.57.where_ref, f32[1024,128]{1,0:T(8,128)S(1)} %rest_of_alpha_kernel.1.same_ref, f32[2,128,128]{2,1,0:T(8,128)S(1)} %get-tuple-element.71.m0, bf16[2,128,128]{2,1,0:T(8,128)(2,1)S(1)} %collective-permute-done.14.m1, bf16[2,128,128]{2,1,0:T(8,128)(2,1)S(1)} %collective-permute-done.15.m2, ...), custom_call_target="tpu_custom_call" | custom-call | flops 262144 | bytes 2097152 | tf_op jit(solution)/shard_map/finished_kernel/pallas_call | solution.py:43
  (28 shorter events, 5.1 us)
Async XLA Ops:
  0.0 4.8 %collective-permute-start = (bf16[1024,128]{1,0:T(8,128)(2,1)}, bf16[1024,128]{1,0:T(8,128)(2,1)S(1)}, u32[]{:S(2)}, u32[]{:S(2)}) collective-permute-start(bf16[1024,128]{1,0:T(8,128)(2,1)} %coef_ref.1), channel_id=1, source_target_pairs={{0,1},{1,0},{2,3},{3,2},{4,5},{5,4},{6,7},{7,6},{8,9},{9,8},{10,11... | collective-permute-start | bytes 786440 | tf_op jit(solution)/shard_map/ppermute | solution.py:26
  3.2 1.6 %collective-permute-start.1 = (bf16[576,128]{1,0:T(8,128)(2,1)}, bf16[576,128]{1,0:T(8,128)(2,1)S(1)}, u32[]{:S(2)}, u32[]{:S(2)}) collective-permute-start(bf16[576,128]{1,0:T(8,128)(2,1)} %bitcast.24), channel_id=1, source_target_pairs={{0,1},{1,0},{2,3},{3,2},{4,5},{5,4},{6,7},{7,6},{8,9},{9,8},{10,11... | collective-permute-start | bytes 442376 | tf_op jit(solution)/shard_map/ppermute | solution.py:26
  5.8 8.9 %collective-permute-start.3 = (bf16[576,128]{1,0:T(8,128)(2,1)S(1)}, bf16[576,128]{1,0:T(8,128)(2,1)S(1)}, u32[]{:S(2)}, u32[]{:S(2)}) collective-permute-start(bf16[576,128]{1,0:T(8,128)(2,1)S(1)} %get-tuple-element.45), channel_id=1, source_target_pairs={{0,24},{1,9},{8,16},{9,1},{16,8},{17,25},{24,0},{25,17},{2,26},{3,... | collective-permute-start | bytes 442376 | tf_op jit(solution)/shard_map/ppermute | solution.py:335
  5.9 26.2 %collective-permute-start.2 = (bf16[2,576,128]{2,1,0:T(8,128)(2,1)S(1)}, bf16[2,576,128]{2,1,0:T(8,128)(2,1)S(1)}, u32[]{:S(2)}, u32[]{:S(2)}) collective-permute-start(bf16[2,576,128]{2,1,0:T(8,128)(2,1)S(1)} %get-tuple-element.43), channel_id=1, source_target_pairs={{0,8},{1,25},{8,0},{9,17},{16,24},{17,9},{24,16},{25,1},{2,10},{3,... | collective-permute-start | bytes 884744 | tf_op jit(solution)/shard_map/ppermute | solution.py:334
  7.4 14.4 %collective-permute-start.5 = (bf16[1024,128]{1,0:T(8,128)(2,1)S(1)}, bf16[1024,128]{1,0:T(8,128)(2,1)S(1)}, u32[]{:S(2)}, u32[]{:S(2)}) collective-permute-start(bf16[1024,128]{1,0:T(8,128)(2,1)S(1)} %get-tuple-element.40.own_ref.b2), channel_id=1, source_target_pairs={{0,2},{1,3},{2,4},{3,5},{4,6},{5,7},{6,8},{7,9},{8,10},{9,11},{10,... | collective-permute-start | bytes 786440 | tf_op jit(solution)/shard_map/ppermute | solution.py:31
  10.4 16.2 %collective-permute-start.6 = (bf16[1024,128]{1,0:T(8,128)(2,1)S(1)}, bf16[1024,128]{1,0:T(8,128)(2,1)S(1)}, u32[]{:S(2)}, u32[]{:S(2)}) collective-permute-start(bf16[1024,128]{1,0:T(8,128)(2,1)S(1)} %get-tuple-element.40.own_ref.b2), channel_id=1, source_target_pairs={{0,30},{1,31},{2,0},{3,1},{4,2},{5,3},{6,4},{7,5},{8,6},{9,7},{10,... | collective-permute-start | bytes 786440 | tf_op jit(solution)/shard_map/ppermute | solution.py:31
  13.9 18.2 %collective-permute-start.7 = (bf16[1024,128]{1,0:T(8,128)(2,1)S(1)}, bf16[1024,128]{1,0:T(8,128)(2,1)S(1)}, u32[]{:S(2)}, u32[]{:S(2)}) collective-permute-start(bf16[1024,128]{1,0:T(8,128)(2,1)S(1)} %get-tuple-element.40.own_ref.b2), channel_id=1, source_target_pairs={{0,32},{32,0},{1,33},{33,1},{2,34},{34,2},{3,35},{35,3},{4,36},{36... | collective-permute-start | bytes 786440 | tf_op jit(solution)/shard_map/ppermute | solution.py:26
  14.7 17.4 %collective-permute-start.4 = (bf16[576,128]{1,0:T(8,128)(2,1)S(1)}, bf16[576,128]{1,0:T(8,128)(2,1)S(1)}, u32[]{:S(2)}, u32[]{:S(2)}) collective-permute-start(bf16[576,128]{1,0:T(8,128)(2,1)S(1)} %get-tuple-element.47), channel_id=1, source_target_pairs={{0,16},{1,17},{8,24},{9,25},{16,0},{17,1},{24,8},{25,9},{2,18},{3,... | collective-permute-start | bytes 442376 | tf_op jit(solution)/shard_map/ppermute | solution.py:337
  32.1 8.0 %collective-permute-start.9 = (bf16[1024,128]{1,0:T(8,128)(2,1)S(1)}, bf16[1024,128]{1,0:T(8,128)(2,1)S(1)}, u32[]{:S(2)}, u32[]{:S(2)}) collective-permute-start(bf16[1024,128]{1,0:T(8,128)(2,1)S(1)} %broadcast_select_fusion), channel_id=1, source_target_pairs={{0,1},{1,0},{2,3},{3,2},{4,5},{5,4},{6,7},{7,6},{8,9},{9,8},{10,11... | collective-permute-start | bytes 786440 | tf_op jit(solution)/shard_map/ppermute | solution.py:26
  33.4 6.8 %collective-permute-start.8 = (bf16[576,128]{1,0:T(8,128)(2,1)S(1)}, bf16[576,128]{1,0:T(8,128)(2,1)S(1)}, u32[]{:S(2)}, u32[]{:S(2)}) collective-permute-start(bf16[576,128]{1,0:T(8,128)(2,1)S(1)} %fusion.2), channel_id=1, source_target_pairs={{0,2},{1,7},{2,0},{3,5},{4,6},{5,3},{6,4},{7,1},{8,10},{9,15},{10,... | collective-permute-start | bytes 442376 | tf_op jit(solution)/shard_map/ppermute | solution.py:348
  35.4 8.9 %collective-permute-start.11 = (bf16[1024,128]{1,0:T(8,128)(2,1)S(1)}, bf16[1024,128]{1,0:T(8,128)(2,1)S(1)}, u32[]{:S(2)}, u32[]{:S(2)}) collective-permute-start(bf16[1024,128]{1,0:T(8,128)(2,1)S(1)} %collective-permute-done.7.near_ref), channel_id=1, source_target_pairs={{0,64},{32,224},{64,128},{96,32},{128,192},{160,96},{192,0},{224,1... | collective-permute-start | bytes 786440 | tf_op jit(solution)/shard_map/ppermute | solution.py:347
  40.2 7.7 %collective-permute-start.10 = (bf16[576,128]{1,0:T(8,128)(2,1)S(1)}, bf16[576,128]{1,0:T(8,128)(2,1)S(1)}, u32[]{:S(2)}, u32[]{:S(2)}) collective-permute-start(bf16[576,128]{1,0:T(8,128)(2,1)S(1)} %add_convert_fusion.near_ref), channel_id=1, source_target_pairs={{0,6},{1,3},{2,4},{3,1},{4,2},{5,7},{6,0},{7,5},{8,14},{9,11},{10,... | collective-permute-start | bytes 442376 | tf_op jit(solution)/shard_map/ppermute | solution.py:353
  42.1 7.2 %collective-permute-start.13 = (bf16[2,576,128]{2,1,0:T(8,128)(2,1)S(1)}, bf16[2,576,128]{2,1,0:T(8,128)(2,1)S(1)}, u32[]{:S(2)}, u32[]{:S(2)}) collective-permute-start(bf16[2,576,128]{2,1,0:T(8,128)(2,1)S(1)} %pad_maximum_fusion), channel_id=1, source_target_pairs={{0,24},{1,9},{8,16},{9,1},{16,8},{17,25},{24,0},{25,17},{2,26},{3,... | collective-permute-start | bytes 884744 | tf_op jit(solution)/shard_map/ppermute | solution.py:352
  47.9 10.2 %copy-start = (f32[1024,128]{1,0:T(8,128)S(1)}, f32[1024,128]{1,0:T(8,128)}, u32[]{:S(2)}) copy-start(f32[1024,128]{1,0:T(8,128)} %den_ref.1) | copy-start | bytes 1572868
  48.3 2.0 %collective-permute-start.12 = (bf16[128,576]{1,0:T(8,128)(2,1)S(1)}, bf16[128,576]{1,0:T(8,128)(2,1)S(1)}, u32[]{:S(2)}, u32[]{:S(2)}) collective-permute-start(bf16[128,576]{1,0:T(8,128)(2,1)S(1)} %excited_block_kernel.1.own_ref), channel_id=1, source_target_pairs={{0,1},{1,0},{2,3},{3,2},{4,5},{5,4},{6,7},{7,6},{8,9},{9,8},{10,11... | collective-permute-start | bytes 442376 | tf_op jit(solution)/shard_map/ppermute | solution.py:26
  50.8 6.4 %collective-permute-start.14 = (bf16[2,128,128]{2,1,0:T(8,128)(2,1)S(1)}, bf16[2,128,128]{2,1,0:T(8,128)(2,1)S(1)}, u32[]{:S(2)}, u32[]{:S(2)}) collective-permute-start(bf16[2,128,128]{2,1,0:T(8,128)(2,1)S(1)} %get-tuple-element.65), channel_id=1, source_target_pairs={{0,8},{1,25},{8,0},{9,17},{16,24},{17,9},{24,16},{25,1},{2,10},{3,... | collective-permute-start | bytes 196616 | tf_op jit(solution)/shard_map/ppermute | solution.py:361
  52.9 5.2 %collective-permute-start.15 = (bf16[2,128,128]{2,1,0:T(8,128)(2,1)S(1)}, bf16[2,128,128]{2,1,0:T(8,128)(2,1)S(1)}, u32[]{:S(2)}, u32[]{:S(2)}) collective-permute-start(bf16[2,128,128]{2,1,0:T(8,128)(2,1)S(1)} %get-tuple-element.66), channel_id=1, source_target_pairs={{0,16},{1,17},{8,24},{9,25},{16,0},{17,1},{24,8},{25,9},{2,18},{3,... | collective-permute-start | bytes 196616 | tf_op jit(solution)/shard_map/ppermute | solution.py:361
  52.9 5.2 %collective-permute-start.16 = (bf16[2,128,128]{2,1,0:T(8,128)(2,1)S(1)}, bf16[2,128,128]{2,1,0:T(8,128)(2,1)S(1)}, u32[]{:S(2)}, u32[]{:S(2)}) collective-permute-start(bf16[2,128,128]{2,1,0:T(8,128)(2,1)S(1)} %get-tuple-element.67), channel_id=1, source_target_pairs={{0,24},{1,9},{8,16},{9,1},{16,8},{17,25},{24,0},{25,17},{2,26},{3,... | collective-permute-start | bytes 196616 | tf_op jit(solution)/shard_map/ppermute | solution.py:361

commit v15 on v13

--- a/solution.py
+++ b/solution.py
@@ -268,7 +268,7 @@
         (where, cols, *blocks, alpha_ops, start),
         [SMEM, SMEM] + [VMEM] * 3 + [HBM, VMEM],
         (rows * width * depth * 4, 5 * MIB),
-        [pltpu.VMEM((2, rows // 4, span), BF16), pltpu.SemaphoreType.DMA((2,))],
+        [pltpu.VMEM((4, rows // 8, span), BF16), pltpu.SemaphoreType.DMA((4,))],
     )
 
 
@@ -285,7 +285,7 @@
         (picked, alpha_ops, start),
         [VMEM, HBM, VMEM],
         (rows * width * span, 5 * MIB),
-        [pltpu.VMEM((2, rows // 4, span), BF16), pltpu.SemaphoreType.DMA((2,))],
+        [pltpu.VMEM((4, rows // 8, span), BF16), pltpu.SemaphoreType.DMA((4,))],
     )[0]
 
 
@@ -314,8 +314,8 @@
     pair_mate = swapped(pair_t, "c", 1)
     coef_v, pair_v = loaded(coef, pair_t)
 
-    below = rotated(coef_v, BETA, 2)
-    above = rotated(coef_v, BETA, -2)
+    below = rotated(coef, BETA, 2)
+    above = rotated(coef, BETA, -2)
     xs, route = lax.axis_size("x"), []
     for i in range(xs):
         route += [(2 * i, 2 * ((i + 1) % xs)), (2 * i + 1, 2 * ((i - 1) % xs) + 1)]
@@ -327,7 +327,7 @@
     turns = (None, crossing((1, 3)), crossing((2, 2)), crossing((3, 1)))
     got = [lax.ppermute(parts[k], ("y", "c"), turns[k]) for k in (1, 3, 2)]
     *got, below, above = lax.optimization_barrier((*got, below, above))
-    near = swapped(coef_v, "zl", 1)
+    near = swapped(coef, "zl", 1)
     total = parts[0].astype(F32)
     for part in got:
         total = total + part.astype(F32)

time: 56.1 us -> 55.2 us (0.984)
  starting transfers between devices: 35.9 us -> 34.4 us
  waiting for transfers between devices: 4.69 us -> 5.46 us
    ppermute x5, starting transfers between devices: 12.4 us -> 11.6 us  [swapped(): return lax.ppermute(block, axis, [(i, i ^ mask) for i in range(count)])]
  transfers between devices with their start and end apart: 18 -> 18, of which waited for: 6 -> 5; matrix products, arithmetic and copies ran while one was open for 2% -> 2% of each run, Pallas kernels for 20% -> 21%
where the time goes in v15:
time: 55.2 us; the launch traced here: 54.4 us
  starting transfers between devices  34.4 us (62%)
  Pallas kernels  13.1 us (24%)
  waiting for transfers between devices  5.46 us (10%)
  other arithmetic  0.93 us (2%)
    pallas_call x9, Pallas kernels, call(): pl.pallas_call(kernel, out_shape=outs, in_specs=specs, out_specs=out_spec...  13.1 us
    ppermute x5, starting transfers between devices, swapped(): return lax.ppermute(block, axis, [(i, i ^ mask) for i in range(count)])  11.6 us
    ppermute x2, starting transfers between devices, rotated(): lax.ppermute(block, axis, [(i, (i + distance) % count) for i in range(cou...  6.74 us
    ppermute x1, starting transfers between devices, local(): beside = lax.ppermute(sent, ('y', 'c'), turns[1])  5.67 us
    ppermute x3, starting transfers between devices, local(): got = [lax.ppermute(parts[k], ('y', 'c'), turns[k]) for k in (1, 3, 2)]  3.95 us
    ppermute x3, starting transfers between devices, local(): back = [lax.ppermute(out[k - 1], ('y', 'c'), turns[k]) for k in (1, 2, 3)]  3.33 us
    ppermute x1, waiting for transfers between devices, local(): far = lax.ppermute(near, ALPHA, route)  1.7 us
    ppermute x3, waiting for transfers between devices, local(): got = [lax.ppermute(parts[k], ('y', 'c'), turns[k]) for k in (1, 3, 2)]  1.51 us
  transfers between devices with their start and end apart: 18, of which 5 were waited for; matrix products, arithmetic and copies ran while one was open for 2% of the time, Pallas kernels for 21%

profile of v15, /device:TPU:1, one launch (start us, length us, event | category | flops | bytes accessed | tf_op | source)
XLA Modules:
  0.0 54.4 jit_solution(3292035558605253652)
XLA Ops:
  0.0 3.2 %collective-permute-start = (bf16[1024,128]{1,0:T(8,128)(2,1)}, bf16[1024,128]{1,0:T(8,128)(2,1)S(1)}, u32[]{:S(2)}, u32[]{:S(2)}) collective-permute-start(bf16[1024,128]{1,0:T(8,128)(2,1)} %coef_ref.1), channel_id=1, source_target_pairs={{0,1},{1,0},{2,3},{3,2},{4,5},{5,4},{6,7},{7,6},{8,9},{9,8},{10,11... | collective-permute-start | bytes 786440 | tf_op jit(solution)/shard_map/ppermute | solution.py:26
  3.2 1.3 %collective-permute-start.5 = (bf16[1024,128]{1,0:T(8,128)(2,1)}, bf16[1024,128]{1,0:T(8,128)(2,1)S(1)}, u32[]{:S(2)}, u32[]{:S(2)}) collective-permute-start(bf16[1024,128]{1,0:T(8,128)(2,1)} %coef_ref.1), channel_id=1, source_target_pairs={{0,2},{1,3},{2,4},{3,5},{4,6},{5,7},{6,8},{7,9},{8,10},{9,11},{10,... | collective-permute-start | bytes 786440 | tf_op jit(solution)/shard_map/ppermute | solution.py:31
  4.5 5.5 %collective-permute-start.6 = (bf16[1024,128]{1,0:T(8,128)(2,1)}, bf16[1024,128]{1,0:T(8,128)(2,1)S(1)}, u32[]{:S(2)}, u32[]{:S(2)}) collective-permute-start(bf16[1024,128]{1,0:T(8,128)(2,1)} %coef_ref.1), channel_id=1, source_target_pairs={{0,30},{1,31},{2,0},{3,1},{4,2},{5,3},{6,4},{7,5},{8,6},{9,7},{10,... | collective-permute-start | bytes 786440 | tf_op jit(solution)/shard_map/ppermute | solution.py:31
  10.0 1.0 %loaded_kernel.1 = (bf16[1024,128]{1,0:T(8,128)(2,1)S(1)}, bf16[576,128]{1,0:T(8,128)(2,1)S(1)}) custom-call(bf16[1024,128]{1,0:T(8,128)(2,1)} %coef_ref.1, bf16[576,128]{1,0:T(8,128)(2,1)} %bitcast.22), custom_call_target="tpu_custom_call" | custom-call | bytes 1048576 | tf_op jit(solution)/shard_map/loaded_kernel/pallas_call | solution.py:43
  11.1 1.0 %density_parts_kernel.1 = (bf16[576,128]{1,0:T(8,128)(2,1)S(1)}, bf16[576,128]{1,0:T(8,128)(2,1)S(1)}, bf16[576,128]{1,0:T(8,128)(2,1)S(1)}, bf16[576,128]{1,0:T(8,128)(2,1)S(1)}) custom-call(s32[12]{0:T(128)S(1)} %stack.60.where_ref, bf16[1024,128]{1,0:T(8,128)(2,1)S(1)} %get-tuple-element.40.own_ref.b2, ...), custom_call_target="tpu_custom_call" | custom-call | flops 150994944 | bytes 1048576 | tf_op jit(solution)/shard_map/density_parts_kernel/pallas_call | solution.py:43
  12.2 0.6 %collective-permute-start.2 = (bf16[576,128]{1,0:T(8,128)(2,1)S(1)}, bf16[576,128]{1,0:T(8,128)(2,1)S(1)}, u32[]{:S(2)}, u32[]{:S(2)}) collective-permute-start(bf16[576,128]{1,0:T(8,128)(2,1)S(1)} %get-tuple-element.43), channel_id=1, source_target_pairs={{0,8},{1,25},{8,0},{9,17},{16,24},{17,9},{24,16},{25,1},{2,10},{3,... | collective-permute-start | bytes 442376 | tf_op jit(solution)/shard_map/ppermute | solution.py:328
  12.7 3.4 %collective-permute-start.4 = (bf16[576,128]{1,0:T(8,128)(2,1)S(1)}, bf16[576,128]{1,0:T(8,128)(2,1)S(1)}, u32[]{:S(2)}, u32[]{:S(2)}) collective-permute-start(bf16[576,128]{1,0:T(8,128)(2,1)S(1)} %get-tuple-element.45), channel_id=1, source_target_pairs={{0,16},{1,17},{8,24},{9,25},{16,0},{17,1},{24,8},{25,9},{2,18},{3,... | collective-permute-start | bytes 442376 | tf_op jit(solution)/shard_map/ppermute | solution.py:328
  16.1 0.7 %pad_add_fusion.cols_ref = s32[8]{0:T(128)S(1)} fusion(s32[4]{0:T(128)} %bitcast.23, s32[4]{0:T(128)} %bitcast.24), kind=kLoop, calls=%fused_computation.4 | loop fusion | flops 8 | bytes 64 | tf_op jit(solution)/shard_map/concatenate | solution.py:310
  16.9 1.8 %staged_kernel.1 = (bf16[576,576]{1,0:T(8,128)(2,1)S(1)}, f32[128,576]{1,0:T(8,128)S(1)}, bf16[128,640]{1,0:T(8,128)(2,1)S(1)}) custom-call(s32[12]{0:T(128)S(1)} %stack.60.where_ref, s32[8]{0:T(128)S(1)} %pad_add_fusion.cols_ref, bf16[576,576]{1,0:T(8,128)(2,1)} %c_ref.1, bf16[576,1024]{1,0:T(8,128)(2,1)} %bitcast.20, bf16[128,512]{1,0:T(8,128)(2,1)} %ops_ref.3, ...), custom_call_target="tpu_custom_call" | custom-call | flops 331776 | bytes 2097152 | tf_op jit(solution)/shard_map/staged_kernel/pallas_call | solution.py:43
  18.7 4.2 %collective-permute-start.11 = (bf16[1024,128]{1,0:T(8,128)(2,1)}, bf16[1024,128]{1,0:T(8,128)(2,1)S(1)}, u32[]{:S(2)}, u32[]{:S(2)}) collective-permute-start(bf16[1024,128]{1,0:T(8,128)(2,1)} %coef_ref.1), channel_id=1, source_target_pairs={{0,32},{32,0},{1,33},{33,1},{2,34},{34,2},{3,35},{35,3},{4,36},{36... | collective-permute-start | bytes 786440 | tf_op jit(solution)/shard_map/ppermute | solution.py:26
  22.9 1.5 %collective-permute-done.4 = bf16[576,128]{1,0:T(8,128)(2,1)S(1)} collective-permute-done((bf16[576,128]{1,0:T(8,128)(2,1)S(1)}, bf16[576,128]{1,0:T(8,128)(2,1)S(1)}, u32[]{:S(2)}, u32[]{:S(2)}) %collective-permute-start.4) | collective-permute-done | bytes 147488 | tf_op jit(solution)/shard_map/ppermute | solution.py:328
  24.6 5.7 %collective-permute-start.8 = (bf16[576,128]{1,0:T(8,128)(2,1)S(1)}, bf16[576,128]{1,0:T(8,128)(2,1)S(1)}, u32[]{:S(2)}, u32[]{:S(2)}) collective-permute-start(bf16[576,128]{1,0:T(8,128)(2,1)S(1)} %get-tuple-element.53.po_ref.pair_ref), channel_id=1, source_target_pairs={{0,8},{1,25},{8,0},{9,17},{16,24},{17,9},{24,16},{25,1},{2,10},{3,... | collective-permute-start | bytes 442376 | tf_op jit(solution)/shard_map/ppermute | solution.py:340
  30.4 1.3 %collective-permute-start.12 = (bf16[1024,128]{1,0:T(8,128)(2,1)S(1)}, bf16[1024,128]{1,0:T(8,128)(2,1)S(1)}, u32[]{:S(2)}, u32[]{:S(2)}) collective-permute-start(bf16[1024,128]{1,0:T(8,128)(2,1)S(1)} %collective-permute-done.11.near_ref), channel_id=1, source_target_pairs={{0,64},{32,224},{64,128},{96,32},{128,192},{160,96},{192,0},{224,1... | collective-permute-start | bytes 786440 | tf_op jit(solution)/shard_map/ppermute | solution.py:337
  31.7 1.1 %collective-permute-done.8.beside_ref = bf16[576,128]{1,0:T(8,128)(2,1)S(1)} collective-permute-done((bf16[576,128]{1,0:T(8,128)(2,1)S(1)}, bf16[576,128]{1,0:T(8,128)(2,1)S(1)}, u32[]{:S(2)}, u32[]{:S(2)}) %collective-permute-start.8) | collective-permute-done | bytes 147488 | tf_op jit(solution)/shard_map/ppermute | solution.py:340
  33.3 1.4 %collective-permute-start.14 = (bf16[2,576,128]{2,1,0:T(8,128)(2,1)S(1)}, bf16[2,576,128]{2,1,0:T(8,128)(2,1)S(1)}, u32[]{:S(2)}, u32[]{:S(2)}) collective-permute-start(bf16[2,576,128]{2,1,0:T(8,128)(2,1)S(1)} %pad_maximum_fusion), channel_id=1, source_target_pairs={{0,24},{1,9},{8,16},{9,1},{16,8},{17,25},{24,0},{25,17},{2,26},{3,... | collective-permute-start | bytes 884744 | tf_op jit(solution)/shard_map/ppermute | solution.py:345
  34.7 0.5 same_spin_beta_kernel.1.start_ref
  35.3 1.7 %collective-permute-done.12.far_ref = bf16[1024,128]{1,0:T(8,128)(2,1)S(1)} collective-permute-done((bf16[1024,128]{1,0:T(8,128)(2,1)S(1)}, bf16[1024,128]{1,0:T(8,128)(2,1)S(1)}, u32[]{:S(2)}, u32[]{:S(2)}) %collective-permute-start.12) | collective-permute-done | bytes 262176 | tf_op jit(solution)/shard_map/ppermute | solution.py:337
  37.0 3.5 %same_spin_alpha_kernel.1 = (f32[1024,128]{1,0:T(8,128)S(1)}, bf16[4096,128]{1,0:T(8,128)(2,1)S(1)}) custom-call(s32[12]{0:T(128)S(1)} %stack.60.where_ref, s32[8]{0:T(128)S(1)} %pad_add_fusion.cols_ref, bf16[1024,128]{1,0:T(8,128)(2,1)S(1)} %get-tuple-element.40.own_ref.b2, bf16[1024,128]{1,0:T(8,128)(2,1)S(1)} %collective-permute-done.11.near_ref, ...), custom_call_target="tpu_custom_call" | custom-call | flops 536870912 | bytes 5242880 | tf_op jit(solution)/shard_map/same_spin_alpha_kernel/pallas_call | solution.py:43
  40.9 4.0 %collective-permute-start.13 = (bf16[128,576]{1,0:T(8,128)(2,1)S(1)}, bf16[128,576]{1,0:T(8,128)(2,1)S(1)}, u32[]{:S(2)}, u32[]{:S(2)}) collective-permute-start(bf16[128,576]{1,0:T(8,128)(2,1)S(1)} %excited_block_kernel.1.own_ref), channel_id=1, source_target_pairs={{0,1},{1,0},{2,3},{3,2},{4,5},{5,4},{6,7},{7,6},{8,9},{9,8},{10,11... | collective-permute-start | bytes 442376 | tf_op jit(solution)/shard_map/ppermute | solution.py:26
  44.9 1.0 %collective-permute-done.13.mate_ref = bf16[128,576]{1,0:T(8,128)(2,1)S(1)} collective-permute-done((bf16[128,576]{1,0:T(8,128)(2,1)S(1)}, bf16[128,576]{1,0:T(8,128)(2,1)S(1)}, u32[]{:S(2)}, u32[]{:S(2)}) %collective-permute-start.13) | collective-permute-done | bytes 147488 | tf_op jit(solution)/shard_map/ppermute | solution.py:26
  45.9 0.5 mixed_blocks_kernel.1
  46.8 3.0 %collective-permute-start.17 = (bf16[2,128,128]{2,1,0:T(8,128)(2,1)S(1)}, bf16[2,128,128]{2,1,0:T(8,128)(2,1)S(1)}, u32[]{:S(2)}, u32[]{:S(2)}) collective-permute-start(bf16[2,128,128]{2,1,0:T(8,128)(2,1)S(1)} %get-tuple-element.67), channel_id=1, source_target_pairs={{0,24},{1,9},{8,16},{9,1},{16,8},{17,25},{24,0},{25,17},{2,26},{3,... | collective-permute-start | bytes 196616 | tf_op jit(solution)/shard_map/ppermute | solution.py:354
  49.7 3.0 %rest_of_alpha_kernel.1.same_ref = f32[1024,128]{1,0:T(8,128)S(1)} custom-call(bf16[4096,128]{1,0:T(8,128)(2,1)S(1)} %get-tuple-element.68.picked, bf16[1024,4096]{1,0:T(8,128)(2,1)} %ops_ref.5, f32[1024,128]{1,0:T(8,128)S(1)} %get-tuple-element.69.start_ref), custom_call_target="tpu_custom_call" | custom-call | flops 536870912 | bytes 5242880 | tf_op jit(solution)/shard_map/rest_of_alpha_kernel/pallas_call | solution.py:43
  52.8 1.4 %finished_kernel.1 = f32[1024,128]{1,0:T(8,128)} custom-call(s32[12]{0:T(128)S(1)} %stack.60.where_ref, f32[1024,128]{1,0:T(8,128)S(1)} %rest_of_alpha_kernel.1.same_ref, f32[2,128,128]{2,1,0:T(8,128)S(1)} %get-tuple-element.71.m0, bf16[2,128,128]{2,1,0:T(8,128)(2,1)S(1)} %collective-permute-done.15.m1, bf16[2,128,128]{2,1,0:T(8,128)(2,1)S(1)} %collective-permute-done.16.m2, ...), custom_call_target="tpu_custom_call" | custom-call | flops 262144 | bytes 2097152 | tf_op jit(solution)/shard_map/finished_kernel/pallas_call | solution.py:43
  (29 shorter events, 1.7 us)
Async XLA Ops:
  0.0 11.1 %collective-permute-start = (bf16[1024,128]{1,0:T(8,128)(2,1)}, bf16[1024,128]{1,0:T(8,128)(2,1)S(1)}, u32[]{:S(2)}, u32[]{:S(2)}) collective-permute-start(bf16[1024,128]{1,0:T(8,128)(2,1)} %coef_ref.1), channel_id=1, source_target_pairs={{0,1},{1,0},{2,3},{3,2},{4,5},{5,4},{6,7},{7,6},{8,9},{9,8},{10,11... | collective-permute-start | bytes 786440 | tf_op jit(solution)/shard_map/ppermute | solution.py:26
  3.2 7.9 %collective-permute-start.1 = (bf16[576,128]{1,0:T(8,128)(2,1)}, bf16[576,128]{1,0:T(8,128)(2,1)S(1)}, u32[]{:S(2)}, u32[]{:S(2)}) collective-permute-start(bf16[576,128]{1,0:T(8,128)(2,1)} %bitcast.21), channel_id=1, source_target_pairs={{0,1},{1,0},{2,3},{3,2},{4,5},{5,4},{6,7},{7,6},{8,9},{9,8},{10,11... | collective-permute-start | bytes 442376 | tf_op jit(solution)/shard_map/ppermute | solution.py:26
  3.2 15.5 %collective-permute-start.5 = (bf16[1024,128]{1,0:T(8,128)(2,1)}, bf16[1024,128]{1,0:T(8,128)(2,1)S(1)}, u32[]{:S(2)}, u32[]{:S(2)}) collective-permute-start(bf16[1024,128]{1,0:T(8,128)(2,1)} %coef_ref.1), channel_id=1, source_target_pairs={{0,2},{1,3},{2,4},{3,5},{4,6},{5,7},{6,8},{7,9},{8,10},{9,11},{10,... | collective-permute-start | bytes 786440 | tf_op jit(solution)/shard_map/ppermute | solution.py:31
  4.5 18.4 %collective-permute-start.6 = (bf16[1024,128]{1,0:T(8,128)(2,1)}, bf16[1024,128]{1,0:T(8,128)(2,1)S(1)}, u32[]{:S(2)}, u32[]{:S(2)}) collective-permute-start(bf16[1024,128]{1,0:T(8,128)(2,1)} %coef_ref.1), channel_id=1, source_target_pairs={{0,30},{1,31},{2,0},{3,1},{4,2},{5,3},{6,4},{7,5},{8,6},{9,7},{10,... | collective-permute-start | bytes 786440 | tf_op jit(solution)/shard_map/ppermute | solution.py:31
  12.2 10.8 %collective-permute-start.2 = (bf16[576,128]{1,0:T(8,128)(2,1)S(1)}, bf16[576,128]{1,0:T(8,128)(2,1)S(1)}, u32[]{:S(2)}, u32[]{:S(2)}) collective-permute-start(bf16[576,128]{1,0:T(8,128)(2,1)S(1)} %get-tuple-element.43), channel_id=1, source_target_pairs={{0,8},{1,25},{8,0},{9,17},{16,24},{17,9},{24,16},{25,1},{2,10},{3,... | collective-permute-start | bytes 442376 | tf_op jit(solution)/shard_map/ppermute | solution.py:328
  12.7 10.2 %collective-permute-start.3 = (bf16[576,128]{1,0:T(8,128)(2,1)S(1)}, bf16[576,128]{1,0:T(8,128)(2,1)S(1)}, u32[]{:S(2)}, u32[]{:S(2)}) collective-permute-start(bf16[576,128]{1,0:T(8,128)(2,1)S(1)} %get-tuple-element.44), channel_id=1, source_target_pairs={{0,24},{1,9},{8,16},{9,1},{16,8},{17,25},{24,0},{25,17},{2,26},{3,... | collective-permute-start | bytes 442376 | tf_op jit(solution)/shard_map/ppermute | solution.py:328
  12.7 11.7 %collective-permute-start.4 = (bf16[576,128]{1,0:T(8,128)(2,1)S(1)}, bf16[576,128]{1,0:T(8,128)(2,1)S(1)}, u32[]{:S(2)}, u32[]{:S(2)}) collective-permute-start(bf16[576,128]{1,0:T(8,128)(2,1)S(1)} %get-tuple-element.45), channel_id=1, source_target_pairs={{0,16},{1,17},{8,24},{9,25},{16,0},{17,1},{24,8},{25,9},{2,18},{3,... | collective-permute-start | bytes 442376 | tf_op jit(solution)/shard_map/ppermute | solution.py:328
  18.7 11.7 %collective-permute-start.11 = (bf16[1024,128]{1,0:T(8,128)(2,1)}, bf16[1024,128]{1,0:T(8,128)(2,1)S(1)}, u32[]{:S(2)}, u32[]{:S(2)}) collective-permute-start(bf16[1024,128]{1,0:T(8,128)(2,1)} %coef_ref.1), channel_id=1, source_target_pairs={{0,32},{32,0},{1,33},{33,1},{2,34},{34,2},{3,35},{35,3},{4,36},{36... | collective-permute-start | bytes 786440 | tf_op jit(solution)/shard_map/ppermute | solution.py:26
  24.5 8.3 %collective-permute-start.7 = (bf16[576,128]{1,0:T(8,128)(2,1)S(1)}, bf16[576,128]{1,0:T(8,128)(2,1)S(1)}, u32[]{:S(2)}, u32[]{:S(2)}) collective-permute-start(bf16[576,128]{1,0:T(8,128)(2,1)S(1)} %add_convert_fusion.1), channel_id=1, source_target_pairs={{0,2},{1,7},{2,0},{3,5},{4,6},{5,3},{6,4},{7,1},{8,10},{9,15},{10,... | collective-permute-start | bytes 442376 | tf_op jit(solution)/shard_map/ppermute | solution.py:338
  24.6 8.2 %collective-permute-start.8 = (bf16[576,128]{1,0:T(8,128)(2,1)S(1)}, bf16[576,128]{1,0:T(8,128)(2,1)S(1)}, u32[]{:S(2)}, u32[]{:S(2)}) collective-permute-start(bf16[576,128]{1,0:T(8,128)(2,1)S(1)} %get-tuple-element.53.po_ref.pair_ref), channel_id=1, source_target_pairs={{0,8},{1,25},{8,0},{9,17},{16,24},{17,9},{24,16},{25,1},{2,10},{3,... | collective-permute-start | bytes 442376 | tf_op jit(solution)/shard_map/ppermute | solution.py:340
  30.3 2.6 %collective-permute-start.9 = (bf16[1024,128]{1,0:T(8,128)(2,1)S(1)}, bf16[1024,128]{1,0:T(8,128)(2,1)S(1)}, u32[]{:S(2)}, u32[]{:S(2)}) collective-permute-start(bf16[1024,128]{1,0:T(8,128)(2,1)S(1)} %broadcast_select_fusion), channel_id=1, source_target_pairs={{0,1},{1,0},{2,3},{3,2},{4,5},{5,4},{6,7},{7,6},{8,9},{9,8},{10,11... | collective-permute-start | bytes 786440 | tf_op jit(solution)/shard_map/ppermute | solution.py:26
  30.4 6.5 %collective-permute-start.12 = (bf16[1024,128]{1,0:T(8,128)(2,1)S(1)}, bf16[1024,128]{1,0:T(8,128)(2,1)S(1)}, u32[]{:S(2)}, u32[]{:S(2)}) collective-permute-start(bf16[1024,128]{1,0:T(8,128)(2,1)S(1)} %collective-permute-done.11.near_ref), channel_id=1, source_target_pairs={{0,64},{32,224},{64,128},{96,32},{128,192},{160,96},{192,0},{224,1... | collective-permute-start | bytes 786440 | tf_op jit(solution)/shard_map/ppermute | solution.py:337
  32.9 7.6 %collective-permute-start.10 = (bf16[576,128]{1,0:T(8,128)(2,1)S(1)}, bf16[576,128]{1,0:T(8,128)(2,1)S(1)}, u32[]{:S(2)}, u32[]{:S(2)}) collective-permute-start(bf16[576,128]{1,0:T(8,128)(2,1)S(1)} %add_convert_fusion.near_ref), channel_id=1, source_target_pairs={{0,6},{1,3},{2,4},{3,1},{4,2},{5,7},{6,0},{7,5},{8,14},{9,11},{10,... | collective-permute-start | bytes 442376 | tf_op jit(solution)/shard_map/ppermute | solution.py:346
  33.3 11.6 %collective-permute-start.14 = (bf16[2,576,128]{2,1,0:T(8,128)(2,1)S(1)}, bf16[2,576,128]{2,1,0:T(8,128)(2,1)S(1)}, u32[]{:S(2)}, u32[]{:S(2)}) collective-permute-start(bf16[2,576,128]{2,1,0:T(8,128)(2,1)S(1)} %pad_maximum_fusion), channel_id=1, source_target_pairs={{0,24},{1,9},{8,16},{9,1},{16,8},{17,25},{24,0},{25,17},{2,26},{3,... | collective-permute-start | bytes 884744 | tf_op jit(solution)/shard_map/ppermute | solution.py:345
  40.5 12.4 %copy-start = (f32[1024,128]{1,0:T(8,128)S(1)}, f32[1024,128]{1,0:T(8,128)}, u32[]{:S(2)}) copy-start(f32[1024,128]{1,0:T(8,128)} %den_ref.1) | copy-start | bytes 1572868
  40.9 5.0 %collective-permute-start.13 = (bf16[128,576]{1,0:T(8,128)(2,1)S(1)}, bf16[128,576]{1,0:T(8,128)(2,1)S(1)}, u32[]{:S(2)}, u32[]{:S(2)}) collective-permute-start(bf16[128,576]{1,0:T(8,128)(2,1)S(1)} %excited_block_kernel.1.own_ref), channel_id=1, source_target_pairs={{0,1},{1,0},{2,3},{3,2},{4,5},{5,4},{6,7},{7,6},{8,9},{9,8},{10,11... | collective-permute-start | bytes 442376 | tf_op jit(solution)/shard_map/ppermute | solution.py:26
  46.4 6.3 %collective-permute-start.15 = (bf16[2,128,128]{2,1,0:T(8,128)(2,1)S(1)}, bf16[2,128,128]{2,1,0:T(8,128)(2,1)S(1)}, u32[]{:S(2)}, u32[]{:S(2)}) collective-permute-start(bf16[2,128,128]{2,1,0:T(8,128)(2,1)S(1)} %get-tuple-element.65), channel_id=1, source_target_pairs={{0,8},{1,25},{8,0},{9,17},{16,24},{17,9},{24,16},{25,1},{2,10},{3,... | collective-permute-start | bytes 196616 | tf_op jit(solution)/shard_map/ppermute | solution.py:354
  46.5 6.2 %collective-permute-start.16 = (bf16[2,128,128]{2,1,0:T(8,128)(2,1)S(1)}, bf16[2,128,128]{2,1,0:T(8,128)(2,1)S(1)}, u32[]{:S(2)}, u32[]{:S(2)}) collective-permute-start(bf16[2,128,128]{2,1,0:T(8,128)(2,1)S(1)} %get-tuple-element.66), channel_id=1, source_target_pairs={{0,16},{1,17},{8,24},{9,25},{16,0},{17,1},{24,8},{25,9},{2,18},{3,... | collective-permute-start | bytes 196616 | tf_op jit(solution)/shard_map/ppermute | solution.py:354
  46.8 6.1 %collective-permute-start.17 = (bf16[2,128,128]{2,1,0:T(8,128)(2,1)S(1)}, bf16[2,128,128]{2,1,0:T(8,128)(2,1)S(1)}, u32[]{:S(2)}, u32[]{:S(2)}) collective-permute-start(bf16[2,128,128]{2,1,0:T(8,128)(2,1)S(1)} %get-tuple-element.67), channel_id=1, source_target_pairs={{0,24},{1,9},{8,16},{9,1},{16,8},{17,25},{24,0},{25,17},{2,26},{3,... | collective-permute-start | bytes 196616 | tf_op jit(solution)/shard_map/ppermute | solution.py:354

commit v16 on v15

--- a/solution.py
+++ b/solution.py
@@ -61,43 +61,36 @@
     return pl.ds(pl.multiple_of(where_ref[k] * width, width), width)
 
 
-def loaded(coef, pair_t):
-    def loaded_kernel(coef_ref, pair_ref, coef_out, pair_out, sems):
+def density_parts(where, coef, mate, pair_t, pair_mate):
+    pairs, width = pair_mate.shape
+
+    def density_parts_kernel(
+        where_ref, coef_ref, mate_ref, pair_ref, pm_ref, o0, o1, o2, o3, coef_out, pair_out, acc, sems
+    ):
         copies = [
             pltpu.make_async_copy(coef_ref, coef_out, sems.at[0]),
             pltpu.make_async_copy(pair_ref, pair_out, sems.at[1]),
         ]
         for copy in copies:
             copy.start()
+        left = pm_ref[...]
+        for k in range(4):
+            rows = block_rows(where_ref, k, width)
+            acc[k] = dot(left, mate_ref[rows, :], ((1,), (1,)))
         for copy in copies:
             copy.wait()
-
-    return call(
-        loaded_kernel,
-        [shape(coef.shape), shape(pair_t.shape)],
-        (coef, pair_t),
-        [HBM, HBM],
-        (0, 1 * MIB),
-        [pltpu.SemaphoreType.DMA((2,))],
-    )
-
-
-def density_parts(where, own, mate, pair_own, pair_mate):
-    pairs, width = pair_mate.shape
-
-    def density_parts_kernel(where_ref, own_ref, mate_ref, po_ref, pm_ref, *outs):
-        left = jnp.concatenate([po_ref[...], pm_ref[...]], axis=1)
-        for k, out in enumerate(outs):
+        left = pair_out[...]
+        for k, out in enumerate((o0, o1, o2, o3)):
             rows = block_rows(where_ref, k, width)
-            right = jnp.concatenate([own_ref[rows, :], mate_ref[rows, :]], axis=1)
-            out[...] = dot(left, right, ((1,), (1,))).astype(BF16)
+            out[...] = (acc[k] + dot(left, coef_out[rows, :], ((1,), (1,)))).astype(BF16)
 
     return call(
         density_parts_kernel,
-        [shape((pairs, width))] * 4,
-        (where, own, mate, pair_own, pair_mate),
-        [SMEM] + [VMEM] * 4,
+        [shape((pairs, width))] * 4 + [shape(coef.shape), shape(pair_t.shape)],
+        (where, coef, mate, pair_t, pair_mate),
+        [SMEM, HBM, VMEM, HBM, VMEM],
         (16 * pairs * width * width, 1 * MIB),
+        [pltpu.VMEM((4, pairs, width), F32), pltpu.SemaphoreType.DMA((2,))],
     )
 
 
@@ -312,7 +305,6 @@
     pair_t = pair_beta.T
     mate = swapped(coef, "c", 1)
     pair_mate = swapped(pair_t, "c", 1)
-    coef_v, pair_v = loaded(coef, pair_t)
 
     below = rotated(coef, BETA, 2)
     above = rotated(coef, BETA, -2)
@@ -320,7 +312,7 @@
     for i in range(xs):
         route += [(2 * i, 2 * ((i + 1) % xs)), (2 * i + 1, 2 * ((i - 1) % xs) + 1)]
 
-    parts = density_parts(where, coef_v, mate, pair_v, pair_mate)
+    *parts, coef_v, pair_v = density_parts(where, coef, mate, pair_t, pair_mate)
     coupling, scale, placed = staged(
         where, cols, pair_coupling, pair_alpha.T, beta_ops, parts[0]
     )

time: 55.2 us -> 55.2 us (level)
    pallas_call x9 -> x8, Pallas kernels: 13.1 us -> 13 us  [call(): pl.pallas_call(kernel, out_shape=outs, in_specs=specs, out_specs=out_spec...]
  transfers between devices with their start and end apart: 18 -> 18, of which waited for: 5 -> 5; matrix products, arithmetic and copies ran while one was open for 2% -> 2% of each run, Pallas kernels for 21% -> 20%
where the time goes in v16:
time: 55.2 us; the launch traced here: 54.3 us
  starting transfers between devices  34.6 us (63%)
  Pallas kernels  13 us (24%)
  waiting for transfers between devices  5.45 us (10%)
  other arithmetic  0.93 us (2%)
    pallas_call x8, Pallas kernels, call(): pl.pallas_call(kernel, out_shape=outs, in_specs=specs, out_specs=out_spec...  13 us
    ppermute x5, starting transfers between devices, swapped(): return lax.ppermute(block, axis, [(i, i ^ mask) for i in range(count)])  11.7 us
    ppermute x2, starting transfers between devices, rotated(): lax.ppermute(block, axis, [(i, (i + distance) % count) for i in range(cou...  6.74 us
    ppermute x1, starting transfers between devices, local(): beside = lax.ppermute(sent, ('y', 'c'), turns[1])  5.66 us
    ppermute x3, starting transfers between devices, local(): got = [lax.ppermute(parts[k], ('y', 'c'), turns[k]) for k in (1, 3, 2)]  3.95 us
    ppermute x3, starting transfers between devices, local(): back = [lax.ppermute(out[k - 1], ('y', 'c'), turns[k]) for k in (1, 2, 3)]  3.33 us
    ppermute x1, waiting for transfers between devices, local(): far = lax.ppermute(near, ALPHA, route)  1.69 us
    ppermute x3, waiting for transfers between devices, local(): got = [lax.ppermute(parts[k], ('y', 'c'), turns[k]) for k in (1, 3, 2)]  1.51 us
  transfers between devices with their start and end apart: 18, of which 5 were waited for; matrix products, arithmetic and copies ran while one was open for 2% of the time, Pallas kernels for 20%

profile of v16, /device:TPU:1, one launch (start us, length us, event | category | flops | bytes accessed | tf_op | source)
XLA Modules:
  0.0 54.3 jit_solution(8311289408547526121)
XLA Ops:
  0.0 3.2 %collective-permute-start = (bf16[1024,128]{1,0:T(8,128)(2,1)}, bf16[1024,128]{1,0:T(8,128)(2,1)S(1)}, u32[]{:S(2)}, u32[]{:S(2)}) collective-permute-start(bf16[1024,128]{1,0:T(8,128)(2,1)} %coef_ref.1), channel_id=1, source_target_pairs={{0,1},{1,0},{2,3},{3,2},{4,5},{5,4},{6,7},{7,6},{8,9},{9,8},{10,11... | collective-permute-start | bytes 786440 | tf_op jit(solution)/shard_map/ppermute | solution.py:26
  3.2 1.3 %collective-permute-start.5 = (bf16[1024,128]{1,0:T(8,128)(2,1)}, bf16[1024,128]{1,0:T(8,128)(2,1)S(1)}, u32[]{:S(2)}, u32[]{:S(2)}) collective-permute-start(bf16[1024,128]{1,0:T(8,128)(2,1)} %coef_ref.1), channel_id=1, source_target_pairs={{0,2},{1,3},{2,4},{3,5},{4,6},{5,7},{6,8},{7,9},{8,10},{9,11},{10,... | collective-permute-start | bytes 786440 | tf_op jit(solution)/shard_map/ppermute | solution.py:31
  4.5 5.5 %collective-permute-start.6 = (bf16[1024,128]{1,0:T(8,128)(2,1)}, bf16[1024,128]{1,0:T(8,128)(2,1)S(1)}, u32[]{:S(2)}, u32[]{:S(2)}) collective-permute-start(bf16[1024,128]{1,0:T(8,128)(2,1)} %coef_ref.1), channel_id=1, source_target_pairs={{0,30},{1,31},{2,0},{3,1},{4,2},{5,3},{6,4},{7,5},{8,6},{9,7},{10,... | collective-permute-start | bytes 786440 | tf_op jit(solution)/shard_map/ppermute | solution.py:31
  10.1 1.9 %density_parts_kernel.1 = (bf16[576,128]{1,0:T(8,128)(2,1)S(1)}, bf16[576,128]{1,0:T(8,128)(2,1)S(1)}, bf16[576,128]{1,0:T(8,128)(2,1)S(1)}, bf16[576,128]{1,0:T...) custom-call(s32[12]{0:T(128)S(1)} %stack.60.where_ref, bf16[1024,128]{1,0:T(8,128)(2,1)} %coef_ref.1, ...), custom_call_target="tpu_custom_call" | custom-call | flops 150994944 | bytes 1048576 | tf_op jit(solution)/shard_map/density_parts_kernel/pallas_call | solution.py:43
  12.0 0.6 %collective-permute-start.2 = (bf16[576,128]{1,0:T(8,128)(2,1)S(1)}, bf16[576,128]{1,0:T(8,128)(2,1)S(1)}, u32[]{:S(2)}, u32[]{:S(2)}) collective-permute-start(bf16[576,128]{1,0:T(8,128)(2,1)S(1)} %get-tuple-element.41), channel_id=1, source_target_pairs={{0,8},{1,25},{8,0},{9,17},{16,24},{17,9},{24,16},{25,1},{2,10},{3,... | collective-permute-start | bytes 442376 | tf_op jit(solution)/shard_map/ppermute | solution.py:320
  12.5 3.4 %collective-permute-start.4 = (bf16[576,128]{1,0:T(8,128)(2,1)S(1)}, bf16[576,128]{1,0:T(8,128)(2,1)S(1)}, u32[]{:S(2)}, u32[]{:S(2)}) collective-permute-start(bf16[576,128]{1,0:T(8,128)(2,1)S(1)} %get-tuple-element.43), channel_id=1, source_target_pairs={{0,16},{1,17},{8,24},{9,25},{16,0},{17,1},{24,8},{25,9},{2,18},{3,... | collective-permute-start | bytes 442376 | tf_op jit(solution)/shard_map/ppermute | solution.py:320
  15.9 0.7 %pad_add_fusion.cols_ref = s32[8]{0:T(128)S(1)} fusion(s32[4]{0:T(128)} %bitcast.23, s32[4]{0:T(128)} %bitcast.24), kind=kLoop, calls=%fused_computation.4 | loop fusion | flops 8 | bytes 64 | tf_op jit(solution)/shard_map/concatenate | solution.py:303
  16.7 1.8 %staged_kernel.1 = (bf16[576,576]{1,0:T(8,128)(2,1)S(1)}, f32[128,576]{1,0:T(8,128)S(1)}, bf16[128,640]{1,0:T(8,128)(2,1)S(1)}) custom-call(s32[12]{0:T(128)S(1)} %stack.60.where_ref, s32[8]{0:T(128)S(1)} %pad_add_fusion.cols_ref, bf16[576,576]{1,0:T(8,128)(2,1)} %c_ref.1, bf16[576,1024]{1,0:T(8,128)(2,1)} %bitcast.20, bf16[128,512]{1,0:T(8,128)(2,1)} %ops_ref.3, ...), custom_call_target="tpu_custom_call" | custom-call | flops 331776 | bytes 2097152 | tf_op jit(solution)/shard_map/staged_kernel/pallas_call | solution.py:43
  18.5 4.4 %collective-permute-start.11 = (bf16[1024,128]{1,0:T(8,128)(2,1)}, bf16[1024,128]{1,0:T(8,128)(2,1)S(1)}, u32[]{:S(2)}, u32[]{:S(2)}) collective-permute-start(bf16[1024,128]{1,0:T(8,128)(2,1)} %coef_ref.1), channel_id=1, source_target_pairs={{0,32},{32,0},{1,33},{33,1},{2,34},{34,2},{3,35},{35,3},{4,36},{36... | collective-permute-start | bytes 786440 | tf_op jit(solution)/shard_map/ppermute | solution.py:26
  22.9 1.5 %collective-permute-done.4 = bf16[576,128]{1,0:T(8,128)(2,1)S(1)} collective-permute-done((bf16[576,128]{1,0:T(8,128)(2,1)S(1)}, bf16[576,128]{1,0:T(8,128)(2,1)S(1)}, u32[]{:S(2)}, u32[]{:S(2)}) %collective-permute-start.4) | collective-permute-done | bytes 147488 | tf_op jit(solution)/shard_map/ppermute | solution.py:320
  24.6 5.7 %collective-permute-start.8 = (bf16[576,128]{1,0:T(8,128)(2,1)S(1)}, bf16[576,128]{1,0:T(8,128)(2,1)S(1)}, u32[]{:S(2)}, u32[]{:S(2)}) collective-permute-start(bf16[576,128]{1,0:T(8,128)(2,1)S(1)} %get-tuple-element.52.pair_ref), channel_id=1, source_target_pairs={{0,8},{1,25},{8,0},{9,17},{16,24},{17,9},{24,16},{25,1},{2,10},{3,... | collective-permute-start | bytes 442376 | tf_op jit(solution)/shard_map/ppermute | solution.py:332
  30.4 1.3 %collective-permute-start.12 = (bf16[1024,128]{1,0:T(8,128)(2,1)S(1)}, bf16[1024,128]{1,0:T(8,128)(2,1)S(1)}, u32[]{:S(2)}, u32[]{:S(2)}) collective-permute-start(bf16[1024,128]{1,0:T(8,128)(2,1)S(1)} %collective-permute-done.11.near_ref), channel_id=1, source_target_pairs={{0,64},{32,224},{64,128},{96,32},{128,192},{160,96},{192,0},{224,1... | collective-permute-start | bytes 786440 | tf_op jit(solution)/shard_map/ppermute | solution.py:329
  31.7 1.1 %collective-permute-done.8.beside_ref = bf16[576,128]{1,0:T(8,128)(2,1)S(1)} collective-permute-done((bf16[576,128]{1,0:T(8,128)(2,1)S(1)}, bf16[576,128]{1,0:T(8,128)(2,1)S(1)}, u32[]{:S(2)}, u32[]{:S(2)}) %collective-permute-start.8) | collective-permute-done | bytes 147488 | tf_op jit(solution)/shard_map/ppermute | solution.py:332
  33.3 1.4 %collective-permute-start.14 = (bf16[2,576,128]{2,1,0:T(8,128)(2,1)S(1)}, bf16[2,576,128]{2,1,0:T(8,128)(2,1)S(1)}, u32[]{:S(2)}, u32[]{:S(2)}) collective-permute-start(bf16[2,576,128]{2,1,0:T(8,128)(2,1)S(1)} %pad_maximum_fusion), channel_id=1, source_target_pairs={{0,24},{1,9},{8,16},{9,1},{16,8},{17,25},{24,0},{25,17},{2,26},{3,... | collective-permute-start | bytes 884744 | tf_op jit(solution)/shard_map/ppermute | solution.py:337
  34.7 0.5 same_spin_beta_kernel.1.start_ref
  35.3 1.7 %collective-permute-done.12.far_ref = bf16[1024,128]{1,0:T(8,128)(2,1)S(1)} collective-permute-done((bf16[1024,128]{1,0:T(8,128)(2,1)S(1)}, bf16[1024,128]{1,0:T(8,128)(2,1)S(1)}, u32[]{:S(2)}, u32[]{:S(2)}) %collective-permute-start.12) | collective-permute-done | bytes 262176 | tf_op jit(solution)/shard_map/ppermute | solution.py:329
  36.9 3.5 %same_spin_alpha_kernel.1 = (f32[1024,128]{1,0:T(8,128)S(1)}, bf16[4096,128]{1,0:T(8,128)(2,1)S(1)}) custom-call(s32[12]{0:T(128)S(1)} %stack.60.where_ref, s32[8]{0:T(128)S(1)} %pad_add_fusion.cols_ref, bf16[1024,128]{1,0:T(8,128)(2,1)S(1)} %get-tuple-element.57.b2.own_ref, bf16[1024,128]{1,0:T(8,128)(2,1)S(1)} %collective-permute-done.11.near_ref, ...), custom_call_target="tpu_custom_call" | custom-call | flops 536870912 | bytes 5242880 | tf_op jit(solution)/shard_map/same_spin_alpha_kernel/pallas_call | solution.py:43
  40.9 3.9 %collective-permute-start.13 = (bf16[128,576]{1,0:T(8,128)(2,1)S(1)}, bf16[128,576]{1,0:T(8,128)(2,1)S(1)}, u32[]{:S(2)}, u32[]{:S(2)}) collective-permute-start(bf16[128,576]{1,0:T(8,128)(2,1)S(1)} %excited_block_kernel.1.own_ref), channel_id=1, source_target_pairs={{0,1},{1,0},{2,3},{3,2},{4,5},{5,4},{6,7},{7,6},{8,9},{9,8},{10,11... | collective-permute-start | bytes 442376 | tf_op jit(solution)/shard_map/ppermute | solution.py:26
  44.8 1.0 %collective-permute-done.13.mate_ref = bf16[128,576]{1,0:T(8,128)(2,1)S(1)} collective-permute-done((bf16[128,576]{1,0:T(8,128)(2,1)S(1)}, bf16[128,576]{1,0:T(8,128)(2,1)S(1)}, u32[]{:S(2)}, u32[]{:S(2)}) %collective-permute-start.13) | collective-permute-done | bytes 147488 | tf_op jit(solution)/shard_map/ppermute | solution.py:26
  45.8 0.5 mixed_blocks_kernel.1
  46.4 0.5 collective-permute-start.16
  46.9 2.7 %collective-permute-start.17 = (bf16[2,128,128]{2,1,0:T(8,128)(2,1)S(1)}, bf16[2,128,128]{2,1,0:T(8,128)(2,1)S(1)}, u32[]{:S(2)}, u32[]{:S(2)}) collective-permute-start(bf16[2,128,128]{2,1,0:T(8,128)(2,1)S(1)} %get-tuple-element.67), channel_id=1, source_target_pairs={{0,24},{1,9},{8,16},{9,1},{16,8},{17,25},{24,0},{25,17},{2,26},{3,... | collective-permute-start | bytes 196616 | tf_op jit(solution)/shard_map/ppermute | solution.py:346
  49.7 3.0 %rest_of_alpha_kernel.1.same_ref = f32[1024,128]{1,0:T(8,128)S(1)} custom-call(bf16[4096,128]{1,0:T(8,128)(2,1)S(1)} %get-tuple-element.68.picked, bf16[1024,4096]{1,0:T(8,128)(2,1)} %ops_ref.5, f32[1024,128]{1,0:T(8,128)S(1)} %get-tuple-element.69.start_ref), custom_call_target="tpu_custom_call" | custom-call | flops 536870912 | bytes 5242880 | tf_op jit(solution)/shard_map/rest_of_alpha_kernel/pallas_call | solution.py:43
  52.8 1.4 %finished_kernel.1 = f32[1024,128]{1,0:T(8,128)} custom-call(s32[12]{0:T(128)S(1)} %stack.60.where_ref, f32[1024,128]{1,0:T(8,128)S(1)} %rest_of_alpha_kernel.1.same_ref, f32[2,128,128]{2,1,0:T(8,128)S(1)} %get-tuple-element.71.m0, bf16[2,128,128]{2,1,0:T(8,128)(2,1)S(1)} %collective-permute-done.15.m1, bf16[2,128,128]{2,1,0:T(8,128)(2,1)S(1)} %collective-permute-done.16.m2, ...), custom_call_target="tpu_custom_call" | custom-call | flops 262144 | bytes 2097152 | tf_op jit(solution)/shard_map/finished_kernel/pallas_call | solution.py:43
  (28 shorter events, 1.5 us)
Async XLA Ops:
  0.0 10.1 %collective-permute-start = (bf16[1024,128]{1,0:T(8,128)(2,1)}, bf16[1024,128]{1,0:T(8,128)(2,1)S(1)}, u32[]{:S(2)}, u32[]{:S(2)}) collective-permute-start(bf16[1024,128]{1,0:T(8,128)(2,1)} %coef_ref.1), channel_id=1, source_target_pairs={{0,1},{1,0},{2,3},{3,2},{4,5},{5,4},{6,7},{7,6},{8,9},{9,8},{10,11... | collective-permute-start | bytes 786440 | tf_op jit(solution)/shard_map/ppermute | solution.py:26
  3.2 6.8 %collective-permute-start.1 = (bf16[576,128]{1,0:T(8,128)(2,1)}, bf16[576,128]{1,0:T(8,128)(2,1)S(1)}, u32[]{:S(2)}, u32[]{:S(2)}) collective-permute-start(bf16[576,128]{1,0:T(8,128)(2,1)} %bitcast.21), channel_id=1, source_target_pairs={{0,1},{1,0},{2,3},{3,2},{4,5},{5,4},{6,7},{7,6},{8,9},{9,8},{10,11... | collective-permute-start | bytes 442376 | tf_op jit(solution)/shard_map/ppermute | solution.py:26
  3.2 15.3 %collective-permute-start.5 = (bf16[1024,128]{1,0:T(8,128)(2,1)}, bf16[1024,128]{1,0:T(8,128)(2,1)S(1)}, u32[]{:S(2)}, u32[]{:S(2)}) collective-permute-start(bf16[1024,128]{1,0:T(8,128)(2,1)} %coef_ref.1), channel_id=1, source_target_pairs={{0,2},{1,3},{2,4},{3,5},{4,6},{5,7},{6,8},{7,9},{8,10},{9,11},{10,... | collective-permute-start | bytes 786440 | tf_op jit(solution)/shard_map/ppermute | solution.py:31
  4.5 18.4 %collective-permute-start.6 = (bf16[1024,128]{1,0:T(8,128)(2,1)}, bf16[1024,128]{1,0:T(8,128)(2,1)S(1)}, u32[]{:S(2)}, u32[]{:S(2)}) collective-permute-start(bf16[1024,128]{1,0:T(8,128)(2,1)} %coef_ref.1), channel_id=1, source_target_pairs={{0,30},{1,31},{2,0},{3,1},{4,2},{5,3},{6,4},{7,5},{8,6},{9,7},{10,... | collective-permute-start | bytes 786440 | tf_op jit(solution)/shard_map/ppermute | solution.py:31
  12.0 10.9 %collective-permute-start.2 = (bf16[576,128]{1,0:T(8,128)(2,1)S(1)}, bf16[576,128]{1,0:T(8,128)(2,1)S(1)}, u32[]{:S(2)}, u32[]{:S(2)}) collective-permute-start(bf16[576,128]{1,0:T(8,128)(2,1)S(1)} %get-tuple-element.41), channel_id=1, source_target_pairs={{0,8},{1,25},{8,0},{9,17},{16,24},{17,9},{24,16},{25,1},{2,10},{3,... | collective-permute-start | bytes 442376 | tf_op jit(solution)/shard_map/ppermute | solution.py:320
  12.5 10.4 %collective-permute-start.3 = (bf16[576,128]{1,0:T(8,128)(2,1)S(1)}, bf16[576,128]{1,0:T(8,128)(2,1)S(1)}, u32[]{:S(2)}, u32[]{:S(2)}) collective-permute-start(bf16[576,128]{1,0:T(8,128)(2,1)S(1)} %get-tuple-element.42), channel_id=1, source_target_pairs={{0,24},{1,9},{8,16},{9,1},{16,8},{17,25},{24,0},{25,17},{2,26},{3,... | collective-permute-start | bytes 442376 | tf_op jit(solution)/shard_map/ppermute | solution.py:320
  12.5 11.9 %collective-permute-start.4 = (bf16[576,128]{1,0:T(8,128)(2,1)S(1)}, bf16[576,128]{1,0:T(8,128)(2,1)S(1)}, u32[]{:S(2)}, u32[]{:S(2)}) collective-permute-start(bf16[576,128]{1,0:T(8,128)(2,1)S(1)} %get-tuple-element.43), channel_id=1, source_target_pairs={{0,16},{1,17},{8,24},{9,25},{16,0},{17,1},{24,8},{25,9},{2,18},{3,... | collective-permute-start | bytes 442376 | tf_op jit(solution)/shard_map/ppermute | solution.py:320
  18.5 11.9 %collective-permute-start.11 = (bf16[1024,128]{1,0:T(8,128)(2,1)}, bf16[1024,128]{1,0:T(8,128)(2,1)S(1)}, u32[]{:S(2)}, u32[]{:S(2)}) collective-permute-start(bf16[1024,128]{1,0:T(8,128)(2,1)} %coef_ref.1), channel_id=1, source_target_pairs={{0,32},{32,0},{1,33},{33,1},{2,34},{34,2},{3,35},{35,3},{4,36},{36... | collective-permute-start | bytes 786440 | tf_op jit(solution)/shard_map/ppermute | solution.py:26
  24.5 8.3 %collective-permute-start.7 = (bf16[576,128]{1,0:T(8,128)(2,1)S(1)}, bf16[576,128]{1,0:T(8,128)(2,1)S(1)}, u32[]{:S(2)}, u32[]{:S(2)}) collective-permute-start(bf16[576,128]{1,0:T(8,128)(2,1)S(1)} %add_convert_fusion.1), channel_id=1, source_target_pairs={{0,2},{1,7},{2,0},{3,5},{4,6},{5,3},{6,4},{7,1},{8,10},{9,15},{10,... | collective-permute-start | bytes 442376 | tf_op jit(solution)/shard_map/ppermute | solution.py:330
  24.6 8.2 %collective-permute-start.8 = (bf16[576,128]{1,0:T(8,128)(2,1)S(1)}, bf16[576,128]{1,0:T(8,128)(2,1)S(1)}, u32[]{:S(2)}, u32[]{:S(2)}) collective-permute-start(bf16[576,128]{1,0:T(8,128)(2,1)S(1)} %get-tuple-element.52.pair_ref), channel_id=1, source_target_pairs={{0,8},{1,25},{8,0},{9,17},{16,24},{17,9},{24,16},{25,1},{2,10},{3,... | collective-permute-start | bytes 442376 | tf_op jit(solution)/shard_map/ppermute | solution.py:332
  30.3 2.6 %collective-permute-start.9 = (bf16[1024,128]{1,0:T(8,128)(2,1)S(1)}, bf16[1024,128]{1,0:T(8,128)(2,1)S(1)}, u32[]{:S(2)}, u32[]{:S(2)}) collective-permute-start(bf16[1024,128]{1,0:T(8,128)(2,1)S(1)} %broadcast_select_fusion), channel_id=1, source_target_pairs={{0,1},{1,0},{2,3},{3,2},{4,5},{5,4},{6,7},{7,6},{8,9},{9,8},{10,11... | collective-permute-start | bytes 786440 | tf_op jit(solution)/shard_map/ppermute | solution.py:26
  30.4 6.5 %collective-permute-start.12 = (bf16[1024,128]{1,0:T(8,128)(2,1)S(1)}, bf16[1024,128]{1,0:T(8,128)(2,1)S(1)}, u32[]{:S(2)}, u32[]{:S(2)}) collective-permute-start(bf16[1024,128]{1,0:T(8,128)(2,1)S(1)} %collective-permute-done.11.near_ref), channel_id=1, source_target_pairs={{0,64},{32,224},{64,128},{96,32},{128,192},{160,96},{192,0},{224,1... | collective-permute-start | bytes 786440 | tf_op jit(solution)/shard_map/ppermute | solution.py:329
  32.9 7.6 %collective-permute-start.10 = (bf16[576,128]{1,0:T(8,128)(2,1)S(1)}, bf16[576,128]{1,0:T(8,128)(2,1)S(1)}, u32[]{:S(2)}, u32[]{:S(2)}) collective-permute-start(bf16[576,128]{1,0:T(8,128)(2,1)S(1)} %add_convert_fusion.near_ref), channel_id=1, source_target_pairs={{0,6},{1,3},{2,4},{3,1},{4,2},{5,7},{6,0},{7,5},{8,14},{9,11},{10,... | collective-permute-start | bytes 442376 | tf_op jit(solution)/shard_map/ppermute | solution.py:338
  33.3 11.5 %collective-permute-start.14 = (bf16[2,576,128]{2,1,0:T(8,128)(2,1)S(1)}, bf16[2,576,128]{2,1,0:T(8,128)(2,1)S(1)}, u32[]{:S(2)}, u32[]{:S(2)}) collective-permute-start(bf16[2,576,128]{2,1,0:T(8,128)(2,1)S(1)} %pad_maximum_fusion), channel_id=1, source_target_pairs={{0,24},{1,9},{8,16},{9,1},{16,8},{17,25},{24,0},{25,17},{2,26},{3,... | collective-permute-start | bytes 884744 | tf_op jit(solution)/shard_map/ppermute | solution.py:337
  40.5 12.3 %copy-start = (f32[1024,128]{1,0:T(8,128)S(1)}, f32[1024,128]{1,0:T(8,128)}, u32[]{:S(2)}) copy-start(f32[1024,128]{1,0:T(8,128)} %den_ref.1) | copy-start | bytes 1572868
  40.9 5.0 %collective-permute-start.13 = (bf16[128,576]{1,0:T(8,128)(2,1)S(1)}, bf16[128,576]{1,0:T(8,128)(2,1)S(1)}, u32[]{:S(2)}, u32[]{:S(2)}) collective-permute-start(bf16[128,576]{1,0:T(8,128)(2,1)S(1)} %excited_block_kernel.1.own_ref), channel_id=1, source_target_pairs={{0,1},{1,0},{2,3},{3,2},{4,5},{5,4},{6,7},{7,6},{8,9},{9,8},{10,11... | collective-permute-start | bytes 442376 | tf_op jit(solution)/shard_map/ppermute | solution.py:26
  46.3 6.3 %collective-permute-start.15 = (bf16[2,128,128]{2,1,0:T(8,128)(2,1)S(1)}, bf16[2,128,128]{2,1,0:T(8,128)(2,1)S(1)}, u32[]{:S(2)}, u32[]{:S(2)}) collective-permute-start(bf16[2,128,128]{2,1,0:T(8,128)(2,1)S(1)} %get-tuple-element.65), channel_id=1, source_target_pairs={{0,8},{1,25},{8,0},{9,17},{16,24},{17,9},{24,16},{25,1},{2,10},{3,... | collective-permute-start | bytes 196616 | tf_op jit(solution)/shard_map/ppermute | solution.py:346
  46.4 6.2 %collective-permute-start.16 = (bf16[2,128,128]{2,1,0:T(8,128)(2,1)S(1)}, bf16[2,128,128]{2,1,0:T(8,128)(2,1)S(1)}, u32[]{:S(2)}, u32[]{:S(2)}) collective-permute-start(bf16[2,128,128]{2,1,0:T(8,128)(2,1)S(1)} %get-tuple-element.66), channel_id=1, source_target_pairs={{0,16},{1,17},{8,24},{9,25},{16,0},{17,1},{24,8},{25,9},{2,18},{3,... | collective-permute-start | bytes 196616 | tf_op jit(solution)/shard_map/ppermute | solution.py:346
  46.9 5.8 %collective-permute-start.17 = (bf16[2,128,128]{2,1,0:T(8,128)(2,1)S(1)}, bf16[2,128,128]{2,1,0:T(8,128)(2,1)S(1)}, u32[]{:S(2)}, u32[]{:S(2)}) collective-permute-start(bf16[2,128,128]{2,1,0:T(8,128)(2,1)S(1)} %get-tuple-element.67), channel_id=1, source_target_pairs={{0,24},{1,9},{8,16},{9,1},{16,8},{17,25},{24,0},{25,17},{2,26},{3,... | collective-permute-start | bytes 196616 | tf_op jit(solution)/shard_map/ppermute | solution.py:346

commit v17 on v15

--- a/solution.py
+++ b/solution.py
@@ -85,16 +85,17 @@
 def density_parts(where, own, mate, pair_own, pair_mate):
     pairs, width = pair_mate.shape
 
-    def density_parts_kernel(where_ref, own_ref, mate_ref, po_ref, pm_ref, *outs):
+    def density_parts_kernel(where_ref, own_ref, mate_ref, po_ref, pm_ref, kept, beside, across):
         left = jnp.concatenate([po_ref[...], pm_ref[...]], axis=1)
-        for k, out in enumerate(outs):
+        for k, out in ((1, beside.at[0]), (5, beside.at[1]), (2, across), (0, kept)):
             rows = block_rows(where_ref, k, width)
             right = jnp.concatenate([own_ref[rows, :], mate_ref[rows, :]], axis=1)
             out[...] = dot(left, right, ((1,), (1,))).astype(BF16)
 
+    one = shape((pairs, width))
     return call(
         density_parts_kernel,
-        [shape((pairs, width))] * 4,
+        [one, shape((2, pairs, width)), one],
         (where, own, mate, pair_own, pair_mate),
         [SMEM] + [VMEM] * 4,
         (16 * pairs * width * width, 1 * MIB),
@@ -320,15 +321,17 @@
     for i in range(xs):
         route += [(2 * i, 2 * ((i + 1) % xs)), (2 * i + 1, 2 * ((i - 1) % xs) + 1)]
 
-    parts = density_parts(where, coef_v, mate, pair_v, pair_mate)
+    kept, sent, across = density_parts(where, coef_v, mate, pair_v, pair_mate)
     coupling, scale, placed = staged(
-        where, cols, pair_coupling, pair_alpha.T, beta_ops, parts[0]
+        where, cols, pair_coupling, pair_alpha.T, beta_ops, kept
     )
     turns = (None, crossing((1, 3)), crossing((2, 2)), crossing((3, 1)))
-    got = [lax.ppermute(parts[k], ("y", "c"), turns[k]) for k in (1, 3, 2)]
+    sent = lax.ppermute(sent, ("y", "c"), turns[1])
+    across = lax.ppermute(across, ("y", "c"), turns[2])
+    got = [sent[0], swapped(sent[1], "c", 1), across]
     *got, below, above = lax.optimization_barrier((*got, below, above))
     near = swapped(coef, "zl", 1)
-    total = parts[0].astype(F32)
+    total = kept.astype(F32)
     for part in got:
         total = total + part.astype(F32)
     total = total.astype(BF16)

time: 55.2 us -> 56 us (1.014)
  waiting for transfers between devices: 5.46 us -> 13.5 us
  starting transfers between devices: 34.4 us -> 27.7 us
    ppermute x2, waiting for transfers between devices: 0.01 us -> 7.88 us  [rotated(): lax.ppermute(block, axis, [(i, (i + distance) % count) for i in range(cou...]
    ppermute x1, starting transfers between devices: 5.67 us -> 0.54 us  [local(): beside = lax.ppermute(sent, ('y', 'c'), turns[1])]
    ppermute x1, starting transfers between devices: 0.09 us -> 3.19 us  [local(): first = lax.ppermute(total, ('zh', 'c'), turns[1])]
    ppermute x5 -> x6, starting transfers between devices: 11.6 us -> 9.08 us  [swapped(): return lax.ppermute(block, axis, [(i, i ^ mask) for i in range(count)])]
    ppermute x3 -> x2, waiting for transfers between devices: 1.51 us -> 0.01 us  [the longest x1 0.01 us: local(): across = lax.ppermute(across, ('y', 'c'), turns[2])]
    ppermute x3 -> x2, starting transfers between devices: 3.95 us -> 2.55 us  [the longest x1 1.47 us: local(): across = lax.ppermute(across, ('y', 'c'), turns[2])]
    ppermute x1, starting transfers between devices: 1.43 us -> 0.09 us  [local(): beyond = lax.ppermute(jnp.stack([pair_v, beside]), ('y', 'c'), turns[3])]
    ppermute x1, starting transfers between devices: 0.4 us -> 1.48 us  [local(): second = lax.ppermute(total, ('zh', 'c'), turns[3])]
  transfers between devices with their start and end apart: 18 -> 18, of which waited for: 5 -> 9; matrix products, arithmetic and copies ran while one was open for 2% -> 2% of each run, Pallas kernels for 21% -> 18%
where the time goes in v17:
time: 56 us; the launch traced here: 55.6 us
  starting transfers between devices  27.7 us (49%)
  waiting for transfers between devices  13.5 us (24%)
  Pallas kernels  13.1 us (23%)
  other arithmetic  0.94 us (2%)
    pallas_call x9, Pallas kernels, call(): pl.pallas_call(kernel, out_shape=outs, in_specs=specs, out_specs=out_spec...  13.1 us
    ppermute x6, starting transfers between devices, swapped(): return lax.ppermute(block, axis, [(i, i ^ mask) for i in range(count)])  9.08 us
    ppermute x2, waiting for transfers between devices, rotated(): lax.ppermute(block, axis, [(i, (i + distance) % count) for i in range(cou...  7.88 us
    ppermute x2, starting transfers between devices, rotated(): lax.ppermute(block, axis, [(i, (i + distance) % count) for i in range(cou...  5.92 us
    ppermute x3, starting transfers between devices, local(): back = [lax.ppermute(out[k - 1], ('y', 'c'), turns[k]) for k in (1, 2, 3)]  3.59 us
    ppermute x1, starting transfers between devices, local(): first = lax.ppermute(total, ('zh', 'c'), turns[1])  3.19 us
    ppermute x1, waiting for transfers between devices, local(): beside = lax.ppermute(sent, ('y', 'c'), turns[1])  2.16 us
    ppermute x6, waiting for transfers between devices, swapped(): return lax.ppermute(block, axis, [(i, i ^ mask) for i in range(count)])  1.76 us
  transfers between devices with their start and end apart: 18, of which 9 were waited for; matrix products, arithmetic and copies ran while one was open for 2% of the time, Pallas kernels for 18%

profile of v17, /device:TPU:1, one launch (start us, length us, event | category | flops | bytes accessed | tf_op | source)
XLA Modules:
  0.0 55.6 jit_solution(15613469890331087959)
XLA Ops:
  0.0 3.2 %collective-permute-start = (bf16[1024,128]{1,0:T(8,128)(2,1)}, bf16[1024,128]{1,0:T(8,128)(2,1)S(1)}, u32[]{:S(2)}, u32[]{:S(2)}) collective-permute-start(bf16[1024,128]{1,0:T(8,128)(2,1)} %coef_ref.1), channel_id=1, source_target_pairs={{0,1},{1,0},{2,3},{3,2},{4,5},{5,4},{6,7},{7,6},{8,9},{9,8},{10,11... | collective-permute-start | bytes 786440 | tf_op jit(solution)/shard_map/ppermute | solution.py:26
  3.2 1.0 %loaded_kernel.1 = (bf16[1024,128]{1,0:T(8,128)(2,1)S(1)}, bf16[576,128]{1,0:T(8,128)(2,1)S(1)}) custom-call(bf16[1024,128]{1,0:T(8,128)(2,1)} %coef_ref.1, bf16[576,128]{1,0:T(8,128)(2,1)} %bitcast.26), custom_call_target="tpu_custom_call" | custom-call | bytes 1048576 | tf_op jit(solution)/shard_map/loaded_kernel/pallas_call | solution.py:43
  4.8 1.0 %density_parts_kernel.1 = (bf16[576,128]{1,0:T(8,128)(2,1)S(1)}, bf16[2,576,128]{2,1,0:T(8,128)(2,1)S(1)}, bf16[576,128]{1,0:T(8,128)(2,1)S(1)}) custom-call(s32[12]{0:T(128)S(1)} %stack.60.where_ref, bf16[1024,128]{1,0:T(8,128)(2,1)S(1)} %get-tuple-element.39.own_ref.b2, bf16[1024,128]{1,0:T(8,128)(2,1)S(1)} %collective-permute-done.mate_ref.b3, ...), custom_call_target="tpu_custom_call" | custom-call | flops 150994944 | bytes 1048576 | tf_op jit(solution)/shard_map/density_parts_kernel/pallas_call | solution.py:43
  5.8 1.1 %collective-permute-start.2 = (bf16[2,576,128]{2,1,0:T(8,128)(2,1)S(1)}, bf16[2,576,128]{2,1,0:T(8,128)(2,1)S(1)}, u32[]{:S(2)}, u32[]{:S(2)}) collective-permute-start(bf16[2,576,128]{2,1,0:T(8,128)(2,1)S(1)} %get-tuple-element.42), channel_id=1, source_target_pairs={{0,8},{1,25},{8,0},{9,17},{16,24},{17,9},{24,16},{25,1},{2,10},{3,... | collective-permute-start | bytes 884744 | tf_op jit(solution)/shard_map/ppermute | solution.py:329
  6.9 3.0 %collective-permute-start.5 = (bf16[1024,128]{1,0:T(8,128)(2,1)}, bf16[1024,128]{1,0:T(8,128)(2,1)S(1)}, u32[]{:S(2)}, u32[]{:S(2)}) collective-permute-start(bf16[1024,128]{1,0:T(8,128)(2,1)} %coef_ref.1), channel_id=1, source_target_pairs={{0,2},{1,3},{2,4},{3,5},{4,6},{5,7},{6,8},{7,9},{8,10},{9,11},{10,... | collective-permute-start | bytes 786440 | tf_op jit(solution)/shard_map/ppermute | solution.py:31
  9.9 2.9 %collective-permute-start.6 = (bf16[1024,128]{1,0:T(8,128)(2,1)}, bf16[1024,128]{1,0:T(8,128)(2,1)S(1)}, u32[]{:S(2)}, u32[]{:S(2)}) collective-permute-start(bf16[1024,128]{1,0:T(8,128)(2,1)} %coef_ref.1), channel_id=1, source_target_pairs={{0,30},{1,31},{2,0},{3,1},{4,2},{5,3},{6,4},{7,5},{8,6},{9,7},{10,... | collective-permute-start | bytes 786440 | tf_op jit(solution)/shard_map/ppermute | solution.py:31
  12.9 1.5 %collective-permute-start.4 = (bf16[576,128]{1,0:T(8,128)(2,1)S(1)}, bf16[576,128]{1,0:T(8,128)(2,1)S(1)}, u32[]{:S(2)}, u32[]{:S(2)}) collective-permute-start(bf16[576,128]{1,0:T(8,128)(2,1)S(1)} %get-tuple-element.43), channel_id=1, source_target_pairs={{0,16},{1,17},{8,24},{9,25},{16,0},{17,1},{24,8},{25,9},{2,18},{3,... | collective-permute-start | bytes 442376 | tf_op jit(solution)/shard_map/ppermute | solution.py:330
  14.5 1.3 %collective-permute-start.11 = (bf16[1024,128]{1,0:T(8,128)(2,1)}, bf16[1024,128]{1,0:T(8,128)(2,1)S(1)}, u32[]{:S(2)}, u32[]{:S(2)}) collective-permute-start(bf16[1024,128]{1,0:T(8,128)(2,1)} %coef_ref.1), channel_id=1, source_target_pairs={{0,32},{32,0},{1,33},{33,1},{2,34},{34,2},{3,35},{35,3},{4,36},{36... | collective-permute-start | bytes 786440 | tf_op jit(solution)/shard_map/ppermute | solution.py:26
  16.6 1.8 %staged_kernel.1 = (bf16[576,576]{1,0:T(8,128)(2,1)S(1)}, f32[128,576]{1,0:T(8,128)S(1)}, bf16[128,640]{1,0:T(8,128)(2,1)S(1)}) custom-call(s32[12]{0:T(128)S(1)} %stack.60.where_ref, s32[8]{0:T(128)S(1)} %pad_add_fusion.cols_ref, bf16[576,576]{1,0:T(8,128)(2,1)} %c_ref.1, bf16[576,1024]{1,0:T(8,128)(2,1)} %bitcast.24, bf16[128,512]{1,0:T(8,128)(2,1)} %ops_ref.3, ...), custom_call_target="tpu_custom_call" | custom-call | flops 331776 | bytes 2097152 | tf_op jit(solution)/shard_map/staged_kernel/pallas_call | solution.py:43
  18.4 1.7 %collective-permute-done.5.b0 = bf16[1024,128]{1,0:T(8,128)(2,1)S(1)} collective-permute-done((bf16[1024,128]{1,0:T(8,128)(2,1)}, bf16[1024,128]{1,0:T(8,128)(2,1)S(1)}, u32[]{:S(2)}, u32[]{:S(2)}) %collective-permute-start.5) | collective-permute-done | bytes 262176 | tf_op jit(solution)/shard_map/ppermute | solution.py:31
  20.1 6.2 %collective-permute-done.6.b4 = bf16[1024,128]{1,0:T(8,128)(2,1)S(1)} collective-permute-done((bf16[1024,128]{1,0:T(8,128)(2,1)}, bf16[1024,128]{1,0:T(8,128)(2,1)S(1)}, u32[]{:S(2)}, u32[]{:S(2)}) %collective-permute-start.6) | collective-permute-done | bytes 262176 | tf_op jit(solution)/shard_map/ppermute | solution.py:31
  26.4 3.2 %collective-permute-start.7 = (bf16[576,128]{1,0:T(8,128)(2,1)S(1)}, bf16[576,128]{1,0:T(8,128)(2,1)S(1)}, u32[]{:S(2)}, u32[]{:S(2)}) collective-permute-start(bf16[576,128]{1,0:T(8,128)(2,1)S(1)} %add_convert_fusion.1), channel_id=1, source_target_pairs={{0,2},{1,7},{2,0},{3,5},{4,6},{5,3},{6,4},{7,1},{8,10},{9,15},{10,... | collective-permute-start | bytes 442376 | tf_op jit(solution)/shard_map/ppermute | solution.py:341
  30.2 1.1 %collective-permute-start.9 = (bf16[1024,128]{1,0:T(8,128)(2,1)S(1)}, bf16[1024,128]{1,0:T(8,128)(2,1)S(1)}, u32[]{:S(2)}, u32[]{:S(2)}) collective-permute-start(bf16[1024,128]{1,0:T(8,128)(2,1)S(1)} %broadcast_select_fusion), channel_id=1, source_target_pairs={{0,1},{1,0},{2,3},{3,2},{4,5},{5,4},{6,7},{7,6},{8,9},{9,8},{10,11... | collective-permute-start | bytes 786440 | tf_op jit(solution)/shard_map/ppermute | solution.py:26
  31.6 1.2 %collective-permute-start.12 = (bf16[1024,128]{1,0:T(8,128)(2,1)S(1)}, bf16[1024,128]{1,0:T(8,128)(2,1)S(1)}, u32[]{:S(2)}, u32[]{:S(2)}) collective-permute-start(bf16[1024,128]{1,0:T(8,128)(2,1)S(1)} %collective-permute-done.11.near_ref), channel_id=1, source_target_pairs={{0,64},{32,224},{64,128},{96,32},{128,192},{160,96},{192,0},{224,1... | collective-permute-start | bytes 786440 | tf_op jit(solution)/shard_map/ppermute | solution.py:340
  32.8 2.2 %collective-permute-done.8.beside_ref = bf16[576,128]{1,0:T(8,128)(2,1)S(1)} collective-permute-done((bf16[576,128]{1,0:T(8,128)(2,1)S(1)}, bf16[576,128]{1,0:T(8,128)(2,1)S(1)}, u32[]{:S(2)}, u32[]{:S(2)}) %collective-permute-start.8) | collective-permute-done | bytes 147488 | tf_op jit(solution)/shard_map/ppermute | solution.py:343
  35.1 1.5 %collective-permute-start.10 = (bf16[576,128]{1,0:T(8,128)(2,1)S(1)}, bf16[576,128]{1,0:T(8,128)(2,1)S(1)}, u32[]{:S(2)}, u32[]{:S(2)}) collective-permute-start(bf16[576,128]{1,0:T(8,128)(2,1)S(1)} %add_convert_fusion.near_ref), channel_id=1, source_target_pairs={{0,6},{1,3},{2,4},{3,1},{4,2},{5,7},{6,0},{7,5},{8,14},{9,11},{10,... | collective-permute-start | bytes 442376 | tf_op jit(solution)/shard_map/ppermute | solution.py:349
  37.2 1.3 %collective-permute-done.12.far_ref = bf16[1024,128]{1,0:T(8,128)(2,1)S(1)} collective-permute-done((bf16[1024,128]{1,0:T(8,128)(2,1)S(1)}, bf16[1024,128]{1,0:T(8,128)(2,1)S(1)}, u32[]{:S(2)}, u32[]{:S(2)}) %collective-permute-start.12) | collective-permute-done | bytes 262176 | tf_op jit(solution)/shard_map/ppermute | solution.py:340
  38.6 3.5 %same_spin_alpha_kernel.1 = (f32[1024,128]{1,0:T(8,128)S(1)}, bf16[4096,128]{1,0:T(8,128)(2,1)S(1)}) custom-call(s32[12]{0:T(128)S(1)} %stack.60.where_ref, s32[8]{0:T(128)S(1)} %pad_add_fusion.cols_ref, bf16[1024,128]{1,0:T(8,128)(2,1)S(1)} %get-tuple-element.39.own_ref.b2, bf16[1024,128]{1,0:T(8,128)(2,1)S(1)} %collective-permute-done.11.near_ref, ...), custom_call_target="tpu_custom_call" | custom-call | flops 536870912 | bytes 5242880 | tf_op jit(solution)/shard_map/same_spin_alpha_kernel/pallas_call | solution.py:43
  42.5 3.2 %collective-permute-start.13 = (bf16[128,576]{1,0:T(8,128)(2,1)S(1)}, bf16[128,576]{1,0:T(8,128)(2,1)S(1)}, u32[]{:S(2)}, u32[]{:S(2)}) collective-permute-start(bf16[128,576]{1,0:T(8,128)(2,1)S(1)} %excited_block_kernel.1.own_ref), channel_id=1, source_target_pairs={{0,1},{1,0},{2,3},{3,2},{4,5},{5,4},{6,7},{7,6},{8,9},{9,8},{10,11... | collective-permute-start | bytes 442376 | tf_op jit(solution)/shard_map/ppermute | solution.py:26
  45.7 1.0 %collective-permute-done.13.mate_ref = bf16[128,576]{1,0:T(8,128)(2,1)S(1)} collective-permute-done((bf16[128,576]{1,0:T(8,128)(2,1)S(1)}, bf16[128,576]{1,0:T(8,128)(2,1)S(1)}, u32[]{:S(2)}, u32[]{:S(2)}) %collective-permute-start.13) | collective-permute-done | bytes 147488 | tf_op jit(solution)/shard_map/ppermute | solution.py:26
  47.2 1.9 %collective-permute-start.15 = (bf16[2,128,128]{2,1,0:T(8,128)(2,1)S(1)}, bf16[2,128,128]{2,1,0:T(8,128)(2,1)S(1)}, u32[]{:S(2)}, u32[]{:S(2)}) collective-permute-start(bf16[2,128,128]{2,1,0:T(8,128)(2,1)S(1)} %get-tuple-element.63), channel_id=1, source_target_pairs={{0,8},{1,25},{8,0},{9,17},{16,24},{17,9},{24,16},{25,1},{2,10},{3,... | collective-permute-start | bytes 196616 | tf_op jit(solution)/shard_map/ppermute | solution.py:357
  49.2 1.7 %collective-permute-start.16 = (bf16[2,128,128]{2,1,0:T(8,128)(2,1)S(1)}, bf16[2,128,128]{2,1,0:T(8,128)(2,1)S(1)}, u32[]{:S(2)}, u32[]{:S(2)}) collective-permute-start(bf16[2,128,128]{2,1,0:T(8,128)(2,1)S(1)} %get-tuple-element.64), channel_id=1, source_target_pairs={{0,16},{1,17},{8,24},{9,25},{16,0},{17,1},{24,8},{25,9},{2,18},{3,... | collective-permute-start | bytes 196616 | tf_op jit(solution)/shard_map/ppermute | solution.py:357
  50.8 3.0 %rest_of_alpha_kernel.1.same_ref = f32[1024,128]{1,0:T(8,128)S(1)} custom-call(bf16[4096,128]{1,0:T(8,128)(2,1)S(1)} %get-tuple-element.66.picked, bf16[1024,4096]{1,0:T(8,128)(2,1)} %ops_ref.5, f32[1024,128]{1,0:T(8,128)S(1)} %get-tuple-element.67.start_ref), custom_call_target="tpu_custom_call" | custom-call | flops 536870912 | bytes 5242880 | tf_op jit(solution)/shard_map/rest_of_alpha_kernel/pallas_call | solution.py:43
  54.0 1.4 %finished_kernel.1 = f32[1024,128]{1,0:T(8,128)} custom-call(s32[12]{0:T(128)S(1)} %stack.60.where_ref, f32[1024,128]{1,0:T(8,128)S(1)} %rest_of_alpha_kernel.1.same_ref, f32[2,128,128]{2,1,0:T(8,128)S(1)} %get-tuple-element.69.m0, bf16[2,128,128]{2,1,0:T(8,128)(2,1)S(1)} %collective-permute-done.15.m1, bf16[2,128,128]{2,1,0:T(8,128)(2,1)S(1)} %collective-permute-done.16.m2, ...), custom_call_target="tpu_custom_call" | custom-call | flops 262144 | bytes 2097152 | tf_op jit(solution)/shard_map/finished_kernel/pallas_call | solution.py:43
  (30 shorter events, 4.3 us)
Async XLA Ops:
  0.0 4.8 %collective-permute-start = (bf16[1024,128]{1,0:T(8,128)(2,1)}, bf16[1024,128]{1,0:T(8,128)(2,1)S(1)}, u32[]{:S(2)}, u32[]{:S(2)}) collective-permute-start(bf16[1024,128]{1,0:T(8,128)(2,1)} %coef_ref.1), channel_id=1, source_target_pairs={{0,1},{1,0},{2,3},{3,2},{4,5},{5,4},{6,7},{7,6},{8,9},{9,8},{10,11... | collective-permute-start | bytes 786440 | tf_op jit(solution)/shard_map/ppermute | solution.py:26
  3.2 1.6 %collective-permute-start.1 = (bf16[576,128]{1,0:T(8,128)(2,1)}, bf16[576,128]{1,0:T(8,128)(2,1)S(1)}, u32[]{:S(2)}, u32[]{:S(2)}) collective-permute-start(bf16[576,128]{1,0:T(8,128)(2,1)} %bitcast.25), channel_id=1, source_target_pairs={{0,1},{1,0},{2,3},{3,2},{4,5},{5,4},{6,7},{7,6},{8,9},{9,8},{10,11... | collective-permute-start | bytes 442376 | tf_op jit(solution)/shard_map/ppermute | solution.py:26
  5.8 8.5 %collective-permute-start.2 = (bf16[2,576,128]{2,1,0:T(8,128)(2,1)S(1)}, bf16[2,576,128]{2,1,0:T(8,128)(2,1)S(1)}, u32[]{:S(2)}, u32[]{:S(2)}) collective-permute-start(bf16[2,576,128]{2,1,0:T(8,128)(2,1)S(1)} %get-tuple-element.42), channel_id=1, source_target_pairs={{0,8},{1,25},{8,0},{9,17},{16,24},{17,9},{24,16},{25,1},{2,10},{3,... | collective-permute-start | bytes 884744 | tf_op jit(solution)/shard_map/ppermute | solution.py:329
  6.9 13.2 %collective-permute-start.5 = (bf16[1024,128]{1,0:T(8,128)(2,1)}, bf16[1024,128]{1,0:T(8,128)(2,1)S(1)}, u32[]{:S(2)}, u32[]{:S(2)}) collective-permute-start(bf16[1024,128]{1,0:T(8,128)(2,1)} %coef_ref.1), channel_id=1, source_target_pairs={{0,2},{1,3},{2,4},{3,5},{4,6},{5,7},{6,8},{7,9},{8,10},{9,11},{10,... | collective-permute-start | bytes 786440 | tf_op jit(solution)/shard_map/ppermute | solution.py:31
  9.9 16.4 %collective-permute-start.6 = (bf16[1024,128]{1,0:T(8,128)(2,1)}, bf16[1024,128]{1,0:T(8,128)(2,1)S(1)}, u32[]{:S(2)}, u32[]{:S(2)}) collective-permute-start(bf16[1024,128]{1,0:T(8,128)(2,1)} %coef_ref.1), channel_id=1, source_target_pairs={{0,30},{1,31},{2,0},{3,1},{4,2},{5,3},{6,4},{7,5},{8,6},{9,7},{10,... | collective-permute-start | bytes 786440 | tf_op jit(solution)/shard_map/ppermute | solution.py:31
  12.9 13.5 %collective-permute-start.4 = (bf16[576,128]{1,0:T(8,128)(2,1)S(1)}, bf16[576,128]{1,0:T(8,128)(2,1)S(1)}, u32[]{:S(2)}, u32[]{:S(2)}) collective-permute-start(bf16[576,128]{1,0:T(8,128)(2,1)S(1)} %get-tuple-element.43), channel_id=1, source_target_pairs={{0,16},{1,17},{8,24},{9,25},{16,0},{17,1},{24,8},{25,9},{2,18},{3,... | collective-permute-start | bytes 442376 | tf_op jit(solution)/shard_map/ppermute | solution.py:330
  14.3 12.0 %collective-permute-start.3 = (bf16[576,128]{1,0:T(8,128)(2,1)S(1)}, bf16[576,128]{1,0:T(8,128)(2,1)S(1)}, u32[]{:S(2)}, u32[]{:S(2)}) collective-permute-start(bf16[576,128]{1,0:T(8,128)(2,1)S(1)} %get-tuple-element.73), channel_id=1, source_target_pairs={{0,1},{1,0},{2,3},{3,2},{4,5},{5,4},{6,7},{7,6},{8,9},{9,8},{10,11... | collective-permute-start | bytes 442376 | tf_op jit(solution)/shard_map/ppermute | solution.py:26
  14.5 17.1 %collective-permute-start.11 = (bf16[1024,128]{1,0:T(8,128)(2,1)}, bf16[1024,128]{1,0:T(8,128)(2,1)S(1)}, u32[]{:S(2)}, u32[]{:S(2)}) collective-permute-start(bf16[1024,128]{1,0:T(8,128)(2,1)} %coef_ref.1), channel_id=1, source_target_pairs={{0,32},{32,0},{1,33},{33,1},{2,34},{34,2},{3,35},{35,3},{4,36},{36... | collective-permute-start | bytes 786440 | tf_op jit(solution)/shard_map/ppermute | solution.py:26
  26.4 8.6 %collective-permute-start.7 = (bf16[576,128]{1,0:T(8,128)(2,1)S(1)}, bf16[576,128]{1,0:T(8,128)(2,1)S(1)}, u32[]{:S(2)}, u32[]{:S(2)}) collective-permute-start(bf16[576,128]{1,0:T(8,128)(2,1)S(1)} %add_convert_fusion.1), channel_id=1, source_target_pairs={{0,2},{1,7},{2,0},{3,5},{4,6},{5,3},{6,4},{7,1},{8,10},{9,15},{10,... | collective-permute-start | bytes 442376 | tf_op jit(solution)/shard_map/ppermute | solution.py:341
  29.6 5.3 %collective-permute-start.8 = (bf16[576,128]{1,0:T(8,128)(2,1)S(1)}, bf16[576,128]{1,0:T(8,128)(2,1)S(1)}, u32[]{:S(2)}, u32[]{:S(2)}) collective-permute-start(bf16[576,128]{1,0:T(8,128)(2,1)S(1)} %get-tuple-element.51.po_ref.pair_ref), channel_id=1, source_target_pairs={{0,8},{1,25},{8,0},{9,17},{16,24},{17,9},{24,16},{25,1},{2,10},{3,... | collective-permute-start | bytes 442376 | tf_op jit(solution)/shard_map/ppermute | solution.py:343
  30.2 4.9 %collective-permute-start.9 = (bf16[1024,128]{1,0:T(8,128)(2,1)S(1)}, bf16[1024,128]{1,0:T(8,128)(2,1)S(1)}, u32[]{:S(2)}, u32[]{:S(2)}) collective-permute-start(bf16[1024,128]{1,0:T(8,128)(2,1)S(1)} %broadcast_select_fusion), channel_id=1, source_target_pairs={{0,1},{1,0},{2,3},{3,2},{4,5},{5,4},{6,7},{7,6},{8,9},{9,8},{10,11... | collective-permute-start | bytes 786440 | tf_op jit(solution)/shard_map/ppermute | solution.py:26
  31.6 7.0 %collective-permute-start.12 = (bf16[1024,128]{1,0:T(8,128)(2,1)S(1)}, bf16[1024,128]{1,0:T(8,128)(2,1)S(1)}, u32[]{:S(2)}, u32[]{:S(2)}) collective-permute-start(bf16[1024,128]{1,0:T(8,128)(2,1)S(1)} %collective-permute-done.11.near_ref), channel_id=1, source_target_pairs={{0,64},{32,224},{64,128},{96,32},{128,192},{160,96},{192,0},{224,1... | collective-permute-start | bytes 786440 | tf_op jit(solution)/shard_map/ppermute | solution.py:340
  35.1 7.0 %collective-permute-start.10 = (bf16[576,128]{1,0:T(8,128)(2,1)S(1)}, bf16[576,128]{1,0:T(8,128)(2,1)S(1)}, u32[]{:S(2)}, u32[]{:S(2)}) collective-permute-start(bf16[576,128]{1,0:T(8,128)(2,1)S(1)} %add_convert_fusion.near_ref), channel_id=1, source_target_pairs={{0,6},{1,3},{2,4},{3,1},{4,2},{5,7},{6,0},{7,5},{8,14},{9,11},{10,... | collective-permute-start | bytes 442376 | tf_op jit(solution)/shard_map/ppermute | solution.py:349
  36.6 9.1 %collective-permute-start.14 = (bf16[2,576,128]{2,1,0:T(8,128)(2,1)S(1)}, bf16[2,576,128]{2,1,0:T(8,128)(2,1)S(1)}, u32[]{:S(2)}, u32[]{:S(2)}) collective-permute-start(bf16[2,576,128]{2,1,0:T(8,128)(2,1)S(1)} %pad_maximum_fusion), channel_id=1, source_target_pairs={{0,24},{1,9},{8,16},{9,1},{16,8},{17,25},{24,0},{25,17},{2,26},{3,... | collective-permute-start | bytes 884744 | tf_op jit(solution)/shard_map/ppermute | solution.py:348
  42.1 11.9 %copy-start = (f32[1024,128]{1,0:T(8,128)S(1)}, f32[1024,128]{1,0:T(8,128)}, u32[]{:S(2)}) copy-start(f32[1024,128]{1,0:T(8,128)} %den_ref.1) | copy-start | bytes 1572868
  42.5 4.2 %collective-permute-start.13 = (bf16[128,576]{1,0:T(8,128)(2,1)S(1)}, bf16[128,576]{1,0:T(8,128)(2,1)S(1)}, u32[]{:S(2)}, u32[]{:S(2)}) collective-permute-start(bf16[128,576]{1,0:T(8,128)(2,1)S(1)} %excited_block_kernel.1.own_ref), channel_id=1, source_target_pairs={{0,1},{1,0},{2,3},{3,2},{4,5},{5,4},{6,7},{7,6},{8,9},{9,8},{10,11... | collective-permute-start | bytes 442376 | tf_op jit(solution)/shard_map/ppermute | solution.py:26
  47.2 6.6 %collective-permute-start.15 = (bf16[2,128,128]{2,1,0:T(8,128)(2,1)S(1)}, bf16[2,128,128]{2,1,0:T(8,128)(2,1)S(1)}, u32[]{:S(2)}, u32[]{:S(2)}) collective-permute-start(bf16[2,128,128]{2,1,0:T(8,128)(2,1)S(1)} %get-tuple-element.63), channel_id=1, source_target_pairs={{0,8},{1,25},{8,0},{9,17},{16,24},{17,9},{24,16},{25,1},{2,10},{3,... | collective-permute-start | bytes 196616 | tf_op jit(solution)/shard_map/ppermute | solution.py:357
  49.2 4.7 %collective-permute-start.16 = (bf16[2,128,128]{2,1,0:T(8,128)(2,1)S(1)}, bf16[2,128,128]{2,1,0:T(8,128)(2,1)S(1)}, u32[]{:S(2)}, u32[]{:S(2)}) collective-permute-start(bf16[2,128,128]{2,1,0:T(8,128)(2,1)S(1)} %get-tuple-element.64), channel_id=1, source_target_pairs={{0,16},{1,17},{8,24},{9,25},{16,0},{17,1},{24,8},{25,9},{2,18},{3,... | collective-permute-start | bytes 196616 | tf_op jit(solution)/shard_map/ppermute | solution.py:357
  50.8 3.2 %collective-permute-start.17 = (bf16[2,128,128]{2,1,0:T(8,128)(2,1)S(1)}, bf16[2,128,128]{2,1,0:T(8,128)(2,1)S(1)}, u32[]{:S(2)}, u32[]{:S(2)}) collective-permute-start(bf16[2,128,128]{2,1,0:T(8,128)(2,1)S(1)} %get-tuple-element.65), channel_id=1, source_target_pairs={{0,24},{1,9},{8,16},{9,1},{16,8},{17,25},{24,0},{25,17},{2,26},{3,... | collective-permute-start | bytes 196616 | tf_op jit(solution)/shard_map/ppermute | solution.py:357

commit v18 on v15

--- a/solution.py
+++ b/solution.py
@@ -223,11 +223,11 @@
     )[0]
 
 
-def alpha_rows(ops_ref, picked, start_ref, out_ref, ops_v, sems, part, select):
+def alpha_rows(ops_ref, picked, start_ref, out_ref, ops_v, sems, first, select):
     step = ops_v.shape[1]
-    half = start_ref.shape[0] // 2
-    mine = range(part * half, (part + 1) * half, step)
-    rest = slice((1 - part) * half, (2 - part) * half)
+    last = first + ops_v.shape[0] * step
+    mine = range(first, last, step)
+    rest = slice(last, None) if first == 0 else slice(0, first)
     copies = [
         pltpu.make_async_copy(ops_ref.at[r : r + step, :], ops_v.at[n], sems.at[n])
         for n, r in enumerate(mine)
@@ -268,7 +268,7 @@
         (where, cols, *blocks, alpha_ops, start),
         [SMEM, SMEM] + [VMEM] * 3 + [HBM, VMEM],
         (rows * width * depth * 4, 5 * MIB),
-        [pltpu.VMEM((4, rows // 8, span), BF16), pltpu.SemaphoreType.DMA((4,))],
+        [pltpu.VMEM((3, rows // 8, span), BF16), pltpu.SemaphoreType.DMA((3,))],
     )
 
 
@@ -277,7 +277,7 @@
     span = alpha_ops.shape[1]
 
     def rest_of_alpha_kernel(picked, ops_ref, start_ref, out_ref, ops_v, sems):
-        alpha_rows(ops_ref, picked, start_ref, out_ref, ops_v, sems, 1, lambda: None)
+        alpha_rows(ops_ref, picked, start_ref, out_ref, ops_v, sems, rows - 5 * (rows // 8), lambda: None)
 
     return call(
         rest_of_alpha_kernel,
@@ -285,7 +285,7 @@
         (picked, alpha_ops, start),
         [VMEM, HBM, VMEM],
         (rows * width * span, 5 * MIB),
-        [pltpu.VMEM((4, rows // 8, span), BF16), pltpu.SemaphoreType.DMA((4,))],
+        [pltpu.VMEM((5, rows // 8, span), BF16), pltpu.SemaphoreType.DMA((5,))],
     )[0]
 
 

time: 55.2 us -> 54.8 us (level)
  transfers between devices with their start and end apart: 18 -> 18, of which waited for: 5 -> 4; matrix products, arithmetic and copies ran while one was open for 2% -> 2% of each run, Pallas kernels for 21% -> 21%
where the time goes in v18:
time: 54.8 us; the launch traced here: 54.3 us
  starting transfers between devices  34.4 us (63%)
  Pallas kernels  13.1 us (24%)
  waiting for transfers between devices  5.37 us (10%)
  other arithmetic  0.93 us (2%)
    pallas_call x9, Pallas kernels, call(): pl.pallas_call(kernel, out_shape=outs, in_specs=specs, out_specs=out_spec...  13.1 us
    ppermute x5, starting transfers between devices, swapped(): return lax.ppermute(block, axis, [(i, i ^ mask) for i in range(count)])  11.5 us
    ppermute x2, starting transfers between devices, rotated(): lax.ppermute(block, axis, [(i, (i + distance) % count) for i in range(cou...  6.74 us
    ppermute x1, starting transfers between devices, local(): beside = lax.ppermute(sent, ('y', 'c'), turns[1])  5.67 us
    ppermute x3, starting transfers between devices, local(): got = [lax.ppermute(parts[k], ('y', 'c'), turns[k]) for k in (1, 3, 2)]  3.95 us
    ppermute x3, starting transfers between devices, local(): back = [lax.ppermute(out[k - 1], ('y', 'c'), turns[k]) for k in (1, 2, 3)]  3.33 us
    ppermute x1, waiting for transfers between devices, local(): far = lax.ppermute(near, ALPHA, route)  1.7 us
    ppermute x3, waiting for transfers between devices, local(): got = [lax.ppermute(parts[k], ('y', 'c'), turns[k]) for k in (1, 3, 2)]  1.51 us
  transfers between devices with their start and end apart: 18, of which 4 were waited for; matrix products, arithmetic and copies ran while one was open for 2% of the time, Pallas kernels for 21%

profile of v18, /device:TPU:1, one launch (start us, length us, event | category | flops | bytes accessed | tf_op | source)
XLA Modules:
  0.0 54.3 jit_solution(11871283500829760394)
XLA Ops:
  0.0 3.2 %collective-permute-start = (bf16[1024,128]{1,0:T(8,128)(2,1)}, bf16[1024,128]{1,0:T(8,128)(2,1)S(1)}, u32[]{:S(2)}, u32[]{:S(2)}) collective-permute-start(bf16[1024,128]{1,0:T(8,128)(2,1)} %coef_ref.1), channel_id=1, source_target_pairs={{0,1},{1,0},{2,3},{3,2},{4,5},{5,4},{6,7},{7,6},{8,9},{9,8},{10,11... | collective-permute-start | bytes 786440 | tf_op jit(solution)/shard_map/ppermute | solution.py:26
  3.2 1.3 %collective-permute-start.5 = (bf16[1024,128]{1,0:T(8,128)(2,1)}, bf16[1024,128]{1,0:T(8,128)(2,1)S(1)}, u32[]{:S(2)}, u32[]{:S(2)}) collective-permute-start(bf16[1024,128]{1,0:T(8,128)(2,1)} %coef_ref.1), channel_id=1, source_target_pairs={{0,2},{1,3},{2,4},{3,5},{4,6},{5,7},{6,8},{7,9},{8,10},{9,11},{10,... | collective-permute-start | bytes 786440 | tf_op jit(solution)/shard_map/ppermute | solution.py:31
  4.5 5.5 %collective-permute-start.6 = (bf16[1024,128]{1,0:T(8,128)(2,1)}, bf16[1024,128]{1,0:T(8,128)(2,1)S(1)}, u32[]{:S(2)}, u32[]{:S(2)}) collective-permute-start(bf16[1024,128]{1,0:T(8,128)(2,1)} %coef_ref.1), channel_id=1, source_target_pairs={{0,30},{1,31},{2,0},{3,1},{4,2},{5,3},{6,4},{7,5},{8,6},{9,7},{10,... | collective-permute-start | bytes 786440 | tf_op jit(solution)/shard_map/ppermute | solution.py:31
  10.0 1.0 %loaded_kernel.1 = (bf16[1024,128]{1,0:T(8,128)(2,1)S(1)}, bf16[576,128]{1,0:T(8,128)(2,1)S(1)}) custom-call(bf16[1024,128]{1,0:T(8,128)(2,1)} %coef_ref.1, bf16[576,128]{1,0:T(8,128)(2,1)} %bitcast.22), custom_call_target="tpu_custom_call" | custom-call | bytes 1048576 | tf_op jit(solution)/shard_map/loaded_kernel/pallas_call | solution.py:43
  11.1 1.0 %density_parts_kernel.1 = (bf16[576,128]{1,0:T(8,128)(2,1)S(1)}, bf16[576,128]{1,0:T(8,128)(2,1)S(1)}, bf16[576,128]{1,0:T(8,128)(2,1)S(1)}, bf16[576,128]{1,0:T(8,128)(2,1)S(1)}) custom-call(s32[12]{0:T(128)S(1)} %stack.60.where_ref, bf16[1024,128]{1,0:T(8,128)(2,1)S(1)} %get-tuple-element.40.own_ref.b2, ...), custom_call_target="tpu_custom_call" | custom-call | flops 150994944 | bytes 1048576 | tf_op jit(solution)/shard_map/density_parts_kernel/pallas_call | solution.py:43
  12.2 0.6 %collective-permute-start.2 = (bf16[576,128]{1,0:T(8,128)(2,1)S(1)}, bf16[576,128]{1,0:T(8,128)(2,1)S(1)}, u32[]{:S(2)}, u32[]{:S(2)}) collective-permute-start(bf16[576,128]{1,0:T(8,128)(2,1)S(1)} %get-tuple-element.43), channel_id=1, source_target_pairs={{0,8},{1,25},{8,0},{9,17},{16,24},{17,9},{24,16},{25,1},{2,10},{3,... | collective-permute-start | bytes 442376 | tf_op jit(solution)/shard_map/ppermute | solution.py:328
  12.7 3.4 %collective-permute-start.4 = (bf16[576,128]{1,0:T(8,128)(2,1)S(1)}, bf16[576,128]{1,0:T(8,128)(2,1)S(1)}, u32[]{:S(2)}, u32[]{:S(2)}) collective-permute-start(bf16[576,128]{1,0:T(8,128)(2,1)S(1)} %get-tuple-element.45), channel_id=1, source_target_pairs={{0,16},{1,17},{8,24},{9,25},{16,0},{17,1},{24,8},{25,9},{2,18},{3,... | collective-permute-start | bytes 442376 | tf_op jit(solution)/shard_map/ppermute | solution.py:328
  16.1 0.7 %pad_add_fusion.cols_ref = s32[8]{0:T(128)S(1)} fusion(s32[4]{0:T(128)} %bitcast.23, s32[4]{0:T(128)} %bitcast.24), kind=kLoop, calls=%fused_computation.4 | loop fusion | flops 8 | bytes 64 | tf_op jit(solution)/shard_map/concatenate | solution.py:310
  16.9 1.8 %staged_kernel.1 = (bf16[576,576]{1,0:T(8,128)(2,1)S(1)}, f32[128,576]{1,0:T(8,128)S(1)}, bf16[128,640]{1,0:T(8,128)(2,1)S(1)}) custom-call(s32[12]{0:T(128)S(1)} %stack.60.where_ref, s32[8]{0:T(128)S(1)} %pad_add_fusion.cols_ref, bf16[576,576]{1,0:T(8,128)(2,1)} %c_ref.1, bf16[576,1024]{1,0:T(8,128)(2,1)} %bitcast.20, bf16[128,512]{1,0:T(8,128)(2,1)} %ops_ref.3, ...), custom_call_target="tpu_custom_call" | custom-call | flops 331776 | bytes 2097152 | tf_op jit(solution)/shard_map/staged_kernel/pallas_call | solution.py:43
  18.7 4.2 %collective-permute-start.11 = (bf16[1024,128]{1,0:T(8,128)(2,1)}, bf16[1024,128]{1,0:T(8,128)(2,1)S(1)}, u32[]{:S(2)}, u32[]{:S(2)}) collective-permute-start(bf16[1024,128]{1,0:T(8,128)(2,1)} %coef_ref.1), channel_id=1, source_target_pairs={{0,32},{32,0},{1,33},{33,1},{2,34},{34,2},{3,35},{35,3},{4,36},{36... | collective-permute-start | bytes 786440 | tf_op jit(solution)/shard_map/ppermute | solution.py:26
  22.9 1.5 %collective-permute-done.4 = bf16[576,128]{1,0:T(8,128)(2,1)S(1)} collective-permute-done((bf16[576,128]{1,0:T(8,128)(2,1)S(1)}, bf16[576,128]{1,0:T(8,128)(2,1)S(1)}, u32[]{:S(2)}, u32[]{:S(2)}) %collective-permute-start.4) | collective-permute-done | bytes 147488 | tf_op jit(solution)/shard_map/ppermute | solution.py:328
  24.6 5.7 %collective-permute-start.8 = (bf16[576,128]{1,0:T(8,128)(2,1)S(1)}, bf16[576,128]{1,0:T(8,128)(2,1)S(1)}, u32[]{:S(2)}, u32[]{:S(2)}) collective-permute-start(bf16[576,128]{1,0:T(8,128)(2,1)S(1)} %get-tuple-element.53.po_ref.pair_ref), channel_id=1, source_target_pairs={{0,8},{1,25},{8,0},{9,17},{16,24},{17,9},{24,16},{25,1},{2,10},{3,... | collective-permute-start | bytes 442376 | tf_op jit(solution)/shard_map/ppermute | solution.py:340
  30.4 1.3 %collective-permute-start.12 = (bf16[1024,128]{1,0:T(8,128)(2,1)S(1)}, bf16[1024,128]{1,0:T(8,128)(2,1)S(1)}, u32[]{:S(2)}, u32[]{:S(2)}) collective-permute-start(bf16[1024,128]{1,0:T(8,128)(2,1)S(1)} %collective-permute-done.11.near_ref), channel_id=1, source_target_pairs={{0,64},{32,224},{64,128},{96,32},{128,192},{160,96},{192,0},{224,1... | collective-permute-start | bytes 786440 | tf_op jit(solution)/shard_map/ppermute | solution.py:337
  31.7 1.1 %collective-permute-done.8.beside_ref = bf16[576,128]{1,0:T(8,128)(2,1)S(1)} collective-permute-done((bf16[576,128]{1,0:T(8,128)(2,1)S(1)}, bf16[576,128]{1,0:T(8,128)(2,1)S(1)}, u32[]{:S(2)}, u32[]{:S(2)}) %collective-permute-start.8) | collective-permute-done | bytes 147488 | tf_op jit(solution)/shard_map/ppermute | solution.py:340
  33.3 1.4 %collective-permute-start.14 = (bf16[2,576,128]{2,1,0:T(8,128)(2,1)S(1)}, bf16[2,576,128]{2,1,0:T(8,128)(2,1)S(1)}, u32[]{:S(2)}, u32[]{:S(2)}) collective-permute-start(bf16[2,576,128]{2,1,0:T(8,128)(2,1)S(1)} %pad_maximum_fusion), channel_id=1, source_target_pairs={{0,24},{1,9},{8,16},{9,1},{16,8},{17,25},{24,0},{25,17},{2,26},{3,... | collective-permute-start | bytes 884744 | tf_op jit(solution)/shard_map/ppermute | solution.py:345
  34.7 0.5 same_spin_beta_kernel.1.start_ref
  35.3 1.7 %collective-permute-done.12.far_ref = bf16[1024,128]{1,0:T(8,128)(2,1)S(1)} collective-permute-done((bf16[1024,128]{1,0:T(8,128)(2,1)S(1)}, bf16[1024,128]{1,0:T(8,128)(2,1)S(1)}, u32[]{:S(2)}, u32[]{:S(2)}) %collective-permute-start.12) | collective-permute-done | bytes 262176 | tf_op jit(solution)/shard_map/ppermute | solution.py:337
  37.0 3.1 %same_spin_alpha_kernel.1 = (f32[1024,128]{1,0:T(8,128)S(1)}, bf16[4096,128]{1,0:T(8,128)(2,1)S(1)}) custom-call(s32[12]{0:T(128)S(1)} %stack.60.where_ref, s32[8]{0:T(128)S(1)} %pad_add_fusion.cols_ref, bf16[1024,128]{1,0:T(8,128)(2,1)S(1)} %get-tuple-element.40.own_ref.b2, bf16[1024,128]{1,0:T(8,128)(2,1)S(1)} %collective-permute-done.11.near_ref, ...), custom_call_target="tpu_custom_call" | custom-call | flops 536870912 | bytes 5242880 | tf_op jit(solution)/shard_map/same_spin_alpha_kernel/pallas_call | solution.py:43
  40.4 4.0 %collective-permute-start.13 = (bf16[128,576]{1,0:T(8,128)(2,1)S(1)}, bf16[128,576]{1,0:T(8,128)(2,1)S(1)}, u32[]{:S(2)}, u32[]{:S(2)}) collective-permute-start(bf16[128,576]{1,0:T(8,128)(2,1)S(1)} %excited_block_kernel.1.own_ref), channel_id=1, source_target_pairs={{0,1},{1,0},{2,3},{3,2},{4,5},{5,4},{6,7},{7,6},{8,9},{9,8},{10,11... | collective-permute-start | bytes 442376 | tf_op jit(solution)/shard_map/ppermute | solution.py:26
  44.4 1.0 %collective-permute-done.13.mate_ref = bf16[128,576]{1,0:T(8,128)(2,1)S(1)} collective-permute-done((bf16[128,576]{1,0:T(8,128)(2,1)S(1)}, bf16[128,576]{1,0:T(8,128)(2,1)S(1)}, u32[]{:S(2)}, u32[]{:S(2)}) %collective-permute-start.13) | collective-permute-done | bytes 147488 | tf_op jit(solution)/shard_map/ppermute | solution.py:26
  45.5 0.5 mixed_blocks_kernel.1
  46.3 3.0 %collective-permute-start.17 = (bf16[2,128,128]{2,1,0:T(8,128)(2,1)S(1)}, bf16[2,128,128]{2,1,0:T(8,128)(2,1)S(1)}, u32[]{:S(2)}, u32[]{:S(2)}) collective-permute-start(bf16[2,128,128]{2,1,0:T(8,128)(2,1)S(1)} %get-tuple-element.67), channel_id=1, source_target_pairs={{0,24},{1,9},{8,16},{9,1},{16,8},{17,25},{24,0},{25,17},{2,26},{3,... | collective-permute-start | bytes 196616 | tf_op jit(solution)/shard_map/ppermute | solution.py:354
  49.3 3.4 %rest_of_alpha_kernel.1.same_ref = f32[1024,128]{1,0:T(8,128)S(1)} custom-call(bf16[4096,128]{1,0:T(8,128)(2,1)S(1)} %get-tuple-element.68.picked, bf16[1024,4096]{1,0:T(8,128)(2,1)} %ops_ref.5, f32[1024,128]{1,0:T(8,128)S(1)} %get-tuple-element.69.start_ref), custom_call_target="tpu_custom_call" | custom-call | flops 536870912 | bytes 5242880 | tf_op jit(solution)/shard_map/rest_of_alpha_kernel/pallas_call | solution.py:43
  52.8 1.4 %finished_kernel.1 = f32[1024,128]{1,0:T(8,128)} custom-call(s32[12]{0:T(128)S(1)} %stack.60.where_ref, f32[1024,128]{1,0:T(8,128)S(1)} %rest_of_alpha_kernel.1.same_ref, f32[2,128,128]{2,1,0:T(8,128)S(1)} %get-tuple-element.71.m0, bf16[2,128,128]{2,1,0:T(8,128)(2,1)S(1)} %collective-permute-done.15.m1, bf16[2,128,128]{2,1,0:T(8,128)(2,1)S(1)} %collective-permute-done.16.m2, ...), custom_call_target="tpu_custom_call" | custom-call | flops 262144 | bytes 2097152 | tf_op jit(solution)/shard_map/finished_kernel/pallas_call | solution.py:43
  (29 shorter events, 1.6 us)
Async XLA Ops:
  0.0 11.1 %collective-permute-start = (bf16[1024,128]{1,0:T(8,128)(2,1)}, bf16[1024,128]{1,0:T(8,128)(2,1)S(1)}, u32[]{:S(2)}, u32[]{:S(2)}) collective-permute-start(bf16[1024,128]{1,0:T(8,128)(2,1)} %coef_ref.1), channel_id=1, source_target_pairs={{0,1},{1,0},{2,3},{3,2},{4,5},{5,4},{6,7},{7,6},{8,9},{9,8},{10,11... | collective-permute-start | bytes 786440 | tf_op jit(solution)/shard_map/ppermute | solution.py:26
  3.2 7.9 %collective-permute-start.1 = (bf16[576,128]{1,0:T(8,128)(2,1)}, bf16[576,128]{1,0:T(8,128)(2,1)S(1)}, u32[]{:S(2)}, u32[]{:S(2)}) collective-permute-start(bf16[576,128]{1,0:T(8,128)(2,1)} %bitcast.21), channel_id=1, source_target_pairs={{0,1},{1,0},{2,3},{3,2},{4,5},{5,4},{6,7},{7,6},{8,9},{9,8},{10,11... | collective-permute-start | bytes 442376 | tf_op jit(solution)/shard_map/ppermute | solution.py:26
  3.2 15.5 %collective-permute-start.5 = (bf16[1024,128]{1,0:T(8,128)(2,1)}, bf16[1024,128]{1,0:T(8,128)(2,1)S(1)}, u32[]{:S(2)}, u32[]{:S(2)}) collective-permute-start(bf16[1024,128]{1,0:T(8,128)(2,1)} %coef_ref.1), channel_id=1, source_target_pairs={{0,2},{1,3},{2,4},{3,5},{4,6},{5,7},{6,8},{7,9},{8,10},{9,11},{10,... | collective-permute-start | bytes 786440 | tf_op jit(solution)/shard_map/ppermute | solution.py:31
  4.5 18.4 %collective-permute-start.6 = (bf16[1024,128]{1,0:T(8,128)(2,1)}, bf16[1024,128]{1,0:T(8,128)(2,1)S(1)}, u32[]{:S(2)}, u32[]{:S(2)}) collective-permute-start(bf16[1024,128]{1,0:T(8,128)(2,1)} %coef_ref.1), channel_id=1, source_target_pairs={{0,30},{1,31},{2,0},{3,1},{4,2},{5,3},{6,4},{7,5},{8,6},{9,7},{10,... | collective-permute-start | bytes 786440 | tf_op jit(solution)/shard_map/ppermute | solution.py:31
  12.2 10.8 %collective-permute-start.2 = (bf16[576,128]{1,0:T(8,128)(2,1)S(1)}, bf16[576,128]{1,0:T(8,128)(2,1)S(1)}, u32[]{:S(2)}, u32[]{:S(2)}) collective-permute-start(bf16[576,128]{1,0:T(8,128)(2,1)S(1)} %get-tuple-element.43), channel_id=1, source_target_pairs={{0,8},{1,25},{8,0},{9,17},{16,24},{17,9},{24,16},{25,1},{2,10},{3,... | collective-permute-start | bytes 442376 | tf_op jit(solution)/shard_map/ppermute | solution.py:328
  12.7 10.2 %collective-permute-start.3 = (bf16[576,128]{1,0:T(8,128)(2,1)S(1)}, bf16[576,128]{1,0:T(8,128)(2,1)S(1)}, u32[]{:S(2)}, u32[]{:S(2)}) collective-permute-start(bf16[576,128]{1,0:T(8,128)(2,1)S(1)} %get-tuple-element.44), channel_id=1, source_target_pairs={{0,24},{1,9},{8,16},{9,1},{16,8},{17,25},{24,0},{25,17},{2,26},{3,... | collective-permute-start | bytes 442376 | tf_op jit(solution)/shard_map/ppermute | solution.py:328
  12.7 11.7 %collective-permute-start.4 = (bf16[576,128]{1,0:T(8,128)(2,1)S(1)}, bf16[576,128]{1,0:T(8,128)(2,1)S(1)}, u32[]{:S(2)}, u32[]{:S(2)}) collective-permute-start(bf16[576,128]{1,0:T(8,128)(2,1)S(1)} %get-tuple-element.45), channel_id=1, source_target_pairs={{0,16},{1,17},{8,24},{9,25},{16,0},{17,1},{24,8},{25,9},{2,18},{3,... | collective-permute-start | bytes 442376 | tf_op jit(solution)/shard_map/ppermute | solution.py:328
  18.7 11.7 %collective-permute-start.11 = (bf16[1024,128]{1,0:T(8,128)(2,1)}, bf16[1024,128]{1,0:T(8,128)(2,1)S(1)}, u32[]{:S(2)}, u32[]{:S(2)}) collective-permute-start(bf16[1024,128]{1,0:T(8,128)(2,1)} %coef_ref.1), channel_id=1, source_target_pairs={{0,32},{32,0},{1,33},{33,1},{2,34},{34,2},{3,35},{35,3},{4,36},{36... | collective-permute-start | bytes 786440 | tf_op jit(solution)/shard_map/ppermute | solution.py:26
  24.5 8.3 %collective-permute-start.7 = (bf16[576,128]{1,0:T(8,128)(2,1)S(1)}, bf16[576,128]{1,0:T(8,128)(2,1)S(1)}, u32[]{:S(2)}, u32[]{:S(2)}) collective-permute-start(bf16[576,128]{1,0:T(8,128)(2,1)S(1)} %add_convert_fusion.1), channel_id=1, source_target_pairs={{0,2},{1,7},{2,0},{3,5},{4,6},{5,3},{6,4},{7,1},{8,10},{9,15},{10,... | collective-permute-start | bytes 442376 | tf_op jit(solution)/shard_map/ppermute | solution.py:338
  24.6 8.2 %collective-permute-start.8 = (bf16[576,128]{1,0:T(8,128)(2,1)S(1)}, bf16[576,128]{1,0:T(8,128)(2,1)S(1)}, u32[]{:S(2)}, u32[]{:S(2)}) collective-permute-start(bf16[576,128]{1,0:T(8,128)(2,1)S(1)} %get-tuple-element.53.po_ref.pair_ref), channel_id=1, source_target_pairs={{0,8},{1,25},{8,0},{9,17},{16,24},{17,9},{24,16},{25,1},{2,10},{3,... | collective-permute-start | bytes 442376 | tf_op jit(solution)/shard_map/ppermute | solution.py:340
  30.3 2.6 %collective-permute-start.9 = (bf16[1024,128]{1,0:T(8,128)(2,1)S(1)}, bf16[1024,128]{1,0:T(8,128)(2,1)S(1)}, u32[]{:S(2)}, u32[]{:S(2)}) collective-permute-start(bf16[1024,128]{1,0:T(8,128)(2,1)S(1)} %broadcast_select_fusion), channel_id=1, source_target_pairs={{0,1},{1,0},{2,3},{3,2},{4,5},{5,4},{6,7},{7,6},{8,9},{9,8},{10,11... | collective-permute-start | bytes 786440 | tf_op jit(solution)/shard_map/ppermute | solution.py:26
  30.4 6.5 %collective-permute-start.12 = (bf16[1024,128]{1,0:T(8,128)(2,1)S(1)}, bf16[1024,128]{1,0:T(8,128)(2,1)S(1)}, u32[]{:S(2)}, u32[]{:S(2)}) collective-permute-start(bf16[1024,128]{1,0:T(8,128)(2,1)S(1)} %collective-permute-done.11.near_ref), channel_id=1, source_target_pairs={{0,64},{32,224},{64,128},{96,32},{128,192},{160,96},{192,0},{224,1... | collective-permute-start | bytes 786440 | tf_op jit(solution)/shard_map/ppermute | solution.py:337
  32.9 7.2 %collective-permute-start.10 = (bf16[576,128]{1,0:T(8,128)(2,1)S(1)}, bf16[576,128]{1,0:T(8,128)(2,1)S(1)}, u32[]{:S(2)}, u32[]{:S(2)}) collective-permute-start(bf16[576,128]{1,0:T(8,128)(2,1)S(1)} %add_convert_fusion.near_ref), channel_id=1, source_target_pairs={{0,6},{1,3},{2,4},{3,1},{4,2},{5,7},{6,0},{7,5},{8,14},{9,11},{10,... | collective-permute-start | bytes 442376 | tf_op jit(solution)/shard_map/ppermute | solution.py:346
  33.3 11.1 %collective-permute-start.14 = (bf16[2,576,128]{2,1,0:T(8,128)(2,1)S(1)}, bf16[2,576,128]{2,1,0:T(8,128)(2,1)S(1)}, u32[]{:S(2)}, u32[]{:S(2)}) collective-permute-start(bf16[2,576,128]{2,1,0:T(8,128)(2,1)S(1)} %pad_maximum_fusion), channel_id=1, source_target_pairs={{0,24},{1,9},{8,16},{9,1},{16,8},{17,25},{24,0},{25,17},{2,26},{3,... | collective-permute-start | bytes 884744 | tf_op jit(solution)/shard_map/ppermute | solution.py:345
  40.0 12.7 %copy-start = (f32[1024,128]{1,0:T(8,128)S(1)}, f32[1024,128]{1,0:T(8,128)}, u32[]{:S(2)}) copy-start(f32[1024,128]{1,0:T(8,128)} %den_ref.1) | copy-start | bytes 1572868
  40.4 5.0 %collective-permute-start.13 = (bf16[128,576]{1,0:T(8,128)(2,1)S(1)}, bf16[128,576]{1,0:T(8,128)(2,1)S(1)}, u32[]{:S(2)}, u32[]{:S(2)}) collective-permute-start(bf16[128,576]{1,0:T(8,128)(2,1)S(1)} %excited_block_kernel.1.own_ref), channel_id=1, source_target_pairs={{0,1},{1,0},{2,3},{3,2},{4,5},{5,4},{6,7},{7,6},{8,9},{9,8},{10,11... | collective-permute-start | bytes 442376 | tf_op jit(solution)/shard_map/ppermute | solution.py:26
  46.0 6.8 %collective-permute-start.15 = (bf16[2,128,128]{2,1,0:T(8,128)(2,1)S(1)}, bf16[2,128,128]{2,1,0:T(8,128)(2,1)S(1)}, u32[]{:S(2)}, u32[]{:S(2)}) collective-permute-start(bf16[2,128,128]{2,1,0:T(8,128)(2,1)S(1)} %get-tuple-element.65), channel_id=1, source_target_pairs={{0,8},{1,25},{8,0},{9,17},{16,24},{17,9},{24,16},{25,1},{2,10},{3,... | collective-permute-start | bytes 196616 | tf_op jit(solution)/shard_map/ppermute | solution.py:354
  46.1 6.7 %collective-permute-start.16 = (bf16[2,128,128]{2,1,0:T(8,128)(2,1)S(1)}, bf16[2,128,128]{2,1,0:T(8,128)(2,1)S(1)}, u32[]{:S(2)}, u32[]{:S(2)}) collective-permute-start(bf16[2,128,128]{2,1,0:T(8,128)(2,1)S(1)} %get-tuple-element.66), channel_id=1, source_target_pairs={{0,16},{1,17},{8,24},{9,25},{16,0},{17,1},{24,8},{25,9},{2,18},{3,... | collective-permute-start | bytes 196616 | tf_op jit(solution)/shard_map/ppermute | solution.py:354
  46.3 6.4 %collective-permute-start.17 = (bf16[2,128,128]{2,1,0:T(8,128)(2,1)S(1)}, bf16[2,128,128]{2,1,0:T(8,128)(2,1)S(1)}, u32[]{:S(2)}, u32[]{:S(2)}) collective-permute-start(bf16[2,128,128]{2,1,0:T(8,128)(2,1)S(1)} %get-tuple-element.67), channel_id=1, source_target_pairs={{0,24},{1,9},{8,16},{9,1},{16,8},{17,25},{24,0},{25,17},{2,26},{3,... | collective-permute-start | bytes 196616 | tf_op jit(solution)/shard_map/ppermute | solution.py:354

commit v19 on v16

--- a/solution.py
+++ b/solution.py
@@ -216,11 +216,11 @@
     )[0]
 
 
-def alpha_rows(ops_ref, picked, start_ref, out_ref, ops_v, sems, part, select):
+def alpha_rows(ops_ref, picked, start_ref, out_ref, ops_v, sems, first, select):
     step = ops_v.shape[1]
-    half = start_ref.shape[0] // 2
-    mine = range(part * half, (part + 1) * half, step)
-    rest = slice((1 - part) * half, (2 - part) * half)
+    last = first + ops_v.shape[0] * step
+    mine = range(first, last, step)
+    rest = slice(last, None) if first == 0 else slice(0, first)
     copies = [
         pltpu.make_async_copy(ops_ref.at[r : r + step, :], ops_v.at[n], sems.at[n])
         for n, r in enumerate(mine)
@@ -261,7 +261,7 @@
         (where, cols, *blocks, alpha_ops, start),
         [SMEM, SMEM] + [VMEM] * 3 + [HBM, VMEM],
         (rows * width * depth * 4, 5 * MIB),
-        [pltpu.VMEM((4, rows // 8, span), BF16), pltpu.SemaphoreType.DMA((4,))],
+        [pltpu.VMEM((3, rows // 8, span), BF16), pltpu.SemaphoreType.DMA((3,))],
     )
 
 
@@ -270,7 +270,7 @@
     span = alpha_ops.shape[1]
 
     def rest_of_alpha_kernel(picked, ops_ref, start_ref, out_ref, ops_v, sems):
-        alpha_rows(ops_ref, picked, start_ref, out_ref, ops_v, sems, 1, lambda: None)
+        alpha_rows(ops_ref, picked, start_ref, out_ref, ops_v, sems, rows - 5 * (rows // 8), lambda: None)
 
     return call(
         rest_of_alpha_kernel,
@@ -278,7 +278,7 @@
         (picked, alpha_ops, start),
         [VMEM, HBM, VMEM],
         (rows * width * span, 5 * MIB),
-        [pltpu.VMEM((4, rows // 8, span), BF16), pltpu.SemaphoreType.DMA((4,))],
+        [pltpu.VMEM((5, rows // 8, span), BF16), pltpu.SemaphoreType.DMA((5,))],
     )[0]
 
 

time: 55.2 us -> 54.8 us (level)
  transfers between devices with their start and end apart: 18 -> 18, of which waited for: 5 -> 4; matrix products, arithmetic and copies ran while one was open for 2% -> 2% of each run, Pallas kernels for 20% -> 20%
where the time goes in v19:
time: 54.8 us; the launch traced here: 54.3 us
  starting transfers between devices  34.6 us (63%)
  Pallas kernels  12.9 us (24%)
  waiting for transfers between devices  5.36 us (10%)
  other arithmetic  0.93 us (2%)
    pallas_call x8, Pallas kernels, call(): pl.pallas_call(kernel, out_shape=outs, in_specs=specs, out_specs=out_spec...  12.9 us
    ppermute x5, starting transfers between devices, swapped(): return lax.ppermute(block, axis, [(i, i ^ mask) for i in range(count)])  11.7 us
    ppermute x2, starting transfers between devices, rotated(): lax.ppermute(block, axis, [(i, (i + distance) % count) for i in range(cou...  6.74 us
    ppermute x1, starting transfers between devices, local(): beside = lax.ppermute(sent, ('y', 'c'), turns[1])  5.66 us
    ppermute x3, starting transfers between devices, local(): got = [lax.ppermute(parts[k], ('y', 'c'), turns[k]) for k in (1, 3, 2)]  3.95 us
    ppermute x3, starting transfers between devices, local(): back = [lax.ppermute(out[k - 1], ('y', 'c'), turns[k]) for k in (1, 2, 3)]  3.33 us
    ppermute x1, waiting for transfers between devices, local(): far = lax.ppermute(near, ALPHA, route)  1.69 us
    ppermute x3, waiting for transfers between devices, local(): got = [lax.ppermute(parts[k], ('y', 'c'), turns[k]) for k in (1, 3, 2)]  1.51 us
  transfers between devices with their start and end apart: 18, of which 4 were waited for; matrix products, arithmetic and copies ran while one was open for 2% of the time, Pallas kernels for 20%

profile of v19, /device:TPU:1, one launch (start us, length us, event | category | flops | bytes accessed | tf_op | source)
XLA Modules:
  0.0 54.3 jit_solution(6933838922653007306)
XLA Ops:
  0.0 3.2 %collective-permute-start = (bf16[1024,128]{1,0:T(8,128)(2,1)}, bf16[1024,128]{1,0:T(8,128)(2,1)S(1)}, u32[]{:S(2)}, u32[]{:S(2)}) collective-permute-start(bf16[1024,128]{1,0:T(8,128)(2,1)} %coef_ref.1), channel_id=1, source_target_pairs={{0,1},{1,0},{2,3},{3,2},{4,5},{5,4},{6,7},{7,6},{8,9},{9,8},{10,11... | collective-permute-start | bytes 786440 | tf_op jit(solution)/shard_map/ppermute | solution.py:26
  3.2 1.3 %collective-permute-start.5 = (bf16[1024,128]{1,0:T(8,128)(2,1)}, bf16[1024,128]{1,0:T(8,128)(2,1)S(1)}, u32[]{:S(2)}, u32[]{:S(2)}) collective-permute-start(bf16[1024,128]{1,0:T(8,128)(2,1)} %coef_ref.1), channel_id=1, source_target_pairs={{0,2},{1,3},{2,4},{3,5},{4,6},{5,7},{6,8},{7,9},{8,10},{9,11},{10,... | collective-permute-start | bytes 786440 | tf_op jit(solution)/shard_map/ppermute | solution.py:31
  4.5 5.5 %collective-permute-start.6 = (bf16[1024,128]{1,0:T(8,128)(2,1)}, bf16[1024,128]{1,0:T(8,128)(2,1)S(1)}, u32[]{:S(2)}, u32[]{:S(2)}) collective-permute-start(bf16[1024,128]{1,0:T(8,128)(2,1)} %coef_ref.1), channel_id=1, source_target_pairs={{0,30},{1,31},{2,0},{3,1},{4,2},{5,3},{6,4},{7,5},{8,6},{9,7},{10,... | collective-permute-start | bytes 786440 | tf_op jit(solution)/shard_map/ppermute | solution.py:31
  10.1 1.9 %density_parts_kernel.1 = (bf16[576,128]{1,0:T(8,128)(2,1)S(1)}, bf16[576,128]{1,0:T(8,128)(2,1)S(1)}, bf16[576,128]{1,0:T(8,128)(2,1)S(1)}, bf16[576,128]{1,0:T...) custom-call(s32[12]{0:T(128)S(1)} %stack.60.where_ref, bf16[1024,128]{1,0:T(8,128)(2,1)} %coef_ref.1, ...), custom_call_target="tpu_custom_call" | custom-call | flops 150994944 | bytes 1048576 | tf_op jit(solution)/shard_map/density_parts_kernel/pallas_call | solution.py:43
  12.0 0.6 %collective-permute-start.2 = (bf16[576,128]{1,0:T(8,128)(2,1)S(1)}, bf16[576,128]{1,0:T(8,128)(2,1)S(1)}, u32[]{:S(2)}, u32[]{:S(2)}) collective-permute-start(bf16[576,128]{1,0:T(8,128)(2,1)S(1)} %get-tuple-element.41), channel_id=1, source_target_pairs={{0,8},{1,25},{8,0},{9,17},{16,24},{17,9},{24,16},{25,1},{2,10},{3,... | collective-permute-start | bytes 442376 | tf_op jit(solution)/shard_map/ppermute | solution.py:320
  12.5 3.4 %collective-permute-start.4 = (bf16[576,128]{1,0:T(8,128)(2,1)S(1)}, bf16[576,128]{1,0:T(8,128)(2,1)S(1)}, u32[]{:S(2)}, u32[]{:S(2)}) collective-permute-start(bf16[576,128]{1,0:T(8,128)(2,1)S(1)} %get-tuple-element.43), channel_id=1, source_target_pairs={{0,16},{1,17},{8,24},{9,25},{16,0},{17,1},{24,8},{25,9},{2,18},{3,... | collective-permute-start | bytes 442376 | tf_op jit(solution)/shard_map/ppermute | solution.py:320
  15.9 0.7 %pad_add_fusion.cols_ref = s32[8]{0:T(128)S(1)} fusion(s32[4]{0:T(128)} %bitcast.23, s32[4]{0:T(128)} %bitcast.24), kind=kLoop, calls=%fused_computation.4 | loop fusion | flops 8 | bytes 64 | tf_op jit(solution)/shard_map/concatenate | solution.py:303
  16.7 1.8 %staged_kernel.1 = (bf16[576,576]{1,0:T(8,128)(2,1)S(1)}, f32[128,576]{1,0:T(8,128)S(1)}, bf16[128,640]{1,0:T(8,128)(2,1)S(1)}) custom-call(s32[12]{0:T(128)S(1)} %stack.60.where_ref, s32[8]{0:T(128)S(1)} %pad_add_fusion.cols_ref, bf16[576,576]{1,0:T(8,128)(2,1)} %c_ref.1, bf16[576,1024]{1,0:T(8,128)(2,1)} %bitcast.20, bf16[128,512]{1,0:T(8,128)(2,1)} %ops_ref.3, ...), custom_call_target="tpu_custom_call" | custom-call | flops 331776 | bytes 2097152 | tf_op jit(solution)/shard_map/staged_kernel/pallas_call | solution.py:43
  18.5 4.4 %collective-permute-start.11 = (bf16[1024,128]{1,0:T(8,128)(2,1)}, bf16[1024,128]{1,0:T(8,128)(2,1)S(1)}, u32[]{:S(2)}, u32[]{:S(2)}) collective-permute-start(bf16[1024,128]{1,0:T(8,128)(2,1)} %coef_ref.1), channel_id=1, source_target_pairs={{0,32},{32,0},{1,33},{33,1},{2,34},{34,2},{3,35},{35,3},{4,36},{36... | collective-permute-start | bytes 786440 | tf_op jit(solution)/shard_map/ppermute | solution.py:26
  22.9 1.5 %collective-permute-done.4 = bf16[576,128]{1,0:T(8,128)(2,1)S(1)} collective-permute-done((bf16[576,128]{1,0:T(8,128)(2,1)S(1)}, bf16[576,128]{1,0:T(8,128)(2,1)S(1)}, u32[]{:S(2)}, u32[]{:S(2)}) %collective-permute-start.4) | collective-permute-done | bytes 147488 | tf_op jit(solution)/shard_map/ppermute | solution.py:320
  24.6 5.7 %collective-permute-start.8 = (bf16[576,128]{1,0:T(8,128)(2,1)S(1)}, bf16[576,128]{1,0:T(8,128)(2,1)S(1)}, u32[]{:S(2)}, u32[]{:S(2)}) collective-permute-start(bf16[576,128]{1,0:T(8,128)(2,1)S(1)} %get-tuple-element.52.pair_ref), channel_id=1, source_target_pairs={{0,8},{1,25},{8,0},{9,17},{16,24},{17,9},{24,16},{25,1},{2,10},{3,... | collective-permute-start | bytes 442376 | tf_op jit(solution)/shard_map/ppermute | solution.py:332
  30.4 1.3 %collective-permute-start.12 = (bf16[1024,128]{1,0:T(8,128)(2,1)S(1)}, bf16[1024,128]{1,0:T(8,128)(2,1)S(1)}, u32[]{:S(2)}, u32[]{:S(2)}) collective-permute-start(bf16[1024,128]{1,0:T(8,128)(2,1)S(1)} %collective-permute-done.11.near_ref), channel_id=1, source_target_pairs={{0,64},{32,224},{64,128},{96,32},{128,192},{160,96},{192,0},{224,1... | collective-permute-start | bytes 786440 | tf_op jit(solution)/shard_map/ppermute | solution.py:329
  31.7 1.1 %collective-permute-done.8.beside_ref = bf16[576,128]{1,0:T(8,128)(2,1)S(1)} collective-permute-done((bf16[576,128]{1,0:T(8,128)(2,1)S(1)}, bf16[576,128]{1,0:T(8,128)(2,1)S(1)}, u32[]{:S(2)}, u32[]{:S(2)}) %collective-permute-start.8) | collective-permute-done | bytes 147488 | tf_op jit(solution)/shard_map/ppermute | solution.py:332
  33.3 1.4 %collective-permute-start.14 = (bf16[2,576,128]{2,1,0:T(8,128)(2,1)S(1)}, bf16[2,576,128]{2,1,0:T(8,128)(2,1)S(1)}, u32[]{:S(2)}, u32[]{:S(2)}) collective-permute-start(bf16[2,576,128]{2,1,0:T(8,128)(2,1)S(1)} %pad_maximum_fusion), channel_id=1, source_target_pairs={{0,24},{1,9},{8,16},{9,1},{16,8},{17,25},{24,0},{25,17},{2,26},{3,... | collective-permute-start | bytes 884744 | tf_op jit(solution)/shard_map/ppermute | solution.py:337
  34.7 0.5 same_spin_beta_kernel.1.start_ref
  35.3 1.7 %collective-permute-done.12.far_ref = bf16[1024,128]{1,0:T(8,128)(2,1)S(1)} collective-permute-done((bf16[1024,128]{1,0:T(8,128)(2,1)S(1)}, bf16[1024,128]{1,0:T(8,128)(2,1)S(1)}, u32[]{:S(2)}, u32[]{:S(2)}) %collective-permute-start.12) | collective-permute-done | bytes 262176 | tf_op jit(solution)/shard_map/ppermute | solution.py:329
  36.9 3.1 %same_spin_alpha_kernel.1 = (f32[1024,128]{1,0:T(8,128)S(1)}, bf16[4096,128]{1,0:T(8,128)(2,1)S(1)}) custom-call(s32[12]{0:T(128)S(1)} %stack.60.where_ref, s32[8]{0:T(128)S(1)} %pad_add_fusion.cols_ref, bf16[1024,128]{1,0:T(8,128)(2,1)S(1)} %get-tuple-element.57.b2.own_ref, bf16[1024,128]{1,0:T(8,128)(2,1)S(1)} %collective-permute-done.11.near_ref, ...), custom_call_target="tpu_custom_call" | custom-call | flops 536870912 | bytes 5242880 | tf_op jit(solution)/shard_map/same_spin_alpha_kernel/pallas_call | solution.py:43
  40.4 3.9 %collective-permute-start.13 = (bf16[128,576]{1,0:T(8,128)(2,1)S(1)}, bf16[128,576]{1,0:T(8,128)(2,1)S(1)}, u32[]{:S(2)}, u32[]{:S(2)}) collective-permute-start(bf16[128,576]{1,0:T(8,128)(2,1)S(1)} %excited_block_kernel.1.own_ref), channel_id=1, source_target_pairs={{0,1},{1,0},{2,3},{3,2},{4,5},{5,4},{6,7},{7,6},{8,9},{9,8},{10,11... | collective-permute-start | bytes 442376 | tf_op jit(solution)/shard_map/ppermute | solution.py:26
  44.4 1.0 %collective-permute-done.13.mate_ref = bf16[128,576]{1,0:T(8,128)(2,1)S(1)} collective-permute-done((bf16[128,576]{1,0:T(8,128)(2,1)S(1)}, bf16[128,576]{1,0:T(8,128)(2,1)S(1)}, u32[]{:S(2)}, u32[]{:S(2)}) %collective-permute-start.13) | collective-permute-done | bytes 147488 | tf_op jit(solution)/shard_map/ppermute | solution.py:26
  45.4 0.5 mixed_blocks_kernel.1
  46.0 0.5 collective-permute-start.16
  46.5 2.7 %collective-permute-start.17 = (bf16[2,128,128]{2,1,0:T(8,128)(2,1)S(1)}, bf16[2,128,128]{2,1,0:T(8,128)(2,1)S(1)}, u32[]{:S(2)}, u32[]{:S(2)}) collective-permute-start(bf16[2,128,128]{2,1,0:T(8,128)(2,1)S(1)} %get-tuple-element.67), channel_id=1, source_target_pairs={{0,24},{1,9},{8,16},{9,1},{16,8},{17,25},{24,0},{25,17},{2,26},{3,... | collective-permute-start | bytes 196616 | tf_op jit(solution)/shard_map/ppermute | solution.py:346
  49.2 3.4 %rest_of_alpha_kernel.1.same_ref = f32[1024,128]{1,0:T(8,128)S(1)} custom-call(bf16[4096,128]{1,0:T(8,128)(2,1)S(1)} %get-tuple-element.68.picked, bf16[1024,4096]{1,0:T(8,128)(2,1)} %ops_ref.5, f32[1024,128]{1,0:T(8,128)S(1)} %get-tuple-element.69.start_ref), custom_call_target="tpu_custom_call" | custom-call | flops 536870912 | bytes 5242880 | tf_op jit(solution)/shard_map/rest_of_alpha_kernel/pallas_call | solution.py:43
  52.7 1.4 %finished_kernel.1 = f32[1024,128]{1,0:T(8,128)} custom-call(s32[12]{0:T(128)S(1)} %stack.60.where_ref, f32[1024,128]{1,0:T(8,128)S(1)} %rest_of_alpha_kernel.1.same_ref, f32[2,128,128]{2,1,0:T(8,128)S(1)} %get-tuple-element.71.m0, bf16[2,128,128]{2,1,0:T(8,128)(2,1)S(1)} %collective-permute-done.15.m1, bf16[2,128,128]{2,1,0:T(8,128)(2,1)S(1)} %collective-permute-done.16.m2, ...), custom_call_target="tpu_custom_call" | custom-call | flops 262144 | bytes 2097152 | tf_op jit(solution)/shard_map/finished_kernel/pallas_call | solution.py:43
  (28 shorter events, 1.4 us)
Async XLA Ops:
  0.0 10.1 %collective-permute-start = (bf16[1024,128]{1,0:T(8,128)(2,1)}, bf16[1024,128]{1,0:T(8,128)(2,1)S(1)}, u32[]{:S(2)}, u32[]{:S(2)}) collective-permute-start(bf16[1024,128]{1,0:T(8,128)(2,1)} %coef_ref.1), channel_id=1, source_target_pairs={{0,1},{1,0},{2,3},{3,2},{4,5},{5,4},{6,7},{7,6},{8,9},{9,8},{10,11... | collective-permute-start | bytes 786440 | tf_op jit(solution)/shard_map/ppermute | solution.py:26
  3.2 6.8 %collective-permute-start.1 = (bf16[576,128]{1,0:T(8,128)(2,1)}, bf16[576,128]{1,0:T(8,128)(2,1)S(1)}, u32[]{:S(2)}, u32[]{:S(2)}) collective-permute-start(bf16[576,128]{1,0:T(8,128)(2,1)} %bitcast.21), channel_id=1, source_target_pairs={{0,1},{1,0},{2,3},{3,2},{4,5},{5,4},{6,7},{7,6},{8,9},{9,8},{10,11... | collective-permute-start | bytes 442376 | tf_op jit(solution)/shard_map/ppermute | solution.py:26
  3.2 15.3 %collective-permute-start.5 = (bf16[1024,128]{1,0:T(8,128)(2,1)}, bf16[1024,128]{1,0:T(8,128)(2,1)S(1)}, u32[]{:S(2)}, u32[]{:S(2)}) collective-permute-start(bf16[1024,128]{1,0:T(8,128)(2,1)} %coef_ref.1), channel_id=1, source_target_pairs={{0,2},{1,3},{2,4},{3,5},{4,6},{5,7},{6,8},{7,9},{8,10},{9,11},{10,... | collective-permute-start | bytes 786440 | tf_op jit(solution)/shard_map/ppermute | solution.py:31
  4.5 18.4 %collective-permute-start.6 = (bf16[1024,128]{1,0:T(8,128)(2,1)}, bf16[1024,128]{1,0:T(8,128)(2,1)S(1)}, u32[]{:S(2)}, u32[]{:S(2)}) collective-permute-start(bf16[1024,128]{1,0:T(8,128)(2,1)} %coef_ref.1), channel_id=1, source_target_pairs={{0,30},{1,31},{2,0},{3,1},{4,2},{5,3},{6,4},{7,5},{8,6},{9,7},{10,... | collective-permute-start | bytes 786440 | tf_op jit(solution)/shard_map/ppermute | solution.py:31
  12.0 10.9 %collective-permute-start.2 = (bf16[576,128]{1,0:T(8,128)(2,1)S(1)}, bf16[576,128]{1,0:T(8,128)(2,1)S(1)}, u32[]{:S(2)}, u32[]{:S(2)}) collective-permute-start(bf16[576,128]{1,0:T(8,128)(2,1)S(1)} %get-tuple-element.41), channel_id=1, source_target_pairs={{0,8},{1,25},{8,0},{9,17},{16,24},{17,9},{24,16},{25,1},{2,10},{3,... | collective-permute-start | bytes 442376 | tf_op jit(solution)/shard_map/ppermute | solution.py:320
  12.5 10.4 %collective-permute-start.3 = (bf16[576,128]{1,0:T(8,128)(2,1)S(1)}, bf16[576,128]{1,0:T(8,128)(2,1)S(1)}, u32[]{:S(2)}, u32[]{:S(2)}) collective-permute-start(bf16[576,128]{1,0:T(8,128)(2,1)S(1)} %get-tuple-element.42), channel_id=1, source_target_pairs={{0,24},{1,9},{8,16},{9,1},{16,8},{17,25},{24,0},{25,17},{2,26},{3,... | collective-permute-start | bytes 442376 | tf_op jit(solution)/shard_map/ppermute | solution.py:320
  12.5 11.9 %collective-permute-start.4 = (bf16[576,128]{1,0:T(8,128)(2,1)S(1)}, bf16[576,128]{1,0:T(8,128)(2,1)S(1)}, u32[]{:S(2)}, u32[]{:S(2)}) collective-permute-start(bf16[576,128]{1,0:T(8,128)(2,1)S(1)} %get-tuple-element.43), channel_id=1, source_target_pairs={{0,16},{1,17},{8,24},{9,25},{16,0},{17,1},{24,8},{25,9},{2,18},{3,... | collective-permute-start | bytes 442376 | tf_op jit(solution)/shard_map/ppermute | solution.py:320
  18.5 11.9 %collective-permute-start.11 = (bf16[1024,128]{1,0:T(8,128)(2,1)}, bf16[1024,128]{1,0:T(8,128)(2,1)S(1)}, u32[]{:S(2)}, u32[]{:S(2)}) collective-permute-start(bf16[1024,128]{1,0:T(8,128)(2,1)} %coef_ref.1), channel_id=1, source_target_pairs={{0,32},{32,0},{1,33},{33,1},{2,34},{34,2},{3,35},{35,3},{4,36},{36... | collective-permute-start | bytes 786440 | tf_op jit(solution)/shard_map/ppermute | solution.py:26
  24.5 8.3 %collective-permute-start.7 = (bf16[576,128]{1,0:T(8,128)(2,1)S(1)}, bf16[576,128]{1,0:T(8,128)(2,1)S(1)}, u32[]{:S(2)}, u32[]{:S(2)}) collective-permute-start(bf16[576,128]{1,0:T(8,128)(2,1)S(1)} %add_convert_fusion.1), channel_id=1, source_target_pairs={{0,2},{1,7},{2,0},{3,5},{4,6},{5,3},{6,4},{7,1},{8,10},{9,15},{10,... | collective-permute-start | bytes 442376 | tf_op jit(solution)/shard_map/ppermute | solution.py:330
  24.6 8.2 %collective-permute-start.8 = (bf16[576,128]{1,0:T(8,128)(2,1)S(1)}, bf16[576,128]{1,0:T(8,128)(2,1)S(1)}, u32[]{:S(2)}, u32[]{:S(2)}) collective-permute-start(bf16[576,128]{1,0:T(8,128)(2,1)S(1)} %get-tuple-element.52.pair_ref), channel_id=1, source_target_pairs={{0,8},{1,25},{8,0},{9,17},{16,24},{17,9},{24,16},{25,1},{2,10},{3,... | collective-permute-start | bytes 442376 | tf_op jit(solution)/shard_map/ppermute | solution.py:332
  30.3 2.6 %collective-permute-start.9 = (bf16[1024,128]{1,0:T(8,128)(2,1)S(1)}, bf16[1024,128]{1,0:T(8,128)(2,1)S(1)}, u32[]{:S(2)}, u32[]{:S(2)}) collective-permute-start(bf16[1024,128]{1,0:T(8,128)(2,1)S(1)} %broadcast_select_fusion), channel_id=1, source_target_pairs={{0,1},{1,0},{2,3},{3,2},{4,5},{5,4},{6,7},{7,6},{8,9},{9,8},{10,11... | collective-permute-start | bytes 786440 | tf_op jit(solution)/shard_map/ppermute | solution.py:26
  30.4 6.5 %collective-permute-start.12 = (bf16[1024,128]{1,0:T(8,128)(2,1)S(1)}, bf16[1024,128]{1,0:T(8,128)(2,1)S(1)}, u32[]{:S(2)}, u32[]{:S(2)}) collective-permute-start(bf16[1024,128]{1,0:T(8,128)(2,1)S(1)} %collective-permute-done.11.near_ref), channel_id=1, source_target_pairs={{0,64},{32,224},{64,128},{96,32},{128,192},{160,96},{192,0},{224,1... | collective-permute-start | bytes 786440 | tf_op jit(solution)/shard_map/ppermute | solution.py:329
  32.9 7.2 %collective-permute-start.10 = (bf16[576,128]{1,0:T(8,128)(2,1)S(1)}, bf16[576,128]{1,0:T(8,128)(2,1)S(1)}, u32[]{:S(2)}, u32[]{:S(2)}) collective-permute-start(bf16[576,128]{1,0:T(8,128)(2,1)S(1)} %add_convert_fusion.near_ref), channel_id=1, source_target_pairs={{0,6},{1,3},{2,4},{3,1},{4,2},{5,7},{6,0},{7,5},{8,14},{9,11},{10,... | collective-permute-start | bytes 442376 | tf_op jit(solution)/shard_map/ppermute | solution.py:338
  33.3 11.0 %collective-permute-start.14 = (bf16[2,576,128]{2,1,0:T(8,128)(2,1)S(1)}, bf16[2,576,128]{2,1,0:T(8,128)(2,1)S(1)}, u32[]{:S(2)}, u32[]{:S(2)}) collective-permute-start(bf16[2,576,128]{2,1,0:T(8,128)(2,1)S(1)} %pad_maximum_fusion), channel_id=1, source_target_pairs={{0,24},{1,9},{8,16},{9,1},{16,8},{17,25},{24,0},{25,17},{2,26},{3,... | collective-permute-start | bytes 884744 | tf_op jit(solution)/shard_map/ppermute | solution.py:337
  40.0 12.7 %copy-start = (f32[1024,128]{1,0:T(8,128)S(1)}, f32[1024,128]{1,0:T(8,128)}, u32[]{:S(2)}) copy-start(f32[1024,128]{1,0:T(8,128)} %den_ref.1) | copy-start | bytes 1572868
  40.4 5.0 %collective-permute-start.13 = (bf16[128,576]{1,0:T(8,128)(2,1)S(1)}, bf16[128,576]{1,0:T(8,128)(2,1)S(1)}, u32[]{:S(2)}, u32[]{:S(2)}) collective-permute-start(bf16[128,576]{1,0:T(8,128)(2,1)S(1)} %excited_block_kernel.1.own_ref), channel_id=1, source_target_pairs={{0,1},{1,0},{2,3},{3,2},{4,5},{5,4},{6,7},{7,6},{8,9},{9,8},{10,11... | collective-permute-start | bytes 442376 | tf_op jit(solution)/shard_map/ppermute | solution.py:26
  45.9 6.8 %collective-permute-start.15 = (bf16[2,128,128]{2,1,0:T(8,128)(2,1)S(1)}, bf16[2,128,128]{2,1,0:T(8,128)(2,1)S(1)}, u32[]{:S(2)}, u32[]{:S(2)}) collective-permute-start(bf16[2,128,128]{2,1,0:T(8,128)(2,1)S(1)} %get-tuple-element.65), channel_id=1, source_target_pairs={{0,8},{1,25},{8,0},{9,17},{16,24},{17,9},{24,16},{25,1},{2,10},{3,... | collective-permute-start | bytes 196616 | tf_op jit(solution)/shard_map/ppermute | solution.py:346
  46.0 6.7 %collective-permute-start.16 = (bf16[2,128,128]{2,1,0:T(8,128)(2,1)S(1)}, bf16[2,128,128]{2,1,0:T(8,128)(2,1)S(1)}, u32[]{:S(2)}, u32[]{:S(2)}) collective-permute-start(bf16[2,128,128]{2,1,0:T(8,128)(2,1)S(1)} %get-tuple-element.66), channel_id=1, source_target_pairs={{0,16},{1,17},{8,24},{9,25},{16,0},{17,1},{24,8},{25,9},{2,18},{3,... | collective-permute-start | bytes 196616 | tf_op jit(solution)/shard_map/ppermute | solution.py:346
  46.5 6.2 %collective-permute-start.17 = (bf16[2,128,128]{2,1,0:T(8,128)(2,1)S(1)}, bf16[2,128,128]{2,1,0:T(8,128)(2,1)S(1)}, u32[]{:S(2)}, u32[]{:S(2)}) collective-permute-start(bf16[2,128,128]{2,1,0:T(8,128)(2,1)S(1)} %get-tuple-element.67), channel_id=1, source_target_pairs={{0,24},{1,9},{8,16},{9,1},{16,8},{17,25},{24,0},{25,17},{2,26},{3,... | collective-permute-start | bytes 196616 | tf_op jit(solution)/shard_map/ppermute | solution.py:346
